TPU v7x, 32 devices: a whole 2x2x4 slice. The times are simulated.
32 devices in a mesh: seq: 8 (over z, core), batch: 4 (over y, x).
Axes of the slice: x: 2, y: 2, z: 4, core: 2. Of those that a mesh axis runs over, the one named last changes fastest.
Arguments:
- tokens: bfloat16 [8, 512, 2048], P('batch', 'seq'), may hold values from -6 to 6
- lengths: int32 [8], P('batch'), may hold values from 256 to 512, as said below
- key_mask: int32 [8, 512], P('batch', 'seq'), may hold values 0 or 1
- top_experts: int32 [8, 512, 4], P('batch', 'seq'), may hold values from 0 to 7, all different within a row
- attn_gain: bfloat16 [2048], P(('seq', 'batch')), may hold values from 0.5 to 2
- query_gain: bfloat16 [2048], P(('seq', 'batch')), may hold values from 0.59765625 to 1.59375
- key_gain: bfloat16 [2048], P(('seq', 'batch')), may hold values from 0.59765625 to 1.59375
- mlp_gain: bfloat16 [2048], P(('seq', 'batch')), may hold values from 0.5 to 2
- w_query: bfloat16 [2048, 2048], P(('seq', 'batch')), may hold values from -0.125 to 0.125
- w_key: bfloat16 [2048, 2048], P(('seq', 'batch')), may hold values from -0.125 to 0.125
- w_value: bfloat16 [2048, 2048], P(('seq', 'batch')), may hold values from -0.125 to 0.125
- w_out: bfloat16 [2048, 2048], P(('seq', 'batch')), may hold values from -1 to 1
- w_router: bfloat16 [2048, 8], P(('seq', 'batch')), may hold values from -0.0625 to 0.0625
- expert_gate: bfloat16 [8, 2048, 1024], P('batch', 'seq'), may hold values from -0.125 to 0.125
- expert_up: bfloat16 [8, 2048, 1024], P('batch', 'seq'), may hold values from -0.125 to 0.125
- expert_down: bfloat16 [8, 1024, 2048], P('batch', 'seq'), may hold values from -1 to 1
- cotangent: bfloat16 [8, 512, 2048], P('batch', 'seq'), may hold values from -6 to 6
Outputs:
- output: bfloat16 [8, 512, 2048], P('batch', 'seq')
- grad_tokens: bfloat16 [8, 512, 2048], P('batch', 'seq')
- grad_attn_gain: float32 [2048], P(('seq', 'batch'))
- grad_query_gain: float32 [2048], P(('seq', 'batch'))
- grad_key_gain: float32 [2048], P(('seq', 'batch'))
- grad_mlp_gain: float32 [2048], P(('seq', 'batch'))
- grad_query: float32 [2048, 2048], P(('seq', 'batch'))
- grad_key: float32 [2048, 2048], P(('seq', 'batch'))
- grad_value: float32 [2048, 2048], P(('seq', 'batch'))
- grad_out: float32 [2048, 2048], P(('seq', 'batch'))
- grad_router: float32 [2048, 8], P(('seq', 'batch'))
- grad_expert_gate: float32 [8, 2048, 1024], P('batch', 'seq')
- grad_expert_up: float32 [8, 2048, 1024], P('batch', 'seq')
- grad_expert_down: float32 [8, 1024, 2048], P('batch', 'seq')
Inputs may be any that keep to these rules, and one draw needn't show every extreme that they name: `lengths`: positions at or past a row's length are padding; some row of every draw is full. `top_experts`: each token names 4 different experts.
All inputs are finite; a program needn't handle non-finite values. No bound on the sum of `key_mask` on one device may be relied on, other than what follows from the above.
Results may differ from a plain program's by a relative error of at most 0.038.
Values may be sent and summed in bfloat16 or wider, within the bound.
A program may use at most 320 MiB of HBM per device.

v0:
```python
import jax
import jax.numpy as jnp
from jax import lax
from jax.sharding import PartitionSpec as P

HEAD = 128
EXPERTS = 8


EPS = 1e-05
HIGHEST_PRECISION = lax.Precision.HIGHEST
NEGATIVE = -1e30


def norm_rows(values_in, gain_row):
    return (
        values_in
        * lax.rsqrt(jnp.mean(values_in * values_in, axis=-1, keepdims=True) + EPS)
        * gain_row
    )


def rotary_tables(positions):
    half_head = HEAD // 2
    frequency = 10000.0 ** (-2.0 * jnp.arange(half_head, dtype=jnp.float32) / HEAD)
    angles = positions.astype(jnp.float32)[:, None] * frequency[None, :]
    return (jnp.cos(angles), jnp.sin(angles))


def rotate(flat_rows, cos_part, sin_part):
    per_head = flat_rows.reshape(flat_rows.shape[0], -1, HEAD)
    half_head = HEAD // 2
    first_half = per_head[..., :half_head]
    second_half = per_head[..., half_head:]
    cos_wide = cos_part[:, None, :]
    sin_wide = sin_part[:, None, :]
    return jnp.concatenate(
        [
            first_half * cos_wide - second_half * sin_wide,
            second_half * cos_wide + first_half * sin_wide,
        ],
        axis=-1,
    )


def allowed_pairs(query_pos, key_pos, key_usable):
    causal = key_pos[None, :] <= query_pos[:, None]
    return causal & ((key_usable[None, :] > 0) | (key_pos[None, :] == query_pos[:, None]))


def fetch_layer(
    attn_gain, query_gain, key_gain, mlp_gain, w_query, w_key, w_value, w_out, w_router
):
    return (
        lax.all_gather(attn_gain, ("seq", "batch"), axis=0, tiled=True),
        lax.all_gather(query_gain, ("seq", "batch"), axis=0, tiled=True),
        lax.all_gather(key_gain, ("seq", "batch"), axis=0, tiled=True),
        lax.all_gather(mlp_gain, ("seq", "batch"), axis=0, tiled=True),
        lax.all_gather(w_query, ("seq", "batch"), axis=0, tiled=True),
        lax.all_gather(w_key, ("seq", "batch"), axis=0, tiled=True),
        lax.all_gather(w_value, ("seq", "batch"), axis=0, tiled=True),
        lax.all_gather(w_out, ("seq", "batch"), axis=0, tiled=True),
        lax.all_gather(w_router, ("seq", "batch"), axis=0, tiled=True),
    )


def fetch_experts(expert_gate, expert_up, expert_down):
    return (
        lax.all_gather(expert_gate, "seq", axis=1, tiled=True),
        lax.all_gather(expert_up, "seq", axis=1, tiled=True),
        lax.all_gather(expert_down, "seq", axis=1, tiled=True),
    )


def router_probs(normed, router_all):
    return jax.nn.softmax(jnp.dot(normed, router_all, preferred_element_type=jnp.float32), axis=-1)


def expert_forward(normed, gate_local, gate_all, up_all, down_all):
    gate_pre = jnp.einsum("td,edf->etf", normed, gate_all, preferred_element_type=jnp.float32)
    up_pre = jnp.einsum("td,edf->etf", normed, up_all, preferred_element_type=jnp.float32)
    active = (jax.nn.silu(gate_pre) * up_pre).astype(jnp.bfloat16)
    branch = jnp.einsum("etf,efd->etd", active, down_all, preferred_element_type=jnp.float32)
    mixture = jnp.sum(gate_local.T[:, :, None] * branch, axis=0)
    return (mixture, (gate_pre, up_pre, active, branch))


def expert_backward(normed, gate_local, saved, upstream, gate_all, up_all, down_all):
    gate_pre, up_pre, active, branch = saved
    grad_branch = (gate_local.T[:, :, None] * upstream[None]).astype(jnp.bfloat16)
    grad_active = jnp.einsum(
        "etd,efd->etf", grad_branch, down_all, preferred_element_type=jnp.float32
    )
    sigmoid_gate = jax.nn.sigmoid(gate_pre)
    grad_gate_pre = (
        grad_active * up_pre * sigmoid_gate * (1.0 + gate_pre * (1.0 - sigmoid_gate))
    ).astype(jnp.bfloat16)
    grad_up_pre = (grad_active * gate_pre * sigmoid_gate).astype(jnp.bfloat16)
    grad_normed = jnp.einsum(
        "etf,edf->td", grad_gate_pre, gate_all, preferred_element_type=jnp.float32
    )
    grad_normed = grad_normed + jnp.einsum(
        "etf,edf->td", grad_up_pre, up_all, preferred_element_type=jnp.float32
    )
    grad_gates = jnp.sum(upstream[None] * branch, axis=-1).T
    grad_gate_w = jnp.einsum(
        "td,etf->edf", normed, grad_gate_pre, preferred_element_type=jnp.float32
    )
    grad_up_w = jnp.einsum("td,etf->edf", normed, grad_up_pre, preferred_element_type=jnp.float32)
    grad_down_w = jnp.einsum(
        "etf,etd->efd", active, grad_branch, preferred_element_type=jnp.float32
    )
    return (grad_normed, grad_gates, (grad_gate_w, grad_up_w, grad_down_w))


def shards(
    tokens,
    lengths,
    key_mask,
    top_experts,
    attn_gain,
    query_gain,
    key_gain,
    mlp_gain,
    w_query,
    w_key,
    w_value,
    w_out,
    w_router,
    expert_gate,
    expert_up,
    expert_down,
    cotangent,
):
    micro_count = tokens.shape[0]
    tok_rows = tokens.shape[1]
    positions = lax.axis_index("seq") * tok_rows + jnp.arange(tok_rows, dtype=jnp.int32)
    cos_part, sin_part = rotary_tables(positions)
    score_scale = HEAD ** (-0.5)
    expert_ids = jnp.arange(EXPERTS, dtype=jnp.int32)
    output_rows = []
    input_grads = []
    layer_sums = None
    expert_sums = None
    for micro_index in range(micro_count):
        layer_all = fetch_layer(
            attn_gain, query_gain, key_gain, mlp_gain, w_query, w_key, w_value, w_out, w_router
        )
        gain_attn = layer_all[0].astype(jnp.float32)
        gain_query = layer_all[1].astype(jnp.float32)
        gain_key = layer_all[2].astype(jnp.float32)
        gain_mlp = layer_all[3].astype(jnp.float32)
        w_query_all, w_key_all, w_value_all, w_out_all, router_all = (
            layer_all[4],
            layer_all[5],
            layer_all[6],
            layer_all[7],
            layer_all[8],
        )
        gate_all, up_all, down_all = fetch_experts(expert_gate, expert_up, expert_down)
        inputs = tokens[micro_index].astype(jnp.float32)
        cot_rows = cotangent[micro_index]
        hidden = norm_rows(inputs, gain_attn).astype(jnp.bfloat16)
        query_pre = jnp.dot(hidden, w_query_all, preferred_element_type=jnp.float32)
        key_pre = jnp.dot(hidden, w_key_all, preferred_element_type=jnp.float32)
        value_rows = jnp.dot(hidden, w_value_all, preferred_element_type=jnp.float32).astype(
            jnp.bfloat16
        )

        def project_query(pre_rows, gain_row):
            return rotate(norm_rows(pre_rows, gain_row), cos_part, sin_part)

        queries = project_query(query_pre, gain_query).astype(jnp.bfloat16)
        key_rows = project_query(key_pre, gain_key).astype(jnp.bfloat16).reshape(tok_rows, -1)
        usable = ((positions < lengths[micro_index]) & (key_mask[micro_index] == 1)).astype(
            jnp.bfloat16
        )
        head_count = queries.shape[1]

        def piece_scores(block_data):
            piece_keys, piece_values, piece_usable = block_data
            piece_len = piece_keys.shape[0]
            key_heads = piece_keys.reshape(piece_len, head_count, HEAD)
            value_heads = piece_values.reshape(piece_len, head_count, HEAD)
            key_pos = jnp.arange(piece_len, dtype=jnp.int32)
            allowed = allowed_pairs(positions, key_pos, piece_usable)[None]
            scores = (
                jnp.einsum("qhd,khd->hqk", queries, key_heads, preferred_element_type=jnp.float32)
                * score_scale
            )
            return (jnp.where(allowed, scores, NEGATIVE), allowed, key_heads, value_heads)

        run_max = jnp.full((head_count, tok_rows), NEGATIVE, jnp.float32)
        attend_scores, attend_allowed, attend_key_heads, attend_value_heads = piece_scores(
            (
                lax.all_gather(key_rows, "seq", axis=0, tiled=True),
                lax.all_gather(value_rows, "seq", axis=0, tiled=True),
                lax.all_gather(usable, "seq", axis=0, tiled=True),
            )
        )
        new_max = jnp.maximum(run_max, jnp.max(attend_scores, axis=-1))
        exp_scores = jnp.where(attend_allowed, jnp.exp(attend_scores - new_max[..., None]), 0.0)
        run_sum = jnp.sum(exp_scores, axis=-1)
        run_acc = jnp.einsum(
            "hqk,khd->hqd",
            exp_scores.astype(jnp.bfloat16),
            attend_value_heads,
            preferred_element_type=jnp.float32,
        )
        run_max, run_sum, run_acc = (new_max, run_sum, run_acc)
        attended = jnp.transpose(run_acc / run_sum[..., None], (1, 0, 2))
        log_total = run_max + jnp.log(run_sum)
        mixed_rows = attended.astype(jnp.bfloat16).reshape(tok_rows, -1)
        residual = inputs + jnp.dot(mixed_rows, w_out_all, preferred_element_type=jnp.float32)
        normed = norm_rows(residual, gain_mlp).astype(jnp.bfloat16)
        chosen = jnp.any(top_experts[micro_index][..., None] == expert_ids, axis=-2).astype(
            jnp.float32
        )
        home_probs = router_probs(normed, router_all)
        upstream = cot_rows.astype(jnp.float32)
        shared_rows, shared_chosen, shared_cot = (
            lax.all_gather(normed, "batch", axis=0, tiled=True),
            lax.all_gather(chosen.astype(jnp.bfloat16), "batch", axis=0, tiled=True),
            lax.all_gather(cot_rows, "batch", axis=0, tiled=True),
        )
        shared_gates = router_probs(shared_rows, router_all) * shared_chosen.astype(jnp.float32)
        local_count = gate_all.shape[0]
        first_expert = lax.axis_index("batch") * local_count
        gate_local = lax.dynamic_slice_in_dim(shared_gates, first_expert, local_count, 1)
        mixture_all, saved = expert_forward(shared_rows, gate_local, gate_all, up_all, down_all)
        mixture = lax.psum_scatter(
            mixture_all.astype(jnp.bfloat16), "batch", scatter_dimension=0, tiled=True
        ).astype(jnp.float32)
        grad_shared, grad_gates_local, expert_terms = expert_backward(
            shared_rows,
            gate_local,
            saved,
            shared_cot.astype(jnp.float32),
            gate_all,
            up_all,
            down_all,
        )
        grad_gates_full = lax.dynamic_update_slice_in_dim(
            jnp.zeros((shared_rows.shape[0], EXPERTS), jnp.float32),
            grad_gates_local,
            first_expert,
            1,
        )
        grad_normed, grad_gates = (
            lax.psum_scatter(
                grad_shared.astype(jnp.bfloat16), "batch", scatter_dimension=0, tiled=True
            ).astype(jnp.float32),
            lax.psum_scatter(
                grad_gates_full.astype(jnp.bfloat16), "batch", scatter_dimension=0, tiled=True
            ).astype(jnp.float32),
        )
        output_rows.append((residual + mixture).astype(jnp.bfloat16))
        grad_probs = grad_gates * chosen
        grad_logits = home_probs * (
            grad_probs - jnp.sum(home_probs * grad_probs, axis=-1, keepdims=True)
        )
        router_f = router_all.astype(jnp.float32)
        grad_router = jnp.dot(
            normed.astype(jnp.float32).T,
            grad_logits,
            precision=HIGHEST_PRECISION,
            preferred_element_type=jnp.float32,
        )
        grad_normed = grad_normed + jnp.dot(
            grad_logits, router_f.T, precision=HIGHEST_PRECISION, preferred_element_type=jnp.float32
        )
        _, mlp_pull = jax.vjp(norm_rows, residual, gain_mlp)
        grad_resid_norm, grad_gain_mlp = mlp_pull(grad_normed)
        grad_residual = upstream + grad_resid_norm
        grad_o = grad_residual.astype(jnp.bfloat16)
        grad_w_out = jnp.dot(mixed_rows.T, grad_o, preferred_element_type=jnp.float32)
        grad_mixed = jnp.dot(grad_o, w_out_all.T, preferred_element_type=jnp.float32).astype(
            jnp.bfloat16
        )
        grad_heads = grad_mixed.reshape(tok_rows, head_count, HEAD)
        row_dot = jnp.sum(grad_heads.astype(jnp.float32) * attended, axis=-1).T

        def attend_back(block_data):
            scores, allowed, key_heads, value_heads = piece_scores(block_data)
            piece_len = key_heads.shape[0]
            probs_block = jnp.where(allowed, jnp.exp(scores - log_total[..., None]), 0.0)
            grad_value_piece = jnp.einsum(
                "hqk,qhd->khd",
                probs_block.astype(jnp.bfloat16),
                grad_heads,
                preferred_element_type=jnp.float32,
            )
            grad_probs_block = jnp.einsum(
                "qhd,khd->hqk", grad_heads, value_heads, preferred_element_type=jnp.float32
            )
            grad_scores = (probs_block * (grad_probs_block - row_dot[..., None])).astype(
                jnp.bfloat16
            )
            grad_query_acc = score_scale * jnp.einsum(
                "hqk,khd->qhd", grad_scores, key_heads, preferred_element_type=jnp.float32
            )
            grad_key_piece = score_scale * jnp.einsum(
                "hqk,qhd->khd", grad_scores, queries, preferred_element_type=jnp.float32
            )
            grad_key_acc = grad_key_piece.reshape(piece_len, -1)
            grad_value_acc = grad_value_piece.reshape(piece_len, -1)
            return (grad_query_acc, grad_key_acc, grad_value_acc)

        grad_queries, grad_key_all, grad_value_all = attend_back(
            (
                lax.all_gather(key_rows, "seq", axis=0, tiled=True),
                lax.all_gather(value_rows, "seq", axis=0, tiled=True),
                lax.all_gather(usable, "seq", axis=0, tiled=True),
            )
        )
        grad_key_rows, grad_value_rows = (
            lax.psum_scatter(
                grad_key_all.astype(jnp.bfloat16), "seq", scatter_dimension=0, tiled=True
            ).astype(jnp.float32),
            lax.psum_scatter(
                grad_value_all.astype(jnp.bfloat16), "seq", scatter_dimension=0, tiled=True
            ).astype(jnp.float32),
        )
        _, query_pull = jax.vjp(project_query, query_pre, gain_query)
        grad_query_pre, grad_gain_query = query_pull(grad_queries)
        _, key_pull = jax.vjp(project_query, key_pre, gain_key)
        grad_key_pre, grad_gain_key = key_pull(grad_key_rows.reshape(tok_rows, head_count, HEAD))
        grad_query_low = grad_query_pre.astype(jnp.bfloat16)
        grad_key_low = grad_key_pre.astype(jnp.bfloat16)
        grad_value_low = grad_value_rows.astype(jnp.bfloat16)
        grad_w_query = jnp.dot(hidden.T, grad_query_low, preferred_element_type=jnp.float32)
        grad_w_key = jnp.dot(hidden.T, grad_key_low, preferred_element_type=jnp.float32)
        grad_w_value = jnp.dot(hidden.T, grad_value_low, preferred_element_type=jnp.float32)
        grad_hidden = jnp.dot(grad_query_low, w_query_all.T, preferred_element_type=jnp.float32)
        grad_hidden = grad_hidden + jnp.dot(
            grad_key_low, w_key_all.T, preferred_element_type=jnp.float32
        )
        grad_hidden = grad_hidden + jnp.dot(
            grad_value_low, w_value_all.T, preferred_element_type=jnp.float32
        )
        _, attn_pull = jax.vjp(norm_rows, inputs, gain_attn)
        grad_inputs_norm, grad_gain_attn = attn_pull(grad_hidden)
        input_grads.append((grad_residual + grad_inputs_norm).astype(jnp.bfloat16))
        expert_terms = (
            lax.psum_scatter(
                expert_terms[0].astype(jnp.bfloat16), "seq", scatter_dimension=1, tiled=True
            ).astype(jnp.float32),
            lax.psum_scatter(
                expert_terms[1].astype(jnp.bfloat16), "seq", scatter_dimension=1, tiled=True
            ).astype(jnp.float32),
            lax.psum_scatter(
                expert_terms[2].astype(jnp.bfloat16), "seq", scatter_dimension=1, tiled=True
            ).astype(jnp.float32),
        )
        layer_terms = (
            lax.psum_scatter(grad_gain_attn, ("seq", "batch"), scatter_dimension=0, tiled=True),
            lax.psum_scatter(grad_gain_query, ("seq", "batch"), scatter_dimension=0, tiled=True),
            lax.psum_scatter(grad_gain_key, ("seq", "batch"), scatter_dimension=0, tiled=True),
            lax.psum_scatter(grad_gain_mlp, ("seq", "batch"), scatter_dimension=0, tiled=True),
            lax.psum_scatter(grad_w_query, ("seq", "batch"), scatter_dimension=0, tiled=True),
            lax.psum_scatter(grad_w_key, ("seq", "batch"), scatter_dimension=0, tiled=True),
            lax.psum_scatter(grad_w_value, ("seq", "batch"), scatter_dimension=0, tiled=True),
            lax.psum_scatter(grad_w_out, ("seq", "batch"), scatter_dimension=0, tiled=True),
            lax.psum_scatter(grad_router, ("seq", "batch"), scatter_dimension=0, tiled=True),
        )
        if layer_sums is None:
            layer_sums = layer_terms
            expert_sums = expert_terms
        else:
            layer_sums = jax.tree.map(jnp.add, layer_sums, layer_terms)
            expert_sums = jax.tree.map(jnp.add, expert_sums, expert_terms)
    return (
        jnp.stack(output_rows),
        jnp.stack(input_grads),
        layer_sums[0],
        layer_sums[1],
        layer_sums[2],
        layer_sums[3],
        layer_sums[4],
        layer_sums[5],
        layer_sums[6],
        layer_sums[7],
        layer_sums[8],
        expert_sums[0],
        expert_sums[1],
        expert_sums[2],
    )


def solution(mesh):
    in_specs = (
        P("batch", "seq", None),
        P("batch"),
        P("batch", "seq"),
        P("batch", "seq", None),
        P(("seq", "batch")),
        P(("seq", "batch")),
        P(("seq", "batch")),
        P(("seq", "batch")),
        P(("seq", "batch"), None),
        P(("seq", "batch"), None),
        P(("seq", "batch"), None),
        P(("seq", "batch"), None),
        P(("seq", "batch"), None),
        P("batch", "seq", None),
        P("batch", "seq", None),
        P("batch", "seq", None),
        P("batch", "seq", None),
    )
    out_specs = (
        P("batch", "seq", None),
        P("batch", "seq", None),
        P(("seq", "batch")),
        P(("seq", "batch")),
        P(("seq", "batch")),
        P(("seq", "batch")),
        P(("seq", "batch"), None),
        P(("seq", "batch"), None),
        P(("seq", "batch"), None),
        P(("seq", "batch"), None),
        P(("seq", "batch"), None),
        P("batch", "seq", None),
        P("batch", "seq", None),
        P("batch", "seq", None),
    )
    return jax.shard_map(shards, mesh=mesh, in_specs=in_specs, out_specs=out_specs, check_vma=False)
```

profile of v0, /device:TPU:9, one launch (start us, length us, event | category | flops | bytes accessed | tf_op | source)
XLA Modules:
  0.0 3297.8 jit_solution(5250748269598765339)
XLA Ops:
  12.9 41.1 %all-reduce.19 = (bf16[2048]{0:T(1024)(128)(2,1)S(1)}, bf16[2048]{0:T(1024)(128)(2,1)S(1)}, bf16[2048]{0:T(1024)(128)(2,1)S(1)}, bf16[2048]{0:T(1024)(128)(2,1)S(1)}) all-reduce(bf16[2048]{0:T(1024)(128)(2,1)S(1)} %dynamic-update-slice.1, bf16[2048]{0:T(1024)(128)(2,1)S(1)} %dynamic-update-slice.3, ...), channel_id=1, replica_groups=mesh['seq'=8,'batch'=4] {'seq','batch'}, use_global_device_ids=true, to_apply=%add.9 | all-reduce | flops 8192 | bytes 32768
  55.6 34.7 %all-gather.21.cloned.1.call-done = bf16[2048,2048]{1,0:T(8,128)(2,1)} async-done(((bf16[64,2048]{1,0:T(8,128)(2,1)}), bf16[2048,2048]{1,0:T(8,128)(2,1)}) %all-gather.21.cloned.1.call-update) | async-done | bytes 8388624 | tf_op jit(solution)/shard_map/all_gather | solution.py:59
  98.6 70.7 %all-gather.23.cloned.1.call-done = bf16[2048,2048]{1,0:T(8,128)(2,1)} async-done(((bf16[64,2048]{1,0:T(8,128)(2,1)}), bf16[2048,2048]{1,0:T(8,128)(2,1)}) %all-gather.23.cloned.1.call-update) | async-done | bytes 8388624 | tf_op jit(solution)/shard_map/all_gather | solution.py:60
  181.9 66.4 %all-gather.27.cloned.1.call-done = bf16[2048,2048]{1,0:T(8,128)(2,1)} async-done(((bf16[64,2048]{1,0:T(8,128)(2,1)}), bf16[2048,2048]{1,0:T(8,128)(2,1)}) %all-gather.27.cloned.1.call-update) | async-done | bytes 8388624 | tf_op jit(solution)/shard_map/all_gather | solution.py:61
  259.5 10.6 all-reduce.20
  270.3 8.1 all-gather.25.cloned.1.call-done
  284.6 24.4 all-gather.29.cloned.1.call-done
  312.1 76.8 %all-gather.31.cloned.1.call-done = bf16[2048,2048]{1,0:T(8,128)(2,1)} async-done(((bf16[64,2048]{1,0:T(8,128)(2,1)}), bf16[2048,2048]{1,0:T(8,128)(2,1)}) %all-gather.31.cloned.1.call-update) | async-done | bytes 8388624 | tf_op jit(solution)/shard_map/all_gather | solution.py:62
  405.9 51.9 %all-gather.2 = bf16[32,64,8]{1,2,0:T(8,128)(2,1)S(1)} all-gather(bf16[1,64,8]{1,2,0:T(8,128)(2,1)S(1)} %bitcast.495), channel_id=1, replica_groups=mesh['seq'=8,'batch'=4] {'seq','batch'}, dimensions={0}, use_global_device_ids=true | all-gather | bytes 33792 | tf_op jit(solution)/shard_map/all_gather | solution.py:63
  468.8 57.6 %all-gather.37.cloned.1.call-done = bf16[2,2048,1024]{2,1,0:T(8,128)(2,1)} async-done(((bf16[2,256,1024]{2,1,0:T(8,128)(2,1)}), bf16[2,2048,1024]{2,1,0:T(8,128)(2,1)}) %all-gather.37.cloned.1.call-update) | async-done | bytes 8388624 | tf_op jit(solution)/shard_map/all_gather | solution.py:70
  526.5 7.4 fusion.84
  533.8 74.7 %all-gather.35.cloned.1.call-done = bf16[2,2048,1024]{2,1,0:T(8,128)(2,1)} async-done(((bf16[2,256,1024]{2,1,0:T(8,128)(2,1)}), bf16[2,2048,1024]{2,1,0:T(8,128)(2,1)}) %all-gather.35.cloned.1.call-update) | async-done | bytes 8388624 | tf_op jit(solution)/shard_map/all_gather | solution.py:69
  608.5 7.4 fusion.86
  615.9 74.9 %all-gather.39.cloned.1.call-done = bf16[2,1024,2048]{2,1,0:T(8,128)(2,1)} async-done(((bf16[2,128,2048]{2,1,0:T(8,128)(2,1)}), bf16[2,1024,2048]{2,1,0:T(8,128)(2,1)}) %all-gather.39.cloned.1.call-update) | async-done | bytes 8388624 | tf_op jit(solution)/shard_map/all_gather | solution.py:71
  690.8 11.9 fusion.27
  713.8 6.9 fusion.5
  730.0 24.0 all-gather.43.cloned.1.call-done
  762.5 17.0 reduce-scatter.64.cloned.1.call-done
  780.3 30.4 reduce-scatter.36.cloned.1.call-done
  820.2 18.9 all-gather.49.cloned.1.call-done
  840.6 27.4 all-gather.45.cloned.1.call-done
  897.7 6.7 fusion.4
  907.2 7.2 reduce-scatter.68.cloned.1.call-done
  915.2 30.6 reduce-scatter.40.cloned.1.call-done
  948.7 27.6 reduce-scatter.32.cloned.1.call-done
  976.3 30.9 reduce-scatter.34.cloned.1.call-done
  1062.4 6.9 convert_bitcast_fusion.2
  1069.6 6.9 convert_bitcast_fusion.1
  1085.1 6.9 convolution_convert_fusion.1
  1093.6 7.0 convolution_convert_fusion
  1104.1 8.2 convolution_add_fusion
  1112.9 9.2 fusion.193
  1122.1 14.2 convolution_add_fusion.1
  1142.9 21.6 reduce-scatter.42.cloned.1.call-done
  1172.6 8.2 convolution_add_fusion.2
  1186.8 8.3 convolution_add_fusion.3
  1195.2 93.5 %reduce-scatter.72.cloned.1.call-done = f32[64,8]{1,0:T(8,128)} async-done(((f32[2048,8]{1,0:T(8,128)}), f32[64,8]{1,0:T(8,128)}) %reduce-scatter.72.cloned.1.call-update) | async-done | bytes 2064
  1314.7 57.6 %all-reduce.18 = (f32[2048]{0:T(1024)S(1)}, f32[2048]{0:T(1024)S(1)}, f32[2048]{0:T(1024)S(1)}, f32[2048]{0:T(1024)S(1)}) all-reduce(f32[2048]{0:T(1024)S(1)} %add.365, f32[2048]{0:T(1024)S(1)} %add.366, f32[2048]{0:T(1024)S(1)} %add.367, f32[2048]{0:T(1024)S(1)} %add.368), channel_id=23, replica_groups=mesh['seq'=8,'batch'=4] {'seq','batch'}, use_global_device_ids=true, to_apply=%region_49.50.clone | all-reduce | flops 8192 | bytes 65536
  1375.8 16.9 reduce-scatter.44.cloned.1.call-done
  1392.7 90.4 %reduce-scatter.46.cloned.1.call-done = bf16[2,256,1024]{1,2,0:T(8,128)(2,1)} async-done(((bf16[2,2048,1024]{1,2,0:T(8,128)(2,1)}), bf16[2,256,1024]{1,2,0:T(8,128)(2,1)}) %reduce-scatter.46.cloned.1.call-update) | async-done | bytes 1048592 | tf_op jit(solution)/shard_map/reduce_scatter | solution.py:345
  1486.7 86.8 %reduce-scatter.48.cloned.1.call-done = bf16[2,256,1024]{1,2,0:T(8,128)(2,1)} async-done(((bf16[2,2048,1024]{1,2,0:T(8,128)(2,1)}), bf16[2,256,1024]{1,2,0:T(8,128)(2,1)}) %reduce-scatter.48.cloned.1.call-update) | async-done | bytes 1048592 | tf_op jit(solution)/shard_map/reduce_scatter | solution.py:348
  1573.5 90.3 %reduce-scatter.50.cloned.1.call-done = bf16[2,256,1024]{1,2,0:T(8,128)(2,1)} async-done(((bf16[2,2048,1024]{1,2,0:T(8,128)(2,1)}), bf16[2,256,1024]{1,2,0:T(8,128)(2,1)}) %reduce-scatter.50.cloned.1.call-update) | async-done | bytes 1048592 | tf_op jit(solution)/shard_map/reduce_scatter | solution.py:348
  1667.4 86.8 %reduce-scatter.52.cloned.1.call-done = bf16[2,128,2048]{2,1,0:T(8,128)(2,1)} async-done(((bf16[2,1024,2048]{2,1,0:T(8,128)(2,1)}), bf16[2,128,2048]{2,1,0:T(8,128)(2,1)}) %reduce-scatter.52.cloned.1.call-update) | async-done | bytes 1048592 | tf_op jit(solution)/shard_map/reduce_scatter | solution.py:351
  1754.2 90.4 %reduce-scatter.54.cloned.1.call-done = bf16[2,128,2048]{2,1,0:T(8,128)(2,1)} async-done(((bf16[2,1024,2048]{2,1,0:T(8,128)(2,1)}), bf16[2,128,2048]{2,1,0:T(8,128)(2,1)}) %reduce-scatter.54.cloned.1.call-update) | async-done | bytes 1048592 | tf_op jit(solution)/shard_map/reduce_scatter | solution.py:351
  1847.8 357.0 %reduce-scatter.62.cloned.1.call-done = f32[64,2048]{1,0:T(8,128)} async-done(((f32[2048,2048]{1,0:T(8,128)}), f32[64,2048]{1,0:T(8,128)}) %reduce-scatter.62.cloned.1.call-update) | async-done | bytes 524304 | tf_op jit(solution)/shard_map/reduce_scatter | solution.py:363
  2204.8 362.1 %reduce-scatter.60.cloned.1.call-done = f32[64,2048]{1,0:T(8,128)} async-done(((f32[2048,2048]{1,0:T(8,128)}), f32[64,2048]{1,0:T(8,128)}) %reduce-scatter.60.cloned.1.call-update) | async-done | bytes 524304 | tf_op jit(solution)/shard_map/reduce_scatter | solution.py:362
  2566.8 362.1 %reduce-scatter.58.cloned.1.call-done = f32[64,2048]{1,0:T(8,128)} async-done(((f32[2048,2048]{1,0:T(8,128)}), f32[64,2048]{1,0:T(8,128)}) %reduce-scatter.58.cloned.1.call-update) | async-done | bytes 524304 | tf_op jit(solution)/shard_map/reduce_scatter | solution.py:361
  2928.9 361.9 %reduce-scatter.56.cloned.1.call-done = f32[64,2048]{1,0:T(8,128)} async-done(((f32[2048,2048]{1,0:T(8,128)}), f32[64,2048]{1,0:T(8,128)}) %reduce-scatter.56.cloned.1.call-update) | async-done | bytes 524304 | tf_op jit(solution)/shard_map/reduce_scatter | solution.py:360
  (573 shorter events, 281.2 us)
Async XLA Ops:
  7.2 83.1 %all-gather.21.cloned.1.call-start = ((), (), s32[]{:S(2)}) async-start(), calls=%async_computation.21 | async-start | bytes 8650752 | tf_op jit(solution)/shard_map/all_gather | solution.py:59
  7.9 161.4 %all-gather.23.cloned.1.call-start = ((), (), s32[]{:S(2)}) async-start(), calls=%async_computation.22 | async-start | bytes 8650752 | tf_op jit(solution)/shard_map/all_gather | solution.py:60
  8.7 239.7 %all-gather.27.cloned.1.call-start = ((), (), s32[]{:S(2)}) async-start(), calls=%async_computation.24 | async-start | bytes 8650752 | tf_op jit(solution)/shard_map/all_gather | solution.py:61
  9.4 269.0 %all-gather.25.cloned.1.call-start = ((), (), s32[]{:S(2)}) async-start(), calls=%async_computation.23 | async-start | bytes 2359296 | tf_op jit(solution)/shard_map/all_gather | solution.py:196
  54.0 122.9 %copy-start.83 = (f32[2048]{0:T(1024)}, f32[2048]{0:T(1024)S(1)}, u32[]{:S(2)}) copy-start(f32[2048]{0:T(1024)S(1)} %convert_element_type.328) | copy-start | bytes 24580
  55.3 193.1 %copy-start.85 = (f32[64]{0:T(128)}, f32[64]{0:T(128)S(1)}, u32[]{:S(2)}) copy-start(f32[64]{0:T(128)S(1)} %fusion.168) | copy-start | bytes 772
  55.3 404.1 %copy-start.87 = (f32[64]{0:T(128)}, f32[64]{0:T(128)S(1)}, u32[]{:S(2)}) copy-start(f32[64]{0:T(128)S(1)} %fusion.172) | copy-start | bytes 772
  55.5 123.0 %copy-start.77 = (f32[64,64]{1,0:T(8,128)}, f32[64,64]{1,0:T(8,128)S(1)}, u32[]{:S(2)}) copy-start(f32[64,64]{1,0:T(8,128)S(1)} %get-tuple-element.179) | copy-start | bytes 49156
  55.5 122.9 %copy-start.79 = (f32[64,64]{1,0:T(8,128)}, f32[64,64]{1,0:T(8,128)S(1)}, u32[]{:S(2)}) copy-start(f32[64,64]{1,0:T(8,128)S(1)} %get-tuple-element.180) | copy-start | bytes 49156
  180.8 545.2 %copy-start.53 = (bf16[64,16,64]{2,0,1:T(8,128)(2,1)}, bf16[64,16,64]{2,0,1:T(8,128)(2,1)S(1)}, u32[]{:S(2)}) copy-start(bf16[64,16,64]{2,0,1:T(8,128)(2,1)S(1)} %get-tuple-element.158) | copy-start | bytes 393220
  181.9 127.2 %all-gather.29.cloned.1.call-start = ((), (), s32[]{:S(2)}) async-start(), calls=%async_computation.25 | async-start | bytes 2359296 | tf_op jit(solution)/shard_map/all_gather | solution.py:197
  254.1 134.8 %all-gather.31.cloned.1.call-start = ((), (), s32[]{:S(2)}) async-start(), calls=%async_computation.26 | async-start | bytes 8650752 | tf_op jit(solution)/shard_map/all_gather | solution.py:62
  254.7 203.2 %all-gather.47.cloned.1.call-start = ((), (), s32[]{:S(2)}) async-start(), calls=%async_computation.46 | async-start | bytes 1310720 | tf_op jit(solution)/shard_map/all_gather | solution.py:224
  255.6 210.9 %all-gather.33.cloned.1.call-start = ((), (), s32[]{:S(2)}) async-start(), calls=%async_computation.27 | async-start | bytes 1310720 | tf_op jit(solution)/shard_map/all_gather | solution.py:222
  394.0 416.7 %copy-start.18 = (f32[64,2048]{1,0:T(8,128)}, f32[64,2048]{1,0:T(8,128)S(1)}, u32[]{:S(2)}) copy-start(f32[64,2048]{1,0:T(8,128)S(1)} %get-tuple-element.196) | copy-start | bytes 1572868
  394.9 131.5 %all-gather.37.cloned.1.call-start = ((), (), s32[]{:S(2)}) async-start(), calls=%async_computation.29 | async-start | bytes 9437184 | tf_op jit(solution)/shard_map/all_gather | solution.py:70
  395.7 212.8 %all-gather.35.cloned.1.call-start = ((), (), s32[]{:S(2)}) async-start(), calls=%async_computation.28 | async-start | bytes 9437184 | tf_op jit(solution)/shard_map/all_gather | solution.py:69
  396.3 294.5 %all-gather.39.cloned.1.call-start = ((), (), s32[]{:S(2)}) async-start(), calls=%async_computation.30 | async-start | bytes 9437184 | tf_op jit(solution)/shard_map/all_gather | solution.py:71
  397.0 326.1 %all-gather.41.cloned.1.call-start = ((), (), s32[]{:S(2)}) async-start(), calls=%async_computation.32 | async-start | bytes 2359296 | tf_op jit(solution)/shard_map/all_gather | solution.py:196
  398.0 356.0 %all-gather.43.cloned.1.call-start = ((), (), s32[]{:S(2)}) async-start(), calls=%async_computation.33 | async-start | bytes 2359296 | tf_op jit(solution)/shard_map/all_gather | solution.py:197
  459.4 243.2 %copy-start.11 = (f32[256,2048]{1,0:T(8,128)}, f32[256,2048]{1,0:T(8,128)S(1)}, u32[]{:S(2)}) copy-start(f32[256,2048]{1,0:T(8,128)S(1)} %bitcast_convert_fusion.1) | copy-start | bytes 6291460
  466.0 313.5 %reduce-scatter.64.cloned.1.call-start = ((), (), s32[]{:S(2)}) async-start(), calls=%async_computation.52 | async-start | bytes 81920
  468.8 233.8 %copy-start.99 = (f32[2,256]{1,0:T(2,128)}, f32[2,256]{1,0:T(2,128)S(1)}, u32[]{:S(2)}) copy-start(f32[2,256]{1,0:T(2,128)S(1)} %fusion.163) | copy-start | bytes 6148
  707.3 103.4 %reduce-scatter.36.cloned.1.call-start = ((), (), s32[]{:S(2)}) async-start(), calls=%async_computation.36 | async-start | bytes 1310720 | tf_op jit(solution)/shard_map/reduce_scatter | solution.py:250
  720.7 118.4 %all-gather.49.cloned.1.call-start = ((), (), s32[]{:S(2)}) async-start(), calls=%async_computation.47 | async-start | bytes 1310720 | tf_op jit(solution)/shard_map/all_gather | solution.py:224
  721.2 146.8 %all-gather.45.cloned.1.call-start = ((), (), s32[]{:S(2)}) async-start(), calls=%async_computation.34 | async-start | bytes 1310720 | tf_op jit(solution)/shard_map/all_gather | solution.py:222
  813.8 100.6 %reduce-scatter.68.cloned.1.call-start = ((), (), s32[]{:S(2)}) async-start(), calls=%async_computation.54 | async-start | bytes 81920
  813.9 131.9 %copy-start.97 = (pred[64,8]{0,1:T(8,128)(4,1)}, pred[64,8]{0,1:T(8,128)(4,1)S(1)}, u32[]{:S(2)}) copy-start(pred[64,8]{0,1:T(8,128)(4,1)S(1)} %fusion.156) | copy-start | bytes 1540
  891.0 54.7 %reduce-scatter.40.cloned.1.call-start = ((), (), s32[]{:S(2)}) async-start(), calls=%async_computation.38 | async-start | bytes 1310720 | tf_op jit(solution)/shard_map/reduce_scatter | solution.py:250
  904.5 102.8 %copy-start.19 = (f32[64,2048]{1,0:T(8,128)S(1)}, f32[64,2048]{1,0:T(8,128)}, u32[]{:S(2)}) copy-start(f32[64,2048]{1,0:T(8,128)} %copy-done.18) | copy-start | bytes 1572868
  904.5 71.8 %reduce-scatter.32.cloned.1.call-start = ((), (), s32[]{:S(2)}) async-start(), calls=%async_computation.31 | async-start | bytes 1310720 | tf_op jit(solution)/shard_map/reduce_scatter | solution.py:231
  905.1 102.1 %reduce-scatter.34.cloned.1.call-start = ((), (), s32[]{:S(2)}) async-start(), calls=%async_computation.35 | async-start | bytes 1310720 | tf_op jit(solution)/shard_map/reduce_scatter | solution.py:231
  905.8 206.6 %reduce-scatter.66.cloned.1.call-start = ((), (), s32[]{:S(2)}) async-start(), calls=%async_computation.53 | async-start | bytes 2359296
  906.7 102.9 %copy-start.108 = (f32[64]{0:T(128)}, f32[64]{0:T(128)S(1)}, u32[]{:S(2)}) copy-start(f32[64]{0:T(128)S(1)} %fusion.160) | copy-start | bytes 772
  1022.0 100.0 %reduce-scatter.70.cloned.1.call-start = ((), (), s32[]{:S(2)}) async-start(), calls=%async_computation.55 | async-start | bytes 2359296
  1035.1 106.8 %reduce-scatter.38.cloned.1.call-start = ((), (), s32[]{:S(2)}) async-start(), calls=%async_computation.37 | async-start | bytes 2359296 | tf_op jit(solution)/shard_map/reduce_scatter | solution.py:317
  1043.7 120.8 %reduce-scatter.42.cloned.1.call-start = ((), (), s32[]{:S(2)}) async-start(), calls=%async_computation.39 | async-start | bytes 2359296 | tf_op jit(solution)/shard_map/reduce_scatter | solution.py:317
  1052.7 236.0 %reduce-scatter.72.cloned.1.call-start = ((), (), s32[]{:S(2)}) async-start(), calls=%async_computation.56 | async-start | bytes 1081344
  1055.4 337.3 %reduce-scatter.44.cloned.1.call-start = ((), (), s32[]{:S(2)}) async-start(), calls=%async_computation.40 | async-start | bytes 9437184 | tf_op jit(solution)/shard_map/reduce_scatter | solution.py:345
  1061.2 421.9 %reduce-scatter.46.cloned.1.call-start = ((), (), s32[]{:S(2)}) async-start(), calls=%async_computation.41 | async-start | bytes 9437184 | tf_op jit(solution)/shard_map/reduce_scatter | solution.py:345
  1069.4 504.1 %reduce-scatter.48.cloned.1.call-start = ((), (), s32[]{:S(2)}) async-start(), calls=%async_computation.42 | async-start | bytes 9437184 | tf_op jit(solution)/shard_map/reduce_scatter | solution.py:348
  1076.5 587.2 %reduce-scatter.50.cloned.1.call-start = ((), (), s32[]{:S(2)}) async-start(), calls=%async_computation.43 | async-start | bytes 9437184 | tf_op jit(solution)/shard_map/reduce_scatter | solution.py:348
  1083.5 670.7 %reduce-scatter.52.cloned.1.call-start = ((), (), s32[]{:S(2)}) async-start(), calls=%async_computation.44 | async-start | bytes 9437184 | tf_op jit(solution)/shard_map/reduce_scatter | solution.py:351
  1092.0 752.5 %reduce-scatter.54.cloned.1.call-start = ((), (), s32[]{:S(2)}) async-start(), calls=%async_computation.45 | async-start | bytes 9437184 | tf_op jit(solution)/shard_map/reduce_scatter | solution.py:351
  1100.6 1104.2 %reduce-scatter.62.cloned.1.call-start = ((), (), s32[]{:S(2)}) async-start(), calls=%async_computation.51 | async-start | bytes 17301504 | tf_op jit(solution)/shard_map/reduce_scatter | solution.py:363
  1112.3 1454.5 %reduce-scatter.60.cloned.1.call-start = ((), (), s32[]{:S(2)}) async-start(), calls=%async_computation.50 | async-start | bytes 17301504 | tf_op jit(solution)/shard_map/reduce_scatter | solution.py:362
  1136.3 1792.6 %reduce-scatter.58.cloned.1.call-start = ((), (), s32[]{:S(2)}) async-start(), calls=%async_computation.49 | async-start | bytes 17301504 | tf_op jit(solution)/shard_map/reduce_scatter | solution.py:361
  1180.9 2110.0 %reduce-scatter.56.cloned.1.call-start = ((), (), s32[]{:S(2)}) async-start(), calls=%async_computation.48 | async-start | bytes 17301504 | tf_op jit(solution)/shard_map/reduce_scatter | solution.py:360
  (144 other events, 2695.2 us)
Sparse Core Ops, SparseCore 0:
  10.9 79.3 all-gather.20
  93.1 76.1 all-gather.22
  172.2 76.1 all-gather.26
  250.4 27.9 all-gather.24
  280.4 28.5 all-gather.28
  311.8 77.0 all-gather.30
  391.3 24.9 all-gather.46
  418.1 26.8 all-gather.32
  446.7 79.7 all-gather.36
  527.9 80.5 all-gather.34
  610.1 80.5 all-gather.38
  692.8 30.2 all-gather.40
  725.3 28.6 all-gather.42
  757.1 22.2 reduce-scatter.63
  782.5 28.2 reduce-scatter.35
  812.4 26.6 all-gather.48
  841.4 26.6 all-gather.44
  891.2 23.1 reduce-scatter.67
  917.5 28.1 reduce-scatter.39
  948.5 27.7 reduce-scatter.31
  979.4 27.7 reduce-scatter.33
  1022.2 30.9 reduce-scatter.65
  1055.5 33.9 reduce-scatter.69
  1092.2 34.4 reduce-scatter.37
  1129.5 34.9 reduce-scatter.41
  1166.6 122.0 reduce-scatter.71
  1291.0 101.6 reduce-scatter.43
  1395.1 87.9 reduce-scatter.45
  1485.5 87.9 reduce-scatter.47
  1575.8 87.9 reduce-scatter.49
  1666.2 87.9 reduce-scatter.51
  1756.6 87.9 reduce-scatter.53
  1847.4 357.3 reduce-scatter.61
  2207.7 359.0 reduce-scatter.59
  2569.8 359.0 reduce-scatter.57
  2931.7 359.0 reduce-scatter.55
where the time goes:
time: 3310 us; the launch traced here: 3300 us
  waiting for transfers between devices  2730 us (82%)
  matrix products  279 us (8%)
  blocking collectives  173 us (5%)
  local copies, waits for them, and re-layouts  57.3 us (2%)
  other arithmetic  36 us (1%)
    reduce_scatter x1, waiting for transfers between devices, shards(): lax.psum_scatter(grad_w_value, ('seq', 'batch'), scatter_dimension=0, til...  362 us
    reduce_scatter x1, waiting for transfers between devices, shards(): lax.psum_scatter(grad_w_key, ('seq', 'batch'), scatter_dimension=0, tiled...  362 us
    reduce_scatter x1, waiting for transfers between devices, shards(): lax.psum_scatter(grad_w_query, ('seq', 'batch'), scatter_dimension=0, til...  362 us
    reduce_scatter x1, waiting for transfers between devices, shards(): lax.psum_scatter(grad_w_out, ('seq', 'batch'), scatter_dimension=0, tiled...  357 us
    reduce_scatter x2, waiting for transfers between devices, shards(): lax.psum_scatter(expert_terms[2].astype(jnp.bfloat16), 'seq', scatter_dim...  177 us
    reduce_scatter x2, waiting for transfers between devices, shards(): lax.psum_scatter(expert_terms[1].astype(jnp.bfloat16), 'seq', scatter_dim...  177 us
    unnamed x41, waiting for transfers between devices  124 us
    unnamed x3, blocking collectives  109 us
  transfers between devices with their start and end apart: 36, of which 31 were waited for; matrix products, arithmetic and copies ran while one was open for 10% of the time, Pallas kernels for 0%

commit v1 on v0

v1 whole, which is shorter than its diff:
```python
import jax
import jax.numpy as jnp
from jax import lax
from jax.sharding import PartitionSpec as P

HEAD = 128
EPS = 1e-05
HIGHEST = lax.Precision.HIGHEST
NEGATIVE = -1e30
BF = jnp.bfloat16
F32 = jnp.float32


def dot(a, b):
    return jnp.dot(a, b, preferred_element_type=F32)


def dot_t(a, b):
    return lax.dot_general(a, b, (((1,), (1,)), ((), ())), preferred_element_type=F32)


def t_dot(a, b):
    return lax.dot_general(a, b, (((0,), (0,)), ((), ())), preferred_element_type=F32)


def rms_scale(v):
    return lax.rsqrt(jnp.mean(v * v, axis=-1, keepdims=True) + EPS)


def rms_back(v, scale, gain, grad):
    normal = v * scale
    weighted = grad * gain
    mean = jnp.mean(weighted * normal, axis=-1, keepdims=True)
    return scale * (weighted - normal * mean), grad * normal


def rotary_tables(positions):
    half_head = HEAD // 2
    frequency = 10000.0 ** (-2.0 * jnp.arange(half_head, dtype=F32) / HEAD)
    angles = positions.astype(F32)[:, None] * frequency[None, :]
    return jnp.cos(angles), jnp.sin(angles)


def rotate(v, cos_part, sin_part):
    first, second = jnp.split(v, 2, axis=-1)
    return jnp.concatenate(
        [first * cos_part - second * sin_part, second * cos_part + first * sin_part], axis=-1
    )


def shards(
    tokens,
    lengths,
    key_mask,
    top_experts,
    attn_gain,
    query_gain,
    key_gain,
    mlp_gain,
    w_query,
    w_key,
    w_value,
    w_out,
    w_router,
    expert_gate,
    expert_up,
    expert_down,
    cotangent,
):
    n_seq = lax.axis_size("seq")
    n_bat = lax.axis_size("batch")
    seq = lax.axis_index("seq")
    bat = lax.axis_index("batch")
    rows, span, dim = tokens.shape
    own = rows * span
    col = n_seq * own
    length = n_seq * span
    shard = w_query.shape[0]
    wide = dim // n_seq
    heads = wide // HEAD
    local_experts, depth, hidden_units = expert_gate.shape
    part = hidden_units // n_seq
    experts = local_experts * n_bat
    every = ("seq", "batch")
    score_scale = HEAD ** (-0.5)

    small = jnp.concatenate(
        [w_router, jnp.stack([attn_gain, query_gain, key_gain, mlp_gain], axis=1)], axis=1
    )
    small_all = lax.all_gather(small, every, axis=0, tiled=True)
    router = small_all[:, :experts]
    gain_attn = small_all[:, experts].astype(F32)
    gain_mlp = small_all[:, experts + 3].astype(F32)
    gain_q = lax.dynamic_slice_in_dim(small_all[:, experts + 1], seq * wide, wide).astype(F32)
    gain_k = lax.dynamic_slice_in_dim(small_all[:, experts + 2], seq * wide, wide).astype(F32)

    qkv_cut = jnp.stack([w_query, w_key, w_value]).reshape(3, shard, n_seq, wide)
    qkv_cut = jnp.transpose(qkv_cut, (2, 1, 0, 3)).reshape(n_seq, shard, 3 * wide)
    qkv_cut = lax.all_to_all(qkv_cut, "seq", 0, 0, tiled=True)
    w_qkv = lax.all_gather(qkv_cut, "batch", axis=1, tiled=True).reshape(dim, 3 * wide)
    w_o = lax.all_gather(w_out, "batch", axis=0, tiled=True)

    gu_cut = jnp.stack([expert_gate, expert_up]).reshape(2, local_experts, depth, n_seq, part)
    gu_cut = jnp.transpose(gu_cut, (3, 2, 0, 1, 4)).reshape(n_seq, depth, 2 * local_experts * part)
    w_gu = lax.all_to_all(gu_cut, "seq", 0, 0, tiled=True).reshape(dim, 2 * local_experts * part)
    w_down = expert_down.reshape(local_experts * part, dim)

    mine = tokens.reshape(own, dim)
    x_col = lax.all_gather(mine, "seq", axis=0, tiled=True).astype(F32)
    scale_x = rms_scale(x_col)
    hidden = (x_col * scale_x * gain_attn).astype(BF)
    qkv = dot(hidden, w_qkv)
    q_pre, k_pre, v_pre = qkv[:, :wide], qkv[:, wide : 2 * wide], qkv[:, 2 * wide :]

    squares = jnp.stack([jnp.sum(q_pre * q_pre, axis=-1), jnp.sum(k_pre * k_pre, axis=-1)])
    squares = lax.psum(squares, "seq")
    scales = lax.rsqrt(squares / dim + EPS)
    scale_q, scale_k = scales[0][:, None], scales[1][:, None]

    def by_row(v):
        v = v.reshape(n_seq, rows, span, heads, HEAD)
        return jnp.transpose(v, (1, 3, 0, 2, 4)).reshape(rows, heads, length, HEAD)

    def by_col(v):
        v = v.reshape(rows, heads, n_seq, span, HEAD)
        return jnp.transpose(v, (2, 0, 3, 1, 4)).reshape(col, wide)

    positions = jnp.arange(length, dtype=jnp.int32)
    cos_part, sin_part = rotary_tables(positions)
    q_norm = by_row(q_pre * scale_q)
    k_norm = by_row(k_pre * scale_k)
    gain_qh = gain_q.reshape(1, heads, 1, HEAD)
    gain_kh = gain_k.reshape(1, heads, 1, HEAD)
    queries = rotate(q_norm * gain_qh, cos_part, sin_part).astype(BF)
    keys = rotate(k_norm * gain_kh, cos_part, sin_part).astype(BF)
    values = by_row(v_pre.astype(BF))

    mask_all = lax.all_gather(key_mask, "seq", axis=1, tiled=True)
    usable = (positions[None, :] < lengths[:, None]) & (mask_all == 1)
    causal = positions[None, :] <= positions[:, None]
    same = positions[None, :] == positions[:, None]
    allowed = (causal[None] & (usable[:, None, :] | same[None]))[:, None]
    scores = jnp.einsum("rhqd,rhkd->rhqk", queries, keys, preferred_element_type=F32) * score_scale
    scores = jnp.where(allowed, scores, NEGATIVE)
    top = jnp.max(scores, axis=-1, keepdims=True)
    raised = jnp.exp(scores - top)
    probs = raised / jnp.sum(raised, axis=-1, keepdims=True)
    probs_low = probs.astype(BF)
    attended = jnp.einsum("rhqk,rhkd->rhqd", probs_low, values, preferred_element_type=F32)
    mixed = by_col(attended.astype(BF))

    mixed_out = lax.psum_scatter(dot(mixed, w_o).astype(BF), "seq", scatter_dimension=0, tiled=True)
    x_own = mine.astype(F32)
    residual = x_own + mixed_out.astype(F32)
    scale_r = rms_scale(residual)
    normed = (residual * scale_r * gain_mlp).astype(BF)
    router_probs = jax.nn.softmax(dot(normed, router), axis=-1)
    expert_ids = jnp.arange(experts, dtype=jnp.int32)
    chosen = jnp.any(top_experts.reshape(own, -1)[:, :, None] == expert_ids, axis=1).astype(F32)
    gates = router_probs * chosen

    normed_all = lax.all_gather(normed, every, axis=0, tiled=True)
    gates_all = lax.all_gather(gates, every, axis=0, tiled=True)
    dy_own = cotangent.reshape(own, dim)
    dy_all = lax.all_gather(dy_own, every, axis=0, tiled=True)
    first_expert = bat * local_experts
    gates_here = lax.dynamic_slice_in_dim(gates_all, first_expert, local_experts, 1)
    units = local_experts * part
    gates_wide = jnp.repeat(gates_here, part, axis=1)
    pre = dot(normed_all, w_gu)
    gate_pre, up_pre = pre[:, :units], pre[:, units:]
    sig = jax.nn.sigmoid(gate_pre)
    silu = gate_pre * sig
    active = (silu * up_pre).astype(BF).astype(F32)
    weighted = (active * gates_wide).astype(BF)
    mixture = dot(weighted, w_down).astype(BF)
    mixture = lax.psum_scatter(mixture, every, scatter_dimension=0, tiled=True)
    output = (residual + mixture.astype(F32)).astype(BF)

    back = dot_t(dy_all, w_down)
    gate_terms = jnp.sum((active * back).reshape(-1, local_experts, part), axis=-1)
    grad_active = back * gates_wide
    grad_gate_pre = (grad_active * up_pre * sig * (1.0 + gate_pre * (1.0 - sig))).astype(BF)
    grad_up_pre = (grad_active * silu).astype(BF)
    grad_pre = jnp.concatenate([grad_gate_pre, grad_up_pre], axis=1)
    grad_down = t_dot(weighted, dy_all)
    grad_gu = t_dot(normed_all, grad_pre).astype(BF)
    grad_normed = dot_t(grad_pre, w_gu).astype(BF)
    grad_normed = lax.psum_scatter(grad_normed, every, scatter_dimension=0, tiled=True).astype(F32)
    grad_gates = lax.dynamic_update_slice_in_dim(
        jnp.zeros((normed_all.shape[0], experts), F32), gate_terms, first_expert, 1
    )
    grad_gates = lax.psum_scatter(grad_gates, every, scatter_dimension=0, tiled=True)

    grad_gu = lax.all_to_all(grad_gu.reshape(n_seq, depth, -1), "seq", 0, 0, tiled=True)
    grad_gu = grad_gu.reshape(n_seq, depth, 2, local_experts, part)
    grad_gu = jnp.transpose(grad_gu, (2, 3, 1, 0, 4)).reshape(2, local_experts, depth, hidden_units)
    grad_gu = grad_gu.astype(F32)
    grad_down = grad_down.reshape(local_experts, part, dim)

    grad_chosen = grad_gates * chosen
    grad_logits = router_probs * (
        grad_chosen - jnp.sum(router_probs * grad_chosen, axis=-1, keepdims=True)
    )
    grad_router = lax.dot_general(
        normed.astype(F32), grad_logits, (((0,), (0,)), ((), ())), precision=HIGHEST
    )
    grad_normed = grad_normed + lax.dot_general(
        grad_logits, router.astype(F32), (((1,), (1,)), ((), ())), precision=HIGHEST
    )
    grad_resid, gain_mlp_terms = rms_back(residual, scale_r, gain_mlp, grad_normed)
    grad_residual = dy_own.astype(F32) + grad_resid
    grad_o = grad_residual.astype(BF)

    grad_o_col = lax.all_gather(grad_o, "seq", axis=0, tiled=True)
    grad_mixed = by_row(dot_t(grad_o_col, w_o).astype(BF))
    grad_w_o = t_dot(mixed, grad_o_col).astype(BF)
    grad_w_o = lax.psum_scatter(grad_w_o, "batch", scatter_dimension=0, tiled=True).astype(F32)
    row_dot = jnp.sum(grad_mixed.astype(F32) * attended, axis=-1, keepdims=True)
    grad_values = jnp.einsum("rhqk,rhqd->rhkd", probs_low, grad_mixed, preferred_element_type=F32)
    grad_probs = jnp.einsum("rhqd,rhkd->rhqk", grad_mixed, values, preferred_element_type=F32)
    grad_scores = (probs * (grad_probs - row_dot)).astype(BF)
    grad_q = score_scale * jnp.einsum(
        "rhqk,rhkd->rhqd", grad_scores, keys, preferred_element_type=F32
    )
    grad_k = score_scale * jnp.einsum(
        "rhqk,rhqd->rhkd", grad_scores, queries, preferred_element_type=F32
    )
    grad_q = rotate(grad_q, cos_part, -sin_part)
    grad_k = rotate(grad_k, cos_part, -sin_part)
    grad_gain_q = jnp.sum(grad_q * q_norm, axis=(0, 2)).reshape(wide)
    grad_gain_k = jnp.sum(grad_k * k_norm, axis=(0, 2)).reshape(wide)
    q_weighted = by_col(grad_q * gain_qh)
    k_weighted = by_col(grad_k * gain_kh)
    q_flat = q_pre * scale_q
    k_flat = k_pre * scale_k
    means = jnp.stack(
        [jnp.sum(q_weighted * q_flat, axis=-1), jnp.sum(k_weighted * k_flat, axis=-1)]
    )
    means = lax.psum(means, "seq") / dim
    grad_q_pre = (scale_q * (q_weighted - q_flat * means[0][:, None])).astype(BF)
    grad_k_pre = (scale_k * (k_weighted - k_flat * means[1][:, None])).astype(BF)
    grad_qkv = jnp.concatenate([grad_q_pre, grad_k_pre, by_col(grad_values).astype(BF)], axis=1)

    grad_hidden = dot_t(grad_qkv, w_qkv).astype(BF)
    grad_hidden = lax.psum_scatter(grad_hidden, "seq", scatter_dimension=0, tiled=True).astype(F32)
    grad_w = t_dot(hidden, grad_qkv).astype(BF).reshape(n_seq, n_bat * shard, 3 * wide)
    grad_w = lax.psum_scatter(grad_w, "batch", scatter_dimension=1, tiled=True)
    grad_w = lax.all_to_all(grad_w, "seq", 0, 0, tiled=True).astype(F32)
    grad_w = grad_w.reshape(n_seq, shard, 3, wide)
    grad_w = jnp.transpose(grad_w, (2, 1, 0, 3)).reshape(3, shard, dim)

    grad_x, gain_attn_terms = rms_back(x_own, rms_scale(x_own), gain_attn, grad_hidden)
    grad_tokens = (grad_residual + grad_x).astype(BF)

    zeros = jnp.zeros((dim,), F32)
    small_grads = jnp.concatenate(
        [
            grad_router,
            jnp.stack(
                [
                    jnp.sum(gain_attn_terms, axis=0),
                    lax.dynamic_update_slice_in_dim(zeros, grad_gain_q, seq * wide, 0),
                    lax.dynamic_update_slice_in_dim(zeros, grad_gain_k, seq * wide, 0),
                    jnp.sum(gain_mlp_terms, axis=0),
                ],
                axis=1,
            ),
        ],
        axis=1,
    )
    small_grads = lax.psum_scatter(small_grads, every, scatter_dimension=0, tiled=True)

    return (
        output.reshape(rows, span, dim),
        grad_tokens.reshape(rows, span, dim),
        small_grads[:, experts],
        small_grads[:, experts + 1],
        small_grads[:, experts + 2],
        small_grads[:, experts + 3],
        grad_w[0],
        grad_w[1],
        grad_w[2],
        grad_w_o,
        small_grads[:, :experts],
        grad_gu[0],
        grad_gu[1],
        grad_down,
    )


def solution(mesh):
    tok = P("batch", "seq", None)
    vec = P(("seq", "batch"))
    mat = P(("seq", "batch"), None)
    in_specs = (tok, P("batch"), P("batch", "seq"), tok) + (vec,) * 4 + (mat,) * 5 + (tok,) * 4
    out_specs = (tok, tok) + (vec,) * 4 + (mat,) * 5 + (tok,) * 3
    return jax.shard_map(shards, mesh=mesh, in_specs=in_specs, out_specs=out_specs, check_vma=False)
```

time: 3310 us -> 1900 us (0.57)
  waiting for transfers between devices: 2730 us -> 1340 us
  matrix products: 279 us -> 138 us
  blocking collectives: 173 us -> 209 us
    reduce_scatter x16 -> x7, waiting for transfers between devices: 2050 us -> 891 us  [the longest x1 373 us: shards(): lax.psum_scatter(grad_normed, every, scatter_dimension=0, tiled=True)]
    all_gather x15 -> x6, waiting for transfers between devices: 560 us -> 203 us  [the longest x1 101 us: shards(): dy_all = lax.all_gather(dy_own, every, axis=0, tiled=True)]
    dot_general x62 -> x20, matrix products: 279 us -> 132 us  [the longest x4 46.4 us: dot_t(): lax.dot_general(a, b, (((1,), (1,)), ((), ())), preferred_element_type=F32)]
    all_to_all x0 -> x3, waiting for transfers between devices: none -> 128 us  [the longest x1 72.9 us: shards(): lax.all_to_all(gu_cut, 'seq', 0, 0, tiled=True)]
    unnamed x3 -> x0, blocking collectives: 109 us -> none
    all_gather x3, blocking collectives: 64.1 us -> 131 us  [the longest x1 64.1 us: shards(): gates_all = lax.all_gather(gates, every, axis=0, tiled=True)]
    all_to_all x0 -> x1, blocking collectives: none -> 42.1 us  [shards(): qkv_cut = lax.all_to_all(qkv_cut, 'seq', 0, 0, tiled=True)]
    psum x0 -> x2, blocking collectives: none -> 36.5 us  [the longest x1 25.1 us: shards(): squares = lax.psum(squares, 'seq')]
  transfers between devices with their start and end apart: 36 -> 17, of which waited for: 31 -> 10; matrix products, arithmetic and copies ran while one was open for 10% -> 9% of each run, Pallas kernels for 0% -> 0%
where the time goes in v1:
time: 1900 us; the launch traced here: 1880 us
  waiting for transfers between devices  1340 us (71%)
  blocking collectives  209 us (11%)
  matrix products  138 us (7%)
  local copies, waits for them, and re-layouts  89.7 us (5%)
  other arithmetic  56.5 us (3%)
  starting transfers between devices  25.6 us (1%)
    reduce_scatter x1, waiting for transfers between devices, shards(): lax.psum_scatter(grad_normed, every, scatter_dimension=0, tiled=True)  373 us
    reduce_scatter x1, waiting for transfers between devices, shards(): mixture = lax.psum_scatter(mixture, every, scatter_dimension=0, tiled=True)  355 us
    unnamed x15, waiting for transfers between devices  121 us
    reduce_scatter x1, waiting for transfers between devices, shards(): lax.psum_scatter(grad_gates, every, scatter_dimension=0, tiled=True)  115 us
    all_gather x1, waiting for transfers between devices, shards(): dy_all = lax.all_gather(dy_own, every, axis=0, tiled=True)  101 us
    all_to_all x1, waiting for transfers between devices, shards(): lax.all_to_all(gu_cut, 'seq', 0, 0, tiled=True)  72.9 us
    all_gather x1, blocking collectives, shards(): gates_all = lax.all_gather(gates, every, axis=0, tiled=True)  64.1 us
    all_to_all x1, waiting for transfers between devices, shards(): lax.all_to_all(grad_gu.reshape(n_seq, depth, -1), 'seq', 0, 0, tiled=True)  55.3 us
  transfers between devices with their start and end apart: 17, of which 10 were waited for; matrix products, arithmetic and copies ran while one was open for 9% of the time, Pallas kernels for 0%

profile of v1, /device:TPU:9, one launch (start us, length us, event | category | flops | bytes accessed | tf_op | source)
XLA Modules:
  0.0 1877.5 jit_solution(7305523587902170462)
XLA Ops:
  15.1 42.1 %all_to_all.20 = bf16[8,64,768]{2,1,0:T(8,128)(2,1)} all-to-all(bf16[8,64,768]{2,1,0:T(8,128)(2,1)S(1)} %reshape.364), channel_id=1, replica_groups=mesh['seq'=8,'batch'=4] {'seq'}, dimensions={0} | all-to-all | bytes 1572864 | tf_op jit(solution)/shard_map/all_to_all | solution.py:99
  58.2 13.3 all-gather
  71.7 53.2 %all-gather.1 = bf16[32,64,12]{1,2,0:T(8,128)(2,1)S(1)} all-gather(bf16[1,64,12]{1,2,0:T(8,128)(2,1)S(1)} %bitcast.250), channel_id=1, replica_groups=mesh['seq'=8,'batch'=4] {'seq','batch'}, dimensions={0}, use_global_device_ids=true | all-gather | bytes 50688 | tf_op jit(solution)/shard_map/all_gather | solution.py:90
  128.2 3.2 fusion.1
  131.5 6.7 fusion.15
  139.9 25.1 %psum.14 = f32[2,1024]{1,0:T(2,128)S(1)} all-reduce(f32[2,1024]{1,0:T(2,128)S(1)} %pad_maximum_fusion.10), channel_id=1, replica_groups=mesh['seq'=8,'batch'=4] {'seq'}, use_global_device_ids=true, to_apply=%region_3.0 | all-reduce | flops 2048 | bytes 16384 | tf_op jit(solution)/shard_map/psum | solution.py:116
  165.6 3.0 slice_multiply_fusion.1
  168.6 2.5 copy.211
  171.1 2.7 reshape.366
  177.5 2.7 reshape.368
  185.0 5.8 fusion.55
  190.7 2.8 fusion.10
  197.3 4.6 convolution_convert_fusion.2
  202.0 48.4 %reduce-scatter.11.cloned.1.call-done = bf16[128,2048]{1,0:T(8,128)(2,1)} async-done(((bf16[1024,2048]{1,0:T(8,128)(2,1)}), bf16[128,2048]{1,0:T(8,128)(2,1)}) %reduce-scatter.11.cloned.1.call-update) | async-done | bytes 524304 | tf_op jit(solution)/shard_map/reduce_scatter | solution.py:152
  262.1 6.7 all-to-all-start.1
  269.7 72.9 %all-to-all-done.1 = bf16[8,256,512]{1,2,0:T(8,128)(2,1)} async-done(((bf16[8,256,512]{1,2,0:T(8,128)(2,1)}), bf16[8,256,512]{1,2,0:T(8,128)(2,1)}, u32[]{:S(2)}, u32[]{:S(2)}) %all-to-all-start.1) | async-done | bytes 2097184 | tf_op jit(solution)/shard_map/all_to_all | solution.py:105
  342.6 3.9 copy.222
  346.6 54.7 %all-gather.15.cloned.1.call-done = bf16[4096,2048]{1,0:T(8,128)(2,1)} async-done(((bf16[128,2048]{1,0:T(8,128)(2,1)}), bf16[4096,2048]{1,0:T(8,128)(2,1)}) %all-gather.15.cloned.1.call-update) | async-done | bytes 16777232 | tf_op jit(solution)/shard_map/all_gather | solution.py:162
  401.3 15.1 fusion.58
  416.4 100.7 %all-gather.17.cloned.1.call-done = bf16[4096,2048]{1,0:T(8,128)(2,1)} async-done(((bf16[128,2048]{1,0:T(8,128)(2,1)}), bf16[4096,2048]{1,0:T(8,128)(2,1)}) %all-gather.17.cloned.1.call-update) | async-done | bytes 16777232 | tf_op jit(solution)/shard_map/all_gather | solution.py:165
  517.1 20.0 %bitcast_reduce_fusion = (f32[4096,2]{0,1:T(2,128)S(1)}, bf16[4096,256]{0,1:T(8,128)(2,1)}, f32[4096,256]{0,1:T(8,128)}) fusion(f32[4096,512]{0,1:T(8,128)} %fusion.58, bf16[4096,2048]{1,0:T(8,128)(2,1)} %all-gather.17.cloned.1.call-done, bf16[256,2048]{1,0:T(8,128)(2,1)S(1)} %bitcast.183), kind=kOutput, calls=%fused_computation.13 | convolution fusion | flops 4304396288 | bytes 32538624 | tf_op jit(solution)/shard_map/dot_general | solution.py:19
  538.9 114.8 %reduce-scatter.17.cloned.1.call-done = f32[128,8]{0,1:T(8,128)} async-done(((f32[4096,8]{0,1:T(8,128)}), f32[128,8]{0,1:T(8,128)}) %reduce-scatter.17.cloned.1.call-update) | async-done | bytes 4112 | tf_op jit(solution)/shard_map/reduce_scatter | solution.py:193
  654.4 64.1 %all_gather.33 = f32[4096,8]{0,1:T(8,128)S(1)} all-gather(f32[128,8]{0,1:T(8,128)S(1)} %get-tuple-element.63), channel_id=1, replica_groups=mesh['seq'=8,'batch'=4] {'seq','batch'}, dimensions={0}, use_global_device_ids=true | all-gather | bytes 135168 | tf_op jit(solution)/shard_map/all_gather | solution.py:163
  718.5 7.3 multiply_convert_fusion.2
  727.9 14.1 convolution_convert_fusion
  742.0 372.9 %reduce-scatter.15.cloned.1.call-done = bf16[128,2048]{1,0:T(8,128)(2,1)} async-done(((bf16[4096,2048]{1,0:T(8,128)(2,1)}), bf16[128,2048]{1,0:T(8,128)(2,1)}) %reduce-scatter.15.cloned.1.call-update) | async-done | bytes 524304 | tf_op jit(solution)/shard_map/reduce_scatter | solution.py:189
  1121.1 47.3 %all-gather.19.cloned.1.call-done = bf16[1024,2048]{1,0:T(8,128)(2,1)} async-done(((bf16[128,2048]{1,0:T(8,128)(2,1)}), bf16[1024,2048]{1,0:T(8,128)(2,1)}) %all-gather.19.cloned.1.call-update) | async-done | bytes 4194320 | tf_op jit(solution)/shard_map/all_gather | solution.py:215
  1168.4 4.6 convolution_convert_fusion.8
  1188.9 4.3 multiply_subtract_fusion.1
  1197.3 2.5 copy.238
  1211.1 11.4 psum.15
  1226.2 5.5 convolution_convert_fusion.4
  1231.9 4.5 convolution_convert_fusion.6
  1236.5 7.7 convolution_convert_fusion.3
  1244.5 10.0 convolution_convert_fusion.1
  1254.5 14.8 convolution_convert_fusion.5
  1269.3 9.5 all-to-all-start.3
  1279.1 55.3 %all-to-all-done.3 = bf16[8,256,512]{2,1,0:T(8,128)(2,1)} async-done(((bf16[8,256,512]{2,1,0:T(8,128)(2,1)}), bf16[8,256,512]{2,1,0:T(8,128)(2,1)}, u32[]{:S(2)}, u32[]{:S(2)}) %all-to-all-start.3) | async-done | bytes 2097184 | tf_op jit(solution)/shard_map/all_to_all | solution.py:195
  1334.4 8.0 all-to-all-start.2
  1342.4 12.4 fusion.59
  1355.1 5.7 reshape.395
  1360.8 4.7 copy.284
  1367.8 2.7 squeeze.39
  1370.5 2.7 squeeze.38
  1376.9 4.7 fusion.51
  1388.4 355.3 %reduce-scatter.13.cloned.1.call-done = bf16[128,2048]{1,0:T(8,128)(2,1)} async-done(((bf16[4096,2048]{1,0:T(8,128)(2,1)}), bf16[128,2048]{1,0:T(8,128)(2,1)}) %reduce-scatter.13.cloned.1.call-update) | async-done | bytes 524304 | tf_op jit(solution)/shard_map/reduce_scatter | solution.py:177
  1743.7 3.3 fusion.19
  1747.0 118.8 %reduce-scatter.25.cloned.1.call-done = f32[64,12]{1,0:T(8,128)} async-done(((f32[2048,12]{1,0:T(8,128)}), f32[64,12]{1,0:T(8,128)}) %reduce-scatter.25.cloned.1.call-update) | async-done | bytes 3088
  (261 shorter events, 103.0 us)
Async XLA Ops:
  7.2 509.9 %copy-start = (bf16[2,128,2048]{2,1,0:T(8,128)(2,1)S(1)}, bf16[2,128,2048]{2,1,0:T(8,128)(2,1)}, u32[]{:S(2)}) copy-start(bf16[2,128,2048]{2,1,0:T(8,128)(2,1)} %param.32) | copy-start | bytes 3145732
  7.2 121.0 %all-gather.9.cloned.1.call-start = ((), (), s32[]{:S(2)}) async-start(), calls=%async_computation.12 | async-start | bytes 4718592 | tf_op jit(solution)/shard_map/all_gather | solution.py:109
  7.9 123.6 %all-gather.11.cloned.1.call-start = ((), (), s32[]{:S(2)}) async-start(), calls=%async_computation.13 | async-start | bytes 3932160 | tf_op jit(solution)/shard_map/all_gather | solution.py:100
  11.8 46.4 %copy-start.52 = (s32[2,64]{1,0:T(2,128)S(1)}, s32[2,64]{1,0:T(2,128)}, u32[]{:S(2)}) copy-start(s32[2,64]{1,0:T(2,128)} %param.19) | copy-start | bytes 1540
  11.8 59.8 %copy-start.49 = (bf16[64,8]{0,1:T(8,128)(2,1)S(1)}, bf16[64,8]{0,1:T(8,128)(2,1)}, u32[]{:S(2)}) copy-start(bf16[64,8]{0,1:T(8,128)(2,1)} %param.29) | copy-start | bytes 3076
  11.8 59.8 %copy-start.53 = (bf16[64]{0:T(256)(128)(2,1)S(1)}, bf16[64]{0:T(256)(128)(2,1)}, u32[]{:S(2)}) copy-start(bf16[64]{0:T(256)(128)(2,1)} %param.21) | copy-start | bytes 388
  11.9 59.8 %copy-start.54 = (bf16[64]{0:T(256)(128)(2,1)S(1)}, bf16[64]{0:T(256)(128)(2,1)}, u32[]{:S(2)}) copy-start(bf16[64]{0:T(256)(128)(2,1)} %param.22) | copy-start | bytes 388
  11.9 59.7 %copy-start.55 = (bf16[64]{0:T(256)(128)(2,1)S(1)}, bf16[64]{0:T(256)(128)(2,1)}, u32[]{:S(2)}) copy-start(bf16[64]{0:T(256)(128)(2,1)} %param.23) | copy-start | bytes 388
  11.9 59.7 %copy-start.56 = (bf16[64]{0:T(256)(128)(2,1)S(1)}, bf16[64]{0:T(256)(128)(2,1)}, u32[]{:S(2)}) copy-start(bf16[64]{0:T(256)(128)(2,1)} %param.24) | copy-start | bytes 388
  12.3 112.8 %copy-start.57 = (s32[2]{0:T(128)S(1)}, s32[2]{0:T(128)}, u32[]{:S(2)}) copy-start(s32[2]{0:T(128)} %param.18) | copy-start | bytes 28
  57.2 140.1 %all-gather.13.cloned.1.call-start = ((), (), s32[]{:S(2)}) async-start(), calls=%async_computation.14 | async-start | bytes 1310720 | tf_op jit(solution)/shard_map/all_gather | solution.py:101
  58.0 192.5 %reduce-scatter.11.cloned.1.call-start = ((), (), s32[]{:S(2)}) async-start(), calls=%async_computation.15 | async-start | bytes 4718592 | tf_op jit(solution)/shard_map/reduce_scatter | solution.py:152
  125.1 13.1 copy-start.30
  127.0 54.6 %copy-start.40 = (f32[256,1]{0,1:T(1,128)}, f32[256,1]{0,1:T(1,128)S(1)}, u32[]{:S(2)}) copy-start(f32[256,1]{0,1:T(1,128)S(1)} %get-tuple-element.77) | copy-start | bytes 3076
  127.0 56.0 %copy-start.38 = (f32[256,1]{0,1:T(1,128)}, f32[256,1]{0,1:T(1,128)S(1)}, u32[]{:S(2)}) copy-start(f32[256,1]{0,1:T(1,128)S(1)} %get-tuple-element.78) | copy-start | bytes 3076
  131.5 6.7 copy-start.47
  165.6 28.0 %copy-start.17 = (bf16[2,2,8,64,128]{4,3,2,1,0:T(8,128)(2,1)}, bf16[2,2,8,64,128]{4,3,2,1,0:T(8,128)(2,1)S(1)}, u32[]{:S(2)}) copy-start(bf16[2,2,8,64,128]{4,3,2,1,0:T(8,128)(2,1)S(1)} %copy.216) | copy-start | bytes 1572868
  197.3 53.1 %copy-start.1 = (bf16[2,64,2048]{2,1,0:T(8,128)(2,1)S(1)}, bf16[2,64,2048]{2,1,0:T(8,128)(2,1)}, u32[]{:S(2)}) copy-start(bf16[2,64,2048]{2,1,0:T(8,128)(2,1)} %param.17) | copy-start | bytes 1572868
  202.0 199.3 %all-gather.15.cloned.1.call-start = ((), (), s32[]{:S(2)}) async-start(), calls=%async_computation.16 | async-start | bytes 17301504 | tf_op jit(solution)/shard_map/all_gather | solution.py:162
  251.7 8.9 copy-start.44
  253.8 263.3 %all-gather.17.cloned.1.call-start = ((), (), s32[]{:S(2)}) async-start(), calls=%async_computation.18 | async-start | bytes 17301504 | tf_op jit(solution)/shard_map/all_gather | solution.py:165
  260.7 8.4 copy-start.46
  262.1 80.5 %all-to-all-start.1 = ((bf16[8,256,512]{1,2,0:T(8,128)(2,1)}), bf16[8,256,512]{1,2,0:T(8,128)(2,1)}, u32[]{:S(2)}, u32[]{:S(2)}) async-start(bf16[8,256,512]{1,2,0:T(8,128)(2,1)} %bitcast.188), calls=%async_computation.2 | async-start | bytes 4194304 | tf_op jit(solution)/shard_map/all_to_all | solution.py:105
  268.9 384.9 %reduce-scatter.17.cloned.1.call-start = ((), (), s32[]{:S(2)}) async-start(), calls=%async_computation.20 | async-start | bytes 135168 | tf_op jit(solution)/shard_map/reduce_scatter | solution.py:193
  517.1 20.8 %copy-start.5 = (bf16[128,2048]{1,0:T(8,128)(2,1)S(1)}, bf16[128,2048]{1,0:T(8,128)(2,1)}, u32[]{:S(2)}) copy-start(bf16[128,2048]{1,0:T(8,128)(2,1)} %multiply_convert_fusion.6) | copy-start | bytes 1572868
  537.8 577.1 %reduce-scatter.15.cloned.1.call-start = ((), (), s32[]{:S(2)}) async-start(), calls=%async_computation.19 | async-start | bytes 17301504 | tf_op jit(solution)/shard_map/reduce_scatter | solution.py:189
  654.4 460.5 %copy-start.50 = (f32[128]{0:T(128)}, f32[128]{0:T(128)S(1)}, u32[]{:S(2)}) copy-start(f32[128]{0:T(128)S(1)} %get-tuple-element.62) | copy-start | bytes 1540
  741.9 373.0 %copy-start.31 = (bf16[2048,12]{0,1:T(8,128)(2,1)S(1)}, bf16[2048,12]{0,1:T(8,128)(2,1)}, u32[]{:S(2)}) copy-start(bf16[2048,12]{0,1:T(8,128)(2,1)} %copy-done.30) | copy-start | bytes 147460
  741.9 373.0 %copy-start.36 = (f32[128,8]{0,1:T(8,128)S(1)}, f32[128,8]{0,1:T(8,128)}, u32[]{:S(2)}) copy-start(f32[128,8]{0,1:T(8,128)} %reduce-scatter.17.cloned.1.call-done) | copy-start | bytes 12292
  741.9 373.0 %copy-start.37 = (pred[128,8]{0,1:T(8,128)(4,1)S(1)}, pred[128,8]{0,1:T(8,128)(4,1)}, u32[]{:S(2)}) copy-start(pred[128,8]{0,1:T(8,128)(4,1)} %fusion.33) | copy-start | bytes 3076
  741.9 373.0 %copy-start.45 = (f32[128]{0:T(128)S(1)}, f32[128]{0:T(128)}, u32[]{:S(2)}) copy-start(f32[128]{0:T(128)} %copy-done.44) | copy-start | bytes 1540
  742.0 426.4 %all-gather.19.cloned.1.call-start = ((), (), s32[]{:S(2)}) async-start(), calls=%async_computation.21 | async-start | bytes 4718592 | tf_op jit(solution)/shard_map/all_gather | solution.py:215
  1120.7 213.7 %reduce-scatter.21.cloned.1.call-start = ((), (), s32[]{:S(2)}) async-start(), calls=%async_computation.23 | async-start | bytes 3932160 | tf_op jit(solution)/shard_map/reduce_scatter | solution.py:248
  1173.0 7.4 copy-start.43
  1197.3 7.2 copy-start.39
  1206.2 16.4 copy-start.35
  1206.2 18.3 copy-start.33
  1209.8 16.4 copy-start.48
  1224.5 7.3 copy-start.25
  1231.8 141.5 %reduce-scatter.23.cloned.1.call-start = ((), (), s32[]{:S(2)}) async-start(), calls=%async_computation.24 | async-start | bytes 1310720 | tf_op jit(solution)/shard_map/reduce_scatter | solution.py:218
  1236.4 149.0 %reduce-scatter.19.cloned.1.call-start = ((), (), s32[]{:S(2)}) async-start(), calls=%async_computation.22 | async-start | bytes 4718592 | tf_op jit(solution)/shard_map/reduce_scatter | solution.py:246
  1244.3 499.4 %reduce-scatter.13.cloned.1.call-start = ((), (), s32[]{:S(2)}) async-start(), calls=%async_computation.17 | async-start | bytes 17301504 | tf_op jit(solution)/shard_map/reduce_scatter | solution.py:177
  1269.3 65.1 %all-to-all-start.3 = ((bf16[8,256,512]{2,1,0:T(8,128)(2,1)}), bf16[8,256,512]{2,1,0:T(8,128)(2,1)}, u32[]{:S(2)}, u32[]{:S(2)}) async-start(bf16[8,256,512]{2,1,0:T(8,128)(2,1)} %bitcast.208), calls=%async_computation.10 | async-start | bytes 4194304 | tf_op jit(solution)/shard_map/all_to_all | solution.py:195
  1334.4 40.6 %all-to-all-start.2 = ((bf16[8,64,768]{2,1,0:T(8,128)(2,1)}), bf16[8,64,768]{2,1,0:T(8,128)(2,1)S(1)}, u32[]{:S(2)}, u32[]{:S(2)}) async-start(bf16[8,64,768]{2,1,0:T(8,128)(2,1)} %reduce-scatter.21.cloned.1.call-done), calls=%async_computation.8 | async-start | bytes 1572864 | tf_op jit(solution)/shard_map/all_to_all | solution.py:249
  1342.4 12.4 copy-start.51
  1342.4 523.4 %reduce-scatter.25.cloned.1.call-start = ((), (), s32[]{:S(2)}) async-start(), calls=%async_computation.25 | async-start | bytes 1081344
  1382.0 361.7 %copy-start.6 = (bf16[128,2048]{1,0:T(8,128)(2,1)S(1)}, bf16[128,2048]{1,0:T(8,128)(2,1)}, u32[]{:S(2)}) copy-start(bf16[128,2048]{1,0:T(8,128)(2,1)} %reduce-scatter.11.cloned.1.call-done) | copy-start | bytes 1572868
  1382.0 361.7 %copy-start.8 = (bf16[2,64,2048]{2,1,0:T(8,128)(2,1)S(1)}, bf16[2,64,2048]{2,1,0:T(8,128)(2,1)}, u32[]{:S(2)}) copy-start(bf16[2,64,2048]{2,1,0:T(8,128)(2,1)} %param.33) | copy-start | bytes 1572868
  (27 other events, 91.2 us)
Sparse Core Ops, SparseCore 0:
  9.6 61.6 all-gather.8
  73.2 47.2 all-gather.10
  122.3 26.4 all-gather.12
  202.1 48.2 reduce-scatter.10
  253.9 147.2 all-gather.14
  404.0 113.0 all-gather.16
  538.0 115.7 reduce-scatter.16
  742.1 372.7 reduce-scatter.14
  1120.8 47.5 all-gather.18
  1231.9 46.6 reduce-scatter.20
  1281.8 27.7 reduce-scatter.22
  1311.7 72.5 reduce-scatter.18
  1386.6 357.0 reduce-scatter.12
  1745.7 120.0 reduce-scatter.24

commit v2 on v1

--- a/solution.py
+++ b/solution.py
@@ -1,6 +1,10 @@
+import functools
+
 import jax
 import jax.numpy as jnp
 from jax import lax
+from jax.experimental import pallas as pl
+from jax.experimental.pallas import tpu as pltpu
 from jax.sharding import PartitionSpec as P
 
 HEAD = 128
@@ -46,6 +50,616 @@
     return jnp.concatenate(
         [first * cos_part - second * sin_part, second * cos_part + first * sin_part], axis=-1
     )
+
+ANY = pl.BlockSpec(memory_space=pl.ANY)
+VMEM_LIMIT = 60 * 1024 * 1024
+
+
+class Place:
+    def __init__(self, n_seq, n_bat):
+        self.n_seq, self.n_bat, self.half = n_seq, n_bat, n_seq // 2
+        self.s = lax.axis_index("seq")
+        self.b = lax.axis_index("batch")
+        self.twin_s = self.s + 1 - 2 * lax.rem(self.s, 2)
+
+    def seq_at(self, k):
+        return lax.rem(self.s + (k + self.n_seq), self.n_seq)
+
+    def twin_at(self, k):
+        return lax.rem(self.twin_s + (k + self.n_seq), self.n_seq)
+
+    def bat_at(self, k):
+        return lax.rem(self.b + (k + self.n_bat), self.n_bat)
+
+    def seq_peer(self, k):
+        return {"seq": self.seq_at(k), "batch": self.b}
+
+    def bat_peer(self, k):
+        return {"seq": self.s, "batch": self.bat_at(k)}
+
+    def twin(self):
+        return {"seq": self.twin_s, "batch": self.b}
+
+    def greet(self, all_seq=False, batch=True):
+        steps = range(1, self.n_seq) if all_seq else range(2, self.n_seq, 2)
+        peers = [self.seq_peer(k) for k in steps]
+        if not all_seq:
+            peers.append(self.twin())
+        if batch:
+            peers += [self.bat_peer(k) for k in range(1, self.n_bat)]
+        barrier = pltpu.get_barrier_semaphore()
+        for peer in peers:
+            pl.semaphore_signal(
+                barrier, inc=1, device_id=peer, device_id_type=pl.DeviceIdType.MESH
+            )
+        pl.semaphore_wait(barrier, len(peers))
+
+
+class Wire:
+    def __init__(self, send_sems, recv_sems):
+        self.send_sems, self.recv_sems = send_sems, recv_sems
+        self.copies = []
+
+    def push(self, src, dst, peer):
+        slot = len(self.copies)
+        copy = pltpu.make_async_remote_copy(
+            src_ref=src,
+            dst_ref=dst,
+            send_sem=self.send_sems.at[slot],
+            recv_sem=self.recv_sems.at[slot],
+            device_id=peer,
+            device_id_type=pl.DeviceIdType.MESH,
+        )
+        copy.start()
+        self.copies.append(copy)
+        return copy
+
+    def drain(self):
+        for copy in self.copies:
+            copy.wait_send()
+
+
+class SeqGather:
+    def __init__(self, place, wire, src, out):
+        self.place, self.wire, self.src, self.out = place, wire, src, out
+        self.late = []
+
+    def start(self):
+        place, mine = self.place, self.out.at[self.place.s]
+        self.line = [
+            self.wire.push(self.src, mine, place.seq_peer(2 * j)) for j in range(1, place.half)
+        ]
+        self.late.append(self.wire.push(self.src, mine, place.twin()))
+
+    def step(self, j):
+        self.line[j - 1].wait_recv()
+        block = self.out.at[self.place.seq_at(-2 * j)]
+        self.late.append(self.wire.push(block, block, self.place.twin()))
+
+    def finish(self):
+        for copy in self.late:
+            copy.wait_recv()
+
+
+class FullGather:
+    def __init__(self, place, wire, src, out):
+        self.place, self.wire, self.src, self.out = place, wire, src, out
+        self.late = []
+        self.across = {}
+
+    def spread(self, j, block):
+        place = self.place
+        self.across[j] = [
+            self.wire.push(block, self.out.at[place.seq_at(-2 * j), place.b], place.bat_peer(k))
+            for k in range(1, place.n_bat)
+        ]
+
+    def start(self):
+        place, mine = self.place, self.out.at[self.place.s, self.place.b]
+        self.line = [
+            self.wire.push(self.src, mine, place.seq_peer(2 * j)) for j in range(1, place.half)
+        ]
+        self.spread(0, self.src)
+        self.late.append(self.wire.push(self.src, mine, place.twin()))
+
+    def step(self, j):
+        self.line[j - 1].wait_recv()
+        block = self.out.at[self.place.seq_at(-2 * j), self.place.b]
+        self.spread(j, block)
+        self.late.append(self.wire.push(block, block, self.place.twin()))
+
+    def collect(self, j):
+        place = self.place
+        for k in range(1, place.n_bat):
+            self.across[j][k - 1].wait_recv()
+            block = self.out.at[place.seq_at(-2 * j), place.bat_at(-k)]
+            self.late.append(self.wire.push(block, block, place.twin()))
+
+    def finish(self):
+        for copy in self.late:
+            copy.wait_recv()
+
+
+def keep_own(src, dst, buffer, sem):
+    first = pltpu.make_async_copy(src, buffer, sem)
+    first.start()
+    first.wait()
+    second = pltpu.make_async_copy(buffer, dst, sem)
+    second.start()
+    return second
+
+
+def comm_call(kernel, outs, scratch, slots, collective_id, name, in_specs, out_specs=None):
+    return pl.pallas_call(
+        kernel,
+        out_shape=outs,
+        in_specs=in_specs,
+        out_specs=out_specs if out_specs is not None else jax.tree.map(lambda _: ANY, outs),
+        scratch_shapes=list(scratch)
+        + [pltpu.SemaphoreType.DMA((slots,)), pltpu.SemaphoreType.DMA((slots,))],
+        compiler_params=pltpu.CompilerParams(
+            collective_id=collective_id, has_side_effects=True, vmem_limit_bytes=VMEM_LIMIT
+        ),
+        name=name,
+    )
+
+
+def shape_of(lead, block):
+    return jax.ShapeDtypeStruct(tuple(lead) + block.shape, block.dtype)
+
+
+def gather_seq(block, n_seq, n_bat, collective_id, name):
+    def kernel(src, out, buffer, own_sem, send_sems, recv_sems):
+        place = Place(n_seq, n_bat)
+        place.greet(batch=False)
+        gather = SeqGather(place, wire := Wire(send_sems, recv_sems), src, out)
+        gather.start()
+        own = keep_own(src, out.at[place.s], buffer, own_sem)
+        for j in range(1, place.half):
+            gather.step(j)
+        gather.finish()
+        own.wait()
+        wire.drain()
+
+    return comm_call(
+        kernel,
+        shape_of((n_seq,), block),
+        [pltpu.VMEM(block.shape, block.dtype), pltpu.SemaphoreType.DMA],
+        n_seq,
+        collective_id,
+        name,
+        [ANY],
+    )(block)
+
+
+def gather_all(blocks, n_seq, n_bat, collective_id, name):
+    count = len(blocks)
+
+    def kernel(*refs):
+        srcs, outs = refs[:count], refs[count : 2 * count]
+        buffers = refs[2 * count : 3 * count]
+        own_sems, send_sems, recv_sems = refs[3 * count :]
+        place = Place(n_seq, n_bat)
+        place.greet()
+        wire = Wire(send_sems, recv_sems)
+        gathers = [FullGather(place, wire, *pair) for pair in zip(srcs, outs)]
+        for gather in gathers:
+            gather.start()
+        own = [
+            keep_own(srcs[i], outs[i].at[place.s, place.b], buffers[i], own_sems.at[i])
+            for i in range(count)
+        ]
+        for j in range(1, place.half):
+            for gather in gathers:
+                gather.step(j)
+            for gather in gathers:
+                gather.collect(j - 1)
+        for gather in gathers:
+            gather.collect(place.half - 1)
+        for gather in gathers:
+            gather.finish()
+        for copy in own:
+            copy.wait()
+        wire.drain()
+
+    return comm_call(
+        kernel,
+        [shape_of((n_seq, n_bat), block) for block in blocks],
+        [pltpu.VMEM(block.shape, block.dtype) for block in blocks]
+        + [pltpu.SemaphoreType.DMA((count,))],
+        n_seq * n_bat * count,
+        collective_id,
+        name,
+        [ANY] * count,
+    )(*blocks)
+
+
+def add_into(target, *others):
+    rows = target.shape[0]
+    step = min(rows, 16)
+
+    def body(i, carry):
+        at = pl.ds(pl.multiple_of(i * step, step), step)
+        total = target[at, :].astype(F32)
+        for other in others:
+            total = total + other[at, :].astype(F32)
+        target[at, :] = total.astype(target.dtype)
+        return carry
+
+    lax.fori_loop(0, rows // step, body, 0)
+
+
+class FullScatter:
+    def __init__(self, place, wire, parts, out, mine, twin, across, line, sems, local):
+        self.place, self.wire, self.parts, self.out = place, wire, parts, out
+        self.mine, self.twin, self.across, self.line = mine, twin, across, line
+        self.sems, self.local = sems, local
+
+    @staticmethod
+    def scratch(n_seq, n_bat, block):
+        half = n_seq // 2
+        return [
+            pltpu.VMEM((half, n_bat) + block.shape, block.dtype),
+            pltpu.VMEM((half, n_bat) + block.shape, block.dtype),
+            pltpu.VMEM((half, n_bat) + block.shape, block.dtype),
+            pltpu.VMEM((half,) + block.shape, block.dtype),
+            pltpu.SemaphoreType.DMA((half, n_bat)),
+        ]
+
+    def order(self):
+        return list(range(1, self.place.half)) + [0]
+
+    def start(self):
+        place = self.place
+        self.from_twin, self.loads, self.from_bat, self.from_seq = {}, {}, {}, {}
+        for j in self.order():
+            for k in list(range(1, place.n_bat)) + [0]:
+                to_bat = place.bat_at(k)
+                self.from_twin[j, k] = self.wire.push(
+                    self.parts.at[place.twin_at(2 * j), to_bat], self.twin.at[j, k], place.twin()
+                )
+                load = pltpu.make_async_copy(
+                    self.parts.at[place.seq_at(2 * j), to_bat],
+                    self.mine.at[j, k],
+                    self.sems.at[j, k],
+                )
+                load.start()
+                self.loads[j, k] = load
+
+    def pair(self, j):
+        place = self.place
+        for k in list(range(1, place.n_bat)) + [0]:
+            self.from_twin[j, k].wait_recv()
+            self.loads[j, k].wait()
+            add_into(self.mine.at[j, k], self.twin.at[j, k])
+        for k in range(1, place.n_bat):
+            self.from_bat[j, k] = self.wire.push(
+                self.mine.at[j, k], self.across.at[j, k], place.bat_peer(k)
+            )
+
+    def merge(self, j):
+        place = self.place
+        for k in range(1, place.n_bat):
+            self.from_bat[j, k].wait_recv()
+        add_into(self.mine.at[j, 0], *[self.across.at[j, k] for k in range(1, place.n_bat)])
+        if j:
+            self.from_seq[j] = self.wire.push(
+                self.mine.at[j, 0], self.line.at[j], place.seq_peer(2 * j)
+            )
+
+    def finish(self):
+        for j in range(1, self.place.half):
+            self.from_seq[j].wait_recv()
+        add_into(self.mine.at[0, 0], *[self.line.at[j] for j in range(1, self.place.half)])
+        self.out[...] = self.mine[0, 0]
+
+
+def scatter_all(parts, n_seq, n_bat, collective_id, name):
+    blocks = [jax.ShapeDtypeStruct(part.shape[2:], part.dtype) for part in parts]
+    count = len(parts)
+
+    def kernel(*refs):
+        ins, outs = refs[:count], refs[count : 2 * count]
+        rest = refs[2 * count :]
+        send_sems, recv_sems = rest[-2:]
+        place = Place(n_seq, n_bat)
+        place.greet()
+        wire = Wire(send_sems, recv_sems)
+        works = [
+            FullScatter(place, wire, ins[i], outs[i], *rest[5 * i : 5 * i + 5], None)
+            for i in range(count)
+        ]
+        for work in works:
+            work.start()
+        order = works[0].order()
+        for at, j in enumerate(order):
+            for work in works:
+                work.pair(j)
+            if at:
+                for work in works:
+                    work.merge(order[at - 1])
+        for work in works:
+            work.merge(order[-1])
+        for work in works:
+            work.finish()
+        wire.drain()
+
+    scratch = []
+    for block in blocks:
+        scratch += FullScatter.scratch(n_seq, n_bat, block)
+    slots = count * (n_seq * n_bat)
+    vmem = pl.BlockSpec(memory_space=pltpu.VMEM)
+    return comm_call(
+        kernel,
+        blocks,
+        scratch,
+        slots,
+        collective_id,
+        name,
+        [ANY] * count,
+        [vmem] * count,
+    )(*parts)
+
+
+def scatter_seq(parts, n_seq, n_bat, collective_id, name):
+    block = jax.ShapeDtypeStruct(parts.shape[1:], parts.dtype)
+    half = n_seq // 2
+
+    def kernel(ref, out, mine, twin, line, sems, send_sems, recv_sems):
+        place = Place(n_seq, n_bat)
+        place.greet(batch=False)
+        wire = Wire(send_sems, recv_sems)
+        order = list(range(1, half)) + [0]
+        from_twin, loads, from_seq = {}, {}, {}
+        for j in order:
+            from_twin[j] = wire.push(ref.at[place.twin_at(2 * j)], twin.at[j], place.twin())
+            loads[j] = pltpu.make_async_copy(ref.at[place.seq_at(2 * j)], mine.at[j], sems.at[j])
+            loads[j].start()
+        for j in order:
+            from_twin[j].wait_recv()
+            loads[j].wait()
+            add_into(mine.at[j], twin.at[j])
+            if j:
+                from_seq[j] = wire.push(mine.at[j], line.at[j], place.seq_peer(2 * j))
+        for j in range(1, half):
+            from_seq[j].wait_recv()
+        add_into(mine.at[0], *[line.at[j] for j in range(1, half)])
+        out[...] = mine[0]
+        wire.drain()
+
+    scratch = [pltpu.VMEM((half,) + block.shape, block.dtype)] * 3
+    return comm_call(
+        kernel,
+        block,
+        scratch + [pltpu.SemaphoreType.DMA((half,))],
+        n_seq,
+        collective_id,
+        name,
+        [ANY],
+        pl.BlockSpec(memory_space=pltpu.VMEM),
+    )(parts)
+
+
+def pack(values):
+    flat = values.astype(F32).reshape(-1)
+    tiles = -(-flat.shape[0] // 1024)
+    return jnp.pad(flat, (0, tiles * 1024 - flat.shape[0])).reshape(tiles * 8, 128)
+
+
+def unpack(tiles, lead, shape):
+    size = 1
+    for extent in shape:
+        size *= extent
+    return tiles.reshape(tuple(lead) + (-1,))[..., :size].reshape(tuple(lead) + tuple(shape))
+
+def sum_seq(values, n_seq, n_bat, collective_id, name):
+    tiles = gather_seq(pack(values), n_seq, n_bat, collective_id, name)
+    return unpack(jnp.sum(tiles, axis=0), (), values.shape)
+
+
+def scatter_blocks(grad_normed, grad_gates, mixture, n_seq, n_bat):
+    dim = grad_normed.shape[-1]
+    pieces = 1
+    while n_seq * n_bat * grad_normed.shape[2] * (dim // pieces) * 4 > 36 * 1024 * 1024:
+        pieces *= 2
+    size = dim // pieces
+    grads, mixtures = [], []
+    for i in range(pieces):
+        at = slice(i * size, (i + 1) * size)
+        parts = [grad_normed[..., at]] + ([grad_gates] if i == 0 else [])
+        done = scatter_all(parts, n_seq, n_bat, 16 + 2 * i, "scatter_normed")
+        grads.append(done[0])
+        if i == 0:
+            gates = done[1]
+        done = scatter_all([mixture[..., at]], n_seq, n_bat, 17 + 2 * i, "scatter_mixture")
+        mixtures.append(done[0])
+    return jnp.concatenate(grads, axis=-1), gates, jnp.concatenate(mixtures, axis=-1)
+
+
+def load_inputs(qkv_cut, w_out, mine, flags, small, gu_cut, dy_own, n_seq, n_bat):
+    n_in = 7
+    slots = 4 * n_seq * n_bat + 3 * n_seq + 2 * n_bat
+
+    def kernel(*refs):
+        cut_ref, wo_ref, x_ref, flag_ref, small_ref, gu_ref, dy_ref = refs[:n_in]
+        w_ref, wo_all, x_col, flag_col, small_all, gu_all, dy_all = refs[n_in : 2 * n_in]
+        buffers = refs[2 * n_in : 3 * n_in]
+        own_sems, send_sems, recv_sems = refs[3 * n_in :]
+        place = Place(n_seq, n_bat)
+        place.greet(all_seq=True)
+        wire = Wire(send_sems, recv_sems)
+        small_work = FullGather(place, wire, small_ref, small_all)
+        flag_work = SeqGather(place, wire, flag_ref, flag_col)
+        x_work = SeqGather(place, wire, x_ref, x_col)
+        dy_work = FullGather(place, wire, dy_ref, dy_all)
+        small_work.start()
+        flag_work.start()
+        cuts = [
+            wire.push(cut_ref.at[place.seq_at(k)], w_ref.at[place.s, place.b], place.seq_peer(k))
+            for k in range(1, n_seq)
+        ]
+        ends = [
+            wire.push(wo_ref, wo_all.at[place.b], place.bat_peer(k)) for k in range(1, n_bat)
+        ]
+        ends += [
+            wire.push(cut_ref.at[place.s], w_ref.at[place.s, place.b], place.bat_peer(k))
+            for k in range(1, n_bat)
+        ]
+        x_work.start()
+        own = [
+            keep_own(src, dst, buffers[i], own_sems.at[i])
+            for i, (src, dst) in enumerate(
+                (
+                    (cut_ref.at[place.s], w_ref.at[place.s, place.b]),
+                    (wo_ref, wo_all.at[place.b]),
+                    (x_ref, x_col.at[place.s]),
+                    (flag_ref, flag_col.at[place.s]),
+                    (small_ref, small_all.at[place.s, place.b]),
+                    (gu_ref.at[place.s], gu_all.at[place.s]),
+                    (dy_ref, dy_all.at[place.s, place.b]),
+                )
+            )
+        ]
+        ends += [
+            wire.push(gu_ref.at[place.seq_at(k)], gu_all.at[place.s], place.seq_peer(k))
+            for k in range(1, n_seq)
+        ]
+        dy_work.start()
+        for j in range(1, place.half):
+            small_work.step(j)
+            flag_work.step(j)
+        for k in range(1, n_seq):
+            cuts[k - 1].wait_recv()
+            block = w_ref.at[place.seq_at(-k), place.b]
+            ends += [wire.push(block, block, place.bat_peer(m)) for m in range(1, n_bat)]
+        for j in range(place.half):
+            small_work.collect(j)
+        for j in range(1, place.half):
+            x_work.step(j)
+        for j in range(1, place.half):
+            dy_work.step(j)
+            dy_work.collect(j - 1)
+        dy_work.collect(place.half - 1)
+        for work in (small_work, flag_work, x_work, dy_work):
+            work.finish()
+        for copy in ends:
+            copy.wait_recv()
+        for copy in own:
+            copy.wait()
+        wire.drain()
+
+    every = (n_seq, n_bat)
+    one = jax.ShapeDtypeStruct(qkv_cut.shape[1:], qkv_cut.dtype)
+    gu_one = jax.ShapeDtypeStruct(gu_cut.shape[1:], gu_cut.dtype)
+    blocks = (one, w_out, mine, flags, small, gu_one, dy_own)
+    leads = (every, (n_bat,), (n_seq,), (n_seq,), every, (n_seq,), every)
+    return comm_call(
+        kernel,
+        [shape_of(lead, block) for lead, block in zip(leads, blocks)],
+        [pltpu.VMEM(block.shape, block.dtype) for block in blocks]
+        + [pltpu.SemaphoreType.DMA((n_in,))],
+        slots,
+        1,
+        "load_inputs",
+        [ANY] * n_in,
+    )(qkv_cut, w_out, mine, flags, small, gu_cut, dy_own)
+
+
+def store_grads(grad_w, grad_wo, grad_gu, small, n_seq, n_bat):
+    one = jax.ShapeDtypeStruct(grad_w.shape[2:], grad_w.dtype)
+    wo_one = jax.ShapeDtypeStruct(grad_wo.shape[1:], grad_wo.dtype)
+    gu_one = jax.ShapeDtypeStruct(grad_gu.shape[1:], grad_gu.dtype)
+    small_one = jax.ShapeDtypeStruct(small.shape[2:], small.dtype)
+    slots = 2 * n_seq * n_bat + 2 * n_seq + n_bat
+
+    def kernel(*refs):
+        w_ref, wo_ref, gu_ref, small_ref = refs[:4]
+        w_out_ref, wo_out_ref, gu_out_ref, small_out_ref = refs[4:8]
+        w_sum, w_got, wo_sum, wo_got, gu_buf, cut_buf = refs[8:14]
+        small_scratch = refs[14:19]
+        w_sems, sems, send_sems, recv_sems = refs[19:]
+        place = Place(n_seq, n_bat)
+        place.greet(all_seq=True)
+        wire = Wire(send_sems, recv_sems)
+        small_work = FullScatter(
+            place, wire, small_ref, small_out_ref, *small_scratch, None
+        )
+        small_work.start()
+        got, loads = {}, {}
+        for i in list(range(1, n_seq)) + [0]:
+            to_seq = place.seq_at(i)
+            for k in range(1, n_bat):
+                got[i, k] = wire.push(
+                    w_ref.at[to_seq, place.bat_at(k)], w_got.at[i, k - 1], place.bat_peer(k)
+                )
+            loads[i] = pltpu.make_async_copy(
+                w_ref.at[to_seq, place.b], w_sum.at[i], w_sems.at[i]
+            )
+            loads[i].start()
+        wo_pushed = [
+            wire.push(wo_ref.at[place.bat_at(k)], wo_got.at[k - 1], place.bat_peer(k))
+            for k in range(1, n_bat)
+        ]
+        wo_load = pltpu.make_async_copy(wo_ref.at[place.b], wo_sum, sems.at[0])
+        wo_load.start()
+        ends = [
+            wire.push(gu_ref.at[place.seq_at(k)], gu_out_ref.at[place.s], place.seq_peer(k))
+            for k in range(1, n_seq)
+        ]
+        gu_own = keep_own(gu_ref.at[place.s], gu_out_ref.at[place.s], gu_buf, sems.at[1])
+        order = small_work.order()
+        for j in order:
+            small_work.pair(j)
+        for i in list(range(1, n_seq)) + [0]:
+            loads[i].wait()
+            for k in range(1, n_bat):
+                got[i, k].wait_recv()
+            add_into(w_sum.at[i], *[w_got.at[i, k] for k in range(n_bat - 1)])
+            if i:
+                ends.append(
+                    wire.push(w_sum.at[i], w_out_ref.at[place.s], place.seq_peer(i))
+                )
+        w_own = pltpu.make_async_copy(w_sum.at[0], w_out_ref.at[place.s], sems.at[2])
+        w_own.start()
+        for j in order:
+            small_work.merge(j)
+        wo_load.wait()
+        for copy in wo_pushed:
+            copy.wait_recv()
+        add_into(wo_sum, *[wo_got.at[k] for k in range(n_bat - 1)])
+        wo_out_ref[...] = wo_sum[...].astype(F32)
+        small_work.finish()
+        for copy in ends:
+            copy.wait_recv()
+        gu_own.wait()
+        w_own.wait()
+        wire.drain()
+
+    vmem = pl.BlockSpec(memory_space=pltpu.VMEM)
+    return comm_call(
+        kernel,
+        [
+            shape_of((n_seq,), one),
+            jax.ShapeDtypeStruct(wo_one.shape, F32),
+            shape_of((n_seq,), gu_one),
+            small_one,
+        ],
+        [
+            pltpu.VMEM((n_seq,) + one.shape, one.dtype),
+            pltpu.VMEM((n_seq, n_bat - 1) + one.shape, one.dtype),
+            pltpu.VMEM(wo_one.shape, wo_one.dtype),
+            pltpu.VMEM((n_bat - 1,) + wo_one.shape, wo_one.dtype),
+            pltpu.VMEM(gu_one.shape, gu_one.dtype),
+            pltpu.VMEM(one.shape, one.dtype),
+        ]
+        + FullScatter.scratch(n_seq, n_bat, small_one)
+        + [pltpu.SemaphoreType.DMA((n_seq,)), pltpu.SemaphoreType.DMA((3,))],
+        slots,
+        8,
+        "store_grads",
+        [ANY] * 4,
+        [ANY, vmem, ANY, vmem],
+    )(grad_w, grad_wo, grad_gu, small)
 
 
 def shards(
@@ -81,39 +695,44 @@
     local_experts, depth, hidden_units = expert_gate.shape
     part = hidden_units // n_seq
     experts = local_experts * n_bat
-    every = ("seq", "batch")
     score_scale = HEAD ** (-0.5)
 
+    mine = tokens.reshape(own, dim)
+    dy_own = cotangent.reshape(own, dim)
     small = jnp.concatenate(
-        [w_router, jnp.stack([attn_gain, query_gain, key_gain, mlp_gain], axis=1)], axis=1
-    )
-    small_all = lax.all_gather(small, every, axis=0, tiled=True)
-    router = small_all[:, :experts]
-    gain_attn = small_all[:, experts].astype(F32)
-    gain_mlp = small_all[:, experts + 3].astype(F32)
-    gain_q = lax.dynamic_slice_in_dim(small_all[:, experts + 1], seq * wide, wide).astype(F32)
-    gain_k = lax.dynamic_slice_in_dim(small_all[:, experts + 2], seq * wide, wide).astype(F32)
-
+        [w_router.T, jnp.stack([attn_gain, query_gain, key_gain, mlp_gain])], axis=0
+    )
+    positions_own = seq * span + jnp.arange(span, dtype=jnp.int32)
+    flags = pack((positions_own[None, :] < lengths[:, None]) & (key_mask == 1))
     qkv_cut = jnp.stack([w_query, w_key, w_value]).reshape(3, shard, n_seq, wide)
     qkv_cut = jnp.transpose(qkv_cut, (2, 1, 0, 3)).reshape(n_seq, shard, 3 * wide)
-    qkv_cut = lax.all_to_all(qkv_cut, "seq", 0, 0, tiled=True)
-    w_qkv = lax.all_gather(qkv_cut, "batch", axis=1, tiled=True).reshape(dim, 3 * wide)
-    w_o = lax.all_gather(w_out, "batch", axis=0, tiled=True)
-
     gu_cut = jnp.stack([expert_gate, expert_up]).reshape(2, local_experts, depth, n_seq, part)
     gu_cut = jnp.transpose(gu_cut, (3, 2, 0, 1, 4)).reshape(n_seq, depth, 2 * local_experts * part)
-    w_gu = lax.all_to_all(gu_cut, "seq", 0, 0, tiled=True).reshape(dim, 2 * local_experts * part)
+    w_qkv, w_o, x_col, flag_col, small_all, w_gu, dy_all = load_inputs(
+        qkv_cut, w_out, mine, flags, pack(small), gu_cut, dy_own, n_seq, n_bat
+    )
+    w_qkv = w_qkv.reshape(dim, 3 * wide)
+    w_o = w_o.reshape(wide, dim)
+    w_gu = w_gu.reshape(dim, 2 * local_experts * part)
     w_down = expert_down.reshape(local_experts * part, dim)
-
-    mine = tokens.reshape(own, dim)
-    x_col = lax.all_gather(mine, "seq", axis=0, tiled=True).astype(F32)
+    dy_all = dy_all.reshape(-1, dim)
+    small_all = unpack(small_all, (n_seq, n_bat), small.shape)
+    small_all = jnp.transpose(small_all, (2, 0, 1, 3)).reshape(-1, dim)
+    router = small_all[:experts].T.astype(BF)
+    gain_attn, gain_mlp = small_all[experts], small_all[experts + 3]
+    gain_q = lax.dynamic_slice_in_dim(small_all[experts + 1], seq * wide, wide)
+    gain_k = lax.dynamic_slice_in_dim(small_all[experts + 2], seq * wide, wide)
+    usable = unpack(flag_col, (n_seq,), key_mask.shape)
+    usable = jnp.transpose(usable, (1, 0, 2)).reshape(rows, length) > 0
+
+    x_col = x_col.reshape(col, dim).astype(F32)
     scale_x = rms_scale(x_col)
     hidden = (x_col * scale_x * gain_attn).astype(BF)
     qkv = dot(hidden, w_qkv)
     q_pre, k_pre, v_pre = qkv[:, :wide], qkv[:, wide : 2 * wide], qkv[:, 2 * wide :]
 
     squares = jnp.stack([jnp.sum(q_pre * q_pre, axis=-1), jnp.sum(k_pre * k_pre, axis=-1)])
-    squares = lax.psum(squares, "seq")
+    squares = sum_seq(squares, n_seq, n_bat, 2, "sum_squares")
     scales = lax.rsqrt(squares / dim + EPS)
     scale_q, scale_k = scales[0][:, None], scales[1][:, None]
 
@@ -135,8 +754,6 @@
     keys = rotate(k_norm * gain_kh, cos_part, sin_part).astype(BF)
     values = by_row(v_pre.astype(BF))
 
-    mask_all = lax.all_gather(key_mask, "seq", axis=1, tiled=True)
-    usable = (positions[None, :] < lengths[:, None]) & (mask_all == 1)
     causal = positions[None, :] <= positions[:, None]
     same = positions[None, :] == positions[:, None]
     allowed = (causal[None] & (usable[:, None, :] | same[None]))[:, None]
@@ -149,7 +766,9 @@
     attended = jnp.einsum("rhqk,rhkd->rhqd", probs_low, values, preferred_element_type=F32)
     mixed = by_col(attended.astype(BF))
 
-    mixed_out = lax.psum_scatter(dot(mixed, w_o).astype(BF), "seq", scatter_dimension=0, tiled=True)
+    mixed_out = scatter_seq(
+        dot(mixed, w_o).astype(BF).reshape(n_seq, own, dim), n_seq, n_bat, 3, "scatter_mixed"
+    )
     x_own = mine.astype(F32)
     residual = x_own + mixed_out.astype(F32)
     scale_r = rms_scale(residual)
@@ -159,10 +778,10 @@
     chosen = jnp.any(top_experts.reshape(own, -1)[:, :, None] == expert_ids, axis=1).astype(F32)
     gates = router_probs * chosen
 
-    normed_all = lax.all_gather(normed, every, axis=0, tiled=True)
-    gates_all = lax.all_gather(gates, every, axis=0, tiled=True)
-    dy_own = cotangent.reshape(own, dim)
-    dy_all = lax.all_gather(dy_own, every, axis=0, tiled=True)
+    normed_all, gates_all = gather_all([normed, pack(gates.T)], n_seq, n_bat, 4, "gather_normed")
+    normed_all = normed_all.reshape(-1, dim)
+    gates_all = unpack(gates_all, (n_seq, n_bat), (experts, own))
+    gates_all = jnp.transpose(gates_all, (0, 1, 3, 2)).reshape(-1, experts)
     first_expert = bat * local_experts
     gates_here = lax.dynamic_slice_in_dim(gates_all, first_expert, local_experts, 1)
     units = local_experts * part
@@ -174,9 +793,7 @@
     active = (silu * up_pre).astype(BF).astype(F32)
     weighted = (active * gates_wide).astype(BF)
     mixture = dot(weighted, w_down).astype(BF)
-    mixture = lax.psum_scatter(mixture, every, scatter_dimension=0, tiled=True)
-    output = (residual + mixture.astype(F32)).astype(BF)
-
+    mixture = mixture.reshape(n_seq, n_bat, own, dim)
     back = dot_t(dy_all, w_down)
     gate_terms = jnp.sum((active * back).reshape(-1, local_experts, part), axis=-1)
     grad_active = back * gates_wide
@@ -186,16 +803,21 @@
     grad_down = t_dot(weighted, dy_all)
     grad_gu = t_dot(normed_all, grad_pre).astype(BF)
     grad_normed = dot_t(grad_pre, w_gu).astype(BF)
-    grad_normed = lax.psum_scatter(grad_normed, every, scatter_dimension=0, tiled=True).astype(F32)
+    gate_terms = gate_terms.reshape(n_seq, n_bat, own, local_experts)
     grad_gates = lax.dynamic_update_slice_in_dim(
-        jnp.zeros((normed_all.shape[0], experts), F32), gate_terms, first_expert, 1
-    )
-    grad_gates = lax.psum_scatter(grad_gates, every, scatter_dimension=0, tiled=True)
-
-    grad_gu = lax.all_to_all(grad_gu.reshape(n_seq, depth, -1), "seq", 0, 0, tiled=True)
-    grad_gu = grad_gu.reshape(n_seq, depth, 2, local_experts, part)
-    grad_gu = jnp.transpose(grad_gu, (2, 3, 1, 0, 4)).reshape(2, local_experts, depth, hidden_units)
-    grad_gu = grad_gu.astype(F32)
+        jnp.zeros((n_seq, n_bat, experts, own), F32),
+        jnp.transpose(gate_terms, (0, 1, 3, 2)),
+        first_expert,
+        2,
+    )
+    grad_gates = jax.vmap(jax.vmap(pack))(grad_gates)
+    grad_normed = grad_normed.reshape(n_seq, n_bat, own, dim)
+    grad_normed, grad_gates, mixture = scatter_blocks(
+        grad_normed, grad_gates, mixture, n_seq, n_bat
+    )
+    grad_normed = grad_normed.astype(F32)
+    grad_gates = unpack(grad_gates, (), (experts, own)).T
+    output = (residual + mixture.astype(F32)).astype(BF)
     grad_down = grad_down.reshape(local_experts, part, dim)
 
     grad_chosen = grad_gates * chosen
@@ -212,10 +834,9 @@
     grad_residual = dy_own.astype(F32) + grad_resid
     grad_o = grad_residual.astype(BF)
 
-    grad_o_col = lax.all_gather(grad_o, "seq", axis=0, tiled=True)
+    grad_o_col = gather_seq(grad_o, n_seq, n_bat, 6, "gather_grad_o").reshape(col, dim)
     grad_mixed = by_row(dot_t(grad_o_col, w_o).astype(BF))
-    grad_w_o = t_dot(mixed, grad_o_col).astype(BF)
-    grad_w_o = lax.psum_scatter(grad_w_o, "batch", scatter_dimension=0, tiled=True).astype(F32)
+    grad_w_o = t_dot(mixed, grad_o_col).astype(BF).reshape(n_bat, shard, dim)
     row_dot = jnp.sum(grad_mixed.astype(F32) * attended, axis=-1, keepdims=True)
     grad_values = jnp.einsum("rhqk,rhqd->rhkd", probs_low, grad_mixed, preferred_element_type=F32)
     grad_probs = jnp.einsum("rhqd,rhkd->rhqk", grad_mixed, values, preferred_element_type=F32)
@@ -237,18 +858,15 @@
     means = jnp.stack(
         [jnp.sum(q_weighted * q_flat, axis=-1), jnp.sum(k_weighted * k_flat, axis=-1)]
     )
-    means = lax.psum(means, "seq") / dim
+    means = sum_seq(means, n_seq, n_bat, 9, "sum_means") / dim
     grad_q_pre = (scale_q * (q_weighted - q_flat * means[0][:, None])).astype(BF)
     grad_k_pre = (scale_k * (k_weighted - k_flat * means[1][:, None])).astype(BF)
     grad_qkv = jnp.concatenate([grad_q_pre, grad_k_pre, by_col(grad_values).astype(BF)], axis=1)
 
     grad_hidden = dot_t(grad_qkv, w_qkv).astype(BF)
-    grad_hidden = lax.psum_scatter(grad_hidden, "seq", scatter_dimension=0, tiled=True).astype(F32)
-    grad_w = t_dot(hidden, grad_qkv).astype(BF).reshape(n_seq, n_bat * shard, 3 * wide)
-    grad_w = lax.psum_scatter(grad_w, "batch", scatter_dimension=1, tiled=True)
-    grad_w = lax.all_to_all(grad_w, "seq", 0, 0, tiled=True).astype(F32)
-    grad_w = grad_w.reshape(n_seq, shard, 3, wide)
-    grad_w = jnp.transpose(grad_w, (2, 1, 0, 3)).reshape(3, shard, dim)
+    grad_hidden = grad_hidden.reshape(n_seq, own, dim)
+    grad_hidden = scatter_seq(grad_hidden, n_seq, n_bat, 7, "scatter_hidden").astype(F32)
+    grad_w = t_dot(hidden, grad_qkv).astype(BF).reshape(n_seq, n_bat, shard, 3 * wide)
 
     grad_x, gain_attn_terms = rms_back(x_own, rms_scale(x_own), gain_attn, grad_hidden)
     grad_tokens = (grad_residual + grad_x).astype(BF)
@@ -256,33 +874,43 @@
     zeros = jnp.zeros((dim,), F32)
     small_grads = jnp.concatenate(
         [
-            grad_router,
+            grad_router.T,
             jnp.stack(
                 [
                     jnp.sum(gain_attn_terms, axis=0),
                     lax.dynamic_update_slice_in_dim(zeros, grad_gain_q, seq * wide, 0),
                     lax.dynamic_update_slice_in_dim(zeros, grad_gain_k, seq * wide, 0),
                     jnp.sum(gain_mlp_terms, axis=0),
-                ],
-                axis=1,
+                ]
             ),
         ],
-        axis=1,
-    )
-    small_grads = lax.psum_scatter(small_grads, every, scatter_dimension=0, tiled=True)
+        axis=0,
+    )
+    small_grads = jnp.transpose(small_grads.reshape(-1, n_seq, n_bat, shard), (1, 2, 0, 3))
+    small_grads = jax.vmap(jax.vmap(pack))(small_grads)
+    grad_gu = grad_gu.reshape(n_seq, depth, -1)
+    grad_w, grad_w_o, grad_gu, small_grads = store_grads(
+        grad_w, grad_w_o, grad_gu, small_grads, n_seq, n_bat
+    )
+    grad_w = grad_w.astype(F32).reshape(n_seq, shard, 3, wide)
+    grad_w = jnp.transpose(grad_w, (2, 1, 0, 3)).reshape(3, shard, dim)
+    grad_gu = grad_gu.reshape(n_seq, depth, 2, local_experts, part)
+    grad_gu = jnp.transpose(grad_gu, (2, 3, 1, 0, 4)).reshape(2, local_experts, depth, hidden_units)
+    grad_gu = grad_gu.astype(F32)
+    small_grads = unpack(small_grads, (), (experts + 4, shard))
 
     return (
         output.reshape(rows, span, dim),
         grad_tokens.reshape(rows, span, dim),
-        small_grads[:, experts],
-        small_grads[:, experts + 1],
-        small_grads[:, experts + 2],
-        small_grads[:, experts + 3],
+        small_grads[experts],
+        small_grads[experts + 1],
+        small_grads[experts + 2],
+        small_grads[experts + 3],
         grad_w[0],
         grad_w[1],
         grad_w[2],
         grad_w_o,
-        small_grads[:, :experts],
+        small_grads[:experts].T,
         grad_gu[0],
         grad_gu[1],
         grad_down,

time: 1900 us -> 1080 us (0.57)
  waiting for transfers between devices: 1340 us -> 0 us
  Pallas kernels: 0 us -> 764 us
  blocking collectives: 209 us -> 0 us
  starting transfers between devices: 25.6 us -> 0 us
    reduce_scatter x7 -> x0, waiting for transfers between devices: 891 us -> none  [the longest x1 373 us: shards(): lax.psum_scatter(grad_normed, every, scatter_dimension=0, tiled=True)]
    pallas_call x0 -> x10, Pallas kernels: none -> 764 us  [the longest x2 206 us: scatter_all(): comm_call(kernel, blocks, scratch, slots, collective_id, name, [ANY] * co...]
    all_gather x6 -> x0, waiting for transfers between devices: 203 us -> none  [the longest x1 101 us: shards(): dy_all = lax.all_gather(dy_own, every, axis=0, tiled=True)]
    all_gather x3 -> x0, blocking collectives: 131 us -> none  [the longest x1 64.1 us: shards(): gates_all = lax.all_gather(gates, every, axis=0, tiled=True)]
    all_to_all x3 -> x0, waiting for transfers between devices: 128 us -> none  [the longest x1 72.9 us: shards(): lax.all_to_all(gu_cut, 'seq', 0, 0, tiled=True)]
    unnamed x15 -> x0, waiting for transfers between devices: 121 us -> none
    all_to_all x1 -> x0, blocking collectives: 42.1 us -> none  [shards(): qkv_cut = lax.all_to_all(qkv_cut, 'seq', 0, 0, tiled=True)]
    psum x2 -> x0, blocking collectives: 36.5 us -> none  [the longest x1 25.1 us: shards(): squares = lax.psum(squares, 'seq')]
  transfers between devices with their start and end apart: 17 -> 0, of which waited for: 10 -> 0; matrix products, arithmetic and copies ran while one was open for 9% -> 0% of each run, Pallas kernels for 0% -> 0%
where the time goes in v2:
time: 1080 us; the launch traced here: 1060 us
  Pallas kernels  764 us (71%)
  matrix products  129 us (12%)
  local copies, waits for them, and re-layouts  104 us (10%)
  other arithmetic  65.7 us (6%)
    pallas_call x2, Pallas kernels, scatter_all(): comm_call(kernel, blocks, scratch, slots, collective_id, name, [ANY] * co...  206 us
    pallas_call x1, Pallas kernels, load_inputs(): comm_call(kernel, [shape_of(lead, block) for lead, block in zip(leads, bl...  188 us
    pallas_call x2, Pallas kernels, scatter_seq(): comm_call(kernel, block, scratch + [pltpu.SemaphoreType.DMA((half,))], n_...  105 us
    pallas_call x1, Pallas kernels, gather_all(): comm_call(kernel, [shape_of((n_seq, n_bat), block) for block in blocks],...  98 us
    pallas_call x3, Pallas kernels, gather_seq(): comm_call(kernel, shape_of((n_seq,), block), [pltpu.VMEM(block.shape, blo...  97.7 us
    pallas_call x1, Pallas kernels, store_grads(): comm_call(kernel, [shape_of((n_seq,), one), jax.ShapeDtypeStruct(wo_one.s...  68.9 us
    dot_general x4, matrix products, dot_t(): lax.dot_general(a, b, (((1,), (1,)), ((), ())), preferred_element_type=F32)  43.3 us
    dot_general x4, matrix products, t_dot(): lax.dot_general(a, b, (((0,), (0,)), ((), ())), preferred_element_type=F32)  32.3 us

profile of v2, /device:TPU:9, one launch (start us, length us, event | category | flops | bytes accessed | tf_op | source)
XLA Modules:
  0.0 1064.2 jit_solution(2941469327949793911)
XLA Ops:
  21.4 3.0 maximum_bitcast_fusion
  24.4 2.6 reshape.500.refs_5_
  27.0 188.4 %load_inputs.1 = (bf16[8,4,64,768]{3,2,1,0:T(8,128)(2,1)}, bf16[4,64,2048]{2,1,0:T(8,128)(2,1)}, bf16[8,128,2048]{2,1,0:T(8,128)(2,1)}, f32[8,8,128]{2,1,0:T(8,1...) custom-call(bf16[8,64,768]{2,1,0:T(8,128)(2,1)} %reshape.494.refs_0_, ...), custom_call_target="tpu_custom_call" | custom-call | tf_op jit(solution)/shard_map/load_inputs/pallas_call | solution.py:556
  217.7 3.1 multiply_reduce_fusion
  221.7 5.3 fusion.2
  228.9 3.6 fusion.48
  235.0 39.5 %sum_squares.1 = f32[8,16,128]{2,1,0:T(8,128)} custom-call(f32[16,128]{1,0:T(8,128)} %reshape.506.src), custom_call_target="tpu_custom_call" | custom-call | tf_op jit(solution)/shard_map/sum_squares/pallas_call | solution.py:224
  276.7 2.8 slice_multiply_fusion.1
  281.2 2.7 reshape.507
  286.4 2.5 copy.163
  288.9 2.9 reshape.509
  293.4 2.9 subtract_convert_fusion.1
  296.2 5.7 fusion.45
  301.9 2.8 fusion.9
  308.0 3.2 convolution_convert_fusion.2
  311.2 52.9 %scatter_mixed.1 = bf16[128,2048]{1,0:T(8,128)(2,1)} custom-call(bf16[8,128,2048]{2,1,0:T(8,128)(2,1)} %bitcast.256), custom_call_target="tpu_custom_call" | custom-call | tf_op jit(solution)/shard_map/scatter_mixed/pallas_call | solution.py:431
  368.2 98.0 %gather_normed.1 = (bf16[8,4,128,2048]{3,2,1,0:T(8,128)(2,1)}, f32[8,4,8,128]{3,2,1,0:T(8,128)}) custom-call(bf16[128,2048]{1,0:T(8,128)(2,1)} %copy-done.11, f32[8,128]{1,0:T(8,128)} %select_bitcast_fusion.refs_1_), custom_call_target="tpu_custom_call" | custom-call | tf_op jit(solution)/shard_map/gather_normed/pallas_call | solution.py:265
  467.1 15.3 %fusion.49 = f32[4096,512]{0,1:T(8,128)} fusion(bf16[4096,2048]{1,0:T(8,128)(2,1)} %bitcast.335, bf16[2048,512]{1,0:T(8,128)(2,1)} %bitcast.339), kind=kOutput, calls=%fused_computation.164 | convolution fusion | flops 8589934592 | bytes 27262976 | tf_op jit(solution)/shard_map/dot_general | solution.py:19
  482.4 19.4 %bitcast_reduce_fusion = (f32[4096,2]{0,1:T(2,128)S(1)}, bf16[4096,256]{0,1:T(8,128)(2,1)}, f32[4096,256]{0,1:T(8,128)S(1)}) fusion(f32[4096,512]{0,1:T(8,128)} %fusion.49, bf16[4096,2048]{1,0:T(8,128)(2,1)} %bitcast.333, bf16[256,2048]{1,0:T(8,128)(2,1)S(1)} %bitcast.254), kind=kOutput, calls=%fused_computation.13 | convolution fusion | flops 4304396288 | bytes 32538624 | tf_op jit(solution)/shard_map/dot_general | solution.py:23
  501.8 5.1 multiply_convert_fusion.3
  507.0 15.4 %convolution_convert_fusion.5 = bf16[2048,512]{1,0:T(8,128)(2,1)} fusion(bf16[4096,2048]{1,0:T(8,128)(2,1)} %bitcast.336, bf16[4096,256]{0,1:T(8,128)(2,1)} %get-tuple-element.53, bf16[4096,256]{0,1:T(8,128)(2,1)} %get-tuple-element.52), kind=kOutput, calls=%fused_computation.26 | convolution fusion | flops 8599371776 | bytes 23068672 | tf_op jit(solution)/shard_map/dot_general | solution.py:27
  522.4 9.6 fusion.50
  532.1 14.1 %convolution_convert_fusion = bf16[4096,2048]{1,0:T(8,128)(2,1)} fusion(bf16[2048,512]{1,0:T(8,128)(2,1)} %bitcast.340, bf16[4096,256]{0,1:T(8,128)(2,1)S(1)} %copy-done.22, bf16[4096,256]{0,1:T(8,128)(2,1)S(1)} %copy-done.21), kind=kOutput, calls=%fused_computation.1 | convolution fusion | flops 8606711808 | bytes 23068672 | tf_op jit(solution)/shard_map/dot_general | solution.py:23
  546.2 104.5 %scatter_normed.1 = (bf16[128,2048]{1,0:T(8,128)(2,1)}, f32[8,128]{1,0:T(8,128)}) custom-call(bf16[8,4,128,2048]{3,2,1,0:T(8,128)(2,1)} %bitcast.258, f32[8,4,8,128]{3,2,1,0:T(8,128)} %copy-done.33), custom_call_target="tpu_custom_call" | custom-call | tf_op jit(solution)/shard_map/scatter_normed/pallas_call | solution.py:392
  654.8 3.6 multiply_reduce_fusion.1
  661.1 2.6 fusion.41.src
  663.7 51.2 %gather_grad_o.1 = bf16[8,128,2048]{2,1,0:T(8,128)(2,1)} custom-call(bf16[128,2048]{1,0:T(8,128)(2,1)} %fusion.41.src), custom_call_target="tpu_custom_call" | custom-call | tf_op jit(solution)/shard_map/gather_grad_o/pallas_call | solution.py:224
  715.0 4.7 convolution_convert_fusion.8
  726.8 4.5 multiply_convert_fusion.1
  735.5 2.8 convolution_multiply_fusion
  743.0 2.8 multiply_reduce_fusion.3
  749.3 2.6 copy.188
  767.8 6.9 sum_means.1
  779.1 5.0 convolution_convert_fusion.4
  784.1 5.1 convolution_convert_fusion.3
  789.1 52.3 %scatter_hidden.1 = bf16[128,2048]{1,0:T(8,128)(2,1)} custom-call(bf16[8,128,2048]{2,1,0:T(8,128)(2,1)} %bitcast.273), custom_call_target="tpu_custom_call" | custom-call | tf_op jit(solution)/shard_map/scatter_hidden/pallas_call | solution.py:431
  844.0 68.9 %store_grads.1 = (bf16[8,64,768]{2,1,0:T(8,128)(2,1)}, f32[64,2048]{1,0:T(8,128)}, bf16[8,256,512]{2,1,0:T(8,128)(2,1)}, f32[8,128]{1,0:T(8,128)}) custom-call(bf16[8,4,64,768]{3,2,1,0:T(8,128)(2,1)} %bitcast.283, bf16[4,64,2048]{2,1,0:T(8,128)(2,1)} %bitcast.295, bf16[8,256,512]{2,1,0:T(8,128)(2,1)} %bitcast.284, f32[8,4,8,128]{3,2,1,0:T(8,128)} %copy.211.refs_3_), custom_call_target="tpu_custom_call" | custom-call | tf_op jit(solution)/shard_map/store_grads/pallas_call | solution.py:639
  915.6 3.5 reshape.548
  919.1 4.7 fusion.43
  927.6 5.4 reshape.549
  933.1 3.8 fusion.42
  936.9 2.5 copy.202
  939.4 2.7 squeeze.43
  942.1 4.1 copy.201
  946.3 2.7 squeeze.42
  949.0 9.7 convolution_convert_fusion.1
  958.7 101.2 %scatter_mixture.1 = bf16[128,2048]{1,0:T(8,128)(2,1)} custom-call(bf16[8,4,128,2048]{3,2,1,0:T(8,128)(2,1)} %bitcast.255), custom_call_target="tpu_custom_call" | custom-call | tf_op jit(solution)/shard_map/scatter_mixture/pallas_call | solution.py:392
  1060.0 3.2 fusion.15
  (265 shorter events, 100.0 us)
Async XLA Ops:
  6.0 361.6 %copy-start.43 = (pred[128,8]{0,1:T(8,128)(4,1)}, pred[128,8]{0,1:T(8,128)(4,1)S(1)}, u32[]{:S(2)}) copy-start(pred[128,8]{0,1:T(8,128)(4,1)S(1)} %fusion.26) | copy-start | bytes 3076
  9.5 9.2 copy-start.27
  15.9 4.1 copy-start.28
  27.0 189.4 %copy-start.30 = (pred[512,512]{0,1:T(8,128)(4,1)S(1)}, pred[512,512]{0,1:T(8,128)(4,1)}, u32[]{:S(2)}) copy-start(pred[512,512]{0,1:T(8,128)(4,1)} %get-tuple-element.105) | copy-start | bytes 786436
  27.0 189.4 %copy-start.31 = (pred[512,512]{0,1:T(8,128)(4,1)S(1)}, pred[512,512]{0,1:T(8,128)(4,1)}, u32[]{:S(2)}) copy-start(pred[512,512]{0,1:T(8,128)(4,1)} %get-tuple-element.106) | copy-start | bytes 786436
  215.4 5.3 copy-start.39
  221.3 146.0 %copy-start.38 = (bf16[8,2048]{1,0:T(8,128)(2,1)}, bf16[8,2048]{1,0:T(8,128)(2,1)S(1)}, u32[]{:S(2)}) copy-start(bf16[8,2048]{1,0:T(8,128)(2,1)S(1)} %convert_element_type.202) | copy-start | bytes 98308
  221.6 63.7 %copy-start.48 = (f32[2,128]{1,0:T(2,128)}, f32[2,128]{1,0:T(2,128)S(1)}, u32[]{:S(2)}) copy-start(f32[2,128]{1,0:T(2,128)S(1)} %get-tuple-element.108) | copy-start | bytes 3076
  221.6 71.7 %copy-start.46 = (f32[2,128]{1,0:T(2,128)}, f32[2,128]{1,0:T(2,128)S(1)}, u32[]{:S(2)}) copy-start(f32[2,128]{1,0:T(2,128)S(1)} %get-tuple-element.107) | copy-start | bytes 3076
  221.7 5.3 copy-start.36
  221.7 5.3 copy-start.1
  275.4 4.5 copy-start.41
  279.9 24.8 %copy-start.23 = (bf16[2,2,8,64,128]{4,3,2,1,0:T(8,128)(2,1)}, bf16[2,2,8,64,128]{4,3,2,1,0:T(8,128)(2,1)S(1)}, u32[]{:S(2)}) copy-start(bf16[2,2,8,64,128]{4,3,2,1,0:T(8,128)(2,1)S(1)} %copy.167) | copy-start | bytes 1572868
  296.2 5.7 copy-start.24
  301.9 4.8 copy-start.50
  304.7 6.5 copy-start.3
  304.7 3.3 copy-start.32
  311.2 52.9 %copy-start.2 = (bf16[2,64,2048]{2,1,0:T(8,128)(2,1)S(1)}, bf16[2,64,2048]{2,1,0:T(8,128)(2,1)}, u32[]{:S(2)}) copy-start(bf16[2,64,2048]{2,1,0:T(8,128)(2,1)} %param.17) | copy-start | bytes 1572868
  367.5 283.9 %copy-start.45 = (f32[128]{0:T(128)}, f32[128]{0:T(128)S(1)}, u32[]{:S(2)}) copy-start(f32[128]{0:T(128)S(1)} %get-tuple-element.101) | copy-start | bytes 1540
  367.6 283.9 %copy-start.51 = (f32[128]{0:T(128)}, f32[128]{0:T(128)S(1)}, u32[]{:S(2)}) copy-start(f32[128]{0:T(128)S(1)} %fusion.28) | copy-start | bytes 1540
  482.4 19.4 %copy-start.10 = (f32[4096,512]{0,1:T(8,128)S(1)}, f32[4096,512]{0,1:T(8,128)}, u32[]{:S(2)}) copy-start(f32[4096,512]{0,1:T(8,128)} %fusion.49) | copy-start | bytes 25165828
  507.0 15.5 %copy-start.6 = (bf16[4096,256]{0,1:T(8,128)(2,1)}, bf16[4096,256]{0,1:T(8,128)(2,1)S(1)}, u32[]{:S(2)}) copy-start(bf16[4096,256]{0,1:T(8,128)(2,1)S(1)} %get-tuple-element.83) | copy-start | bytes 6291460
  522.4 9.7 copy-start.21
  522.4 9.7 copy-start.22
  532.1 14.1 %copy-start.33 = (f32[8,4,8,128]{3,2,1,0:T(8,128)}, f32[8,4,8,128]{3,2,1,0:T(8,128)S(1)}, u32[]{:S(2)}) copy-start(f32[8,4,8,128]{3,2,1,0:T(8,128)S(1)} %constant_dynamic-update-slice_fusion.2.refs_1_) | copy-start | bytes 393220
  546.2 104.5 %copy-start.44 = (pred[128,8]{0,1:T(8,128)(4,1)S(1)}, pred[128,8]{0,1:T(8,128)(4,1)}, u32[]{:S(2)}) copy-start(pred[128,8]{0,1:T(8,128)(4,1)} %copy-done.43) | copy-start | bytes 3076
  546.2 105.8 %copy-start.12 = (bf16[128,2048]{1,0:T(8,128)(2,1)S(1)}, bf16[128,2048]{1,0:T(8,128)(2,1)}, u32[]{:S(2)}) copy-start(bf16[128,2048]{1,0:T(8,128)(2,1)} %copy-done.11) | copy-start | bytes 1572868
  546.2 108.5 %copy-start.5 = (bf16[128,2048]{1,0:T(8,128)(2,1)S(1)}, bf16[128,2048]{1,0:T(8,128)(2,1)}, u32[]{:S(2)}) copy-start(bf16[128,2048]{1,0:T(8,128)(2,1)} %scatter_mixed.1) | copy-start | bytes 1572868
  658.4 61.3 %copy-start.55 = (f32[128]{0:T(128)}, f32[128]{0:T(128)S(1)}, u32[]{:S(2)}) copy-start(f32[128]{0:T(128)S(1)} %broadcast_multiply_fusion.4) | copy-start | bytes 1540
  715.0 4.8 copy-start.17
  715.0 4.7 copy-start.20
  726.7 4.5 copy-start.4
  735.4 2.8 copy-start.26
  735.5 3.9 copy-start.29
  749.3 8.2 copy-start.47
  753.3 4.2 copy-start.7
  759.9 15.7 %copy-start.42 = (f32[1024]{0:T(1024)S(1)}, f32[1024]{0:T(1024)}, u32[]{:S(2)}) copy-start(f32[1024]{0:T(1024)} %copy-done.41) | copy-start | bytes 12292
  775.6 3.5 copy-start.18
  775.6 3.5 copy-start.34
  779.1 5.0 copy-start.59
  789.1 52.3 %copy-start.37 = (f32[2048]{0:T(1024)S(1)}, f32[2048]{0:T(1024)}, u32[]{:S(2)}) copy-start(f32[2048]{0:T(1024)} %copy-done.36) | copy-start | bytes 24580
  789.1 52.3 %copy-start.54 = (f32[128]{0:T(128)S(1)}, f32[128]{0:T(128)}, u32[]{:S(2)}) copy-start(f32[128]{0:T(128)} %rsqrt.39) | copy-start | bytes 1540
  789.1 53.9 %copy-start.40 = (f32[1,8,4,64]{3,0,1,2:T(1,128)S(1)}, f32[1,8,4,64]{3,0,1,2:T(1,128)}, u32[]{:S(2)}) copy-start(f32[1,8,4,64]{3,0,1,2:T(1,128)} %copy.196) | copy-start | bytes 24580
  958.7 101.2 %copy-start.15 = (bf16[128,2048]{1,0:T(8,128)(2,1)S(1)}, bf16[128,2048]{1,0:T(8,128)(2,1)}, u32[]{:S(2)}) copy-start(bf16[128,2048]{1,0:T(8,128)(2,1)} %scatter_hidden.1) | copy-start | bytes 1572868
  958.7 101.2 %copy-start.16 = (bf16[2,64,2048]{2,1,0:T(8,128)(2,1)S(1)}, bf16[2,64,2048]{2,1,0:T(8,128)(2,1)}, u32[]{:S(2)}) copy-start(bf16[2,64,2048]{2,1,0:T(8,128)(2,1)} %param.33) | copy-start | bytes 1572868
  958.7 101.3 %copy-start.53 = (f32[128]{0:T(128)S(1)}, f32[128]{0:T(128)}, u32[]{:S(2)}) copy-start(f32[128]{0:T(128)} %copy-done.52) | copy-start | bytes 1540
  958.7 101.3 %copy-start.56 = (f32[128]{0:T(128)S(1)}, f32[128]{0:T(128)}, u32[]{:S(2)}) copy-start(f32[128]{0:T(128)} %copy-done.55) | copy-start | bytes 1540
  1060.0 3.2 copy-start.35
  (12 other events, 18.0 us)

commit v3 on v2

--- a/solution.py
+++ b/solution.py
@@ -44,12 +44,6 @@
     angles = positions.astype(F32)[:, None] * frequency[None, :]
     return jnp.cos(angles), jnp.sin(angles)
 
-
-def rotate(v, cos_part, sin_part):
-    first, second = jnp.split(v, 2, axis=-1)
-    return jnp.concatenate(
-        [first * cos_part - second * sin_part, second * cos_part + first * sin_part], axis=-1
-    )
 
 ANY = pl.BlockSpec(memory_space=pl.ANY)
 VMEM_LIMIT = 60 * 1024 * 1024
@@ -206,30 +200,6 @@
 
 def shape_of(lead, block):
     return jax.ShapeDtypeStruct(tuple(lead) + block.shape, block.dtype)
-
-
-def gather_seq(block, n_seq, n_bat, collective_id, name):
-    def kernel(src, out, buffer, own_sem, send_sems, recv_sems):
-        place = Place(n_seq, n_bat)
-        place.greet(batch=False)
-        gather = SeqGather(place, wire := Wire(send_sems, recv_sems), src, out)
-        gather.start()
-        own = keep_own(src, out.at[place.s], buffer, own_sem)
-        for j in range(1, place.half):
-            gather.step(j)
-        gather.finish()
-        own.wait()
-        wire.drain()
-
-    return comm_call(
-        kernel,
-        shape_of((n_seq,), block),
-        [pltpu.VMEM(block.shape, block.dtype), pltpu.SemaphoreType.DMA],
-        n_seq,
-        collective_id,
-        name,
-        [ANY],
-    )(block)
 
 
 def gather_all(blocks, n_seq, n_bat, collective_id, name):
@@ -401,45 +371,6 @@
     )(*parts)
 
 
-def scatter_seq(parts, n_seq, n_bat, collective_id, name):
-    block = jax.ShapeDtypeStruct(parts.shape[1:], parts.dtype)
-    half = n_seq // 2
-
-    def kernel(ref, out, mine, twin, line, sems, send_sems, recv_sems):
-        place = Place(n_seq, n_bat)
-        place.greet(batch=False)
-        wire = Wire(send_sems, recv_sems)
-        order = list(range(1, half)) + [0]
-        from_twin, loads, from_seq = {}, {}, {}
-        for j in order:
-            from_twin[j] = wire.push(ref.at[place.twin_at(2 * j)], twin.at[j], place.twin())
-            loads[j] = pltpu.make_async_copy(ref.at[place.seq_at(2 * j)], mine.at[j], sems.at[j])
-            loads[j].start()
-        for j in order:
-            from_twin[j].wait_recv()
-            loads[j].wait()
-            add_into(mine.at[j], twin.at[j])
-            if j:
-                from_seq[j] = wire.push(mine.at[j], line.at[j], place.seq_peer(2 * j))
-        for j in range(1, half):
-            from_seq[j].wait_recv()
-        add_into(mine.at[0], *[line.at[j] for j in range(1, half)])
-        out[...] = mine[0]
-        wire.drain()
-
-    scratch = [pltpu.VMEM((half,) + block.shape, block.dtype)] * 3
-    return comm_call(
-        kernel,
-        block,
-        scratch + [pltpu.SemaphoreType.DMA((half,))],
-        n_seq,
-        collective_id,
-        name,
-        [ANY],
-        pl.BlockSpec(memory_space=pltpu.VMEM),
-    )(parts)
-
-
 def pack(values):
     flat = values.astype(F32).reshape(-1)
     tiles = -(-flat.shape[0] // 1024)
@@ -451,10 +382,6 @@
     for extent in shape:
         size *= extent
     return tiles.reshape(tuple(lead) + (-1,))[..., :size].reshape(tuple(lead) + tuple(shape))
-
-def sum_seq(values, n_seq, n_bat, collective_id, name):
-    tiles = gather_seq(pack(values), n_seq, n_bat, collective_id, name)
-    return unpack(jnp.sum(tiles, axis=0), (), values.shape)
 
 
 def scatter_blocks(grad_normed, grad_gates, mixture, n_seq, n_bat):
@@ -474,6 +401,320 @@
         done = scatter_all([mixture[..., at]], n_seq, n_bat, 17 + 2 * i, "scatter_mixture")
         mixtures.append(done[0])
     return jnp.concatenate(grads, axis=-1), gates, jnp.concatenate(mixtures, axis=-1)
+
+
+class SeqScatter:
+    def __init__(self, place, wire, away, mine, twin, line):
+        self.place, self.wire = place, wire
+        self.away, self.mine, self.twin, self.line = away, mine, twin, line
+        self.from_twin, self.from_seq = {}, {}
+        self.order = list(range(1, place.half)) + [0]
+
+    @staticmethod
+    def scratch(n_seq, block):
+        return [pltpu.VMEM((n_seq // 2,) + block.shape, block.dtype)] * 4
+
+    def run(self, compute, out):
+        place, wire = self.place, self.wire
+        waiting = None
+        for j in self.order:
+            self.away[j] = compute(place.twin_at(2 * j)).astype(self.away.dtype)
+            if waiting is not None:
+                self.send(waiting)
+            waiting = j
+        for j in self.order:
+            self.mine[j] = compute(place.seq_at(2 * j)).astype(self.mine.dtype)
+            if waiting is not None:
+                self.send(waiting)
+                waiting = None
+        waiting = None
+        for j in self.order:
+            self.from_twin[j].wait_recv()
+            add_into(self.mine.at[j], self.twin.at[j])
+            if waiting:
+                self.pass_on(waiting)
+            waiting = j
+
+    def send(self, j):
+        self.from_twin[j] = self.wire.push(self.away.at[j], self.twin.at[j], self.place.twin())
+
+    def pass_on(self, j):
+        self.from_seq[j] = self.wire.push(
+            self.mine.at[j], self.line.at[j], self.place.seq_peer(2 * j)
+        )
+
+    def finish(self, out):
+        for j in range(1, self.place.half):
+            self.from_seq[j].wait_recv()
+        add_into(self.mine.at[0], *[self.line.at[j] for j in range(1, self.place.half)])
+        out[...] = self.mine[0]
+
+
+def turn(v, cos_wide, sin_wide):
+    return v * cos_wide + pltpu.roll(v, HEAD // 2, axis=1) * sin_wide
+
+
+def exchange_rows(place, wire, local, got):
+    copies = [
+        wire.push(local, got.at[k - 1], place.seq_peer(k)) for k in range(1, place.n_seq)
+    ]
+    for copy in copies:
+        copy.wait_recv()
+    total = local[...]
+    for k in range(place.n_seq - 1):
+        total = total + got[k]
+    return total
+
+
+def lane_sums(v):
+    ones = jnp.ones((8, v.shape[1]), F32)
+    sums = lax.dot_general(
+        ones, v, (((1,), (1,)), ((), ())), precision=HIGHEST, preferred_element_type=F32
+    )
+    return sums[0:1]
+
+
+def allowed_block(use, first, count, keys):
+    at_query = first + lax.broadcasted_iota(jnp.int32, (count, keys), 0)
+    at_key = lax.broadcasted_iota(jnp.int32, (count, keys), 1)
+    return (at_key == at_query) | ((at_key < at_query) & (use > 0))
+
+
+def attend_forward(qkv, usable, w_o, gain_q, gain_k, cos_wide, sin_wide, n_seq, n_bat, span):
+    col, three = qkv.shape
+    wide = three // 3
+    heads = wide // HEAD
+    own = col // n_seq
+    rows = own // span
+    length = n_seq * span
+    dim = w_o.shape[1]
+    chunk = min(256, length)
+    scale = HEAD ** (-0.5)
+    block = jax.ShapeDtypeStruct((own, dim), BF)
+
+    def kernel(*refs):
+        qkv_ref, use_ref, wo_ref, gq_ref, gk_ref, cos_ref, sin_ref = refs[:7]
+        q_ref, k_ref, v_ref, mix_ref, stat_ref, out_ref = refs[7:13]
+        local, got, away, mine, twin, line, send_sems, recv_sems = refs[13:]
+        place = Place(n_seq, n_bat)
+        place.greet(all_seq=True, batch=False)
+        wire = Wire(send_sems, recv_sems)
+        for i in range(n_seq):
+            for which in range(2):
+                v = qkv_ref[i * own : (i + 1) * own, which * wide : (which + 1) * wide]
+                local[which * n_seq + i : which * n_seq + i + 1, :] = lane_sums(v * v)
+        for i in range(n_seq):
+            for r in range(rows):
+                for h in range(heads):
+                    at = slice(i * own + r * span, i * own + (r + 1) * span)
+                    lanes = slice(2 * wide + h * HEAD, 2 * wide + (h + 1) * HEAD)
+                    v_ref[r, h, i * span : (i + 1) * span, :] = qkv_ref[at, lanes].astype(BF)
+        total = exchange_rows(place, wire, local, got)
+        stat_ref[...] = total
+        columns = lax.rsqrt(total / dim + EPS).T
+        for which, gain_ref, target in ((0, gq_ref, q_ref), (1, gk_ref, k_ref)):
+            for i in range(n_seq):
+                at_pos = slice(i * span, (i + 1) * span)
+                for r in range(rows):
+                    at = slice(i * own + r * span, i * own + (r + 1) * span)
+                    factor = columns[
+                        r * span : (r + 1) * span, which * n_seq + i : which * n_seq + i + 1
+                    ]
+                    for h in range(heads):
+                        lanes = slice(which * wide + h * HEAD, which * wide + (h + 1) * HEAD)
+                        gain = gain_ref[0:1, h * HEAD : (h + 1) * HEAD]
+                        v = qkv_ref[at, lanes] * factor * gain
+                        target[r, h, at_pos, :] = turn(
+                            v, cos_ref[at_pos, :], sin_ref[at_pos, :]
+                        ).astype(BF)
+        for r in range(rows):
+            for c in range(length // chunk):
+                keys = (c + 1) * chunk
+                allowed = allowed_block(use_ref[r : r + 1, :keys], c * chunk, chunk, keys)
+                for h in range(heads):
+                    query = q_ref[r, h, c * chunk : keys, :]
+                    scores = dot_t(query, k_ref[r, h, :keys, :]) * scale
+                    scores = jnp.where(allowed, scores, NEGATIVE)
+                    raised = jnp.exp(scores - jnp.max(scores, axis=-1, keepdims=True))
+                    probs = raised / jnp.sum(raised, axis=-1, keepdims=True)
+                    mixed = dot(probs.astype(BF), v_ref[r, h, :keys, :]).astype(BF)
+                    for p in range(chunk // span):
+                        i = c * (chunk // span) + p
+                        mix_ref[
+                            i * own + r * span : i * own + (r + 1) * span,
+                            h * HEAD : (h + 1) * HEAD,
+                        ] = mixed[p * span : (p + 1) * span, :]
+        scatter = SeqScatter(place, wire, away, mine, twin, line)
+
+        def project(i):
+            rows_at = pl.ds(pl.multiple_of(i * own, own), own)
+            return dot(mix_ref[rows_at, :], wo_ref[...])
+
+        scatter.run(project, out_ref)
+        scatter.finish(out_ref)
+        wire.drain()
+
+    vmem = pl.BlockSpec(memory_space=pltpu.VMEM)
+    head_block = jax.ShapeDtypeStruct((rows, heads, length, HEAD), BF)
+    stats = jax.ShapeDtypeStruct((2 * n_seq, own), F32)
+    return comm_call(
+        kernel,
+        [head_block] * 3 + [jax.ShapeDtypeStruct((col, wide), BF), stats, block],
+        [pltpu.VMEM(stats.shape, F32), pltpu.VMEM((n_seq - 1,) + stats.shape, F32)]
+        + SeqScatter.scratch(n_seq, block),
+        3 * n_seq,
+        2,
+        "attend_forward",
+        [vmem] * 7,
+        [vmem] * 6,
+    )(qkv, usable, w_o, gain_q, gain_k, cos_wide, sin_wide)
+
+
+def attend_backward(
+    grad_o, q, k, v, mixed, qkv, stats, hidden, usable, w_o, w_qkv, gain_q, gain_k,
+    cos_wide, sin_wide, n_seq, n_bat,
+):
+    rows, heads, length, _ = q.shape
+    own, dim = grad_o.shape
+    span = own // rows
+    col, three = qkv.shape
+    wide = three // 3
+    chunk = min(256, length)
+    scale = HEAD ** (-0.5)
+
+    def kernel(*refs):
+        (go_ref, q_ref, k_ref, v_ref, mix_ref, qkv_ref, stat_ref, hid_ref, use_ref, wo_ref,
+         w_ref, gq_ref, gk_ref, cos_ref, sin_ref) = refs[:15]
+        gwo_ref, gw_ref, gain_ref, out_ref = refs[15:19]
+        go_all, gm, dq, dk, dv, dqkv, local, got = refs[19:27]
+        away, mine, twin, line, send_sems, recv_sems = refs[27:]
+        place = Place(n_seq, n_bat)
+        place.greet(all_seq=True, batch=False)
+        wire = Wire(send_sems, recv_sems)
+        gather = SeqGather(place, wire, go_ref, go_all)
+        gather.start()
+        go_all[place.s] = go_ref[...]
+        for j in range(1, place.half):
+            gather.step(j)
+        gather.finish()
+        for i in range(n_seq):
+            part = dot_t(go_all[i], wo_ref[...]).astype(BF)
+            for r in range(rows):
+                gm[r, i * span : (i + 1) * span, :] = part[r * span : (r + 1) * span, :]
+        dk[...] = jnp.zeros_like(dk)
+        dv[...] = jnp.zeros_like(dv)
+        for r in range(rows):
+            for c in range(length // chunk):
+                keys = (c + 1) * chunk
+                now = slice(c * chunk, keys)
+                allowed = allowed_block(use_ref[r : r + 1, :keys], c * chunk, chunk, keys)
+                for h in range(heads):
+                    lanes = slice(h * HEAD, (h + 1) * HEAD)
+                    query = q_ref[r, h, now, :]
+                    key = k_ref[r, h, :keys, :]
+                    scores = jnp.where(allowed, dot_t(query, key) * scale, NEGATIVE)
+                    raised = jnp.exp(scores - jnp.max(scores, axis=-1, keepdims=True))
+                    probs = raised / jnp.sum(raised, axis=-1, keepdims=True)
+                    low = probs.astype(BF)
+                    grad_mix = gm[r, now, lanes]
+                    grad_probs = dot_t(grad_mix, v_ref[r, h, :keys, :])
+                    row_dot = jnp.sum(low.astype(F32) * grad_probs, axis=-1, keepdims=True)
+                    grad_scores = (probs * (grad_probs - row_dot)).astype(BF)
+                    dq[r, now, lanes] = scale * dot(grad_scores, key)
+                    dk[r, :keys, lanes] += scale * t_dot(grad_scores, query)
+                    dv[r, :keys, lanes] += t_dot(low, grad_mix)
+        columns = lax.rsqrt(stat_ref[...] / dim + EPS).T
+        for which, g_ref, grads in ((0, gq_ref, dq), (1, gk_ref, dk)):
+            sums = [jnp.zeros((1, HEAD), F32) for _ in range(heads)]
+            for i in range(n_seq):
+                at_pos = slice(i * span, (i + 1) * span)
+                products = []
+                for r in range(rows):
+                    at = slice(i * own + r * span, i * own + (r + 1) * span)
+                    factor = columns[
+                        r * span : (r + 1) * span, which * n_seq + i : which * n_seq + i + 1
+                    ]
+                    parts = []
+                    for h in range(heads):
+                        lanes = slice(h * HEAD, (h + 1) * HEAD)
+                        flat = qkv_ref[at, which * wide + h * HEAD : which * wide + (h + 1) * HEAD]
+                        flat = flat * factor
+                        back = turn(
+                            grads[r, at_pos, lanes], cos_ref[at_pos, :], -sin_ref[at_pos, :]
+                        )
+                        sums[h] = sums[h] + jnp.sum(back * flat, axis=0, keepdims=True)
+                        weighted = back * g_ref[0:1, lanes]
+                        grads[r, at_pos, lanes] = weighted
+                        parts.append(weighted * flat)
+                    products.append(sum(parts))
+                local[which * n_seq + i : which * n_seq + i + 1, :] = lane_sums(
+                    jnp.concatenate(products, axis=0)
+                )
+            for h in range(heads):
+                gain_ref[which : which + 1, h * HEAD : (h + 1) * HEAD] = sums[h]
+        for i in range(n_seq):
+            for r in range(rows):
+                at = slice(i * own + r * span, i * own + (r + 1) * span)
+                dqkv[at, 2 * wide :] = dv[r, i * span : (i + 1) * span, :].astype(BF)
+        means = (exchange_rows(place, wire, local, got) / dim).T
+        for which, grads in ((0, dq), (1, dk)):
+            for i in range(n_seq):
+                at_pos = slice(i * span, (i + 1) * span)
+                column = which * n_seq + i
+                for r in range(rows):
+                    at = slice(i * own + r * span, i * own + (r + 1) * span)
+                    inside = slice(r * span, (r + 1) * span)
+                    factor = columns[inside, column : column + 1]
+                    mean = means[inside, column : column + 1]
+                    lanes = slice(which * wide, (which + 1) * wide)
+                    flat = qkv_ref[at, lanes] * factor
+                    dqkv[at, lanes] = (factor * (grads[r, at_pos, :] - flat * mean)).astype(BF)
+        scatter = SeqScatter(place, wire, away, mine, twin, line)
+
+        def project(i):
+            rows_at = pl.ds(pl.multiple_of(i * own, own), own)
+            return dot_t(dqkv[rows_at, :], w_ref[...])
+
+        scatter.run(project, out_ref)
+        for part in range(dim // 256):
+            at = slice(part * 256, (part + 1) * 256)
+            gw_ref[at, :] = t_dot(hid_ref[:, at], dqkv[...]).astype(BF)
+            total = t_dot(mix_ref[0:own, :], go_all[0, :, at])
+            for i in range(1, n_seq):
+                total = total + t_dot(mix_ref[i * own : (i + 1) * own, :], go_all[i, :, at])
+            gwo_ref[:, at] = total.astype(BF)
+        scatter.finish(out_ref)
+        wire.drain()
+
+    vmem = pl.BlockSpec(memory_space=pltpu.VMEM)
+    block = jax.ShapeDtypeStruct((own, dim), BF)
+    stat_shape = (2 * n_seq, own)
+    return comm_call(
+        kernel,
+        [
+            jax.ShapeDtypeStruct((wide, dim), BF),
+            jax.ShapeDtypeStruct((dim, three), BF),
+            jax.ShapeDtypeStruct((2, wide), F32),
+            block,
+        ],
+        [
+            pltpu.VMEM((n_seq, own, dim), BF),
+            pltpu.VMEM((rows, length, wide), BF),
+            pltpu.VMEM((rows, length, wide), F32),
+            pltpu.VMEM((rows, length, wide), F32),
+            pltpu.VMEM((rows, length, wide), F32),
+            pltpu.VMEM((col, three), BF),
+            pltpu.VMEM(stat_shape, F32),
+            pltpu.VMEM((n_seq - 1,) + stat_shape, F32),
+        ]
+        + SeqScatter.scratch(n_seq, block),
+        4 * n_seq,
+        6,
+        "attend_backward",
+        [vmem] * 15,
+        [vmem] * 4,
+    )(grad_o, q, k, v, mixed, qkv, stats, hidden, usable, w_o, w_qkv, gain_q, gain_k,
+      cos_wide, sin_wide)
 
 
 def load_inputs(qkv_cut, w_out, mine, flags, small, gu_cut, dy_own, n_seq, n_bat):
@@ -695,7 +936,6 @@
     local_experts, depth, hidden_units = expert_gate.shape
     part = hidden_units // n_seq
     experts = local_experts * n_bat
-    score_scale = HEAD ** (-0.5)
 
     mine = tokens.reshape(own, dim)
     dy_own = cotangent.reshape(own, dim)
@@ -723,51 +963,18 @@
     gain_q = lax.dynamic_slice_in_dim(small_all[experts + 1], seq * wide, wide)
     gain_k = lax.dynamic_slice_in_dim(small_all[experts + 2], seq * wide, wide)
     usable = unpack(flag_col, (n_seq,), key_mask.shape)
-    usable = jnp.transpose(usable, (1, 0, 2)).reshape(rows, length) > 0
+    usable = jnp.transpose(usable, (1, 0, 2)).reshape(rows, length)
 
     x_col = x_col.reshape(col, dim).astype(F32)
     scale_x = rms_scale(x_col)
     hidden = (x_col * scale_x * gain_attn).astype(BF)
     qkv = dot(hidden, w_qkv)
-    q_pre, k_pre, v_pre = qkv[:, :wide], qkv[:, wide : 2 * wide], qkv[:, 2 * wide :]
-
-    squares = jnp.stack([jnp.sum(q_pre * q_pre, axis=-1), jnp.sum(k_pre * k_pre, axis=-1)])
-    squares = sum_seq(squares, n_seq, n_bat, 2, "sum_squares")
-    scales = lax.rsqrt(squares / dim + EPS)
-    scale_q, scale_k = scales[0][:, None], scales[1][:, None]
-
-    def by_row(v):
-        v = v.reshape(n_seq, rows, span, heads, HEAD)
-        return jnp.transpose(v, (1, 3, 0, 2, 4)).reshape(rows, heads, length, HEAD)
-
-    def by_col(v):
-        v = v.reshape(rows, heads, n_seq, span, HEAD)
-        return jnp.transpose(v, (2, 0, 3, 1, 4)).reshape(col, wide)
-
-    positions = jnp.arange(length, dtype=jnp.int32)
-    cos_part, sin_part = rotary_tables(positions)
-    q_norm = by_row(q_pre * scale_q)
-    k_norm = by_row(k_pre * scale_k)
-    gain_qh = gain_q.reshape(1, heads, 1, HEAD)
-    gain_kh = gain_k.reshape(1, heads, 1, HEAD)
-    queries = rotate(q_norm * gain_qh, cos_part, sin_part).astype(BF)
-    keys = rotate(k_norm * gain_kh, cos_part, sin_part).astype(BF)
-    values = by_row(v_pre.astype(BF))
-
-    causal = positions[None, :] <= positions[:, None]
-    same = positions[None, :] == positions[:, None]
-    allowed = (causal[None] & (usable[:, None, :] | same[None]))[:, None]
-    scores = jnp.einsum("rhqd,rhkd->rhqk", queries, keys, preferred_element_type=F32) * score_scale
-    scores = jnp.where(allowed, scores, NEGATIVE)
-    top = jnp.max(scores, axis=-1, keepdims=True)
-    raised = jnp.exp(scores - top)
-    probs = raised / jnp.sum(raised, axis=-1, keepdims=True)
-    probs_low = probs.astype(BF)
-    attended = jnp.einsum("rhqk,rhkd->rhqd", probs_low, values, preferred_element_type=F32)
-    mixed = by_col(attended.astype(BF))
-
-    mixed_out = scatter_seq(
-        dot(mixed, w_o).astype(BF).reshape(n_seq, own, dim), n_seq, n_bat, 3, "scatter_mixed"
+    cos_part, sin_part = rotary_tables(jnp.arange(length, dtype=jnp.int32))
+    cos_wide = jnp.concatenate([cos_part, cos_part], axis=1)
+    sin_wide = jnp.concatenate([-sin_part, sin_part], axis=1)
+    gain_q, gain_k = gain_q[None, :], gain_k[None, :]
+    q, k, v, mixed, stats, mixed_out = attend_forward(
+        qkv, usable, w_o, gain_q, gain_k, cos_wide, sin_wide, n_seq, n_bat, span
     )
     x_own = mine.astype(F32)
     residual = x_own + mixed_out.astype(F32)
@@ -834,40 +1041,13 @@
     grad_residual = dy_own.astype(F32) + grad_resid
     grad_o = grad_residual.astype(BF)
 
-    grad_o_col = gather_seq(grad_o, n_seq, n_bat, 6, "gather_grad_o").reshape(col, dim)
-    grad_mixed = by_row(dot_t(grad_o_col, w_o).astype(BF))
-    grad_w_o = t_dot(mixed, grad_o_col).astype(BF).reshape(n_bat, shard, dim)
-    row_dot = jnp.sum(grad_mixed.astype(F32) * attended, axis=-1, keepdims=True)
-    grad_values = jnp.einsum("rhqk,rhqd->rhkd", probs_low, grad_mixed, preferred_element_type=F32)
-    grad_probs = jnp.einsum("rhqd,rhkd->rhqk", grad_mixed, values, preferred_element_type=F32)
-    grad_scores = (probs * (grad_probs - row_dot)).astype(BF)
-    grad_q = score_scale * jnp.einsum(
-        "rhqk,rhkd->rhqd", grad_scores, keys, preferred_element_type=F32
-    )
-    grad_k = score_scale * jnp.einsum(
-        "rhqk,rhqd->rhkd", grad_scores, queries, preferred_element_type=F32
-    )
-    grad_q = rotate(grad_q, cos_part, -sin_part)
-    grad_k = rotate(grad_k, cos_part, -sin_part)
-    grad_gain_q = jnp.sum(grad_q * q_norm, axis=(0, 2)).reshape(wide)
-    grad_gain_k = jnp.sum(grad_k * k_norm, axis=(0, 2)).reshape(wide)
-    q_weighted = by_col(grad_q * gain_qh)
-    k_weighted = by_col(grad_k * gain_kh)
-    q_flat = q_pre * scale_q
-    k_flat = k_pre * scale_k
-    means = jnp.stack(
-        [jnp.sum(q_weighted * q_flat, axis=-1), jnp.sum(k_weighted * k_flat, axis=-1)]
-    )
-    means = sum_seq(means, n_seq, n_bat, 9, "sum_means") / dim
-    grad_q_pre = (scale_q * (q_weighted - q_flat * means[0][:, None])).astype(BF)
-    grad_k_pre = (scale_k * (k_weighted - k_flat * means[1][:, None])).astype(BF)
-    grad_qkv = jnp.concatenate([grad_q_pre, grad_k_pre, by_col(grad_values).astype(BF)], axis=1)
-
-    grad_hidden = dot_t(grad_qkv, w_qkv).astype(BF)
-    grad_hidden = grad_hidden.reshape(n_seq, own, dim)
-    grad_hidden = scatter_seq(grad_hidden, n_seq, n_bat, 7, "scatter_hidden").astype(F32)
-    grad_w = t_dot(hidden, grad_qkv).astype(BF).reshape(n_seq, n_bat, shard, 3 * wide)
-
+    grad_w_o, grad_w, grad_gains, grad_hidden = attend_backward(
+        grad_o, q, k, v, mixed, qkv, stats, hidden, usable, w_o, w_qkv, gain_q, gain_k,
+        cos_wide, sin_wide, n_seq, n_bat,
+    )
+    grad_w_o = grad_w_o.reshape(n_bat, shard, dim)
+    grad_w = grad_w.reshape(n_seq, n_bat, shard, 3 * wide)
+    grad_hidden = grad_hidden.astype(F32)
     grad_x, gain_attn_terms = rms_back(x_own, rms_scale(x_own), gain_attn, grad_hidden)
     grad_tokens = (grad_residual + grad_x).astype(BF)
 
@@ -878,8 +1058,8 @@
             jnp.stack(
                 [
                     jnp.sum(gain_attn_terms, axis=0),
-                    lax.dynamic_update_slice_in_dim(zeros, grad_gain_q, seq * wide, 0),
-                    lax.dynamic_update_slice_in_dim(zeros, grad_gain_k, seq * wide, 0),
+                    lax.dynamic_update_slice_in_dim(zeros, grad_gains[0], seq * wide, 0),
+                    lax.dynamic_update_slice_in_dim(zeros, grad_gains[1], seq * wide, 0),
                     jnp.sum(gain_mlp_terms, axis=0),
                 ]
             ),

time: 1080 us -> 994 us (0.920)
  local copies, waits for them, and re-layouts: 104 us -> 60.7 us
  matrix products: 129 us -> 93.2 us
  other arithmetic: 65.7 us -> 37 us
  Pallas kernels: 764 us -> 790 us
    pallas_call x5 -> x2, Pallas kernels: 203 us -> 230 us  [the longest x1 129 us: attend_backward(): comm_call(kernel, [jax.ShapeDtypeStruct((wide, dim), BF), jax.ShapeDtypeS...]
    reshape x8 -> x1, local copies, waits for them, and re-layouts: 14.6 us -> 0.67 us  [shards(): usable = jnp.transpose(usable, (1, 0, 2)).reshape(rows, length)]
    reduce_sum x8 -> x0, other arithmetic: 11.7 us -> none  [the longest x1 2.83 us: shards(): grad_gain_q = jnp.sum(grad_q * q_norm, axis=(0, 2)).reshape(wide)]
    dot_general x5 -> x0, matrix products: 11 us -> none  [the longest x1 4.5 us: shards(): jnp.einsum('rhqd,rhkd->rhqk', grad_mixed, values, preferred_element_type=...]
    dot_general x4 -> x2, matrix products: 43.3 us -> 34 us  [dot_t(): lax.dot_general(a, b, (((1,), (1,)), ((), ())), preferred_element_type=F32)]
    dot_general x4 -> x2, matrix products: 32.3 us -> 25.1 us  [t_dot(): lax.dot_general(a, b, (((0,), (0,)), ((), ())), preferred_element_type=F32)]
    dot_general x5 -> x4, matrix products: 32.1 us -> 30.1 us  [dot(): return jnp.dot(a, b, preferred_element_type=F32)]
where the time goes in v3:
time: 994 us; the launch traced here: 983 us
  Pallas kernels  790 us (79%)
  matrix products  93.2 us (9%)
  local copies, waits for them, and re-layouts  60.7 us (6%)
  other arithmetic  37 us (4%)
    pallas_call x2, Pallas kernels, scatter_all(): comm_call(kernel, blocks, scratch, slots, collective_id, name, [ANY] * co...  205 us
    pallas_call x1, Pallas kernels, load_inputs(): comm_call(kernel, [shape_of(lead, block) for lead, block in zip(leads, bl...  188 us
    pallas_call x1, Pallas kernels, attend_backward(): comm_call(kernel, [jax.ShapeDtypeStruct((wide, dim), BF), jax.ShapeDtypeS...  129 us
    pallas_call x1, Pallas kernels, attend_forward(): comm_call(kernel, [head_block] * 3 + [jax.ShapeDtypeStruct((col, wide), B...  100 us
    pallas_call x1, Pallas kernels, gather_all(): comm_call(kernel, [shape_of((n_seq, n_bat), block) for block in blocks],...  98 us
    pallas_call x1, Pallas kernels, store_grads(): comm_call(kernel, [shape_of((n_seq,), one), jax.ShapeDtypeStruct(wo_one.s...  69.5 us
    dot_general x2, matrix products, dot_t(): lax.dot_general(a, b, (((1,), (1,)), ((), ())), preferred_element_type=F32)  34 us
    dot_general x4, matrix products, dot(): return jnp.dot(a, b, preferred_element_type=F32)  30.1 us

profile of v3, /device:TPU:9, one launch (start us, length us, event | category | flops | bytes accessed | tf_op | source)
XLA Modules:
  0.0 982.5 jit_solution(254166319837105302)
XLA Ops:
  0.7 1.2 copy-done
  2.7 1.2 multiply_reduce_fusion.2
  5.4 1.4 concatenate.28
  7.5 1.0 copy.110
  9.0 1.0 copy.111
  10.4 1.0 copy.112
  11.8 1.8 maximum_bitcast_fusion.1
  13.6 1.7 reshape.284.refs_0_
  15.3 1.0 fusion.13
  16.3 1.0 pad_maximum_fusion.3
  17.6 1.1 copy.86
  19.0 1.1 copy.87
  20.0 3.0 maximum_bitcast_fusion
  23.0 2.6 reshape.290.refs_5_
  25.7 188.4 %load_inputs.1 = (bf16[8,4,64,768]{3,2,1,0:T(8,128)(2,1)}, bf16[4,64,2048]{2,1,0:T(8,128)(2,1)}, bf16[8,128,2048]{2,1,0:T(8,128)(2,1)}, f32[8,8,128]{2,1,0:T(8,1...) custom-call(bf16[8,64,768]{2,1,0:T(8,128)(2,1)} %reshape.284.refs_0_, ...), custom_call_target="tpu_custom_call" | custom-call | tf_op jit(solution)/shard_map/load_inputs/pallas_call | solution.py:797
  215.1 3.1 multiply_reduce_fusion
  221.0 5.3 fusion.1.refs_7_
  226.2 1.0 multiply_convert_fusion
  228.1 5.0 fusion.30.refs_0_.refs_5_
  233.1 100.3 %attend_forward.1 = (bf16[2,2,512,128]{3,2,1,0:T(8,128)(2,1)}, bf16[2,2,512,128]{3,2,1,0:T(8,128)(2,1)}, bf16[2,2,512,128]{3,2,1,0:T(8,128)(2,1)}, bf16[1024,256...) custom-call(f32[1024,768]{1,0:T(8,128)} %fusion.30.refs_0_.refs_5_, ...), custom_call_target="tpu_custom_call" | custom-call | tf_op jit(solution)/shard_map/attend_forward/pallas_call | solution.py:560
  333.5 1.3 multiply_reduce_fusion.4
  334.8 1.3 multiply_convert_fusion.4.refs_0_
  337.0 98.0 %gather_normed.1 = (bf16[8,4,128,2048]{3,2,1,0:T(8,128)(2,1)}, f32[8,4,8,128]{3,2,1,0:T(8,128)}) custom-call(bf16[128,2048]{1,0:T(8,128)(2,1)} %copy-done.5, f32[8,128]{1,0:T(8,128)} %select_bitcast_fusion.refs_1_), custom_call_target="tpu_custom_call" | custom-call | tf_op jit(solution)/shard_map/gather_normed/pallas_call | solution.py:235
  435.9 15.1 %fusion.31 = f32[4096,512]{0,1:T(8,128)} fusion(bf16[4096,2048]{1,0:T(8,128)(2,1)} %bitcast.231, bf16[2048,512]{1,0:T(8,128)(2,1)} %bitcast.233), kind=kOutput, calls=%fused_computation.91 | convolution fusion | flops 8589934592 | bytes 27262976 | tf_op jit(solution)/shard_map/dot_general | solution.py:19
  451.0 19.8 %bitcast_reduce_fusion = (f32[4096,2]{0,1:T(2,128)S(1)}, bf16[4096,256]{0,1:T(8,128)(2,1)}, f32[4096,256]{0,1:T(8,128)S(1)}) fusion(f32[4096,512]{0,1:T(8,128)} %fusion.31, bf16[4096,2048]{1,0:T(8,128)(2,1)} %bitcast.229, bf16[256,2048]{1,0:T(8,128)(2,1)S(1)} %bitcast.175), kind=kOutput, calls=%fused_computation.12 | convolution fusion | flops 4304396288 | bytes 32538624 | tf_op jit(solution)/shard_map/dot_general | solution.py:23
  470.8 5.1 multiply_convert_fusion.2
  476.0 15.5 %convolution_convert_fusion.2 = bf16[2048,512]{1,0:T(8,128)(2,1)} fusion(bf16[4096,2048]{1,0:T(8,128)(2,1)} %bitcast.232, bf16[4096,256]{0,1:T(8,128)(2,1)} %get-tuple-element.71, bf16[4096,256]{0,1:T(8,128)(2,1)} %get-tuple-element.70), kind=kOutput, calls=%fused_computation.18 | convolution fusion | flops 8599371776 | bytes 23068672 | tf_op jit(solution)/shard_map/dot_general | solution.py:27
  491.5 9.6 fusion.32
  501.1 14.2 %convolution_convert_fusion = bf16[4096,2048]{1,0:T(8,128)(2,1)} fusion(bf16[2048,512]{1,0:T(8,128)(2,1)} %bitcast.234, bf16[4096,256]{0,1:T(8,128)(2,1)S(1)} %copy-done.11, bf16[4096,256]{0,1:T(8,128)(2,1)S(1)} %copy-done.10), kind=kOutput, calls=%fused_computation | convolution fusion | flops 8606711808 | bytes 23068672 | tf_op jit(solution)/shard_map/dot_general | solution.py:23
  515.4 103.9 %scatter_normed.1 = (bf16[128,2048]{1,0:T(8,128)(2,1)}, f32[8,128]{1,0:T(8,128)}) custom-call(bf16[8,4,128,2048]{3,2,1,0:T(8,128)(2,1)} %bitcast.178, f32[8,4,8,128]{3,2,1,0:T(8,128)} %copy-done.15), custom_call_target="tpu_custom_call" | custom-call | tf_op jit(solution)/shard_map/scatter_normed/pallas_call | solution.py:362
  620.0 1.0 fusion.17
  621.3 3.0 multiply_reduce_fusion.1
  624.4 2.5 fusion.25.refs_0_
  626.9 129.5 %attend_backward.1 = (bf16[256,2048]{1,0:T(8,128)(2,1)}, bf16[2048,768]{1,0:T(8,128)(2,1)}, f32[2,256]{1,0:T(2,128)}, bf16[128,2048]{1,0:T(8,128)(2,1)}) custom-call(bf16[128,2048]{1,0:T(8,128)(2,1)} %fusion.25.refs_0_, bf16[2,2,512,128]{3,2,1,0:T(8,128)(2,1)} %get-tuple-element.51.refs_1_, bf16[2,2,512,128]{3,2,1,0:T(8,128)(2,1)} %get-tuple-element.52.refs_2_, ...), custom_call_target="tpu_custom_call" | custom-call | tf_op jit(solution)/shard_map/attend_backward/pallas_call | solution.py:692
  759.8 1.5 fusion.11
  762.4 69.5 %store_grads.1 = (bf16[8,64,768]{2,1,0:T(8,128)(2,1)}, f32[64,2048]{1,0:T(8,128)}, bf16[8,256,512]{2,1,0:T(8,128)(2,1)}, f32[8,128]{1,0:T(8,128)}) custom-call(bf16[8,4,64,768]{3,2,1,0:T(8,128)(2,1)} %bitcast.188, bf16[4,64,2048]{2,1,0:T(8,128)(2,1)} %bitcast.195, bf16[8,256,512]{2,1,0:T(8,128)(2,1)} %bitcast.191, f32[8,4,8,128]{3,2,1,0:T(8,128)} %copy.108.refs_3_), custom_call_target="tpu_custom_call" | custom-call | tf_op jit(solution)/shard_map/store_grads/pallas_call | solution.py:880
  834.4 3.7 reshape.323
  838.1 4.6 fusion.27
  843.1 1.0 copy.119
  846.5 5.4 reshape.324
  851.9 3.8 fusion.26
  855.8 2.6 copy.107
  858.3 2.7 squeeze.45
  861.0 4.2 copy.106
  865.2 2.7 squeeze.44
  867.9 9.8 convolution_convert_fusion.1
  877.7 100.6 %scatter_mixture.1 = bf16[128,2048]{1,0:T(8,128)(2,1)} custom-call(bf16[8,4,128,2048]{3,2,1,0:T(8,128)(2,1)} %bitcast.176), custom_call_target="tpu_custom_call" | custom-call | tf_op jit(solution)/shard_map/scatter_mixture/pallas_call | solution.py:362
  978.3 3.2 fusion.9
  (119 shorter events, 23.1 us)
Async XLA Ops:
  0.6 1.2 copy-start
  10.0 7.3 copy-start.13
  15.3 3.4 copy-start.14
  214.1 4.1 copy-start.17
  221.0 5.3 copy-start.1
  226.2 1.9 copy-start.9
  233.1 100.3 %copy-start.2 = (bf16[2,64,2048]{2,1,0:T(8,128)(2,1)S(1)}, bf16[2,64,2048]{2,1,0:T(8,128)(2,1)}, u32[]{:S(2)}) copy-start(bf16[2,64,2048]{2,1,0:T(8,128)(2,1)} %param.17) | copy-start | bytes 1572868
  336.1 0.9 copy-start.5
  451.0 19.8 %copy-start.4 = (f32[4096,512]{0,1:T(8,128)S(1)}, f32[4096,512]{0,1:T(8,128)}, u32[]{:S(2)}) copy-start(f32[4096,512]{0,1:T(8,128)} %fusion.31) | copy-start | bytes 25165828
  476.0 15.5 %copy-start.3 = (bf16[4096,256]{0,1:T(8,128)(2,1)}, bf16[4096,256]{0,1:T(8,128)(2,1)S(1)}, u32[]{:S(2)}) copy-start(bf16[4096,256]{0,1:T(8,128)(2,1)S(1)} %get-tuple-element.83) | copy-start | bytes 6291460
  491.4 9.7 copy-start.10
  491.4 9.7 copy-start.11
  501.1 14.2 %copy-start.15 = (f32[8,4,8,128]{3,2,1,0:T(8,128)}, f32[8,4,8,128]{3,2,1,0:T(8,128)S(1)}, u32[]{:S(2)}) copy-start(f32[8,4,8,128]{3,2,1,0:T(8,128)S(1)} %constant_dynamic-update-slice_fusion.refs_1_) | copy-start | bytes 393220
  515.4 104.7 %copy-start.6 = (bf16[128,2048]{1,0:T(8,128)(2,1)S(1)}, bf16[128,2048]{1,0:T(8,128)(2,1)}, u32[]{:S(2)}) copy-start(bf16[128,2048]{1,0:T(8,128)(2,1)} %copy-done.5) | copy-start | bytes 1572868
  515.4 105.9 %copy-start.7 = (bf16[128,2048]{1,0:T(8,128)(2,1)S(1)}, bf16[128,2048]{1,0:T(8,128)(2,1)}, u32[]{:S(2)}) copy-start(bf16[128,2048]{1,0:T(8,128)(2,1)} %get-tuple-element.44) | copy-start | bytes 1572868
  619.2 5.1 copy-start.8
  877.7 100.7 %copy-start.12 = (bf16[128,2048]{1,0:T(8,128)(2,1)S(1)}, bf16[128,2048]{1,0:T(8,128)(2,1)}, u32[]{:S(2)}) copy-start(bf16[128,2048]{1,0:T(8,128)(2,1)} %get-tuple-element.56) | copy-start | bytes 1572868
  978.3 3.2 copy-start.16

commit v4 on v3

--- a/solution.py
+++ b/solution.py
@@ -46,7 +46,7 @@
 
 
 ANY = pl.BlockSpec(memory_space=pl.ANY)
-VMEM_LIMIT = 60 * 1024 * 1024
+VMEM_LIMIT = 67043328
 
 
 class Place:
@@ -55,6 +55,9 @@
         self.s = lax.axis_index("seq")
         self.b = lax.axis_index("batch")
         self.twin_s = self.s + 1 - 2 * lax.rem(self.s, 2)
+        self.bat_x = self.b + 1 - 2 * lax.rem(self.b, 2)
+        self.bat_y = lax.rem(self.b + 2, 4)
+        self.bat_d = lax.rem(self.bat_x + 2, 4)
 
     def seq_at(self, k):
         return lax.rem(self.s + (k + self.n_seq), self.n_seq)
@@ -70,6 +73,12 @@
 
     def bat_peer(self, k):
         return {"seq": self.s, "batch": self.bat_at(k)}
+
+    def x_peer(self):
+        return {"seq": self.s, "batch": self.bat_x}
+
+    def y_peer(self):
+        return {"seq": self.s, "batch": self.bat_y}
 
     def twin(self):
         return {"seq": self.twin_s, "batch": self.b}
@@ -92,10 +101,11 @@
 class Wire:
     def __init__(self, send_sems, recv_sems):
         self.send_sems, self.recv_sems = send_sems, recv_sems
-        self.copies = []
+        self.copies, self.used = [], 0
 
     def push(self, src, dst, peer):
-        slot = len(self.copies)
+        slot = self.used
+        self.used += 1
         copy = pltpu.make_async_remote_copy(
             src_ref=src,
             dst_ref=dst,
@@ -108,6 +118,10 @@
         self.copies.append(copy)
         return copy
 
+    def settle(self, copy):
+        copy.wait_send()
+        self.copies = [other for other in self.copies if other is not copy]
+
     def drain(self):
         for copy in self.copies:
             copy.wait_send()
@@ -183,7 +197,9 @@
     return second
 
 
-def comm_call(kernel, outs, scratch, slots, collective_id, name, in_specs, out_specs=None):
+def comm_call(
+    kernel, outs, scratch, slots, collective_id, name, in_specs, out_specs=None, aliases=None
+):
     return pl.pallas_call(
         kernel,
         out_shape=outs,
@@ -195,6 +211,7 @@
             collective_id=collective_id, has_side_effects=True, vmem_limit_bytes=VMEM_LIMIT
         ),
         name=name,
+        input_output_aliases=aliases or {},
     )
 
 
@@ -454,10 +471,12 @@
     return v * cos_wide + pltpu.roll(v, HEAD // 2, axis=1) * sin_wide
 
 
-def exchange_rows(place, wire, local, got):
+def exchange_rows(place, wire, local, got, between=None):
     copies = [
         wire.push(local, got.at[k - 1], place.seq_peer(k)) for k in range(1, place.n_seq)
     ]
+    if between is not None:
+        between()
     for copy in copies:
         copy.wait_recv()
     total = local[...]
@@ -480,7 +499,9 @@
     return (at_key == at_query) | ((at_key < at_query) & (use > 0))
 
 
-def attend_forward(qkv, usable, w_o, gain_q, gain_k, cos_wide, sin_wide, n_seq, n_bat, span):
+def attend_forward(
+    qkv, usable, w_o, gain_q, gain_k, cos_wide, sin_wide, n_seq, n_bat, span, side=None
+):
     col, three = qkv.shape
     wide = three // 3
     heads = wide // HEAD
@@ -494,11 +515,59 @@
 
     def kernel(*refs):
         qkv_ref, use_ref, wo_ref, gq_ref, gk_ref, cos_ref, sin_ref = refs[:7]
-        q_ref, k_ref, v_ref, mix_ref, stat_ref, out_ref = refs[7:13]
-        local, got, away, mine, twin, line, send_sems, recv_sems = refs[13:]
+        refs = refs[7:]
+        if side:
+            _, gate_ref, up_ref = refs[:3]
+            refs = refs[3:]
+        q_ref, k_ref, v_ref, mix_ref, stat_ref, out_ref = refs[:6]
+        refs = refs[6:]
+        if side:
+            dy_all, gu_all = refs[:2]
+            gu_own, gu_sems = refs[-4:-2]
+            refs = refs[2:-4] + refs[-2:]
+        local, got, away, mine, twin, line, send_sems, recv_sems = refs
         place = Place(n_seq, n_bat)
-        place.greet(all_seq=True, batch=False)
+        place.greet(all_seq=True, batch=bool(side))
         wire = Wire(send_sems, recv_sems)
+        dy_works, gu_copies, gu_here = [], [], []
+        if side:
+            for j in range(place.half):
+                at_seq = place.seq_at(-2 * j)
+                dy_works.append(
+                    Across(
+                        place,
+                        wire,
+                        dy_all.at[at_seq, place.b],
+                        lambda i, at_seq=at_seq: dy_all.at[at_seq, i],
+                    )
+                )
+                dy_works[-1].start()
+
+        def send_experts():
+            if not side:
+                return
+            count, _, hidden = gate_ref.shape
+            part = hidden // n_seq
+            for k in list(range(1, n_seq)) + [0]:
+                lanes = pl.ds(pl.multiple_of(place.seq_at(k) * part, part), part)
+                for m, ref in enumerate((gate_ref, up_ref)):
+                    for e in range(count):
+                        to = pl.ds((m * count + e) * part, part)
+                        if k:
+                            gu_copies.append(
+                                wire.push(
+                                    ref.at[e, :, lanes],
+                                    gu_all.at[place.s, :, to],
+                                    place.seq_peer(k),
+                                )
+                            )
+                        else:
+                            copy = pltpu.make_async_copy(
+                                ref.at[e, :, lanes], gu_own.at[:, to], gu_sems.at[m * count + e]
+                            )
+                            copy.start()
+                            gu_here.append(copy)
+
         for i in range(n_seq):
             for which in range(2):
                 v = qkv_ref[i * own : (i + 1) * own, which * wide : (which + 1) * wide]
@@ -509,7 +578,7 @@
                     at = slice(i * own + r * span, i * own + (r + 1) * span)
                     lanes = slice(2 * wide + h * HEAD, 2 * wide + (h + 1) * HEAD)
                     v_ref[r, h, i * span : (i + 1) * span, :] = qkv_ref[at, lanes].astype(BF)
-        total = exchange_rows(place, wire, local, got)
+        total = exchange_rows(place, wire, local, got, send_experts)
         stat_ref[...] = total
         columns = lax.rsqrt(total / dim + EPS).T
         for which, gain_ref, target in ((0, gq_ref, q_ref), (1, gk_ref, k_ref)):
@@ -551,28 +620,63 @@
             return dot(mix_ref[rows_at, :], wo_ref[...])
 
         scatter.run(project, out_ref)
+        if side:
+            for copy in gu_here:
+                copy.wait()
+            gu_store = pltpu.make_async_copy(gu_own, gu_all.at[place.s], gu_sems.at[0])
+            gu_store.start()
+            for work in dy_works:
+                work.relay()
+            passed = []
+            for j, work in enumerate(dy_works):
+                work.finish()
+                group = dy_all.at[place.seq_at(-2 * j)]
+                passed.append(wire.push(group, group, place.twin()))
         scatter.finish(out_ref)
+        if side:
+            for copy in passed + gu_copies:
+                copy.wait_recv()
+            gu_store.wait()
         wire.drain()
 
     vmem = pl.BlockSpec(memory_space=pltpu.VMEM)
+    side_in, side_out, side_scratch, aliases = [], [], [], {}
+    slots = 3 * n_seq
+    if side:
+        dy_part, gate, up = side
+        count, depth, hidden = gate.shape
+        lanes = 2 * count * (hidden // n_seq)
+        side_in = [ANY] * 3
+        side_out = [
+            jax.ShapeDtypeStruct(dy_part.shape, dy_part.dtype),
+            jax.ShapeDtypeStruct((n_seq, depth, lanes), gate.dtype),
+        ]
+        side_scratch = [
+            pltpu.VMEM((depth, lanes), gate.dtype),
+            pltpu.SemaphoreType.DMA((2 * count,)),
+        ]
+        aliases = {7: 6}
+        slots += 3 * n_seq + 2 * count * n_seq
     head_block = jax.ShapeDtypeStruct((rows, heads, length, HEAD), BF)
     stats = jax.ShapeDtypeStruct((2 * n_seq, own), F32)
     return comm_call(
         kernel,
-        [head_block] * 3 + [jax.ShapeDtypeStruct((col, wide), BF), stats, block],
+        [head_block] * 3 + [jax.ShapeDtypeStruct((col, wide), BF), stats, block] + side_out,
         [pltpu.VMEM(stats.shape, F32), pltpu.VMEM((n_seq - 1,) + stats.shape, F32)]
-        + SeqScatter.scratch(n_seq, block),
-        3 * n_seq,
+        + SeqScatter.scratch(n_seq, block)
+        + side_scratch,
+        slots,
         2,
         "attend_forward",
-        [vmem] * 7,
-        [vmem] * 6,
-    )(qkv, usable, w_o, gain_q, gain_k, cos_wide, sin_wide)
+        [vmem] * 7 + side_in,
+        [vmem] * 6 + [ANY] * len(side_out),
+        aliases,
+    )(qkv, usable, w_o, gain_q, gain_k, cos_wide, sin_wide, *(side or ()))
 
 
 def attend_backward(
     grad_o, q, k, v, mixed, qkv, stats, hidden, usable, w_o, w_qkv, gain_q, gain_k,
-    cos_wide, sin_wide, n_seq, n_bat,
+    cos_wide, sin_wide, n_seq, n_bat, side=None,
 ):
     rows, heads, length, _ = q.shape
     own, dim = grad_o.shape
@@ -585,22 +689,67 @@
     def kernel(*refs):
         (go_ref, q_ref, k_ref, v_ref, mix_ref, qkv_ref, stat_ref, hid_ref, use_ref, wo_ref,
          w_ref, gq_ref, gk_ref, cos_ref, sin_ref) = refs[:15]
-        gwo_ref, gw_ref, gain_ref, out_ref = refs[15:19]
-        go_all, gm, dq, dk, dv, dqkv, local, got = refs[19:27]
-        away, mine, twin, line, send_sems, recv_sems = refs[27:]
+        refs = refs[15:]
+        if side:
+            weighted_ref, down_ref = refs[:2]
+            refs = refs[2:]
+        gwo_ref, gw_ref, gain_ref, out_ref = refs[:4]
+        refs = refs[4:]
+        if side:
+            mixture_ref = refs[0]
+            mix_away, mix_twin, mix_halves, mix_full = refs[-6:-2]
+            refs = refs[1:-6] + refs[-2:]
+        go_all, gm, dq, dk, dv, dqkv, local, got, hid_buf, hid_sems = refs[:10]
+        away, mine, twin, line, send_sems, recv_sems = refs[10:]
         place = Place(n_seq, n_bat)
-        place.greet(all_seq=True, batch=False)
+        place.greet(all_seq=True, batch=bool(side))
         wire = Wire(send_sems, recv_sems)
         gather = SeqGather(place, wire, go_ref, go_all)
         gather.start()
         go_all[place.s] = go_ref[...]
-        for j in range(1, place.half):
-            gather.step(j)
+        order = list(range(1, place.half)) + [0]
+        works, from_twin = {}, {}
+
+        def mixture_of(i):
+            group = n_bat * own
+            at = pl.ds(pl.multiple_of(i * group, group), group)
+            return dot(weighted_ref[at, :], down_ref[...])
+
+        if side:
+            waiting = None
+            for n, j in enumerate(order):
+                if n >= 2:
+                    wire.settle(from_twin[order[n - 2]])
+                mix_away[n % 2] = (
+                    mixture_of(place.twin_at(2 * j)).astype(BF).reshape(n_bat, own, dim)
+                )
+                total = mixture_of(place.seq_at(2 * j))
+                from_twin[j] = wire.push(mix_away.at[n % 2], mix_twin.at[j], place.twin())
+                from_twin[j].wait_recv()
+                mix_twin[j] = (
+                    (total + mix_twin[j].reshape(n_bat * own, dim).astype(F32))
+                    .astype(BF)
+                    .reshape(n_bat, own, dim)
+                )
+                works[j] = AcrossSum(
+                    place, wire, mix_twin.at[j], mix_halves.at[j], mix_full.at[j]
+                )
+                if waiting is not None:
+                    works[waiting].start()
+                waiting = j
+                if j:
+                    gather.step(j)
+            works[waiting].start()
+        else:
+            for j in range(1, place.half):
+                gather.step(j)
         gather.finish()
         for i in range(n_seq):
             part = dot_t(go_all[i], wo_ref[...]).astype(BF)
             for r in range(rows):
                 gm[r, i * span : (i + 1) * span, :] = part[r * span : (r + 1) * span, :]
+        for j in works:
+            works[j].middle()
         dk[...] = jnp.zeros_like(dk)
         dv[...] = jnp.zeros_like(dv)
         for r in range(rows):
@@ -675,20 +824,42 @@
             rows_at = pl.ds(pl.multiple_of(i * own, own), own)
             return dot_t(dqkv[rows_at, :], w_ref[...])
 
+        def hidden_load(part):
+            return pltpu.make_async_copy(
+                hid_ref.at[:, pl.ds(part * 256, 256)], hid_buf.at[part % 2], hid_sems.at[part % 2]
+            )
+
+        hidden_load(0).start()
         scatter.run(project, out_ref)
         for part in range(dim // 256):
             at = slice(part * 256, (part + 1) * 256)
-            gw_ref[at, :] = t_dot(hid_ref[:, at], dqkv[...]).astype(BF)
+            if part + 1 < dim // 256:
+                hidden_load(part + 1).start()
+            hidden_load(part).wait()
+            gw_ref[at, :] = t_dot(hid_buf[part % 2], dqkv[...]).astype(BF)
             total = t_dot(mix_ref[0:own, :], go_all[0, :, at])
             for i in range(1, n_seq):
                 total = total + t_dot(mix_ref[i * own : (i + 1) * own, :], go_all[i, :, at])
             gwo_ref[:, at] = total.astype(BF)
+        for j in works:
+            works[j].finish()
+            mixture_ref[j] = mix_twin[j, place.b]
         scatter.finish(out_ref)
         wire.drain()
 
     vmem = pl.BlockSpec(memory_space=pltpu.VMEM)
     block = jax.ShapeDtypeStruct((own, dim), BF)
     stat_shape = (2 * n_seq, own)
+    side_out, side_scratch = [], []
+    if side:
+        half = n_seq // 2
+        side_out = [jax.ShapeDtypeStruct((half, own, dim), BF)]
+        side_scratch = [
+            pltpu.VMEM((2, n_bat, own, dim), BF),
+            pltpu.VMEM((half, n_bat, own, dim), BF),
+            pltpu.VMEM((half, 2, own // 2, dim), BF),
+            pltpu.VMEM((half, 2, own, dim), BF),
+        ]
     return comm_call(
         kernel,
         [
@@ -696,7 +867,8 @@
             jax.ShapeDtypeStruct((dim, three), BF),
             jax.ShapeDtypeStruct((2, wide), F32),
             block,
-        ],
+        ]
+        + side_out,
         [
             pltpu.VMEM((n_seq, own, dim), BF),
             pltpu.VMEM((rows, length, wide), BF),
@@ -706,15 +878,625 @@
             pltpu.VMEM((col, three), BF),
             pltpu.VMEM(stat_shape, F32),
             pltpu.VMEM((n_seq - 1,) + stat_shape, F32),
-        ]
-        + SeqScatter.scratch(n_seq, block),
-        4 * n_seq,
+            pltpu.VMEM((2, col, 256), BF),
+            pltpu.SemaphoreType.DMA((2,)),
+        ]
+        + SeqScatter.scratch(n_seq, block)
+        + side_scratch,
+        4 * n_seq + (3 * n_seq if side else 0),
         6,
         "attend_backward",
-        [vmem] * 15,
-        [vmem] * 4,
+        [vmem] * 7 + [ANY] + [vmem] * (7 + len(side or ())),
+        [vmem] * (4 + len(side_out)),
     )(grad_o, q, k, v, mixed, qkv, stats, hidden, usable, w_o, w_qkv, gain_q, gain_k,
-      cos_wide, sin_wide)
+      cos_wide, sin_wide, *(side or ()))
+
+
+class Across:
+    def __init__(self, place, wire, src, at):
+        self.place, self.wire, self.src, self.at = place, wire, src, at
+        self.half = src.shape[0] // 2
+
+    def start(self):
+        place, own = self.place, self.at(self.place.b)
+        self.to_x = self.wire.push(self.src, own, place.x_peer())
+        self.to_y = self.wire.push(self.src, own, place.y_peer())
+
+    def relay(self):
+        place, half = self.place, self.half
+        self.to_x.wait_recv()
+        top = self.at(place.bat_x).at[pl.ds(0, half)]
+        self.top = self.wire.push(top, top, place.y_peer())
+        self.to_y.wait_recv()
+        low = self.at(place.bat_y).at[pl.ds(half, half)]
+        self.low = self.wire.push(low, low, place.x_peer())
+
+    def finish(self):
+        self.top.wait_recv()
+        self.low.wait_recv()
+
+
+class AcrossSum:
+    def __init__(self, place, wire, group, halves, full):
+        self.place, self.wire = place, wire
+        self.group, self.halves, self.full = group, halves, full
+        self.half = halves.shape[1]
+
+    def start(self):
+        place, half = self.place, self.half
+        far = self.group.at[place.bat_d]
+        self.top = self.wire.push(far.at[pl.ds(0, half)], self.halves.at[0], place.x_peer())
+        self.low = self.wire.push(far.at[pl.ds(half, half)], self.halves.at[1], place.y_peer())
+
+    def middle(self):
+        place, half = self.place, self.half
+        self.top.wait_recv()
+        add_into(self.group.at[place.bat_y].at[pl.ds(0, half)], self.halves.at[0])
+        self.low.wait_recv()
+        add_into(self.group.at[place.bat_x].at[pl.ds(half, half)], self.halves.at[1])
+        self.y = self.wire.push(self.group.at[place.bat_y], self.full.at[0], place.y_peer())
+        self.x = self.wire.push(self.group.at[place.bat_x], self.full.at[1], place.x_peer())
+
+    def finish(self):
+        self.y.wait_recv()
+        self.x.wait_recv()
+        add_into(self.group.at[self.place.b], self.full.at[0], self.full.at[1])
+
+
+def load_first(weights, w_out, mine, flags, small, dy_own, n_seq, n_bat):
+    shard, dim = weights[0].shape
+    wide = dim // n_seq
+    own = mine.shape[0]
+    slots = 12 * n_seq + n_seq * n_bat
+
+    def kernel(*refs):
+        parts = refs[:3]
+        wo_ref, x_ref, flag_ref, small_ref, dy_ref = refs[3:8]
+        w_ref, wo_all, x_col, flag_col, small_all, dy_all = refs[8:14]
+        buffers = refs[14:20]
+        own_sems, cut_sems, send_sems, recv_sems = refs[20:]
+        place = Place(n_seq, n_bat)
+        place.greet(all_seq=True)
+        wire = Wire(send_sems, recv_sems)
+        small_work = FullGather(place, wire, small_ref, small_all)
+        flag_work = SeqGather(place, wire, flag_ref, flag_col)
+        x_work = SeqGather(place, wire, x_ref, x_col)
+        small_work.start()
+        flag_work.start()
+
+        def cut(k):
+            return pl.ds(pl.multiple_of(place.seq_at(k) * wide, wide), wide)
+
+        def columns(m):
+            return pl.ds(m * wide, wide)
+
+        own_cuts = []
+        for m in range(3):
+            copy = pltpu.make_async_copy(
+                parts[m].at[:, cut(0)], buffers[0].at[:, columns(m)], cut_sems.at[m]
+            )
+            copy.start()
+            own_cuts.append(copy)
+        cuts = {}
+        for k in range(1, n_seq):
+            for m in range(3):
+                cuts[k, m] = wire.push(
+                    parts[m].at[:, cut(k)],
+                    w_ref.at[place.s, place.b, :, columns(m)],
+                    place.seq_peer(k),
+                )
+        wo_work = Across(place, wire, wo_ref, lambda i: wo_all.at[i])
+        wo_work.start()
+        x_work.start()
+        line = [
+            wire.push(dy_ref, dy_all.at[place.s, place.b], place.seq_peer(2 * j))
+            for j in range(1, place.half)
+        ]
+        for copy in own_cuts:
+            copy.wait()
+        spreads = []
+
+        def spread(src, from_seq):
+            work = Across(place, wire, src, lambda i: w_ref.at[from_seq, i])
+            work.start()
+            spreads.append(work)
+
+        spread(buffers[0], place.s)
+        own_w = pltpu.make_async_copy(buffers[0], w_ref.at[place.s, place.b], own_sems.at[0])
+        own_w.start()
+        copies = [own_w] + [
+            keep_own(src, dst, buffers[i + 1], own_sems.at[i + 1])
+            for i, (src, dst) in enumerate(
+                (
+                    (wo_ref, wo_all.at[place.b]),
+                    (x_ref, x_col.at[place.s]),
+                    (flag_ref, flag_col.at[place.s]),
+                    (small_ref, small_all.at[place.s, place.b]),
+                    (dy_ref, dy_all.at[place.s, place.b]),
+                )
+            )
+        ]
+        for j in range(1, place.half):
+            small_work.step(j)
+            flag_work.step(j)
+        for k in range(1, n_seq):
+            for m in range(3):
+                cuts[k, m].wait_recv()
+            spread(w_ref.at[place.seq_at(-k), place.b], place.seq_at(-k))
+        for j in range(place.half):
+            small_work.collect(j)
+        wo_work.relay()
+        for work in spreads:
+            work.relay()
+        for j in range(1, place.half):
+            x_work.step(j)
+        wo_work.finish()
+        for work in spreads:
+            work.finish()
+        for work in (small_work, flag_work, x_work):
+            work.finish()
+        for copy in line:
+            copy.wait_recv()
+        for copy in copies:
+            copy.wait()
+        wire.drain()
+
+    every = (n_seq, n_bat)
+    one = jax.ShapeDtypeStruct((shard, 3 * wide), BF)
+    blocks = (one, w_out, mine, flags, small, dy_own)
+    leads = (every, (n_bat,), (n_seq,), (n_seq,), every, every)
+    return comm_call(
+        kernel,
+        [shape_of(lead, block) for lead, block in zip(leads, blocks)],
+        [pltpu.VMEM(block.shape, block.dtype) for block in blocks]
+        + [pltpu.SemaphoreType.DMA((6,)), pltpu.SemaphoreType.DMA((3,))],
+        slots,
+        1,
+        "load_first",
+        [ANY] * 8,
+    )(*weights, w_out, mine, flags, small, dy_own)
+
+
+def pick_units(first, experts, units, part):
+    at_expert = lax.broadcasted_iota(jnp.int32, (experts, units), 0)
+    at_unit = lax.broadcasted_iota(jnp.int32, (experts, units), 1)
+    low = (at_expert - first) * part
+    return jnp.where((at_unit >= low) & (at_unit < low + part), 1.0, 0.0).astype(F32)
+
+
+def experts_forward(normed, gates, dy_all, w_gu, w_down, local_experts, n_seq, n_bat):
+    own, dim = normed.shape
+    units = w_down.shape[0]
+    part = units // local_experts
+    group = n_bat * own
+    tokens = n_seq * group
+    experts = gates.shape[0]
+    slots = 64 + 2 * n_seq * n_bat
+
+    def kernel(*refs):
+        x_ref, gate_ref, dy_ref, gu_ref, down_ref = refs[:5]
+        x_all, weighted_ref, grad_ref, term_ref = refs[5:9]
+        gates_all, back, x_buf, dy_buf, keep, own_sems, x_sems, dy_sems = refs[9:17]
+        send_sems, recv_sems = refs[17:]
+        place = Place(n_seq, n_bat)
+        place.greet()
+        wire = Wire(send_sems, recv_sems)
+        gate_work = FullGather(place, wire, gate_ref, gates_all)
+        gate_work.start()
+        gates_all[place.s, place.b] = gate_ref[...]
+        line = [
+            wire.push(x_ref, x_all.at[place.s, place.b], place.seq_peer(2 * j))
+            for j in range(1, place.half)
+        ]
+        works = []
+        for j in range(place.half):
+            at_seq = place.seq_at(-2 * j)
+            src = x_ref if j == 0 else x_all.at[at_seq, place.b]
+            works.append(
+                Across(place, wire, src, lambda i, at_seq=at_seq: x_all.at[at_seq, i])
+            )
+        works[0].start()
+        own = keep_own(x_ref, x_all.at[place.s, place.b], keep, own_sems.at[0])
+        selected = pick_units(place.b * local_experts, experts, units, part)
+
+        def dy_load(g, slot):
+            return pltpu.make_async_copy(dy_ref.at[g], dy_buf.at[slot], dy_sems.at[slot])
+
+        def rows_of(g):
+            return pl.ds(pl.multiple_of(g * group, group), group)
+
+        def backs(first, count):
+            dy_load(first, first % 2).start()
+            for g in range(first, first + count):
+                if g + 1 < first + count:
+                    dy_load(g + 1, (g + 1) % 2).start()
+                dy_load(g, g % 2).wait()
+                block = dy_buf[g % 2].reshape(group, dim)
+                back[g * group : (g + 1) * group, :] = dot_t(block, down_ref[...])
+
+        passed = []
+
+        def hand_over(j):
+            at_seq = place.seq_at(-2 * j)
+            works[j].finish()
+            if j == 0:
+                own.wait()
+            passed.append(wire.push(x_all.at[at_seq], x_all.at[at_seq], place.twin()))
+
+        loads = {}
+
+        def fetch(g, slot):
+            loads[slot] = pltpu.make_async_copy(x_all.at[g], x_buf.at[slot], x_sems.at[slot])
+            loads[slot].start()
+
+        def units_on(g, slot):
+            loads[slot].wait()
+            at = rows_of(g)
+            pre = dot(x_buf[slot].reshape(group, dim), gu_ref[...])
+            gate_pre, up_pre = pre[:, :units], pre[:, units:]
+            sig = jax.nn.sigmoid(gate_pre)
+            silu = gate_pre * sig
+            active = (silu * up_pre).astype(BF).astype(F32)
+            grad_back = back[at, :]
+            product = active * grad_back
+            wide_gates = []
+            for i in range(n_bat):
+                inside = slice(i * x_ref.shape[0], (i + 1) * x_ref.shape[0])
+                wide_gates.append(
+                    lax.dot_general(
+                        gates_all[g, i],
+                        selected,
+                        (((0,), (0,)), ((), ())),
+                        precision=HIGHEST,
+                        preferred_element_type=F32,
+                    )
+                )
+                term_ref[g, i] = lax.dot_general(
+                    selected,
+                    product[inside, :],
+                    (((1,), (1,)), ((), ())),
+                    precision=HIGHEST,
+                    preferred_element_type=F32,
+                )
+            wide_gate = jnp.concatenate(wide_gates, axis=0)
+            weighted_ref[at, :] = (active * wide_gate).astype(BF)
+            grad_active = grad_back * wide_gate
+            grad_ref[at, :units] = (
+                grad_active * up_pre * sig * (1.0 + gate_pre * (1.0 - sig))
+            ).astype(BF)
+            grad_ref[at, units:] = (grad_active * silu).astype(BF)
+
+        half = place.half
+        per = n_seq // half
+        for j in range(1, half):
+            backs((j - 1) * per, per)
+            gate_work.step(j)
+            gate_work.collect(j - 1)
+            line[j - 1].wait_recv()
+            works[j].start()
+            works[j - 1].relay()
+        backs((half - 1) * per, per)
+        gate_work.collect(half - 1)
+        gate_work.finish()
+        hand_over(0)
+        fetch(place.seq_at(0), 0)
+        for j in range(half):
+            units_on(place.seq_at(-2 * j), (2 * j) % 4)
+            passed[j].wait_recv()
+            fetch(place.twin_at(-2 * j), (2 * j + 1) % 4)
+            if j + 1 < half:
+                hand_over(j + 1)
+                fetch(place.seq_at(-2 * (j + 1)), (2 * j + 2) % 4)
+            units_on(place.twin_at(-2 * j), (2 * j + 1) % 4)
+            if j == max(0, half - 4):
+                works[half - 1].relay()
+        wire.drain()
+
+    vmem = pl.BlockSpec(memory_space=pltpu.VMEM)
+    return comm_call(
+        kernel,
+        [
+            shape_of((n_seq, n_bat), normed),
+            jax.ShapeDtypeStruct((tokens, units), BF),
+            jax.ShapeDtypeStruct((tokens, 2 * units), BF),
+            shape_of((n_seq, n_bat), gates),
+        ],
+        [
+            pltpu.VMEM((n_seq, n_bat) + gates.shape, F32),
+            pltpu.VMEM((tokens, units), F32),
+            pltpu.VMEM((4, n_bat, own, dim), BF),
+            pltpu.VMEM((2, n_bat, own, dim), BF),
+            pltpu.VMEM((own, dim), BF),
+            pltpu.SemaphoreType.DMA((1,)),
+            pltpu.SemaphoreType.DMA((4,)),
+            pltpu.SemaphoreType.DMA((2,)),
+        ],
+        slots,
+        4,
+        "experts_forward",
+        [ANY, vmem, ANY, vmem, vmem],
+        [ANY, vmem, vmem, vmem],
+    )(normed, gates, dy_all, w_gu, w_down)
+
+
+def experts_backward(
+    grad_pre, weighted, w_gu, terms, x_all, dy_all, local_experts, n_seq, n_bat, own
+):
+    tokens, dim = x_all.shape
+    units = weighted.shape[1]
+    part = units // local_experts
+    group = n_bat * own
+    depth = dim // n_seq
+    hidden = n_seq * part
+    half = n_seq // 2
+    slots = 128 + 2 * n_seq * n_bat
+    block = jax.ShapeDtypeStruct((own, dim), BF)
+    term = jax.ShapeDtypeStruct(terms.shape[2:], F32)
+
+    def kernel(*refs):
+        grad_ref, weighted_ref, gu_ref, term_in, x_ref, dy_ref = refs[:6]
+        out_ref, term_out, gate_out, up_out, down_out = refs[6:11]
+        away, twin, halves, full, line = refs[11:16]
+        columns, sent, got, column_sems = refs[16:20]
+        term_scratch = refs[20:25]
+        send_sems, recv_sems = refs[25:]
+        place = Place(n_seq, n_bat)
+        place.greet(all_seq=True)
+        wire = Wire(send_sems, recv_sems)
+        term_work = FullScatter(place, wire, term_in, term_out, *term_scratch, None)
+        term_work.start()
+
+        def product(i):
+            at = pl.ds(pl.multiple_of(i * group, group), group)
+            return dot_t(grad_ref[at, :], gu_ref[...])
+
+        order = list(range(1, half)) + [0]
+        from_twin, from_seq, works = {}, {}, {}
+
+        def send(j):
+            from_twin[j] = wire.push(away.at[j], twin.at[j], place.twin())
+
+        waiting = None
+        for j in order:
+            away[j] = product(place.twin_at(2 * j)).astype(BF).reshape(n_bat, own, dim)
+            if waiting is not None:
+                send(waiting)
+            waiting = j
+        chunks = [("x", k) for k in list(range(1, n_seq)) + [0]] + [
+            ("y", k) for k in range(dim // 256)
+        ]
+
+        def chunk_load(n):
+            kind, k = chunks[n]
+            if kind == "x":
+                src = x_ref.at[:, pl.ds(pl.multiple_of(place.seq_at(k) * depth, depth), depth)]
+            else:
+                src = dy_ref.at[:, pl.ds(k * 256, 256)]
+            return pltpu.make_async_copy(src, columns.at[n % 2], column_sems.at[n % 2])
+
+        chunk_load(0).start()
+        for j in order:
+            part_sum = product(place.seq_at(2 * j))
+            if waiting is not None:
+                send(waiting)
+                waiting = None
+            from_twin[j].wait_recv()
+            twin[j] = (
+                (part_sum + twin[j].reshape(group, dim).astype(F32))
+                .astype(BF)
+                .reshape(n_bat, own, dim)
+            )
+            works[j] = AcrossSum(place, wire, twin.at[j], halves.at[j], full.at[j])
+            if len(works) > 1:
+                works[order[len(works) - 2]].start()
+        term_order = term_work.order()
+        for j in term_order:
+            term_work.pair(j)
+        works[order[-1]].start()
+
+        arrivals = []
+        done = [0]
+
+        def work_chunk():
+            n = done[0]
+            if n >= len(chunks):
+                return
+            done[0] = n + 1
+            if n + 1 < len(chunks):
+                chunk_load(n + 1).start()
+            chunk_load(n).wait()
+            kind, k = chunks[n]
+            if kind == "y":
+                down_out[:, k * 256 : (k + 1) * 256] = t_dot(weighted_ref[...], columns[n % 2])
+                return
+            value = t_dot(columns[n % 2], grad_ref[...]).astype(BF)
+            if k == 0:
+                got[place.s] = value
+            else:
+                sent[k] = value
+            if n:
+                push_chunk(chunks[n - 1][1])
+
+        def push_chunk(k):
+            if k:
+                arrivals.append(wire.push(sent.at[k], got.at[place.s], place.seq_peer(k)))
+
+        def pass_on(j):
+            works[j].finish()
+            if j:
+                from_seq[j] = wire.push(twin.at[j, place.b], line.at[j], place.seq_peer(2 * j))
+
+        steps = []
+        for n, j in enumerate(order):
+            steps.append(("middle", j))
+            if n:
+                steps.append(("finish", order[n - 1]))
+        steps.append(("finish", order[-1]))
+        share = -(-len(chunks) // len(steps))
+        for kind, j in steps:
+            for _ in range(share):
+                work_chunk()
+            if kind == "middle":
+                works[j].middle()
+            else:
+                pass_on(j)
+        for j in term_order:
+            term_work.merge(j)
+        while done[0] < len(chunks):
+            work_chunk()
+        for copy in arrivals:
+            copy.wait_recv()
+        for i in range(n_seq):
+            lanes = slice(i * part, (i + 1) * part)
+            for e in range(local_experts):
+                gate_out[e, :, lanes] = got[i, :, e * part : (e + 1) * part].astype(F32)
+                up_out[e, :, lanes] = got[i, :, units + e * part : units + (e + 1) * part].astype(
+                    F32
+                )
+        term_work.finish()
+        for j in range(1, half):
+            from_seq[j].wait_recv()
+        total = twin[0, place.b].astype(F32)
+        for j in range(1, half):
+            total = total + line[j].astype(F32)
+        out_ref[...] = total
+        wire.drain()
+
+    vmem = pl.BlockSpec(memory_space=pltpu.VMEM)
+    expert = jax.ShapeDtypeStruct((local_experts, depth, hidden), F32)
+    return comm_call(
+        kernel,
+        [
+            jax.ShapeDtypeStruct((own, dim), F32),
+            term,
+            expert,
+            expert,
+            jax.ShapeDtypeStruct((units, dim), F32),
+        ],
+        [
+            pltpu.VMEM((half, n_bat, own, dim), BF),
+            pltpu.VMEM((half, n_bat, own, dim), BF),
+            pltpu.VMEM((half, 2, own // 2, dim), BF),
+            pltpu.VMEM((half, 2, own, dim), BF),
+            pltpu.VMEM((half, own, dim), BF),
+            pltpu.VMEM((2, tokens, 256), BF),
+            pltpu.VMEM((n_seq, depth, 2 * units), BF),
+            pltpu.VMEM((n_seq, depth, 2 * units), BF),
+            pltpu.SemaphoreType.DMA((2,)),
+        ]
+        + FullScatter.scratch(n_seq, n_bat, term),
+        slots,
+        5,
+        "experts_backward",
+        [vmem] * 3 + [ANY] * 3,
+        [vmem] * 5,
+    )(grad_pre, weighted, w_gu, terms, x_all, dy_all)
+
+
+def store_last(grad_w, grad_wo, small, mixture, n_seq, n_bat):
+    one = jax.ShapeDtypeStruct(grad_w.shape[2:], grad_w.dtype)
+    shard, three = one.shape
+    wide = three // 3
+    wo_one = jax.ShapeDtypeStruct(grad_wo.shape[1:], grad_wo.dtype)
+    small_one = jax.ShapeDtypeStruct(small.shape[2:], small.dtype)
+    half = n_seq // 2
+    dim = wo_one.shape[1]
+    slots = 64 + n_seq * n_bat + 5 * n_seq
+
+    def kernel(*refs):
+        w_ref, wo_ref, small_ref, mix_ref = refs[:4]
+        q_out, k_out, v_out, wo_out, small_out, mix_out = refs[4:10]
+        w_sum, w_halves, w_full, w_got, wo_sum, wo_halves, wo_full, line = refs[10:18]
+        small_scratch = refs[18:23]
+        w_sems, wo_sem, send_sems, recv_sems = refs[23:]
+        place = Place(n_seq, n_bat)
+        place.greet(all_seq=True)
+        wire = Wire(send_sems, recv_sems)
+        small_work = FullScatter(place, wire, small_ref, small_out, *small_scratch, None)
+        small_work.start()
+        order = list(range(1, n_seq)) + [0]
+        loads = {}
+        for k in order:
+            loads[k] = pltpu.make_async_copy(
+                w_ref.at[place.seq_at(k)], w_sum.at[k], w_sems.at[k]
+            )
+            loads[k].start()
+        wo_load = pltpu.make_async_copy(wo_ref, wo_sum, wo_sem.at[0])
+        wo_load.start()
+        works = {}
+        for k in order:
+            loads[k].wait()
+            works[k] = AcrossSum(place, wire, w_sum.at[k], w_halves.at[k], w_full.at[k])
+            works[k].start()
+        wo_load.wait()
+        wo_work = AcrossSum(place, wire, wo_sum, wo_halves, wo_full)
+        wo_work.start()
+        term_order = small_work.order()
+        for j in term_order:
+            small_work.pair(j)
+        mix_line = {
+            j: wire.push(mix_ref.at[j], line.at[j], place.seq_peer(2 * j)) for j in range(1, half)
+        }
+        arrivals = []
+        ready = None
+
+        def ship(k):
+            if k:
+                arrivals.append(
+                    wire.push(w_sum.at[k, place.b], w_got.at[place.s], place.seq_peer(k))
+                )
+
+        for k in order:
+            works[k].middle()
+        wo_work.middle()
+        for j in term_order:
+            small_work.merge(j)
+        for k in order:
+            works[k].finish()
+            if ready is not None:
+                ship(ready)
+            ready = k
+        w_got[place.s] = w_sum[0, place.b]
+        wo_work.finish()
+        wo_out[...] = wo_sum[place.b].astype(F32)
+        small_work.finish()
+        for copy in arrivals:
+            copy.wait_recv()
+        for i in range(n_seq):
+            at = slice(i * wide, (i + 1) * wide)
+            for m, out in enumerate((q_out, k_out, v_out)):
+                out[:, at] = w_got[i, :, m * wide : (m + 1) * wide].astype(F32)
+        for copy in mix_line.values():
+            copy.wait_recv()
+        total = mix_ref[0].astype(F32)
+        for j in range(1, half):
+            total = total + line[j].astype(F32)
+        mix_out[...] = total
+        wire.drain()
+
+    vmem = pl.BlockSpec(memory_space=pltpu.VMEM)
+    matrix = jax.ShapeDtypeStruct((shard, dim), F32)
+    return comm_call(
+        kernel,
+        [matrix] * 4 + [small_one, jax.ShapeDtypeStruct(mixture.shape[1:], F32)],
+        [
+            pltpu.VMEM((n_seq, n_bat, shard, three), BF),
+            pltpu.VMEM((n_seq, 2, shard // 2, three), BF),
+            pltpu.VMEM((n_seq, 2, shard, three), BF),
+            pltpu.VMEM((n_seq, shard, three), BF),
+            pltpu.VMEM((n_bat, shard, dim), BF),
+            pltpu.VMEM((2, shard // 2, dim), BF),
+            pltpu.VMEM((2, shard, dim), BF),
+            pltpu.VMEM(mixture.shape, BF),
+        ]
+        + FullScatter.scratch(n_seq, n_bat, small_one)
+        + [pltpu.SemaphoreType.DMA((n_seq,)), pltpu.SemaphoreType.DMA((1,))],
+        slots,
+        8,
+        "store_last",
+        [ANY] * 3 + [vmem],
+        [vmem] * 6,
+    )(grad_w, grad_wo, small, mixture)
 
 
 def load_inputs(qkv_cut, w_out, mine, flags, small, gu_cut, dy_own, n_seq, n_bat):
@@ -944,18 +1726,31 @@
     )
     positions_own = seq * span + jnp.arange(span, dtype=jnp.int32)
     flags = pack((positions_own[None, :] < lengths[:, None]) & (key_mask == 1))
-    qkv_cut = jnp.stack([w_query, w_key, w_value]).reshape(3, shard, n_seq, wide)
-    qkv_cut = jnp.transpose(qkv_cut, (2, 1, 0, 3)).reshape(n_seq, shard, 3 * wide)
-    gu_cut = jnp.stack([expert_gate, expert_up]).reshape(2, local_experts, depth, n_seq, part)
-    gu_cut = jnp.transpose(gu_cut, (3, 2, 0, 1, 4)).reshape(n_seq, depth, 2 * local_experts * part)
-    w_qkv, w_o, x_col, flag_col, small_all, w_gu, dy_all = load_inputs(
-        qkv_cut, w_out, mine, flags, pack(small), gu_cut, dy_own, n_seq, n_bat
+    units = local_experts * part
+    fused = (
+        n_bat == 4
+        and part % 128 == 0
+        and own == 128
+        and shard % 32 == 0
+        and n_seq * n_bat * own * dim <= 8 * 1024 * 1024
     )
+    if fused:
+        w_qkv, w_o, x_col, flag_col, small_all, dy_part = load_first(
+            (w_query, w_key, w_value), w_out, mine, flags, pack(small), dy_own, n_seq, n_bat
+        )
+    else:
+        qkv_cut = jnp.stack([w_query, w_key, w_value]).reshape(3, shard, n_seq, wide)
+        qkv_cut = jnp.transpose(qkv_cut, (2, 1, 0, 3)).reshape(n_seq, shard, 3 * wide)
+        gu_cut = jnp.stack([expert_gate, expert_up]).reshape(2, local_experts, depth, n_seq, part)
+        gu_cut = jnp.transpose(gu_cut, (3, 2, 0, 1, 4)).reshape(n_seq, depth, 2 * units)
+        w_qkv, w_o, x_col, flag_col, small_all, w_gu, dy_all = load_inputs(
+            qkv_cut, w_out, mine, flags, pack(small), gu_cut, dy_own, n_seq, n_bat
+        )
+        w_gu = w_gu.reshape(dim, 2 * units)
+        dy_all = dy_all.reshape(-1, dim)
     w_qkv = w_qkv.reshape(dim, 3 * wide)
     w_o = w_o.reshape(wide, dim)
-    w_gu = w_gu.reshape(dim, 2 * local_experts * part)
     w_down = expert_down.reshape(local_experts * part, dim)
-    dy_all = dy_all.reshape(-1, dim)
     small_all = unpack(small_all, (n_seq, n_bat), small.shape)
     small_all = jnp.transpose(small_all, (2, 0, 1, 3)).reshape(-1, dim)
     router = small_all[:experts].T.astype(BF)
@@ -973,8 +1768,9 @@
     cos_wide = jnp.concatenate([cos_part, cos_part], axis=1)
     sin_wide = jnp.concatenate([-sin_part, sin_part], axis=1)
     gain_q, gain_k = gain_q[None, :], gain_k[None, :]
-    q, k, v, mixed, stats, mixed_out = attend_forward(
-        qkv, usable, w_o, gain_q, gain_k, cos_wide, sin_wide, n_seq, n_bat, span
+    q, k, v, mixed, stats, mixed_out, *extra = attend_forward(
+        qkv, usable, w_o, gain_q, gain_k, cos_wide, sin_wide, n_seq, n_bat, span,
+        (dy_part, expert_gate, expert_up) if fused else None,
     )
     x_own = mine.astype(F32)
     residual = x_own + mixed_out.astype(F32)
@@ -985,47 +1781,66 @@
     chosen = jnp.any(top_experts.reshape(own, -1)[:, :, None] == expert_ids, axis=1).astype(F32)
     gates = router_probs * chosen
 
-    normed_all, gates_all = gather_all([normed, pack(gates.T)], n_seq, n_bat, 4, "gather_normed")
-    normed_all = normed_all.reshape(-1, dim)
-    gates_all = unpack(gates_all, (n_seq, n_bat), (experts, own))
-    gates_all = jnp.transpose(gates_all, (0, 1, 3, 2)).reshape(-1, experts)
-    first_expert = bat * local_experts
-    gates_here = lax.dynamic_slice_in_dim(gates_all, first_expert, local_experts, 1)
-    units = local_experts * part
-    gates_wide = jnp.repeat(gates_here, part, axis=1)
-    pre = dot(normed_all, w_gu)
-    gate_pre, up_pre = pre[:, :units], pre[:, units:]
-    sig = jax.nn.sigmoid(gate_pre)
-    silu = gate_pre * sig
-    active = (silu * up_pre).astype(BF).astype(F32)
-    weighted = (active * gates_wide).astype(BF)
-    mixture = dot(weighted, w_down).astype(BF)
-    mixture = mixture.reshape(n_seq, n_bat, own, dim)
-    back = dot_t(dy_all, w_down)
-    gate_terms = jnp.sum((active * back).reshape(-1, local_experts, part), axis=-1)
-    grad_active = back * gates_wide
-    grad_gate_pre = (grad_active * up_pre * sig * (1.0 + gate_pre * (1.0 - sig))).astype(BF)
-    grad_up_pre = (grad_active * silu).astype(BF)
-    grad_pre = jnp.concatenate([grad_gate_pre, grad_up_pre], axis=1)
-    grad_down = t_dot(weighted, dy_all)
-    grad_gu = t_dot(normed_all, grad_pre).astype(BF)
-    grad_normed = dot_t(grad_pre, w_gu).astype(BF)
-    gate_terms = gate_terms.reshape(n_seq, n_bat, own, local_experts)
-    grad_gates = lax.dynamic_update_slice_in_dim(
-        jnp.zeros((n_seq, n_bat, experts, own), F32),
-        jnp.transpose(gate_terms, (0, 1, 3, 2)),
-        first_expert,
-        2,
-    )
-    grad_gates = jax.vmap(jax.vmap(pack))(grad_gates)
-    grad_normed = grad_normed.reshape(n_seq, n_bat, own, dim)
-    grad_normed, grad_gates, mixture = scatter_blocks(
-        grad_normed, grad_gates, mixture, n_seq, n_bat
-    )
-    grad_normed = grad_normed.astype(F32)
-    grad_gates = unpack(grad_gates, (), (experts, own)).T
-    output = (residual + mixture.astype(F32)).astype(BF)
-    grad_down = grad_down.reshape(local_experts, part, dim)
+    if fused:
+        dy_all, w_gu = extra[0], extra[1].reshape(dim, 2 * units)
+        normed_all, weighted, grad_pre, gate_terms = experts_forward(
+            normed, gates.T, dy_all, w_gu, w_down, local_experts, n_seq, n_bat
+        )
+        grad_normed, grad_gates, grad_gate, grad_up, grad_down = experts_backward(
+            grad_pre,
+            weighted,
+            w_gu,
+            gate_terms,
+            normed_all.reshape(-1, dim),
+            dy_all.reshape(-1, dim),
+            local_experts,
+            n_seq,
+            n_bat,
+            own,
+        )
+        grad_gates = grad_gates.T
+        grad_down = grad_down.reshape(local_experts, part, dim)
+    else:
+        normed_all, gates_all = gather_all([normed, pack(gates.T)], n_seq, n_bat, 4, "gather_normed")
+        normed_all = normed_all.reshape(-1, dim)
+        gates_all = unpack(gates_all, (n_seq, n_bat), (experts, own))
+        gates_all = jnp.transpose(gates_all, (0, 1, 3, 2)).reshape(-1, experts)
+        first_expert = bat * local_experts
+        gates_here = lax.dynamic_slice_in_dim(gates_all, first_expert, local_experts, 1)
+        gates_wide = jnp.repeat(gates_here, part, axis=1)
+        pre = dot(normed_all, w_gu)
+        gate_pre, up_pre = pre[:, :units], pre[:, units:]
+        sig = jax.nn.sigmoid(gate_pre)
+        silu = gate_pre * sig
+        active = (silu * up_pre).astype(BF).astype(F32)
+        weighted = (active * gates_wide).astype(BF)
+        mixture = dot(weighted, w_down).astype(BF)
+        mixture = mixture.reshape(n_seq, n_bat, own, dim)
+        back = dot_t(dy_all, w_down)
+        gate_terms = jnp.sum((active * back).reshape(-1, local_experts, part), axis=-1)
+        grad_active = back * gates_wide
+        grad_gate_pre = (grad_active * up_pre * sig * (1.0 + gate_pre * (1.0 - sig))).astype(BF)
+        grad_up_pre = (grad_active * silu).astype(BF)
+        grad_pre = jnp.concatenate([grad_gate_pre, grad_up_pre], axis=1)
+        grad_down = t_dot(weighted, dy_all)
+        grad_gu = t_dot(normed_all, grad_pre).astype(BF)
+        grad_normed = dot_t(grad_pre, w_gu).astype(BF)
+        gate_terms = gate_terms.reshape(n_seq, n_bat, own, local_experts)
+        grad_gates = lax.dynamic_update_slice_in_dim(
+            jnp.zeros((n_seq, n_bat, experts, own), F32),
+            jnp.transpose(gate_terms, (0, 1, 3, 2)),
+            first_expert,
+            2,
+        )
+        grad_gates = jax.vmap(jax.vmap(pack))(grad_gates)
+        grad_normed = grad_normed.reshape(n_seq, n_bat, own, dim)
+        grad_normed, grad_gates, mixture = scatter_blocks(
+            grad_normed, grad_gates, mixture, n_seq, n_bat
+        )
+        grad_normed = grad_normed.astype(F32)
+        grad_gates = unpack(grad_gates, (), (experts, own)).T
+        output = (residual + mixture.astype(F32)).astype(BF)
+        grad_down = grad_down.reshape(local_experts, part, dim)
 
     grad_chosen = grad_gates * chosen
     grad_logits = router_probs * (
@@ -1041,9 +1856,9 @@
     grad_residual = dy_own.astype(F32) + grad_resid
     grad_o = grad_residual.astype(BF)
 
-    grad_w_o, grad_w, grad_gains, grad_hidden = attend_backward(
+    grad_w_o, grad_w, grad_gains, grad_hidden, *extra = attend_backward(
         grad_o, q, k, v, mixed, qkv, stats, hidden, usable, w_o, w_qkv, gain_q, gain_k,
-        cos_wide, sin_wide, n_seq, n_bat,
+        cos_wide, sin_wide, n_seq, n_bat, (weighted, w_down) if fused else None,
     )
     grad_w_o = grad_w_o.reshape(n_bat, shard, dim)
     grad_w = grad_w.reshape(n_seq, n_bat, shard, 3 * wide)
@@ -1068,15 +1883,22 @@
     )
     small_grads = jnp.transpose(small_grads.reshape(-1, n_seq, n_bat, shard), (1, 2, 0, 3))
     small_grads = jax.vmap(jax.vmap(pack))(small_grads)
-    grad_gu = grad_gu.reshape(n_seq, depth, -1)
-    grad_w, grad_w_o, grad_gu, small_grads = store_grads(
-        grad_w, grad_w_o, grad_gu, small_grads, n_seq, n_bat
-    )
-    grad_w = grad_w.astype(F32).reshape(n_seq, shard, 3, wide)
-    grad_w = jnp.transpose(grad_w, (2, 1, 0, 3)).reshape(3, shard, dim)
-    grad_gu = grad_gu.reshape(n_seq, depth, 2, local_experts, part)
-    grad_gu = jnp.transpose(grad_gu, (2, 3, 1, 0, 4)).reshape(2, local_experts, depth, hidden_units)
-    grad_gu = grad_gu.astype(F32)
+    if fused:
+        *grad_w, grad_w_o, small_grads, mixture = store_last(
+            grad_w, grad_w_o, small_grads, extra[0], n_seq, n_bat
+        )
+        output = (residual + mixture).astype(BF)
+    else:
+        grad_gu = grad_gu.reshape(n_seq, depth, -1)
+        grad_w, grad_w_o, grad_gu, small_grads = store_grads(
+            grad_w, grad_w_o, grad_gu, small_grads, n_seq, n_bat
+        )
+        grad_w = grad_w.astype(F32).reshape(n_seq, shard, 3, wide)
+        grad_w = jnp.transpose(grad_w, (2, 1, 0, 3)).reshape(3, shard, dim)
+        grad_gu = grad_gu.reshape(n_seq, depth, 2, local_experts, part)
+        grad_gu = jnp.transpose(grad_gu, (2, 3, 1, 0, 4)).reshape(2, local_experts, depth, hidden_units)
+        grad_gu = grad_gu.astype(F32)
+        grad_gate, grad_up = grad_gu[0], grad_gu[1]
     small_grads = unpack(small_grads, (), (experts + 4, shard))
 
     return (
@@ -1091,8 +1913,8 @@
         grad_w[2],
         grad_w_o,
         small_grads[:experts].T,
-        grad_gu[0],
-        grad_gu[1],
+        grad_gate,
+        grad_up,
         grad_down,
     )
 

time: 994 us -> 750 us (0.75)
  Pallas kernels: 790 us -> 675 us
  matrix products: 93.2 us -> 10.4 us
  local copies, waits for them, and re-layouts: 60.7 us -> 26.3 us
  other arithmetic: 37 us -> 27 us
    pallas_call x5 -> x4, Pallas kernels: 560 us -> 424 us  [the longest x1 143 us: experts_backward(): comm_call(kernel, [jax.ShapeDtypeStruct((own, dim), F32), term, expert, e...]
    dot_general x4 -> x0, matrix products: 59.1 us -> none  [the longest x2 34 us: dot_t(): lax.dot_general(a, b, (((1,), (1,)), ((), ())), preferred_element_type=F32)]
    dot_general x4 -> x2, matrix products: 30.1 us -> 5.36 us  [dot(): return jnp.dot(a, b, preferred_element_type=F32)]
    pallas_call x1, Pallas kernels: 129 us -> 148 us  [attend_backward(): comm_call(kernel, [jax.ShapeDtypeStruct((wide, dim), BF), jax.ShapeDtypeS...]
    slice x7 -> x0, local copies, waits for them, and re-layouts: 16.1 us -> none  [the longest x2 6.38 us: shards(): grad_gu[1]]
where the time goes in v4:
time: 750 us; the launch traced here: 740 us
  Pallas kernels  675 us (90%)
  other arithmetic  27 us (4%)
  local copies, waits for them, and re-layouts  26.3 us (4%)
  matrix products  10.4 us (1%)
    pallas_call x1, Pallas kernels, attend_backward(): comm_call(kernel, [jax.ShapeDtypeStruct((wide, dim), BF), jax.ShapeDtypeS...  148 us
    pallas_call x1, Pallas kernels, experts_backward(): comm_call(kernel, [jax.ShapeDtypeStruct((own, dim), F32), term, expert, e...  143 us
    pallas_call x1, Pallas kernels, load_first(): comm_call(kernel, [shape_of(lead, block) for lead, block in zip(leads, bl...  114 us
    pallas_call x1, Pallas kernels, attend_forward(): comm_call(kernel, [head_block] * 3 + [jax.ShapeDtypeStruct((col, wide), B...  103 us
    pallas_call x1, Pallas kernels, experts_forward(): comm_call(kernel, [shape_of((n_seq, n_bat), normed), jax.ShapeDtypeStruct...  90.6 us
    pallas_call x1, Pallas kernels, store_last(): comm_call(kernel, [matrix] * 4 + [small_one, jax.ShapeDtypeStruct(mixture...  76.5 us

profile of v4, /device:TPU:9, one launch (start us, length us, event | category | flops | bytes accessed | tf_op | source)
XLA Modules:
  0.0 739.9 jit_solution(1185036898413271840)
XLA Ops:
  0.7 0.8 compare_and_fusion
  2.1 1.4 concatenate.23
  4.2 114.0 %load_first.1 = (bf16[8,4,64,768]{3,2,1,0:T(8,128)(2,1)}, bf16[4,64,2048]{2,1,0:T(8,128)(2,1)}, bf16[8,128,2048]{2,1,0:T(8,128)(2,1)}, f32[8,8,128]{2,1,0:T(8,12...) custom-call(bf16[64,2048]{1,0:T(8,128)(2,1)} %refs_0_.1, bf16[64,2048]{1,0:T(8,128)(2,1)} %refs_1_.1, ...), custom_call_target="tpu_custom_call" | custom-call | tf_op jit(solution)/shard_map/load_first/pallas_call | solution.py:1048
  118.2 0.9 reshape.227
  119.4 0.7 fusion.22
  120.1 3.2 multiply_reduce_fusion
  124.0 1.0 multiply_convert_fusion
  125.0 0.8 copy-done.7
  125.9 5.1 fusion.24.refs_0_.refs_5_
  131.1 0.7 dynamic_slice.6
  132.5 1.0 fusion.11
  133.5 1.0 pad_maximum_fusion
  134.6 0.7 reshape.232.refs_1_.refs_8_
  135.2 103.1 %attend_forward.1 = (bf16[2,2,512,128]{3,2,1,0:T(8,128)(2,1)}, bf16[2,2,512,128]{3,2,1,0:T(8,128)(2,1)}, bf16[2,2,512,128]{3,2,1,0:T(8,128)(2,1)}, bf16[1024,256...) custom-call(f32[1024,768]{1,0:T(8,128)} %fusion.24.refs_0_.refs_5_, ...), custom_call_target="tpu_custom_call", output_to_operand_aliasing={{6}: (7, {})} | custom-call | tf_op jit(solution)/shard_map/attend_forward/pallas_call | solution.py:662
  238.4 1.5 multiply_reduce_fusion.4
  239.8 0.7 copy.60
  240.6 1.4 multiply_convert_fusion.1.refs_0_
  242.1 1.1 slice.90
  244.0 0.7 copy.61
  245.4 90.6 %experts_forward.1 = (bf16[8,4,128,2048]{3,2,1,0:T(8,128)(2,1)}, bf16[4096,256]{1,0:T(8,128)(2,1)}, bf16[4096,512]{1,0:T(8,128)(2,1)}, f32[8,4,8,128]{3,2,1,0:T(8,128)}) custom-call(bf16[128,2048]{1,0:T(8,128)(2,1)} %copy-done.5, f32[8,128]{1,0:T(8,128)} %select_bitcast_fusion.refs_1_, bf16[8,4,128,2048]{3,2,1,0:T(8,128)(2,1)} %get-tuple-element.55.refs_2_, ...), custom_call_target="tpu_custom_call" | custom-call | tf_op jit(solution)/shard_map/experts_forward/pallas_call | solution.py:1196
  336.0 142.5 %experts_backward.1 = (f32[128,2048]{1,0:T(8,128)}, f32[8,128]{1,0:T(8,128)}, f32[2,256,1024]{2,1,0:T(8,128)}, f32[2,256,1024]{2,1,0:T(8,128)}, f32[256,2048]{1,0:T(8,128)}) custom-call(bf16[4096,512]{1,0:T(8,128)(2,1)} %get-tuple-element.57.refs_0_, bf16[4096,256]{1,0:T(8,128)(2,1)} %get-tuple-element.58.refs_1_.refs_15_, bf16[2048,512]{1,0:T(8,128)(2,1)} %bitcast.108, ...), custom_call_target="tpu_custom_call" | custom-call | tf_op jit(solution)/shard_map/experts_backward/pallas_call | solution.py:1367
  478.6 0.8 multiply_reduce_fusion.5
  479.4 1.4 fusion.15
  481.0 0.7 copy.63
  481.7 3.6 multiply_reduce_fusion.1
  485.4 1.3 fusion.21.refs_0_
  486.7 3.0 fusion.1.refs_7_
  489.7 148.2 %attend_backward.1 = (bf16[256,2048]{1,0:T(8,128)(2,1)}, bf16[2048,768]{1,0:T(8,128)(2,1)}, f32[2,256]{1,0:T(2,128)}, bf16[128,2048]{1,0:T(8,128)(2,1)}, bf16[4,128,2048]{2,1,0:T(8,128)(2,1)}) custom-call(bf16[128,2048]{1,0:T(8,128)(2,1)} %fusion.21.refs_0_, bf16[2,2,512,128]{3,2,1,0:T(8,128)(2,1)} %get-tuple-element.63.refs_1_, ...), custom_call_target="tpu_custom_call" | custom-call | tf_op jit(solution)/shard_map/attend_backward/pallas_call | solution.py:863
  638.0 0.7 slice_dynamic-update-slice_fusion.1
  639.2 0.7 reduce.8
  639.9 0.7 slice_dynamic-update-slice_fusion
  640.6 0.7 reduce.9
  641.4 1.2 multiply_reduce_fusion.2
  642.7 2.1 fusion.8
  645.0 0.8 concatenate.30
  645.8 1.0 concatenate.31
  646.9 0.7 copy.69.refs_2_
  647.6 76.5 %store_last.1 = (f32[64,2048]{1,0:T(8,128)}, f32[64,2048]{1,0:T(8,128)}, f32[64,2048]{1,0:T(8,128)}, f32[64,2048]{1,0:T(8,128)}, f32[8,128]{1,0:T(8,128)}, /*index=5*/f32[128,2048]{1,0:T(8,128)}) custom-call(bf16[8,4,64,768]{3,2,1,0:T(8,128)(2,1)} %bitcast.117, bf16[4,64,2048]{2,1,0:T(8,128)(2,1)} %bitcast.119, f32[8,4,8,128]{3,2,1,0:T(8,128)} %copy.69.refs_2_, ...), custom_call_target="tpu_custom_call" | custom-call | tf_op jit(solution)/shard_map/store_last/pallas_call | solution.py:1479
  724.1 0.7 broadcast_multiply_fusion
  724.8 4.1 fusion.7
  729.5 0.7 slice.71
  730.2 2.0 copy.87
  732.2 1.9 copy.88
  734.1 0.8 copy.89
  734.9 0.8 copy.90
  735.7 1.3 copy.91
  737.0 1.3 copy.92
  738.3 1.3 copy.93
  (110 shorter events, 6.6 us)
Async XLA Ops:
  119.3 5.7 copy-start.11
  120.1 4.9 copy-start.15
  120.1 3.8 copy-start
  124.0 1.9 copy-start.7
  125.9 8.6 %copy-start.20 = (f32[8,8,128]{2,1,0:T(8,128)S(1)}, f32[8,8,128]{2,1,0:T(8,128)}, u32[]{:S(2)}) copy-start(f32[8,8,128]{2,1,0:T(8,128)} %get-tuple-element.51) | copy-start | bytes 98308
  239.8 3.3 copy-start.26
  240.6 2.5 copy-start.17
  242.1 1.3 copy-start.5
  243.4 0.6 copy-start.14
  244.0 0.8 copy-start.19
  244.0 1.4 copy-start.22
  244.0 1.4 copy-start.24
  244.8 0.6 copy-start.21
  478.5 6.8 copy-start.2
  478.5 6.8 copy-start.3
  478.5 6.8 copy-start.6
  478.6 6.8 copy-start.18
  478.6 6.8 copy-start.27
  478.6 8.1 %copy-start.16 = (f32[2048]{0:T(1024)S(1)}, f32[2048]{0:T(1024)}, u32[]{:S(2)}) copy-start(f32[2048]{0:T(1024)} %copy-done.15) | copy-start | bytes 24580
  478.6 8.1 %copy-start.23 = (f32[1024]{0:T(1024)S(1)}, f32[1024]{0:T(1024)}, u32[]{:S(2)}) copy-start(f32[1024]{0:T(1024)} %get-tuple-element.96) | copy-start | bytes 12292
  481.0 5.8 copy-start.1
  485.4 1.4 copy-start.4
  485.4 1.4 copy-start.29
  642.7 2.1 copy-start.28
  724.1 4.8 copy-start.25
  724.1 10.0 %copy-start.13 = (f32[64,2048]{1,0:T(8,128)S(1)}, f32[64,2048]{1,0:T(8,128)}, u32[]{:S(2)}) copy-start(f32[64,2048]{1,0:T(8,128)} %get-tuple-element.128) | copy-start | bytes 1572868
  724.8 10.1 %copy-start.12 = (f32[64,2048]{1,0:T(8,128)S(1)}, f32[64,2048]{1,0:T(8,128)}, u32[]{:S(2)}) copy-start(f32[64,2048]{1,0:T(8,128)} %get-tuple-element.129) | copy-start | bytes 1572868
  724.8 10.9 %copy-start.10 = (f32[2,256,1024]{2,1,0:T(8,128)S(1)}, f32[2,256,1024]{2,1,0:T(8,128)}, u32[]{:S(2)}) copy-start(f32[2,256,1024]{2,1,0:T(8,128)} %get-tuple-element.131) | copy-start | bytes 6291460
  730.2 6.8 copy-start.9
  735.7 2.6 copy-start.8

commit v5 on v4

--- a/solution.py
+++ b/solution.py
@@ -54,10 +54,30 @@
         self.n_seq, self.n_bat, self.half = n_seq, n_bat, n_seq // 2
         self.s = lax.axis_index("seq")
         self.b = lax.axis_index("batch")
-        self.twin_s = self.s + 1 - 2 * lax.rem(self.s, 2)
+        self.core = lax.rem(self.s, 2)
+        self.z = lax.div(self.s, 2)
+        self.twin_s = self.s + 1 - 2 * self.core
         self.bat_x = self.b + 1 - 2 * lax.rem(self.b, 2)
         self.bat_y = lax.rem(self.b + 2, 4)
         self.bat_d = lax.rem(self.bat_x + 2, 4)
+
+    def chip(self, i):
+        return 2 * i + self.core
+
+    def chip_twin(self, i):
+        return 2 * i + 1 - self.core
+
+    def chip_peer(self, i):
+        return {"seq": self.chip(lax.rem(i + self.half, self.half)), "batch": self.b}
+
+    def origin(self, m):
+        if m == 0:
+            return self.z
+        last = self.half - 1
+        upper = lax.div(2 * self.z, self.half)
+        mirrored = self.z + upper * (last - 2 * self.z)
+        place = m - 1 + lax.div(m - mirrored + last, self.half)
+        return place + upper * (last - 2 * place)
 
     def seq_at(self, k):
         return lax.rem(self.s + (k + self.n_seq), self.n_seq)
@@ -103,28 +123,73 @@
         self.send_sems, self.recv_sems = send_sems, recv_sems
         self.copies, self.used = [], 0
 
-    def push(self, src, dst, peer):
-        slot = self.used
-        self.used += 1
-        copy = pltpu.make_async_remote_copy(
+    def reserve(self, count):
+        first = self.used
+        self.used += count
+        return first
+
+    def make(self, src, dst, peer, send_slot, recv_slot):
+        return pltpu.make_async_remote_copy(
             src_ref=src,
             dst_ref=dst,
-            send_sem=self.send_sems.at[slot],
-            recv_sem=self.recv_sems.at[slot],
+            send_sem=self.send_sems.at[send_slot],
+            recv_sem=self.recv_sems.at[recv_slot],
             device_id=peer,
             device_id_type=pl.DeviceIdType.MESH,
         )
+
+    def push(self, src, dst, peer):
+        slot = self.reserve(1)
+        copy = self.make(src, dst, peer, slot, slot)
         copy.start()
-        self.copies.append(copy)
+        self.copies.append((copy, None))
         return copy
+
+    def push_if(self, there, copy):
+        pl.when(there)(copy.start)
+        self.copies.append((copy, there))
 
     def settle(self, copy):
         copy.wait_send()
-        self.copies = [other for other in self.copies if other is not copy]
+        self.copies = [other for other in self.copies if other[0] is not copy]
 
     def drain(self):
-        for copy in self.copies:
-            copy.wait_send()
+        for copy, there in self.copies:
+            if there is None:
+                copy.wait_send()
+            else:
+                pl.when(there)(copy.wait_send)
+
+
+class Line:
+    def __init__(self, place, wire, src, at):
+        self.place, self.wire, self.src, self.at = place, wire, src, at
+        self.base = wire.reserve(place.half + 2)
+        self.sends = 0
+
+    def copy(self, src, origin, peer):
+        return self.wire.make(
+            src, self.at(origin), peer, self.base + self.sends, self.base + origin
+        )
+
+    def send(self, there, src, origin, to):
+        copy = self.copy(src, origin, self.place.chip_peer(to))
+        self.sends += 1
+        self.wire.push_if(there, copy)
+
+    def start(self):
+        place = self.place
+        self.send(place.z < place.half - 1, self.src, place.z, place.z + 1)
+        self.send(place.z > 0, self.src, place.z, place.z - 1)
+
+    def step(self, m):
+        place = self.place
+        origin = place.origin(m)
+        self.copy(self.at(origin), origin, place.chip_peer(place.z)).wait_recv()
+        from_left = lax.div(place.z - origin - 1 + place.half, place.half)
+        to = place.z + 2 * from_left - 1
+        self.send((to >= 0) & (to < place.half), self.at(origin), origin, to)
+        return origin
 
 
 class SeqGather:
@@ -133,15 +198,13 @@
         self.late = []
 
     def start(self):
-        place, mine = self.place, self.out.at[self.place.s]
-        self.line = [
-            self.wire.push(self.src, mine, place.seq_peer(2 * j)) for j in range(1, place.half)
-        ]
-        self.late.append(self.wire.push(self.src, mine, place.twin()))
+        place = self.place
+        self.line = Line(place, self.wire, self.src, lambda i: self.out.at[place.chip(i)])
+        self.line.start()
+        self.late.append(self.wire.push(self.src, self.out.at[place.s], place.twin()))
 
     def step(self, j):
-        self.line[j - 1].wait_recv()
-        block = self.out.at[self.place.seq_at(-2 * j)]
+        block = self.out.at[self.place.chip(self.line.step(j))]
         self.late.append(self.wire.push(block, block, self.place.twin()))
 
     def finish(self):
@@ -421,68 +484,59 @@
 
 
 class SeqScatter:
-    def __init__(self, place, wire, away, mine, twin, line):
+    def __init__(self, place, wire, full, twin, line):
         self.place, self.wire = place, wire
-        self.away, self.mine, self.twin, self.line = away, mine, twin, line
-        self.from_twin, self.from_seq = {}, {}
+        self.full, self.twin, self.line = full, twin, line
         self.order = list(range(1, place.half)) + [0]
 
     @staticmethod
-    def scratch(n_seq, block):
-        return [pltpu.VMEM((n_seq // 2,) + block.shape, block.dtype)] * 4
-
-    def run(self, compute, out):
-        place, wire = self.place, self.wire
-        waiting = None
-        for j in self.order:
-            self.away[j] = compute(place.twin_at(2 * j)).astype(self.away.dtype)
-            if waiting is not None:
-                self.send(waiting)
-            waiting = j
-        for j in self.order:
-            self.mine[j] = compute(place.seq_at(2 * j)).astype(self.mine.dtype)
-            if waiting is not None:
-                self.send(waiting)
-                waiting = None
-        waiting = None
+    def scratch(rows, n_seq, block):
+        lead = ((rows, n_seq), (rows, n_seq // 2), (rows, n_seq // 2))
+        return [pltpu.VMEM(extent + block.shape, block.dtype) for extent in lead]
+
+    def start(self):
+        place = self.place
+        self.from_twin = {
+            j: self.wire.push(self.full.at[place.twin_at(2 * j)], self.twin.at[j], place.twin())
+            for j in self.order
+        }
+
+    def pass_on(self):
+        place = self.place
+        self.from_seq = {}
         for j in self.order:
             self.from_twin[j].wait_recv()
-            add_into(self.mine.at[j], self.twin.at[j])
-            if waiting:
-                self.pass_on(waiting)
-            waiting = j
-
-    def send(self, j):
-        self.from_twin[j] = self.wire.push(self.away.at[j], self.twin.at[j], self.place.twin())
-
-    def pass_on(self, j):
-        self.from_seq[j] = self.wire.push(
-            self.mine.at[j], self.line.at[j], self.place.seq_peer(2 * j)
-        )
-
-    def finish(self, out):
-        for j in range(1, self.place.half):
-            self.from_seq[j].wait_recv()
-        add_into(self.mine.at[0], *[self.line.at[j] for j in range(1, self.place.half)])
-        out[...] = self.mine[0]
+            block = self.full.at[place.seq_at(2 * j)]
+            add_into(block, self.twin.at[j])
+            if j:
+                self.from_seq[j] = self.wire.push(block, self.line.at[j], place.seq_peer(2 * j))
+
+    def finish(self, out, at):
+        for copy in self.from_seq.values():
+            copy.wait_recv()
+        own = self.full.at[self.place.s]
+        add_into(own, *[self.line.at[j] for j in range(1, self.place.half)])
+        out[at, :] = own[...]
 
 
 def turn(v, cos_wide, sin_wide):
     return v * cos_wide + pltpu.roll(v, HEAD // 2, axis=1) * sin_wide
 
 
-def exchange_rows(place, wire, local, got, between=None):
-    copies = [
-        wire.push(local, got.at[k - 1], place.seq_peer(k)) for k in range(1, place.n_seq)
-    ]
-    if between is not None:
-        between()
-    for copy in copies:
-        copy.wait_recv()
-    total = local[...]
-    for k in range(place.n_seq - 1):
-        total = total + got[k]
-    return total
+class Exchange:
+    def __init__(self, place, wire, local, got):
+        self.local, self.got, self.count = local, got, place.n_seq - 1
+        self.copies = [
+            wire.push(local, got.at[k - 1], place.seq_peer(k)) for k in range(1, place.n_seq)
+        ]
+
+    def total(self):
+        for copy in self.copies:
+            copy.wait_recv()
+        total = self.local[...]
+        for k in range(self.count):
+            total = total + self.got[k]
+        return total
 
 
 def lane_sums(v):
@@ -499,33 +553,38 @@
     return (at_key == at_query) | ((at_key < at_query) & (use > 0))
 
 
+STEP = 128
+
+
 def attend_forward(
-    qkv, usable, w_o, gain_q, gain_k, cos_wide, sin_wide, n_seq, n_bat, span, side=None
+    x_col, w_qkv, gain_attn, usable, w_o, gain_q, gain_k, cos_wide, sin_wide, n_seq, n_bat, rows,
+    side=None,
 ):
-    col, three = qkv.shape
+    col, dim = x_col.shape
+    three = w_qkv.shape[1]
     wide = three // 3
     heads = wide // HEAD
-    own = col // n_seq
-    rows = own // span
-    length = n_seq * span
-    dim = w_o.shape[1]
+    length = col // rows
+    span = length // n_seq
+    own = rows * span
+    steps = length // STEP
     chunk = min(256, length)
     scale = HEAD ** (-0.5)
-    block = jax.ShapeDtypeStruct((own, dim), BF)
+    block = jax.ShapeDtypeStruct((span, dim), BF)
 
     def kernel(*refs):
-        qkv_ref, use_ref, wo_ref, gq_ref, gk_ref, cos_ref, sin_ref = refs[:7]
-        refs = refs[7:]
+        (x_ref, w_ref, ga_ref, use_ref, wo_ref, gq_ref, gk_ref, cos_ref, sin_ref) = refs[:9]
+        refs = refs[9:]
         if side:
             _, gate_ref, up_ref = refs[:3]
             refs = refs[3:]
-        q_ref, k_ref, v_ref, mix_ref, stat_ref, out_ref = refs[:6]
-        refs = refs[6:]
+        hid_ref, qkv_ref, q_ref, k_ref, v_ref, mix_ref, stat_ref, out_ref = refs[:8]
+        refs = refs[8:]
         if side:
             dy_all, gu_all = refs[:2]
             gu_own, gu_sems = refs[-4:-2]
             refs = refs[2:-4] + refs[-2:]
-        local, got, away, mine, twin, line, send_sems, recv_sems = refs
+        local, got, full, twin, line, send_sems, recv_sems = refs
         place = Place(n_seq, n_bat)
         place.greet(all_seq=True, batch=bool(side))
         wire = Wire(send_sems, recv_sems)
@@ -543,12 +602,12 @@
                 )
                 dy_works[-1].start()
 
-        def send_experts():
+        def send_experts(steps_of):
             if not side:
                 return
             count, _, hidden = gate_ref.shape
             part = hidden // n_seq
-            for k in list(range(1, n_seq)) + [0]:
+            for k in steps_of:
                 lanes = pl.ds(pl.multiple_of(place.seq_at(k) * part, part), part)
                 for m, ref in enumerate((gate_ref, up_ref)):
                     for e in range(count):
@@ -568,35 +627,46 @@
                             copy.start()
                             gu_here.append(copy)
 
-        for i in range(n_seq):
-            for which in range(2):
-                v = qkv_ref[i * own : (i + 1) * own, which * wide : (which + 1) * wide]
-                local[which * n_seq + i : which * n_seq + i + 1, :] = lane_sums(v * v)
-        for i in range(n_seq):
-            for r in range(rows):
-                for h in range(heads):
-                    at = slice(i * own + r * span, i * own + (r + 1) * span)
-                    lanes = slice(2 * wide + h * HEAD, 2 * wide + (h + 1) * HEAD)
-                    v_ref[r, h, i * span : (i + 1) * span, :] = qkv_ref[at, lanes].astype(BF)
-        total = exchange_rows(place, wire, local, got, send_experts)
+        send_experts([0, 2, 3])
+        for first in range(0, col, chunk):
+            at = slice(first, first + chunk)
+            x = x_ref[at, :].astype(F32)
+            hidden = (x * rms_scale(x) * ga_ref[...]).astype(BF)
+            hid_ref[at, :] = hidden
+            qkv_ref[at, :] = dot(hidden, w_ref[...])
+        for r in range(rows):
+            for c in range(steps):
+                at = slice(r * length + c * STEP, r * length + (c + 1) * STEP)
+                for which in range(2):
+                    v = qkv_ref[at, which * wide : (which + 1) * wide]
+                    row = (r * 2 + which) * steps + c
+                    local[row : row + 1, :] = lane_sums(v * v)
+        for r in range(rows):
+            for h in range(heads):
+                lanes = slice(2 * wide + h * HEAD, 2 * wide + (h + 1) * HEAD)
+                v_ref[r, h] = qkv_ref[r * length : (r + 1) * length, lanes].astype(BF)
+        exchange = Exchange(place, wire, local, got)
+        send_experts([k for k in range(1, n_seq) if k not in (2, 3)])
+        total = exchange.total()
         stat_ref[...] = total
         columns = lax.rsqrt(total / dim + EPS).T
-        for which, gain_ref, target in ((0, gq_ref, q_ref), (1, gk_ref, k_ref)):
-            for i in range(n_seq):
-                at_pos = slice(i * span, (i + 1) * span)
-                for r in range(rows):
-                    at = slice(i * own + r * span, i * own + (r + 1) * span)
-                    factor = columns[
-                        r * span : (r + 1) * span, which * n_seq + i : which * n_seq + i + 1
-                    ]
+        scatters = [
+            SeqScatter(place, wire, full.at[r], twin.at[r], line.at[r]) for r in range(rows)
+        ]
+        for r in range(rows):
+            for c in range(steps):
+                inside = slice(c * STEP, (c + 1) * STEP)
+                at = slice(r * length + c * STEP, r * length + (c + 1) * STEP)
+                for which, gain_ref, target in ((0, gq_ref, q_ref), (1, gk_ref, k_ref)):
+                    row = (r * 2 + which) * steps + c
+                    factor = columns[:, row : row + 1]
                     for h in range(heads):
                         lanes = slice(which * wide + h * HEAD, which * wide + (h + 1) * HEAD)
                         gain = gain_ref[0:1, h * HEAD : (h + 1) * HEAD]
                         v = qkv_ref[at, lanes] * factor * gain
-                        target[r, h, at_pos, :] = turn(
-                            v, cos_ref[at_pos, :], sin_ref[at_pos, :]
+                        target[r, h, inside, :] = turn(
+                            v, cos_ref[inside, :], sin_ref[inside, :]
                         ).astype(BF)
-        for r in range(rows):
             for c in range(length // chunk):
                 keys = (c + 1) * chunk
                 allowed = allowed_block(use_ref[r : r + 1, :keys], c * chunk, chunk, keys)
@@ -607,32 +677,27 @@
                     raised = jnp.exp(scores - jnp.max(scores, axis=-1, keepdims=True))
                     probs = raised / jnp.sum(raised, axis=-1, keepdims=True)
                     mixed = dot(probs.astype(BF), v_ref[r, h, :keys, :]).astype(BF)
-                    for p in range(chunk // span):
-                        i = c * (chunk // span) + p
-                        mix_ref[
-                            i * own + r * span : i * own + (r + 1) * span,
-                            h * HEAD : (h + 1) * HEAD,
-                        ] = mixed[p * span : (p + 1) * span, :]
-        scatter = SeqScatter(place, wire, away, mine, twin, line)
-
-        def project(i):
-            rows_at = pl.ds(pl.multiple_of(i * own, own), own)
-            return dot(mix_ref[rows_at, :], wo_ref[...])
-
-        scatter.run(project, out_ref)
+                    mix_ref[r, c * chunk : keys, h * HEAD : (h + 1) * HEAD] = mixed
+                if r and c == 0:
+                    scatters[r - 1].pass_on()
+            full[r] = dot(mix_ref[r], wo_ref[...]).astype(BF).reshape(n_seq, span, dim)
+            if side and r == 0:
+                for work in dy_works:
+                    work.relay()
+            scatters[r].start()
         if side:
             for copy in gu_here:
                 copy.wait()
             gu_store = pltpu.make_async_copy(gu_own, gu_all.at[place.s], gu_sems.at[0])
             gu_store.start()
-            for work in dy_works:
-                work.relay()
-            passed = []
-            for j, work in enumerate(dy_works):
-                work.finish()
-                group = dy_all.at[place.seq_at(-2 * j)]
-                passed.append(wire.push(group, group, place.twin()))
-        scatter.finish(out_ref)
+        scatters[-1].pass_on()
+        passed = []
+        for j, work in enumerate(dy_works):
+            work.finish()
+            group = dy_all.at[place.seq_at(-2 * j)]
+            passed.append(wire.push(group, group, place.twin()))
+        for r in range(rows):
+            scatters[r].finish(out_ref, slice(r * span, (r + 1) * span))
         if side:
             for copy in passed + gu_copies:
                 copy.wait_recv()
@@ -641,7 +706,7 @@
 
     vmem = pl.BlockSpec(memory_space=pltpu.VMEM)
     side_in, side_out, side_scratch, aliases = [], [], [], {}
-    slots = 3 * n_seq
+    slots = (1 + rows) * n_seq
     if side:
         dy_part, gate, up = side
         count, depth, hidden = gate.shape
@@ -655,23 +720,33 @@
             pltpu.VMEM((depth, lanes), gate.dtype),
             pltpu.SemaphoreType.DMA((2 * count,)),
         ]
-        aliases = {7: 6}
+        aliases = {9: 8}
         slots += 3 * n_seq + 2 * count * n_seq
     head_block = jax.ShapeDtypeStruct((rows, heads, length, HEAD), BF)
-    stats = jax.ShapeDtypeStruct((2 * n_seq, own), F32)
+    stats = jax.ShapeDtypeStruct((2 * rows * steps, STEP), F32)
+    outs = [
+        jax.ShapeDtypeStruct((col, dim), BF),
+        jax.ShapeDtypeStruct((col, three), F32),
+        head_block,
+        head_block,
+        head_block,
+        jax.ShapeDtypeStruct((rows, length, wide), BF),
+        stats,
+        jax.ShapeDtypeStruct((own, dim), BF),
+    ]
     return comm_call(
         kernel,
-        [head_block] * 3 + [jax.ShapeDtypeStruct((col, wide), BF), stats, block] + side_out,
+        outs + side_out,
         [pltpu.VMEM(stats.shape, F32), pltpu.VMEM((n_seq - 1,) + stats.shape, F32)]
-        + SeqScatter.scratch(n_seq, block)
+        + SeqScatter.scratch(rows, n_seq, block)
         + side_scratch,
         slots,
         2,
         "attend_forward",
-        [vmem] * 7 + side_in,
-        [vmem] * 6 + [ANY] * len(side_out),
+        [vmem] * 9 + side_in,
+        [vmem] * 8 + [ANY] * len(side_out),
         aliases,
-    )(qkv, usable, w_o, gain_q, gain_k, cos_wide, sin_wide, *(side or ()))
+    )(x_col, w_qkv, gain_attn, usable, w_o, gain_q, gain_k, cos_wide, sin_wide, *(side or ()))
 
 
 def attend_backward(
@@ -683,8 +758,10 @@
     span = own // rows
     col, three = qkv.shape
     wide = three // 3
+    steps = length // STEP
     chunk = min(256, length)
     scale = HEAD ** (-0.5)
+    group = n_bat * own
 
     def kernel(*refs):
         (go_ref, q_ref, k_ref, v_ref, mix_ref, qkv_ref, stat_ref, hid_ref, use_ref, wo_ref,
@@ -700,20 +777,31 @@
             mix_away, mix_twin, mix_halves, mix_full = refs[-6:-2]
             refs = refs[1:-6] + refs[-2:]
         go_all, gm, dq, dk, dv, dqkv, local, got, hid_buf, hid_sems = refs[:10]
-        away, mine, twin, line, send_sems, recv_sems = refs[10:]
+        full, twin, line, send_sems, recv_sems = refs[10:]
         place = Place(n_seq, n_bat)
         place.greet(all_seq=True, batch=bool(side))
         wire = Wire(send_sems, recv_sems)
-        gather = SeqGather(place, wire, go_ref, go_all)
-        gather.start()
-        go_all[place.s] = go_ref[...]
+        gathers = [
+            SeqGather(place, wire, go_ref.at[pl.ds(r * span, span)], go_all.at[r])
+            for r in range(rows)
+        ]
+        for gather in gathers:
+            gather.start()
+        for r in range(rows):
+            go_all[r, place.s] = go_ref[r * span : (r + 1) * span, :]
         order = list(range(1, place.half)) + [0]
         works, from_twin = {}, {}
 
         def mixture_of(i):
-            group = n_bat * own
             at = pl.ds(pl.multiple_of(i * group, group), group)
             return dot(weighted_ref[at, :], down_ref[...])
+
+        todo = [(gather, m) for gather in gathers for m in range(1, place.half)]
+
+        def forward(count):
+            for _ in range(min(count, len(todo))):
+                gather, m = todo.pop(0)
+                gather.step(m)
 
         if side:
             waiting = None
@@ -727,7 +815,7 @@
                 from_twin[j] = wire.push(mix_away.at[n % 2], mix_twin.at[j], place.twin())
                 from_twin[j].wait_recv()
                 mix_twin[j] = (
-                    (total + mix_twin[j].reshape(n_bat * own, dim).astype(F32))
+                    (total + mix_twin[j].reshape(group, dim).astype(F32))
                     .astype(BF)
                     .reshape(n_bat, own, dim)
                 )
@@ -737,92 +825,91 @@
                 if waiting is not None:
                     works[waiting].start()
                 waiting = j
-                if j:
-                    gather.step(j)
+                forward(1)
             works[waiting].start()
-        else:
-            for j in range(1, place.half):
-                gather.step(j)
-        gather.finish()
-        for i in range(n_seq):
-            part = dot_t(go_all[i], wo_ref[...]).astype(BF)
-            for r in range(rows):
-                gm[r, i * span : (i + 1) * span, :] = part[r * span : (r + 1) * span, :]
-        for j in works:
-            works[j].middle()
-        dk[...] = jnp.zeros_like(dk)
-        dv[...] = jnp.zeros_like(dv)
+        forward(max(0, len(todo) - (rows - 1) * (place.half - 1)))
+        columns = lax.rsqrt(stat_ref[...] / dim + EPS).T
+        scatters = [
+            SeqScatter(place, wire, full.at[r], twin.at[r], line.at[r]) for r in range(rows)
+        ]
+        gain_sums = [[jnp.zeros((1, HEAD), F32) for _ in range(heads)] for _ in range(2)]
+        middles = [works[j] for j in works]
+
+        def attend(r, c, h):
+            keys = (c + 1) * chunk
+            now = slice(c * chunk, keys)
+            allowed = allowed_block(use_ref[r : r + 1, :keys], c * chunk, chunk, keys)
+            lanes = slice(h * HEAD, (h + 1) * HEAD)
+            query = q_ref[r, h, now, :]
+            key = k_ref[r, h, :keys, :]
+            scores = jnp.where(allowed, dot_t(query, key) * scale, NEGATIVE)
+            raised = jnp.exp(scores - jnp.max(scores, axis=-1, keepdims=True))
+            probs = raised / jnp.sum(raised, axis=-1, keepdims=True)
+            low = probs.astype(BF)
+            grad_mix = gm[now, lanes]
+            grad_probs = dot_t(grad_mix, v_ref[r, h, :keys, :])
+            row_dot = jnp.sum(low.astype(F32) * grad_probs, axis=-1, keepdims=True)
+            grad_scores = (probs * (grad_probs - row_dot)).astype(BF)
+            dq[now, lanes] = scale * dot(grad_scores, key)
+            dk[:keys, lanes] += scale * t_dot(grad_scores, query)
+            dv[:keys, lanes] += t_dot(low, grad_mix)
+
         for r in range(rows):
-            for c in range(length // chunk):
-                keys = (c + 1) * chunk
-                now = slice(c * chunk, keys)
-                allowed = allowed_block(use_ref[r : r + 1, :keys], c * chunk, chunk, keys)
-                for h in range(heads):
-                    lanes = slice(h * HEAD, (h + 1) * HEAD)
-                    query = q_ref[r, h, now, :]
-                    key = k_ref[r, h, :keys, :]
-                    scores = jnp.where(allowed, dot_t(query, key) * scale, NEGATIVE)
-                    raised = jnp.exp(scores - jnp.max(scores, axis=-1, keepdims=True))
-                    probs = raised / jnp.sum(raised, axis=-1, keepdims=True)
-                    low = probs.astype(BF)
-                    grad_mix = gm[r, now, lanes]
-                    grad_probs = dot_t(grad_mix, v_ref[r, h, :keys, :])
-                    row_dot = jnp.sum(low.astype(F32) * grad_probs, axis=-1, keepdims=True)
-                    grad_scores = (probs * (grad_probs - row_dot)).astype(BF)
-                    dq[r, now, lanes] = scale * dot(grad_scores, key)
-                    dk[r, :keys, lanes] += scale * t_dot(grad_scores, query)
-                    dv[r, :keys, lanes] += t_dot(low, grad_mix)
-        columns = lax.rsqrt(stat_ref[...] / dim + EPS).T
-        for which, g_ref, grads in ((0, gq_ref, dq), (1, gk_ref, dk)):
-            sums = [jnp.zeros((1, HEAD), F32) for _ in range(heads)]
-            for i in range(n_seq):
-                at_pos = slice(i * span, (i + 1) * span)
-                products = []
-                for r in range(rows):
-                    at = slice(i * own + r * span, i * own + (r + 1) * span)
-                    factor = columns[
-                        r * span : (r + 1) * span, which * n_seq + i : which * n_seq + i + 1
-                    ]
-                    parts = []
+            gathers[r].finish()
+            gm[...] = dot_t(go_all[r].reshape(length, dim), wo_ref[...]).astype(BF)
+            if r:
+                scatters[r - 1].pass_on()
+            dk[...] = jnp.zeros_like(dk)
+            dv[...] = jnp.zeros_like(dv)
+            for h in range(heads):
+                for c in range(length // chunk):
+                    attend(r, c, h)
+                    forward(1)
+                    if middles:
+                        middles.pop(0).middle()
+            if r == 0:
+                forward(len(todo))
+                while middles:
+                    middles.pop(0).middle()
+            for which, g_ref, grads in ((0, gq_ref, dq), (1, gk_ref, dk)):
+                for c in range(steps):
+                    inside = slice(c * STEP, (c + 1) * STEP)
+                    at = slice(r * length + c * STEP, r * length + (c + 1) * STEP)
+                    row = (r * 2 + which) * steps + c
+                    factor = columns[:, row : row + 1]
+                    products = None
                     for h in range(heads):
                         lanes = slice(h * HEAD, (h + 1) * HEAD)
                         flat = qkv_ref[at, which * wide + h * HEAD : which * wide + (h + 1) * HEAD]
                         flat = flat * factor
-                        back = turn(
-                            grads[r, at_pos, lanes], cos_ref[at_pos, :], -sin_ref[at_pos, :]
+                        back = turn(grads[inside, lanes], cos_ref[inside, :], -sin_ref[inside, :])
+                        gain_sums[which][h] = gain_sums[which][h] + jnp.sum(
+                            back * flat, axis=0, keepdims=True
                         )
-                        sums[h] = sums[h] + jnp.sum(back * flat, axis=0, keepdims=True)
                         weighted = back * g_ref[0:1, lanes]
-                        grads[r, at_pos, lanes] = weighted
-                        parts.append(weighted * flat)
-                    products.append(sum(parts))
-                local[which * n_seq + i : which * n_seq + i + 1, :] = lane_sums(
-                    jnp.concatenate(products, axis=0)
-                )
+                        grads[inside, lanes] = weighted
+                        product = weighted * flat
+                        products = product if products is None else products + product
+                    row = which * steps + c
+                    local[r, row : row + 1, :] = lane_sums(products)
+            exchange = Exchange(place, wire, local.at[r], got.at[r])
+            dqkv[r, :, 2 * wide :] = dv[...].astype(BF)
+            means = (exchange.total() / dim).T
+            for which, grads in ((0, dq), (1, dk)):
+                lanes = slice(which * wide, (which + 1) * wide)
+                for c in range(steps):
+                    inside = slice(c * STEP, (c + 1) * STEP)
+                    at = slice(r * length + c * STEP, r * length + (c + 1) * STEP)
+                    row = (r * 2 + which) * steps + c
+                    factor = columns[:, row : row + 1]
+                    mean = means[:, which * steps + c : which * steps + c + 1]
+                    flat = qkv_ref[at, lanes] * factor
+                    dqkv[r, inside, lanes] = (factor * (grads[inside, :] - flat * mean)).astype(BF)
+            full[r] = dot_t(dqkv[r], w_ref[...]).astype(BF).reshape(n_seq, span, dim)
+            scatters[r].start()
+        for which in range(2):
             for h in range(heads):
-                gain_ref[which : which + 1, h * HEAD : (h + 1) * HEAD] = sums[h]
-        for i in range(n_seq):
-            for r in range(rows):
-                at = slice(i * own + r * span, i * own + (r + 1) * span)
-                dqkv[at, 2 * wide :] = dv[r, i * span : (i + 1) * span, :].astype(BF)
-        means = (exchange_rows(place, wire, local, got) / dim).T
-        for which, grads in ((0, dq), (1, dk)):
-            for i in range(n_seq):
-                at_pos = slice(i * span, (i + 1) * span)
-                column = which * n_seq + i
-                for r in range(rows):
-                    at = slice(i * own + r * span, i * own + (r + 1) * span)
-                    inside = slice(r * span, (r + 1) * span)
-                    factor = columns[inside, column : column + 1]
-                    mean = means[inside, column : column + 1]
-                    lanes = slice(which * wide, (which + 1) * wide)
-                    flat = qkv_ref[at, lanes] * factor
-                    dqkv[at, lanes] = (factor * (grads[r, at_pos, :] - flat * mean)).astype(BF)
-        scatter = SeqScatter(place, wire, away, mine, twin, line)
-
-        def project(i):
-            rows_at = pl.ds(pl.multiple_of(i * own, own), own)
-            return dot_t(dqkv[rows_at, :], w_ref[...])
+                gain_ref[which : which + 1, h * HEAD : (h + 1) * HEAD] = gain_sums[which][h]
 
         def hidden_load(part):
             return pltpu.make_async_copy(
@@ -830,26 +917,27 @@
             )
 
         hidden_load(0).start()
-        scatter.run(project, out_ref)
+        scatters[-1].pass_on()
         for part in range(dim // 256):
             at = slice(part * 256, (part + 1) * 256)
             if part + 1 < dim // 256:
                 hidden_load(part + 1).start()
             hidden_load(part).wait()
-            gw_ref[at, :] = t_dot(hid_buf[part % 2], dqkv[...]).astype(BF)
-            total = t_dot(mix_ref[0:own, :], go_all[0, :, at])
-            for i in range(1, n_seq):
-                total = total + t_dot(mix_ref[i * own : (i + 1) * own, :], go_all[i, :, at])
+            gw_ref[at, :] = t_dot(hid_buf[part % 2], dqkv[...].reshape(col, three)).astype(BF)
+            total = t_dot(mix_ref[0], go_all[0, :, :, at].reshape(length, 256))
+            for r in range(1, rows):
+                total = total + t_dot(mix_ref[r], go_all[r, :, :, at].reshape(length, 256))
             gwo_ref[:, at] = total.astype(BF)
         for j in works:
             works[j].finish()
             mixture_ref[j] = mix_twin[j, place.b]
-        scatter.finish(out_ref)
+        for r in range(rows):
+            scatters[r].finish(out_ref, slice(r * span, (r + 1) * span))
         wire.drain()
 
     vmem = pl.BlockSpec(memory_space=pltpu.VMEM)
-    block = jax.ShapeDtypeStruct((own, dim), BF)
-    stat_shape = (2 * n_seq, own)
+    block = jax.ShapeDtypeStruct((span, dim), BF)
+    stat_shape = (2 * steps, STEP)
     side_out, side_scratch = [], []
     if side:
         half = n_seq // 2
@@ -866,24 +954,24 @@
             jax.ShapeDtypeStruct((wide, dim), BF),
             jax.ShapeDtypeStruct((dim, three), BF),
             jax.ShapeDtypeStruct((2, wide), F32),
-            block,
+            jax.ShapeDtypeStruct((own, dim), BF),
         ]
         + side_out,
         [
-            pltpu.VMEM((n_seq, own, dim), BF),
-            pltpu.VMEM((rows, length, wide), BF),
-            pltpu.VMEM((rows, length, wide), F32),
-            pltpu.VMEM((rows, length, wide), F32),
-            pltpu.VMEM((rows, length, wide), F32),
-            pltpu.VMEM((col, three), BF),
-            pltpu.VMEM(stat_shape, F32),
-            pltpu.VMEM((n_seq - 1,) + stat_shape, F32),
+            pltpu.VMEM((rows, n_seq, span, dim), BF),
+            pltpu.VMEM((length, wide), BF),
+            pltpu.VMEM((length, wide), F32),
+            pltpu.VMEM((length, wide), F32),
+            pltpu.VMEM((length, wide), F32),
+            pltpu.VMEM((rows, length, three), BF),
+            pltpu.VMEM((rows,) + stat_shape, F32),
+            pltpu.VMEM((rows, n_seq - 1) + stat_shape, F32),
             pltpu.VMEM((2, col, 256), BF),
             pltpu.SemaphoreType.DMA((2,)),
         ]
-        + SeqScatter.scratch(n_seq, block)
+        + SeqScatter.scratch(rows, n_seq, block)
         + side_scratch,
-        4 * n_seq + (3 * n_seq if side else 0),
+        5 * rows * n_seq + (3 * n_seq if side else 0),
         6,
         "attend_backward",
         [vmem] * 7 + [ANY] + [vmem] * (7 + len(side or ())),
@@ -943,24 +1031,28 @@
         add_into(self.group.at[self.place.b], self.full.at[0], self.full.at[1])
 
 
-def load_first(weights, w_out, mine, flags, small, dy_own, n_seq, n_bat):
+def load_first(weights, w_out, mine, flags, small, dy_own, rows, n_seq, n_bat):
     shard, dim = weights[0].shape
     wide = dim // n_seq
     own = mine.shape[0]
-    slots = 12 * n_seq + n_seq * n_bat
+    span = own // rows
+    slots = 15 * n_seq + n_seq * n_bat
 
     def kernel(*refs):
         parts = refs[:3]
         wo_ref, x_ref, flag_ref, small_ref, dy_ref = refs[3:8]
         w_ref, wo_all, x_col, flag_col, small_all, dy_all = refs[8:14]
         buffers = refs[14:20]
-        own_sems, cut_sems, send_sems, recv_sems = refs[20:]
+        own_sems, cut_sems, x_sems, send_sems, recv_sems = refs[20:]
         place = Place(n_seq, n_bat)
         place.greet(all_seq=True)
         wire = Wire(send_sems, recv_sems)
         small_work = FullGather(place, wire, small_ref, small_all)
         flag_work = SeqGather(place, wire, flag_ref, flag_col)
-        x_work = SeqGather(place, wire, x_ref, x_col)
+        x_works = [
+            SeqGather(place, wire, x_ref.at[pl.ds(r * span, span)], x_col.at[r])
+            for r in range(rows)
+        ]
         small_work.start()
         flag_work.start()
 
@@ -987,11 +1079,10 @@
                 )
         wo_work = Across(place, wire, wo_ref, lambda i: wo_all.at[i])
         wo_work.start()
-        x_work.start()
-        line = [
-            wire.push(dy_ref, dy_all.at[place.s, place.b], place.seq_peer(2 * j))
-            for j in range(1, place.half)
-        ]
+        for work in x_works:
+            work.start()
+        dy_line = Line(place, wire, dy_ref, lambda i: dy_all.at[place.chip(i), place.b])
+        dy_line.start()
         for copy in own_cuts:
             copy.wait()
         spreads = []
@@ -1004,12 +1095,21 @@
         spread(buffers[0], place.s)
         own_w = pltpu.make_async_copy(buffers[0], w_ref.at[place.s, place.b], own_sems.at[0])
         own_w.start()
-        copies = [own_w] + [
+        copies = [own_w]
+        fetched = pltpu.make_async_copy(x_ref, buffers[5], own_sems.at[5])
+        fetched.start()
+        fetched.wait()
+        for r in range(rows):
+            copy = pltpu.make_async_copy(
+                buffers[5].at[pl.ds(r * span, span)], x_col.at[r, place.s], x_sems.at[r]
+            )
+            copy.start()
+            copies.append(copy)
+        copies += [
             keep_own(src, dst, buffers[i + 1], own_sems.at[i + 1])
             for i, (src, dst) in enumerate(
                 (
                     (wo_ref, wo_all.at[place.b]),
-                    (x_ref, x_col.at[place.s]),
                     (flag_ref, flag_col.at[place.s]),
                     (small_ref, small_all.at[place.s, place.b]),
                     (dy_ref, dy_all.at[place.s, place.b]),
@@ -1025,31 +1125,41 @@
             spread(w_ref.at[place.seq_at(-k), place.b], place.seq_at(-k))
         for j in range(place.half):
             small_work.collect(j)
+        todo = [(work, m) for work in x_works for m in range(1, place.half)]
+
+        def forward(count):
+            for _ in range(min(count, len(todo))):
+                work, m = todo.pop(0)
+                work.step(m)
+
+        forward(1)
         wo_work.relay()
         for work in spreads:
             work.relay()
+            forward(1)
+        forward(len(todo))
         for j in range(1, place.half):
-            x_work.step(j)
+            dy_line.step(j)
         wo_work.finish()
         for work in spreads:
             work.finish()
-        for work in (small_work, flag_work, x_work):
+        for work in [small_work, flag_work] + x_works:
             work.finish()
-        for copy in line:
-            copy.wait_recv()
         for copy in copies:
             copy.wait()
         wire.drain()
 
     every = (n_seq, n_bat)
     one = jax.ShapeDtypeStruct((shard, 3 * wide), BF)
-    blocks = (one, w_out, mine, flags, small, dy_own)
-    leads = (every, (n_bat,), (n_seq,), (n_seq,), every, every)
+    x_one = jax.ShapeDtypeStruct((span, dim), BF)
+    blocks = (one, w_out, x_one, flags, small, dy_own)
+    leads = (every, (n_bat,), (rows, n_seq), (n_seq,), every, every)
+    held = (one, w_out, flags, small, dy_own, mine)
     return comm_call(
         kernel,
         [shape_of(lead, block) for lead, block in zip(leads, blocks)],
-        [pltpu.VMEM(block.shape, block.dtype) for block in blocks]
-        + [pltpu.SemaphoreType.DMA((6,)), pltpu.SemaphoreType.DMA((3,))],
+        [pltpu.VMEM(block.shape, block.dtype) for block in held]
+        + [pltpu.SemaphoreType.DMA((n,)) for n in (6, 3, rows)],
         slots,
         1,
         "load_first",
@@ -1084,13 +1194,13 @@
         gate_work = FullGather(place, wire, gate_ref, gates_all)
         gate_work.start()
         gates_all[place.s, place.b] = gate_ref[...]
-        line = [
-            wire.push(x_ref, x_all.at[place.s, place.b], place.seq_peer(2 * j))
-            for j in range(1, place.half)
-        ]
+        line = Line(place, wire, x_ref, lambda i: x_all.at[place.chip(i), place.b])
+        line.start()
         works = []
+        here = [place.chip(place.origin(m)) for m in range(place.half)]
+        there = [place.chip_twin(place.origin(m)) for m in range(place.half)]
         for j in range(place.half):
-            at_seq = place.seq_at(-2 * j)
+            at_seq = here[j]
             src = x_ref if j == 0 else x_all.at[at_seq, place.b]
             works.append(
                 Across(place, wire, src, lambda i, at_seq=at_seq: x_all.at[at_seq, i])
@@ -1117,7 +1227,7 @@
         passed = []
 
         def hand_over(j):
-            at_seq = place.seq_at(-2 * j)
+            at_seq = here[j]
             works[j].finish()
             if j == 0:
                 own.wait()
@@ -1172,22 +1282,22 @@
             backs((j - 1) * per, per)
             gate_work.step(j)
             gate_work.collect(j - 1)
-            line[j - 1].wait_recv()
+            line.step(j)
             works[j].start()
             works[j - 1].relay()
         backs((half - 1) * per, per)
         gate_work.collect(half - 1)
         gate_work.finish()
         hand_over(0)
-        fetch(place.seq_at(0), 0)
+        fetch(here[0], 0)
         for j in range(half):
-            units_on(place.seq_at(-2 * j), (2 * j) % 4)
+            units_on(here[j], (2 * j) % 4)
             passed[j].wait_recv()
-            fetch(place.twin_at(-2 * j), (2 * j + 1) % 4)
+            fetch(there[j], (2 * j + 1) % 4)
             if j + 1 < half:
                 hand_over(j + 1)
-                fetch(place.seq_at(-2 * (j + 1)), (2 * j + 2) % 4)
-            units_on(place.twin_at(-2 * j), (2 * j + 1) % 4)
+                fetch(here[j + 1], (2 * j + 2) % 4)
+            units_on(there[j], (2 * j + 1) % 4)
             if j == max(0, half - 4):
                 works[half - 1].relay()
         wire.drain()
@@ -1275,11 +1385,9 @@
             return pltpu.make_async_copy(src, columns.at[n % 2], column_sems.at[n % 2])
 
         chunk_load(0).start()
-        for j in order:
+
+        def pair(j):
             part_sum = product(place.seq_at(2 * j))
-            if waiting is not None:
-                send(waiting)
-                waiting = None
             from_twin[j].wait_recv()
             twin[j] = (
                 (part_sum + twin[j].reshape(group, dim).astype(F32))
@@ -1287,63 +1395,66 @@
                 .reshape(n_bat, own, dim)
             )
             works[j] = AcrossSum(place, wire, twin.at[j], halves.at[j], full.at[j])
-            if len(works) > 1:
-                works[order[len(works) - 2]].start()
-        term_order = term_work.order()
-        for j in term_order:
-            term_work.pair(j)
-        works[order[-1]].start()
 
         arrivals = []
         done = [0]
 
-        def work_chunk():
-            n = done[0]
-            if n >= len(chunks):
-                return
-            done[0] = n + 1
-            if n + 1 < len(chunks):
-                chunk_load(n + 1).start()
-            chunk_load(n).wait()
-            kind, k = chunks[n]
-            if kind == "y":
-                down_out[:, k * 256 : (k + 1) * 256] = t_dot(weighted_ref[...], columns[n % 2])
-                return
-            value = t_dot(columns[n % 2], grad_ref[...]).astype(BF)
-            if k == 0:
-                got[place.s] = value
-            else:
-                sent[k] = value
-            if n:
-                push_chunk(chunks[n - 1][1])
-
-        def push_chunk(k):
-            if k:
-                arrivals.append(wire.push(sent.at[k], got.at[place.s], place.seq_peer(k)))
+        def work_chunks(count):
+            for n in range(done[0], min(done[0] + count, len(chunks))):
+                done[0] = n + 1
+                if n + 1 < len(chunks):
+                    chunk_load(n + 1).start()
+                chunk_load(n).wait()
+                kind, k = chunks[n]
+                if kind == "y":
+                    down_out[:, k * 256 : (k + 1) * 256] = t_dot(
+                        weighted_ref[...], columns[n % 2]
+                    )
+                else:
+                    value = t_dot(columns[n % 2], grad_ref[...]).astype(BF)
+                    if k == 0:
+                        got[place.s] = value
+                    else:
+                        sent[k] = value
+                if n and chunks[n - 1][0] == "x" and chunks[n - 1][1]:
+                    k = chunks[n - 1][1]
+                    arrivals.append(wire.push(sent.at[k], got.at[place.s], place.seq_peer(k)))
 
         def pass_on(j):
             works[j].finish()
             if j:
                 from_seq[j] = wire.push(twin.at[j, place.b], line.at[j], place.seq_peer(2 * j))
 
-        steps = []
-        for n, j in enumerate(order):
-            steps.append(("middle", j))
-            if n:
-                steps.append(("finish", order[n - 1]))
-        steps.append(("finish", order[-1]))
-        share = -(-len(chunks) // len(steps))
-        for kind, j in steps:
-            for _ in range(share):
-                work_chunk()
-            if kind == "middle":
-                works[j].middle()
-            else:
-                pass_on(j)
+        first, rest = order[:2], order[2:]
+        pair(order[0])
+        send(waiting)
+        for j in first[1:]:
+            pair(j)
+            works[first[0]].start()
+        works[first[-1]].start()
+        for j in rest:
+            pair(j)
+        term_order = term_work.order()
+        for j in term_order:
+            term_work.pair(j)
+        works[first[0]].middle()
+        work_chunks(1)
+        for j in first[1:]:
+            works[j].middle()
+        for j in rest:
+            works[j].start()
         for j in term_order:
             term_work.merge(j)
-        while done[0] < len(chunks):
-            work_chunk()
+        for j in first:
+            work_chunks(3)
+            pass_on(j)
+        for j in rest:
+            work_chunks(1)
+            works[j].middle()
+        for j in rest:
+            work_chunks(4)
+            pass_on(j)
+        work_chunks(len(chunks))
         for copy in arrivals:
             copy.wait_recv()
         for i in range(n_seq):
@@ -1501,7 +1612,7 @@
 
 def load_inputs(qkv_cut, w_out, mine, flags, small, gu_cut, dy_own, n_seq, n_bat):
     n_in = 7
-    slots = 4 * n_seq * n_bat + 3 * n_seq + 2 * n_bat
+    slots = 4 * n_seq * n_bat + 5 * n_seq + 2 * n_bat
 
     def kernel(*refs):
         cut_ref, wo_ref, x_ref, flag_ref, small_ref, gu_ref, dy_ref = refs[:n_in]
@@ -1736,7 +1847,7 @@
     )
     if fused:
         w_qkv, w_o, x_col, flag_col, small_all, dy_part = load_first(
-            (w_query, w_key, w_value), w_out, mine, flags, pack(small), dy_own, n_seq, n_bat
+            (w_query, w_key, w_value), w_out, mine, flags, pack(small), dy_own, rows, n_seq, n_bat
         )
     else:
         qkv_cut = jnp.stack([w_query, w_key, w_value]).reshape(3, shard, n_seq, wide)
@@ -1748,6 +1859,7 @@
         )
         w_gu = w_gu.reshape(dim, 2 * units)
         dy_all = dy_all.reshape(-1, dim)
+        x_col = jnp.transpose(x_col.reshape(n_seq, rows, span, dim), (1, 0, 2, 3))
     w_qkv = w_qkv.reshape(dim, 3 * wide)
     w_o = w_o.reshape(wide, dim)
     w_down = expert_down.reshape(local_experts * part, dim)
@@ -1760,16 +1872,13 @@
     usable = unpack(flag_col, (n_seq,), key_mask.shape)
     usable = jnp.transpose(usable, (1, 0, 2)).reshape(rows, length)
 
-    x_col = x_col.reshape(col, dim).astype(F32)
-    scale_x = rms_scale(x_col)
-    hidden = (x_col * scale_x * gain_attn).astype(BF)
-    qkv = dot(hidden, w_qkv)
     cos_part, sin_part = rotary_tables(jnp.arange(length, dtype=jnp.int32))
     cos_wide = jnp.concatenate([cos_part, cos_part], axis=1)
     sin_wide = jnp.concatenate([-sin_part, sin_part], axis=1)
     gain_q, gain_k = gain_q[None, :], gain_k[None, :]
-    q, k, v, mixed, stats, mixed_out, *extra = attend_forward(
-        qkv, usable, w_o, gain_q, gain_k, cos_wide, sin_wide, n_seq, n_bat, span,
+    hidden, qkv, q, k, v, mixed, stats, mixed_out, *extra = attend_forward(
+        x_col.reshape(col, dim), w_qkv, gain_attn[None, :], usable, w_o, gain_q, gain_k,
+        cos_wide, sin_wide, n_seq, n_bat, rows,
         (dy_part, expert_gate, expert_up) if fused else None,
     )
     x_own = mine.astype(F32)

time: 750 us -> 679 us (0.905)
  Pallas kernels: 675 us -> 617 us
  other arithmetic: 27 us -> 19 us
    pallas_call x1, Pallas kernels: 148 us -> 117 us  [attend_backward(): comm_call(kernel, [jax.ShapeDtypeStruct((wide, dim), BF), jax.ShapeDtypeS...]
    pallas_call x1, Pallas kernels: 114 us -> 93 us  [load_first(): comm_call(kernel, [shape_of(lead, block) for lead, block in zip(leads, bl...]
    pallas_call x1, Pallas kernels: 143 us -> 130 us  [experts_backward(): comm_call(kernel, [jax.ShapeDtypeStruct((own, dim), F32), term, expert, e...]
    pallas_call x1, Pallas kernels: 103 us -> 111 us  [attend_forward(): comm_call(kernel, outs + side_out, [pltpu.VMEM(stats.shape, F32), pltpu.V...]
where the time goes in v5:
time: 679 us; the launch traced here: 670 us
  Pallas kernels  617 us (91%)
  local copies, waits for them, and re-layouts  27.5 us (4%)
  other arithmetic  19 us (3%)
    pallas_call x1, Pallas kernels, experts_backward(): comm_call(kernel, [jax.ShapeDtypeStruct((own, dim), F32), term, expert, e...  130 us
    pallas_call x1, Pallas kernels, attend_backward(): comm_call(kernel, [jax.ShapeDtypeStruct((wide, dim), BF), jax.ShapeDtypeS...  117 us
    pallas_call x1, Pallas kernels, attend_forward(): comm_call(kernel, outs + side_out, [pltpu.VMEM(stats.shape, F32), pltpu.V...  111 us
    pallas_call x1, Pallas kernels, load_first(): comm_call(kernel, [shape_of(lead, block) for lead, block in zip(leads, bl...  93 us
    pallas_call x1, Pallas kernels, experts_forward(): comm_call(kernel, [shape_of((n_seq, n_bat), normed), jax.ShapeDtypeStruct...  90.6 us
    pallas_call x1, Pallas kernels, store_last(): comm_call(kernel, [matrix] * 4 + [small_one, jax.ShapeDtypeStruct(mixture...  75.3 us

profile of v5, /device:TPU:9, one launch (start us, length us, event | category | flops | bytes accessed | tf_op | source)
XLA Modules:
  0.0 669.6 jit_solution(12646212198851275756)
XLA Ops:
  0.7 0.8 compare_and_fusion
  1.5 0.6 convert_bitcast_fusion.refs_5_
  2.1 1.4 concatenate.23
  4.2 93.0 %load_first.1 = (bf16[8,4,64,768]{3,2,1,0:T(8,128)(2,1)}, bf16[4,64,2048]{2,1,0:T(8,128)(2,1)}, bf16[2,8,64,2048]{3,2,1,0:T(8,128)(2,1)}, f32[8,8,128]{2,1,0:T(8...) custom-call(bf16[64,2048]{1,0:T(8,128)(2,1)} %refs_0_.1, bf16[64,2048]{1,0:T(8,128)(2,1)} %refs_1_.1, ...), custom_call_target="tpu_custom_call" | custom-call | tf_op jit(solution)/shard_map/load_first/pallas_call | solution.py:1158
  97.2 1.0 reshape.201
  98.3 0.7 fusion.19
  99.1 0.6 dynamic_slice.6
  99.8 0.6 dynamic_slice.7
  100.5 0.7 slice.60.refs_2_
  101.2 1.0 fusion.9
  102.2 1.0 pad_maximum_fusion
  103.3 0.7 reshape.205.refs_3_.refs_8_
  104.0 110.9 %attend_forward.1 = (bf16[1024,2048]{1,0:T(8,128)(2,1)}, f32[1024,768]{1,0:T(8,128)}, bf16[2,2,512,128]{3,2,1,0:T(8,128)(2,1)}, bf16[2,2,512,128]{3,2,1,0:T(8,12...) custom-call(bf16[1024,2048]{1,0:T(8,128)(2,1)} %bitcast.106, ...), custom_call_target="tpu_custom_call", output_to_operand_aliasing={{8}: (9, {})} | custom-call | tf_op jit(solution)/shard_map/attend_forward/pallas_call | solution.py:737
  214.9 1.5 multiply_reduce_fusion.3
  216.4 0.7 copy.61
  217.2 1.4 multiply_convert_fusion.refs_0_
  218.6 1.1 slice.93
  221.1 0.6 select_bitcast_fusion.refs_1_
  221.7 90.6 %experts_forward.1 = (bf16[8,4,128,2048]{3,2,1,0:T(8,128)(2,1)}, bf16[4096,256]{1,0:T(8,128)(2,1)}, bf16[4096,512]{1,0:T(8,128)(2,1)}, f32[8,4,8,128]{3,2,1,0:T(8,128)}) custom-call(bf16[128,2048]{1,0:T(8,128)(2,1)} %copy-done.3, f32[8,128]{1,0:T(8,128)} %select_bitcast_fusion.refs_1_, bf16[8,4,128,2048]{3,2,1,0:T(8,128)(2,1)} %get-tuple-element.57.refs_2_, ...), custom_call_target="tpu_custom_call" | custom-call | tf_op jit(solution)/shard_map/experts_forward/pallas_call | solution.py:1306
  312.3 130.1 %experts_backward.1 = (f32[128,2048]{1,0:T(8,128)}, f32[8,128]{1,0:T(8,128)}, f32[2,256,1024]{2,1,0:T(8,128)}, f32[2,256,1024]{2,1,0:T(8,128)}, f32[256,2048]{1,0:T(8,128)}) custom-call(bf16[4096,512]{1,0:T(8,128)(2,1)} %get-tuple-element.59.refs_0_, bf16[4096,256]{1,0:T(8,128)(2,1)} %get-tuple-element.60.refs_1_.refs_15_, bf16[2048,512]{1,0:T(8,128)(2,1)} %bitcast.100, ...), custom_call_target="tpu_custom_call" | custom-call | tf_op jit(solution)/shard_map/experts_backward/pallas_call | solution.py:1478
  442.5 0.8 multiply_reduce_fusion.4
  443.3 1.4 fusion.13
  444.8 0.7 copy.64
  445.6 3.3 multiply_reduce_fusion
  448.9 1.3 fusion.18.refs_0_
  450.2 116.8 %attend_backward.1 = (bf16[256,2048]{1,0:T(8,128)(2,1)}, bf16[2048,768]{1,0:T(8,128)(2,1)}, f32[2,256]{1,0:T(2,128)}, bf16[128,2048]{1,0:T(8,128)(2,1)}, bf16[4,128,2048]{2,1,0:T(8,128)(2,1)}) custom-call(bf16[128,2048]{1,0:T(8,128)(2,1)} %fusion.18.refs_0_, bf16[2,2,512,128]{3,2,1,0:T(8,128)(2,1)} %get-tuple-element.65.refs_1_, ...), custom_call_target="tpu_custom_call" | custom-call | tf_op jit(solution)/shard_map/attend_backward/pallas_call | solution.py:951
  567.0 0.7 slice_dynamic-update-slice_fusion.1
  568.2 0.7 reduce.7
  569.0 0.7 slice_dynamic-update-slice_fusion
  569.7 0.7 reduce.8
  570.4 0.8 mul.176
  571.2 1.2 multiply_reduce_fusion.1
  572.6 2.1 fusion.6
  574.8 0.8 concatenate.30
  575.6 1.0 concatenate.31
  576.8 0.7 copy.71.refs_2_
  577.5 75.3 %store_last.1 = (f32[64,2048]{1,0:T(8,128)}, f32[64,2048]{1,0:T(8,128)}, f32[64,2048]{1,0:T(8,128)}, f32[64,2048]{1,0:T(8,128)}, f32[8,128]{1,0:T(8,128)}, /*index=5*/f32[128,2048]{1,0:T(8,128)}) custom-call(bf16[8,4,64,768]{3,2,1,0:T(8,128)(2,1)} %bitcast.107, bf16[4,64,2048]{2,1,0:T(8,128)(2,1)} %bitcast.109, f32[8,4,8,128]{3,2,1,0:T(8,128)} %copy.71.refs_2_, ...), custom_call_target="tpu_custom_call" | custom-call | tf_op jit(solution)/shard_map/store_last/pallas_call | solution.py:1590
  652.8 0.7 broadcast_multiply_fusion
  653.5 4.0 fusion.5
  658.1 0.7 slice.74
  658.8 1.9 copy.89
  660.7 1.9 copy.90
  662.5 0.8 copy.91
  663.3 0.8 copy.92
  664.1 1.3 copy.93
  665.5 1.3 copy.94
  666.8 1.0 copy-done.5
  667.8 1.3 copy.95
  (100 shorter events, 4.5 us)
Async XLA Ops:
  97.2 6.0 copy-start.17
  98.3 4.9 copy-start.8
  100.5 2.7 copy-start.15
  214.9 5.7 copy-start.24
  216.4 3.3 copy-start.22
  217.2 2.5 copy-start.12
  218.6 1.3 copy-start.3
  219.9 0.6 copy-start.11
  220.5 0.6 copy-start.14
  220.5 1.2 copy-start.19
  220.6 1.2 copy-start.20
  221.1 0.6 copy-start.18
  442.4 6.4 copy-start
  442.4 6.4 copy-start.1
  442.4 6.4 copy-start.4
  442.4 6.4 copy-start.13
  442.5 6.4 copy-start.23
  448.8 1.4 copy-start.2
  448.8 1.4 copy-start.26
  571.2 4.3 copy-start.16
  572.6 2.1 copy-start.25
  652.8 4.7 copy-start.21
  653.5 9.1 %copy-start.10 = (f32[64,2048]{1,0:T(8,128)S(1)}, f32[64,2048]{1,0:T(8,128)}, u32[]{:S(2)}) copy-start(f32[64,2048]{1,0:T(8,128)} %get-tuple-element.130) | copy-start | bytes 1572868
  653.5 9.9 %copy-start.9 = (f32[64,2048]{1,0:T(8,128)S(1)}, f32[64,2048]{1,0:T(8,128)}, u32[]{:S(2)}) copy-start(f32[64,2048]{1,0:T(8,128)} %get-tuple-element.131) | copy-start | bytes 1572868
  657.5 6.6 copy-start.7
  662.5 2.9 copy-start.6
  665.5 2.3 copy-start.5

commit v6 on v5

--- a/solution.py
+++ b/solution.py
@@ -340,10 +340,11 @@
 
 
 class FullScatter:
-    def __init__(self, place, wire, parts, out, mine, twin, across, line, sems, local):
-        self.place, self.wire, self.parts, self.out = place, wire, parts, out
+    def __init__(self, place, wire, parts, out, mine, twin, across, line, sems, pick=None):
+        self.place, self.wire, self.out = place, wire, out
         self.mine, self.twin, self.across, self.line = mine, twin, across, line
-        self.sems, self.local = sems, local
+        self.sems = sems
+        self.pick = pick or (lambda i, j: parts.at[i, j])
 
     @staticmethod
     def scratch(n_seq, n_bat, block):
@@ -366,10 +367,10 @@
             for k in list(range(1, place.n_bat)) + [0]:
                 to_bat = place.bat_at(k)
                 self.from_twin[j, k] = self.wire.push(
-                    self.parts.at[place.twin_at(2 * j), to_bat], self.twin.at[j, k], place.twin()
+                    self.pick(place.twin_at(2 * j), to_bat), self.twin.at[j, k], place.twin()
                 )
                 load = pltpu.make_async_copy(
-                    self.parts.at[place.seq_at(2 * j), to_bat],
+                    self.pick(place.seq_at(2 * j), to_bat),
                     self.mine.at[j, k],
                     self.sems.at[j, k],
                 )
@@ -416,7 +417,7 @@
         place.greet()
         wire = Wire(send_sems, recv_sems)
         works = [
-            FullScatter(place, wire, ins[i], outs[i], *rest[5 * i : 5 * i + 5], None)
+            FullScatter(place, wire, ins[i], outs[i], *rest[5 * i : 5 * i + 5])
             for i in range(count)
         ]
         for work in works:
@@ -511,6 +512,14 @@
             if j:
                 self.from_seq[j] = self.wire.push(block, self.line.at[j], place.seq_peer(2 * j))
 
+    def total(self):
+        for copy in self.from_seq.values():
+            copy.wait_recv()
+        total = self.full[self.place.s].astype(F32)
+        for j in range(1, self.place.half):
+            total = total + self.line[j].astype(F32)
+        return total
+
     def finish(self, out, at):
         for copy in self.from_seq.values():
             copy.wait_recv()
@@ -575,59 +584,36 @@
     def kernel(*refs):
         (x_ref, w_ref, ga_ref, use_ref, wo_ref, gq_ref, gk_ref, cos_ref, sin_ref) = refs[:9]
         refs = refs[9:]
-        if side:
-            _, gate_ref, up_ref = refs[:3]
-            refs = refs[3:]
+        if side is not None:
+            dy_ref, own_ref, gm_ref, router_ref, chosen_ref = refs[:5]
+            refs = refs[5:]
         hid_ref, qkv_ref, q_ref, k_ref, v_ref, mix_ref, stat_ref, out_ref = refs[:8]
         refs = refs[8:]
-        if side:
-            dy_all, gu_all = refs[:2]
-            gu_own, gu_sems = refs[-4:-2]
-            refs = refs[2:-4] + refs[-2:]
+        if side is not None:
+            dy_all, res_ref, normed_ref, probs_ref, gates_ref = refs[:5]
+            dy_keep, dy_sem = refs[-4:-2]
+            refs = refs[5:-4] + refs[-2:]
         local, got, full, twin, line, send_sems, recv_sems = refs
         place = Place(n_seq, n_bat)
-        place.greet(all_seq=True, batch=bool(side))
+        place.greet(all_seq=True, batch=side is not None)
         wire = Wire(send_sems, recv_sems)
-        dy_works, gu_copies, gu_here = [], [], []
-        if side:
-            for j in range(place.half):
-                at_seq = place.seq_at(-2 * j)
-                dy_works.append(
-                    Across(
-                        place,
-                        wire,
-                        dy_all.at[at_seq, place.b],
-                        lambda i, at_seq=at_seq: dy_all.at[at_seq, i],
-                    )
-                )
-                dy_works[-1].start()
-
-        def send_experts(steps_of):
-            if not side:
+        dy_works, dy_here = [], [place.chip(place.origin(m)) for m in range(place.half)]
+
+        def dy_spread(m):
+            if side is None:
                 return
-            count, _, hidden = gate_ref.shape
-            part = hidden // n_seq
-            for k in steps_of:
-                lanes = pl.ds(pl.multiple_of(place.seq_at(k) * part, part), part)
-                for m, ref in enumerate((gate_ref, up_ref)):
-                    for e in range(count):
-                        to = pl.ds((m * count + e) * part, part)
-                        if k:
-                            gu_copies.append(
-                                wire.push(
-                                    ref.at[e, :, lanes],
-                                    gu_all.at[place.s, :, to],
-                                    place.seq_peer(k),
-                                )
-                            )
-                        else:
-                            copy = pltpu.make_async_copy(
-                                ref.at[e, :, lanes], gu_own.at[:, to], gu_sems.at[m * count + e]
-                            )
-                            copy.start()
-                            gu_here.append(copy)
-
-        send_experts([0, 2, 3])
+            if m:
+                dy_line.step(m)
+            src = dy_all.at[dy_here[m], place.b] if m else dy_ref
+            work = Across(place, wire, src, lambda i: dy_all.at[dy_here[m], i])
+            work.start()
+            dy_works.append(work)
+
+        if side is not None:
+            dy_line = Line(place, wire, dy_ref, lambda i: dy_all.at[place.chip(i), place.b])
+            dy_line.start()
+            dy_spread(0)
+            dy_own = keep_own(dy_ref, dy_all.at[place.s, place.b], dy_keep, dy_sem)
         for first in range(0, col, chunk):
             at = slice(first, first + chunk)
             x = x_ref[at, :].astype(F32)
@@ -646,7 +632,7 @@
                 lanes = slice(2 * wide + h * HEAD, 2 * wide + (h + 1) * HEAD)
                 v_ref[r, h] = qkv_ref[r * length : (r + 1) * length, lanes].astype(BF)
         exchange = Exchange(place, wire, local, got)
-        send_experts([k for k in range(1, n_seq) if k not in (2, 3)])
+        dy_spread(1)
         total = exchange.total()
         stat_ref[...] = total
         columns = lax.rsqrt(total / dim + EPS).T
@@ -680,48 +666,59 @@
                     mix_ref[r, c * chunk : keys, h * HEAD : (h + 1) * HEAD] = mixed
                 if r and c == 0:
                     scatters[r - 1].pass_on()
+                if r == 0 and c == 0 and side is not None:
+                    dy_works[0].relay()
+                    dy_spread(2)
             full[r] = dot(mix_ref[r], wo_ref[...]).astype(BF).reshape(n_seq, span, dim)
-            if side and r == 0:
-                for work in dy_works:
-                    work.relay()
             scatters[r].start()
-        if side:
-            for copy in gu_here:
-                copy.wait()
-            gu_store = pltpu.make_async_copy(gu_own, gu_all.at[place.s], gu_sems.at[0])
-            gu_store.start()
+            if r == 0 and side is not None:
+                dy_works[1].relay()
+                for m in range(3, place.half):
+                    dy_spread(m)
         scatters[-1].pass_on()
+        for work in dy_works[2:]:
+            work.relay()
         passed = []
-        for j, work in enumerate(dy_works):
+        if side is not None:
+            dy_own.wait()
+        for m, work in enumerate(dy_works):
             work.finish()
-            group = dy_all.at[place.seq_at(-2 * j)]
+            group = dy_all.at[dy_here[m]]
             passed.append(wire.push(group, group, place.twin()))
         for r in range(rows):
-            scatters[r].finish(out_ref, slice(r * span, (r + 1) * span))
-        if side:
-            for copy in passed + gu_copies:
-                copy.wait_recv()
-            gu_store.wait()
+            at = slice(r * span, (r + 1) * span)
+            if side is None:
+                scatters[r].finish(out_ref, at)
+                continue
+            residual = own_ref[at, :].astype(F32) + scatters[r].total()
+            res_ref[at, :] = residual
+            normed_ref[at, :] = (residual * rms_scale(residual) * gm_ref[...]).astype(BF)
+        if side is not None:
+            out_ref[...] = jnp.zeros_like(out_ref)
+            logits = dot_t(router_ref[...].astype(BF), normed_ref[...])
+            raised = jnp.exp(logits - jnp.max(logits, axis=0, keepdims=True))
+            probs = raised / jnp.sum(raised, axis=0, keepdims=True)
+            probs_ref[...] = probs
+            gates_ref[...] = probs * chosen_ref[...]
+        for copy in passed:
+            copy.wait_recv()
         wire.drain()
 
     vmem = pl.BlockSpec(memory_space=pltpu.VMEM)
-    side_in, side_out, side_scratch, aliases = [], [], [], {}
+    side_in, side_out, side_scratch = [], [], []
     slots = (1 + rows) * n_seq
-    if side:
-        dy_part, gate, up = side
-        count, depth, hidden = gate.shape
-        lanes = 2 * count * (hidden // n_seq)
-        side_in = [ANY] * 3
+    if side is not None:
+        dy, _, _, router, _ = side
+        side_in = list(side)
         side_out = [
-            jax.ShapeDtypeStruct(dy_part.shape, dy_part.dtype),
-            jax.ShapeDtypeStruct((n_seq, depth, lanes), gate.dtype),
-        ]
-        side_scratch = [
-            pltpu.VMEM((depth, lanes), gate.dtype),
-            pltpu.SemaphoreType.DMA((2 * count,)),
-        ]
-        aliases = {9: 8}
-        slots += 3 * n_seq + 2 * count * n_seq
+            shape_of((n_seq, n_bat), dy),
+            jax.ShapeDtypeStruct((own, dim), F32),
+            jax.ShapeDtypeStruct((own, dim), BF),
+            jax.ShapeDtypeStruct((router.shape[0], own), F32),
+            jax.ShapeDtypeStruct((router.shape[0], own), F32),
+        ]
+        side_scratch = [pltpu.VMEM(dy.shape, dy.dtype), pltpu.SemaphoreType.DMA]
+        slots += 4 * n_seq
     head_block = jax.ShapeDtypeStruct((rows, heads, length, HEAD), BF)
     stats = jax.ShapeDtypeStruct((2 * rows * steps, STEP), F32)
     outs = [
@@ -732,7 +729,7 @@
         head_block,
         jax.ShapeDtypeStruct((rows, length, wide), BF),
         stats,
-        jax.ShapeDtypeStruct((own, dim), BF),
+        jax.ShapeDtypeStruct((own, dim) if side is None else (8, HEAD), BF),
     ]
     return comm_call(
         kernel,
@@ -743,10 +740,9 @@
         slots,
         2,
         "attend_forward",
-        [vmem] * 9 + side_in,
-        [vmem] * 8 + [ANY] * len(side_out),
-        aliases,
-    )(x_col, w_qkv, gain_attn, usable, w_o, gain_q, gain_k, cos_wide, sin_wide, *(side or ()))
+        [vmem] * 9 + ([ANY] + [vmem] * 4 if side_in else []),
+        [vmem] * 8 + ([ANY] + [vmem] * 4 if side_in else []),
+    )(x_col, w_qkv, gain_attn, usable, w_o, gain_q, gain_k, cos_wide, sin_wide, *side_in)
 
 
 def attend_backward(
@@ -768,14 +764,14 @@
          w_ref, gq_ref, gk_ref, cos_ref, sin_ref) = refs[:15]
         refs = refs[15:]
         if side:
-            weighted_ref, down_ref = refs[:2]
-            refs = refs[2:]
+            weighted_ref, down_ref, own_ref, res_ref, ga_ref, small_in = refs[:6]
+            refs = refs[6:]
         gwo_ref, gw_ref, gain_ref, out_ref = refs[:4]
         refs = refs[4:]
         if side:
-            mixture_ref = refs[0]
+            mixture_ref, small_ref = refs[:2]
             mix_away, mix_twin, mix_halves, mix_full = refs[-6:-2]
-            refs = refs[1:-6] + refs[-2:]
+            refs = refs[2:-6] + refs[-2:]
         go_all, gm, dq, dk, dv, dqkv, local, got, hid_buf, hid_sems = refs[:10]
         full, twin, line, send_sems, recv_sems = refs[10:]
         place = Place(n_seq, n_bat)
@@ -804,15 +800,28 @@
                 gather.step(m)
 
         if side:
-            waiting = None
-            for n, j in enumerate(order):
+
+            def send_mixture(n):
+                j = order[n]
                 if n >= 2:
                     wire.settle(from_twin[order[n - 2]])
                 mix_away[n % 2] = (
                     mixture_of(place.twin_at(2 * j)).astype(BF).reshape(n_bat, own, dim)
                 )
+
+            def push_mixture(n):
+                j = order[n]
+                from_twin[j] = wire.push(mix_away.at[n % 2], mix_twin.at[j], place.twin())
+
+            waiting = None
+            send_mixture(0)
+            push_mixture(0)
+            for n, j in enumerate(order):
+                if n + 1 < len(order):
+                    send_mixture(n + 1)
                 total = mixture_of(place.seq_at(2 * j))
-                from_twin[j] = wire.push(mix_away.at[n % 2], mix_twin.at[j], place.twin())
+                if n + 1 < len(order):
+                    push_mixture(n + 1)
                 from_twin[j].wait_recv()
                 mix_twin[j] = (
                     (total + mix_twin[j].reshape(group, dim).astype(F32))
@@ -846,7 +855,7 @@
             raised = jnp.exp(scores - jnp.max(scores, axis=-1, keepdims=True))
             probs = raised / jnp.sum(raised, axis=-1, keepdims=True)
             low = probs.astype(BF)
-            grad_mix = gm[now, lanes]
+            grad_mix = gm[r, now, lanes]
             grad_probs = dot_t(grad_mix, v_ref[r, h, :keys, :])
             row_dot = jnp.sum(low.astype(F32) * grad_probs, axis=-1, keepdims=True)
             grad_scores = (probs * (grad_probs - row_dot)).astype(BF)
@@ -854,9 +863,12 @@
             dk[:keys, lanes] += scale * t_dot(grad_scores, query)
             dv[:keys, lanes] += t_dot(low, grad_mix)
 
+        def take(r):
+            gathers[r].finish()
+            gm[r] = dot_t(go_all[r].reshape(length, dim), wo_ref[...]).astype(BF)
+
+        take(0)
         for r in range(rows):
-            gathers[r].finish()
-            gm[...] = dot_t(go_all[r].reshape(length, dim), wo_ref[...]).astype(BF)
             if r:
                 scatters[r - 1].pass_on()
             dk[...] = jnp.zeros_like(dk)
@@ -894,6 +906,8 @@
                     local[r, row : row + 1, :] = lane_sums(products)
             exchange = Exchange(place, wire, local.at[r], got.at[r])
             dqkv[r, :, 2 * wide :] = dv[...].astype(BF)
+            if r + 1 < rows:
+                take(r + 1)
             means = (exchange.total() / dim).T
             for which, grads in ((0, dq), (1, dk)):
                 lanes = slice(which * wide, (which + 1) * wide)
@@ -931,8 +945,22 @@
         for j in works:
             works[j].finish()
             mixture_ref[j] = mix_twin[j, place.b]
+        sums = jnp.zeros((1, dim), F32)
         for r in range(rows):
-            scatters[r].finish(out_ref, slice(r * span, (r + 1) * span))
+            at = slice(r * span, (r + 1) * span)
+            if not side:
+                scatters[r].finish(out_ref, at)
+                continue
+            x = own_ref[at, :].astype(F32)
+            grad, terms = rms_back(x, rms_scale(x), ga_ref[...], scatters[r].total())
+            sums = sums + jnp.sum(terms, axis=0, keepdims=True)
+            out_ref[at, :] = (res_ref[at, :] + grad).astype(BF)
+        if side:
+            small_ref[...] = small_in[...]
+            small_ref[8:9, :] = sums
+            lanes = pl.ds(pl.multiple_of(place.s * wide, wide), wide)
+            for which in range(2):
+                small_ref[9 + which : 10 + which, lanes] = gain_ref[which : which + 1, :]
         wire.drain()
 
     vmem = pl.BlockSpec(memory_space=pltpu.VMEM)
@@ -941,7 +969,10 @@
     side_out, side_scratch = [], []
     if side:
         half = n_seq // 2
-        side_out = [jax.ShapeDtypeStruct((half, own, dim), BF)]
+        side_out = [
+            jax.ShapeDtypeStruct((half, own, dim), BF),
+            jax.ShapeDtypeStruct((16, dim), F32),
+        ]
         side_scratch = [
             pltpu.VMEM((2, n_bat, own, dim), BF),
             pltpu.VMEM((half, n_bat, own, dim), BF),
@@ -959,7 +990,7 @@
         + side_out,
         [
             pltpu.VMEM((rows, n_seq, span, dim), BF),
-            pltpu.VMEM((length, wide), BF),
+            pltpu.VMEM((rows, length, wide), BF),
             pltpu.VMEM((length, wide), F32),
             pltpu.VMEM((length, wide), F32),
             pltpu.VMEM((length, wide), F32),
@@ -1031,7 +1062,7 @@
         add_into(self.group.at[self.place.b], self.full.at[0], self.full.at[1])
 
 
-def load_first(weights, w_out, mine, flags, small, dy_own, rows, n_seq, n_bat):
+def load_first(weights, w_out, mine, flags, small, rows, n_seq, n_bat):
     shard, dim = weights[0].shape
     wide = dim // n_seq
     own = mine.shape[0]
@@ -1040,10 +1071,10 @@
 
     def kernel(*refs):
         parts = refs[:3]
-        wo_ref, x_ref, flag_ref, small_ref, dy_ref = refs[3:8]
-        w_ref, wo_all, x_col, flag_col, small_all, dy_all = refs[8:14]
-        buffers = refs[14:20]
-        own_sems, cut_sems, x_sems, send_sems, recv_sems = refs[20:]
+        wo_ref, x_ref, flag_ref, small_ref = refs[3:7]
+        w_ref, wo_all, x_col, flag_col, small_all = refs[7:12]
+        buffers = refs[12:17]
+        own_sems, cut_sems, x_sems, send_sems, recv_sems = refs[17:]
         place = Place(n_seq, n_bat)
         place.greet(all_seq=True)
         wire = Wire(send_sems, recv_sems)
@@ -1081,8 +1112,6 @@
         wo_work.start()
         for work in x_works:
             work.start()
-        dy_line = Line(place, wire, dy_ref, lambda i: dy_all.at[place.chip(i), place.b])
-        dy_line.start()
         for copy in own_cuts:
             copy.wait()
         spreads = []
@@ -1096,12 +1125,12 @@
         own_w = pltpu.make_async_copy(buffers[0], w_ref.at[place.s, place.b], own_sems.at[0])
         own_w.start()
         copies = [own_w]
-        fetched = pltpu.make_async_copy(x_ref, buffers[5], own_sems.at[5])
+        fetched = pltpu.make_async_copy(x_ref, buffers[4], own_sems.at[4])
         fetched.start()
         fetched.wait()
         for r in range(rows):
             copy = pltpu.make_async_copy(
-                buffers[5].at[pl.ds(r * span, span)], x_col.at[r, place.s], x_sems.at[r]
+                buffers[4].at[pl.ds(r * span, span)], x_col.at[r, place.s], x_sems.at[r]
             )
             copy.start()
             copies.append(copy)
@@ -1112,7 +1141,6 @@
                     (wo_ref, wo_all.at[place.b]),
                     (flag_ref, flag_col.at[place.s]),
                     (small_ref, small_all.at[place.s, place.b]),
-                    (dy_ref, dy_all.at[place.s, place.b]),
                 )
             )
         ]
@@ -1138,8 +1166,6 @@
             work.relay()
             forward(1)
         forward(len(todo))
-        for j in range(1, place.half):
-            dy_line.step(j)
         wo_work.finish()
         for work in spreads:
             work.finish()
@@ -1152,19 +1178,19 @@
     every = (n_seq, n_bat)
     one = jax.ShapeDtypeStruct((shard, 3 * wide), BF)
     x_one = jax.ShapeDtypeStruct((span, dim), BF)
-    blocks = (one, w_out, x_one, flags, small, dy_own)
-    leads = (every, (n_bat,), (rows, n_seq), (n_seq,), every, every)
-    held = (one, w_out, flags, small, dy_own, mine)
+    blocks = (one, w_out, x_one, flags, small)
+    leads = (every, (n_bat,), (rows, n_seq), (n_seq,), every)
+    held = (one, w_out, flags, small, mine)
     return comm_call(
         kernel,
         [shape_of(lead, block) for lead, block in zip(leads, blocks)],
         [pltpu.VMEM(block.shape, block.dtype) for block in held]
-        + [pltpu.SemaphoreType.DMA((n,)) for n in (6, 3, rows)],
+        + [pltpu.SemaphoreType.DMA((n,)) for n in (5, 3, rows)],
         slots,
         1,
         "load_first",
-        [ANY] * 8,
-    )(*weights, w_out, mine, flags, small, dy_own)
+        [ANY] * 7,
+    )(*weights, w_out, mine, flags, small)
 
 
 def pick_units(first, experts, units, part):
@@ -1174,22 +1200,23 @@
     return jnp.where((at_unit >= low) & (at_unit < low + part), 1.0, 0.0).astype(F32)
 
 
-def experts_forward(normed, gates, dy_all, w_gu, w_down, local_experts, n_seq, n_bat):
+def experts_forward(normed, gates, dy_all, gate, up, w_down, n_seq, n_bat):
     own, dim = normed.shape
+    local_experts, depth, hidden = gate.shape
     units = w_down.shape[0]
-    part = units // local_experts
+    part = hidden // n_seq
     group = n_bat * own
     tokens = n_seq * group
     experts = gates.shape[0]
-    slots = 64 + 2 * n_seq * n_bat
+    slots = 64 + 2 * n_seq * n_bat + 2 * local_experts * n_seq
 
     def kernel(*refs):
-        x_ref, gate_ref, dy_ref, gu_ref, down_ref = refs[:5]
-        x_all, weighted_ref, grad_ref, term_ref = refs[5:9]
-        gates_all, back, x_buf, dy_buf, keep, own_sems, x_sems, dy_sems = refs[9:17]
-        send_sems, recv_sems = refs[17:]
+        x_ref, gate_ref, dy_ref, wg_ref, wu_ref, down_ref = refs[:6]
+        x_all, weighted_ref, grad_ref, term_ref, gu_ref = refs[6:11]
+        gates_all, back, gate_buf, x_buf, dy_buf, keep = refs[11:17]
+        own_sems, x_sems, dy_sems, gu_sems, send_sems, recv_sems = refs[17:]
         place = Place(n_seq, n_bat)
-        place.greet()
+        place.greet(all_seq=True)
         wire = Wire(send_sems, recv_sems)
         gate_work = FullGather(place, wire, gate_ref, gates_all)
         gate_work.start()
@@ -1224,6 +1251,21 @@
                 block = dy_buf[g % 2].reshape(group, dim)
                 back[g * group : (g + 1) * group, :] = dot_t(block, down_ref[...])
 
+        gu_copies = ([], [])
+
+        def send_units(m, ref, offsets):
+            for k in offsets:
+                lanes = pl.ds(pl.multiple_of(place.seq_at(k) * part, part), part)
+                for e in range(local_experts):
+                    src = ref.at[e, :, lanes]
+                    dst = gu_ref.at[place.s, :, pl.ds(m * units + e * part, part)]
+                    if k:
+                        gu_copies[m].append(wire.push(src, dst, place.seq_peer(k)).wait_recv)
+                    else:
+                        copy = pltpu.make_async_copy(src, dst, gu_sems.at[m, e])
+                        copy.start()
+                        gu_copies[m].append(copy.wait)
+
         passed = []
 
         def hand_over(j):
@@ -1239,11 +1281,20 @@
             loads[slot] = pltpu.make_async_copy(x_all.at[g], x_buf.at[slot], x_sems.at[slot])
             loads[slot].start()
 
-        def units_on(g, slot):
+        def weight(m):
+            return gu_ref[:, :, m * units : (m + 1) * units].reshape(dim, units)
+
+        def gate_on(g, slot):
             loads[slot].wait()
+            gate_buf[rows_of(g), :] = dot(x_buf[slot].reshape(group, dim), weight(0))
+
+        def units_on(g, slot, gated=False):
+            if not gated:
+                loads[slot].wait()
             at = rows_of(g)
-            pre = dot(x_buf[slot].reshape(group, dim), gu_ref[...])
-            gate_pre, up_pre = pre[:, :units], pre[:, units:]
+            block = x_buf[slot].reshape(group, dim)
+            gate_pre = gate_buf[at, :] if gated else dot(block, weight(0))
+            up_pre = dot(block, weight(1))
             sig = jax.nn.sigmoid(gate_pre)
             silu = gate_pre * sig
             active = (silu * up_pre).astype(BF).astype(F32)
@@ -1278,6 +1329,7 @@
 
         half = place.half
         per = n_seq // half
+        offsets = list(range(1, n_seq)) + [0]
         for j in range(1, half):
             backs((j - 1) * per, per)
             gate_work.step(j)
@@ -1285,21 +1337,40 @@
             line.step(j)
             works[j].start()
             works[j - 1].relay()
+            if j < half - 1:
+                send_units(0, wg_ref, offsets[2 * j - 2 : 2 * j])
+            else:
+                send_units(0, wg_ref, offsets[2 * j - 2 :])
+                send_units(1, wu_ref, offsets)
         backs((half - 1) * per, per)
         gate_work.collect(half - 1)
         gate_work.finish()
         hand_over(0)
         fetch(here[0], 0)
+        for wait in gu_copies[0]:
+            wait()
+        gate_on(here[0], 0)
+        passed[0].wait_recv()
+        fetch(there[0], 1)
+        hand_over(1)
+        fetch(here[1], 2)
+        gate_on(there[0], 1)
+        gate_on(here[1], 2)
+        works[half - 1].relay()
+        passed[1].wait_recv()
+        fetch(there[1], 3)
+        gate_on(there[1], 3)
+        for wait in gu_copies[1]:
+            wait()
         for j in range(half):
-            units_on(here[j], (2 * j) % 4)
-            passed[j].wait_recv()
-            fetch(there[j], (2 * j + 1) % 4)
-            if j + 1 < half:
-                hand_over(j + 1)
-                fetch(here[j + 1], (2 * j + 2) % 4)
-            units_on(there[j], (2 * j + 1) % 4)
-            if j == max(0, half - 4):
-                works[half - 1].relay()
+            units_on(here[j], (2 * j) % 4, j < 2)
+            if j + 2 < half:
+                hand_over(j + 2)
+                fetch(here[j + 2], (2 * j) % 4)
+            units_on(there[j], (2 * j + 1) % 4, j < 2)
+            if j + 2 < half:
+                passed[j + 2].wait_recv()
+                fetch(there[j + 2], (2 * j + 1) % 4)
         wire.drain()
 
     vmem = pl.BlockSpec(memory_space=pltpu.VMEM)
@@ -1310,9 +1381,11 @@
             jax.ShapeDtypeStruct((tokens, units), BF),
             jax.ShapeDtypeStruct((tokens, 2 * units), BF),
             shape_of((n_seq, n_bat), gates),
+            jax.ShapeDtypeStruct((n_seq, depth, 2 * units), BF),
         ],
         [
             pltpu.VMEM((n_seq, n_bat) + gates.shape, F32),
+            pltpu.VMEM((tokens, units), F32),
             pltpu.VMEM((tokens, units), F32),
             pltpu.VMEM((4, n_bat, own, dim), BF),
             pltpu.VMEM((2, n_bat, own, dim), BF),
@@ -1320,18 +1393,21 @@
             pltpu.SemaphoreType.DMA((1,)),
             pltpu.SemaphoreType.DMA((4,)),
             pltpu.SemaphoreType.DMA((2,)),
+            pltpu.SemaphoreType.DMA((2, local_experts)),
         ],
         slots,
         4,
         "experts_forward",
-        [ANY, vmem, ANY, vmem, vmem],
-        [ANY, vmem, vmem, vmem],
-    )(normed, gates, dy_all, w_gu, w_down)
+        [ANY, vmem, ANY, ANY, ANY, vmem],
+        [ANY, vmem, vmem, vmem, vmem],
+    )(normed, gates, dy_all, gate, up, w_down)
 
 
 def experts_backward(
-    grad_pre, weighted, w_gu, terms, x_all, dy_all, local_experts, n_seq, n_bat, own
+    grad_pre, weighted, w_gu, terms, x_all, dy_all, residual, dy_own, gain_mlp, router, probs, chosen,
+    local_experts, n_seq, n_bat,
 ):
+    own = residual.shape[0]
     tokens, dim = x_all.shape
     units = weighted.shape[1]
     part = units // local_experts
@@ -1345,15 +1421,17 @@
 
     def kernel(*refs):
         grad_ref, weighted_ref, gu_ref, term_in, x_ref, dy_ref = refs[:6]
-        out_ref, term_out, gate_out, up_out, down_out = refs[6:11]
-        away, twin, halves, full, line = refs[11:16]
-        columns, sent, got, column_sems = refs[16:20]
-        term_scratch = refs[20:25]
-        send_sems, recv_sems = refs[25:]
+        res_ref, own_dy_ref, gm_ref, router_ref, probs_ref, chosen_ref = refs[6:12]
+        out_ref, low_ref, small_ref, gate_out, up_out, down_out = refs[12:18]
+        refs = refs[18:]
+        away, twin, halves, full, line = refs[:5]
+        columns, sent, got, column_sems, term_out = refs[5:10]
+        term_scratch = refs[10:15]
+        send_sems, recv_sems = refs[15:]
         place = Place(n_seq, n_bat)
         place.greet(all_seq=True)
         wire = Wire(send_sems, recv_sems)
-        term_work = FullScatter(place, wire, term_in, term_out, *term_scratch, None)
+        term_work = FullScatter(place, wire, term_in, term_out, *term_scratch)
         term_work.start()
 
         def product(i):
@@ -1366,12 +1444,6 @@
         def send(j):
             from_twin[j] = wire.push(away.at[j], twin.at[j], place.twin())
 
-        waiting = None
-        for j in order:
-            away[j] = product(place.twin_at(2 * j)).astype(BF).reshape(n_bat, own, dim)
-            if waiting is not None:
-                send(waiting)
-            waiting = j
         chunks = [("x", k) for k in list(range(1, n_seq)) + [0]] + [
             ("y", k) for k in range(dim // 256)
         ]
@@ -1425,6 +1497,14 @@
             if j:
                 from_seq[j] = wire.push(twin.at[j, place.b], line.at[j], place.seq_peer(2 * j))
 
+        work_chunks(1)
+        waiting = None
+        for j in order:
+            away[j] = product(place.twin_at(2 * j)).astype(BF).reshape(n_bat, own, dim)
+            if waiting is not None:
+                send(waiting)
+            waiting = j
+            work_chunks(1)
         first, rest = order[:2], order[2:]
         pair(order[0])
         send(waiting)
@@ -1470,7 +1550,30 @@
         total = twin[0, place.b].astype(F32)
         for j in range(1, half):
             total = total + line[j].astype(F32)
-        out_ref[...] = total
+        grad_chosen = term_out[...] * chosen_ref[...]
+        probs = probs_ref[...]
+        grad_logits = probs * (
+            grad_chosen - jnp.sum(probs * grad_chosen, axis=0, keepdims=True)
+        )
+        small_ref[...] = jnp.zeros_like(small_ref)
+        residual = res_ref[...]
+        scale = rms_scale(residual)
+        normal = residual * scale
+        normed = (normal * gm_ref[...]).astype(BF).astype(F32)
+        experts = probs.shape[0]
+        small_ref[0:experts, :] = lax.dot_general(
+            grad_logits, normed, (((1,), (0,)), ((), ())), precision=HIGHEST,
+            preferred_element_type=F32,
+        )
+        total = total + lax.dot_general(
+            grad_logits, router_ref[...], (((0,), (0,)), ((), ())), precision=HIGHEST,
+            preferred_element_type=F32,
+        )
+        grad, terms_of = rms_back(residual, scale, gm_ref[...], total)
+        small_ref[experts + 3 : experts + 4, :] = jnp.sum(terms_of, axis=0, keepdims=True)
+        grad = own_dy_ref[...].astype(F32) + grad
+        out_ref[...] = grad
+        low_ref[...] = grad.astype(BF)
         wire.drain()
 
     vmem = pl.BlockSpec(memory_space=pltpu.VMEM)
@@ -1479,7 +1582,8 @@
         kernel,
         [
             jax.ShapeDtypeStruct((own, dim), F32),
-            term,
+            jax.ShapeDtypeStruct((own, dim), BF),
+            jax.ShapeDtypeStruct((16, dim), F32),
             expert,
             expert,
             jax.ShapeDtypeStruct((units, dim), F32),
@@ -1494,14 +1598,15 @@
             pltpu.VMEM((n_seq, depth, 2 * units), BF),
             pltpu.VMEM((n_seq, depth, 2 * units), BF),
             pltpu.SemaphoreType.DMA((2,)),
+            pltpu.VMEM(term.shape, F32),
         ]
         + FullScatter.scratch(n_seq, n_bat, term),
         slots,
         5,
         "experts_backward",
-        [vmem] * 3 + [ANY] * 3,
-        [vmem] * 5,
-    )(grad_pre, weighted, w_gu, terms, x_all, dy_all)
+        [vmem] * 3 + [ANY] * 3 + [vmem] * 6,
+        [vmem] * 6,
+    )(grad_pre, weighted, w_gu, terms, x_all, dy_all, residual, dy_own, gain_mlp, router, probs, chosen)
 
 
 def store_last(grad_w, grad_wo, small, mixture, n_seq, n_bat):
@@ -1509,7 +1614,7 @@
     shard, three = one.shape
     wide = three // 3
     wo_one = jax.ShapeDtypeStruct(grad_wo.shape[1:], grad_wo.dtype)
-    small_one = jax.ShapeDtypeStruct(small.shape[2:], small.dtype)
+    small_one = jax.ShapeDtypeStruct((16, 2 * shard), small.dtype)
     half = n_seq // 2
     dim = wo_one.shape[1]
     slots = 64 + n_seq * n_bat + 5 * n_seq
@@ -1523,7 +1628,12 @@
         place = Place(n_seq, n_bat)
         place.greet(all_seq=True)
         wire = Wire(send_sems, recv_sems)
-        small_work = FullScatter(place, wire, small_ref, small_out, *small_scratch, None)
+
+        def pick(i, m):
+            tile = i * (n_bat // 2) + lax.div(m, 2)
+            return small_ref.at[:, pl.ds(pl.multiple_of(tile * 2 * shard, 128), 2 * shard)]
+
+        small_work = FullScatter(place, wire, small_ref, small_out, *small_scratch, pick)
         small_work.start()
         order = list(range(1, n_seq)) + [0]
         loads = {}
@@ -1610,6 +1720,42 @@
     )(grad_w, grad_wo, small, mixture)
 
 
+def finish(residual, mixture, grads):
+    count = len(grads)
+
+    def kernel(*refs):
+        res_ref, mix_ref = refs[:2]
+        ins, out_ref, outs = refs[2 : 2 + count], refs[2 + count], refs[3 + count : 3 + 2 * count]
+        buffers, sems = refs[3 + 2 * count : 3 + 3 * count], refs[-1]
+        loads = []
+        for i in range(count):
+            copy = pltpu.make_async_copy(ins[i], buffers[i], sems.at[0, i])
+            copy.start()
+            loads.append(copy)
+        out_ref[...] = (res_ref[...] + mix_ref[...]).astype(BF)
+        stores = []
+        for i in range(count):
+            loads[i].wait()
+            copy = pltpu.make_async_copy(buffers[i], outs[i], sems.at[1, i])
+            copy.start()
+            stores.append(copy)
+        for copy in stores:
+            copy.wait()
+
+    vmem = pl.BlockSpec(memory_space=pltpu.VMEM)
+    return pl.pallas_call(
+        kernel,
+        out_shape=[jax.ShapeDtypeStruct(residual.shape, BF)]
+        + [jax.ShapeDtypeStruct(grad.shape, grad.dtype) for grad in grads],
+        in_specs=[vmem] * 2 + [ANY] * count,
+        out_specs=[vmem] + [ANY] * count,
+        scratch_shapes=[pltpu.VMEM(grad.shape, grad.dtype) for grad in grads]
+        + [pltpu.SemaphoreType.DMA((2, count))],
+        compiler_params=pltpu.CompilerParams(vmem_limit_bytes=VMEM_LIMIT),
+        name="finish",
+    )(residual, mixture, *grads)
+
+
 def load_inputs(qkv_cut, w_out, mine, flags, small, gu_cut, dy_own, n_seq, n_bat):
     n_in = 7
     slots = 4 * n_seq * n_bat + 5 * n_seq + 2 * n_bat
@@ -1716,7 +1862,7 @@
         place.greet(all_seq=True)
         wire = Wire(send_sems, recv_sems)
         small_work = FullScatter(
-            place, wire, small_ref, small_out_ref, *small_scratch, None
+            place, wire, small_ref, small_out_ref, *small_scratch
         )
         small_work.start()
         got, loads = {}, {}
@@ -1843,11 +1989,14 @@
         and part % 128 == 0
         and own == 128
         and shard % 32 == 0
+        and n_seq == 8
+        and shard == 64
+        and experts == 8
         and n_seq * n_bat * own * dim <= 8 * 1024 * 1024
     )
     if fused:
-        w_qkv, w_o, x_col, flag_col, small_all, dy_part = load_first(
-            (w_query, w_key, w_value), w_out, mine, flags, pack(small), dy_own, rows, n_seq, n_bat
+        w_qkv, w_o, x_col, flag_col, small_all = load_first(
+            (w_query, w_key, w_value), w_out, mine, flags, pack(small), rows, n_seq, n_bat
         )
     else:
         qkv_cut = jnp.stack([w_query, w_key, w_value]).reshape(3, shard, n_seq, wide)
@@ -1872,6 +2021,9 @@
     usable = unpack(flag_col, (n_seq,), key_mask.shape)
     usable = jnp.transpose(usable, (1, 0, 2)).reshape(rows, length)
 
+    expert_ids = jnp.arange(experts, dtype=jnp.int32)
+    chosen_t = jnp.any(top_experts.reshape(own, -1).T[None] == expert_ids[:, None, None], axis=1)
+    chosen_t = chosen_t.astype(F32)
     cos_part, sin_part = rotary_tables(jnp.arange(length, dtype=jnp.int32))
     cos_wide = jnp.concatenate([cos_part, cos_part], axis=1)
     sin_wide = jnp.concatenate([-sin_part, sin_part], axis=1)
@@ -1879,35 +2031,40 @@
     hidden, qkv, q, k, v, mixed, stats, mixed_out, *extra = attend_forward(
         x_col.reshape(col, dim), w_qkv, gain_attn[None, :], usable, w_o, gain_q, gain_k,
         cos_wide, sin_wide, n_seq, n_bat, rows,
-        (dy_part, expert_gate, expert_up) if fused else None,
+        (dy_own, mine, gain_mlp[None, :], small_all[:experts], chosen_t) if fused else None,
     )
-    x_own = mine.astype(F32)
-    residual = x_own + mixed_out.astype(F32)
-    scale_r = rms_scale(residual)
-    normed = (residual * scale_r * gain_mlp).astype(BF)
-    router_probs = jax.nn.softmax(dot(normed, router), axis=-1)
-    expert_ids = jnp.arange(experts, dtype=jnp.int32)
-    chosen = jnp.any(top_experts.reshape(own, -1)[:, :, None] == expert_ids, axis=1).astype(F32)
-    gates = router_probs * chosen
+    if not fused:
+        x_own = mine.astype(F32)
+        residual = x_own + mixed_out.astype(F32)
+        scale_r = rms_scale(residual)
+        normed = (residual * scale_r * gain_mlp).astype(BF)
+        router_probs = jax.nn.softmax(dot(normed, router), axis=-1)
+        chosen = chosen_t.T
+        gates = router_probs * chosen
 
     if fused:
-        dy_all, w_gu = extra[0], extra[1].reshape(dim, 2 * units)
-        normed_all, weighted, grad_pre, gate_terms = experts_forward(
-            normed, gates.T, dy_all, w_gu, w_down, local_experts, n_seq, n_bat
+        dy_all, residual, normed, probs_t, gates_t = extra
+        normed_all, weighted, grad_pre, gate_terms, w_gu = experts_forward(
+            normed, gates_t, dy_all, expert_gate, expert_up, w_down, n_seq, n_bat
         )
-        grad_normed, grad_gates, grad_gate, grad_up, grad_down = experts_backward(
+        w_gu = w_gu.reshape(dim, 2 * units)
+        grad_residual, grad_o, small_grads, grad_gate, grad_up, grad_down = experts_backward(
             grad_pre,
             weighted,
             w_gu,
             gate_terms,
             normed_all.reshape(-1, dim),
             dy_all.reshape(-1, dim),
+            residual,
+            dy_own,
+            gain_mlp[None, :],
+            small_all[:experts],
+            probs_t,
+            chosen_t,
             local_experts,
             n_seq,
             n_bat,
-            own,
         )
-        grad_gates = grad_gates.T
         grad_down = grad_down.reshape(local_experts, part, dim)
     else:
         normed_all, gates_all = gather_all([normed, pack(gates.T)], n_seq, n_bat, 4, "gather_normed")
@@ -1951,52 +2108,59 @@
         output = (residual + mixture.astype(F32)).astype(BF)
         grad_down = grad_down.reshape(local_experts, part, dim)
 
-    grad_chosen = grad_gates * chosen
-    grad_logits = router_probs * (
-        grad_chosen - jnp.sum(router_probs * grad_chosen, axis=-1, keepdims=True)
-    )
-    grad_router = lax.dot_general(
-        normed.astype(F32), grad_logits, (((0,), (0,)), ((), ())), precision=HIGHEST
-    )
-    grad_normed = grad_normed + lax.dot_general(
-        grad_logits, router.astype(F32), (((1,), (1,)), ((), ())), precision=HIGHEST
-    )
-    grad_resid, gain_mlp_terms = rms_back(residual, scale_r, gain_mlp, grad_normed)
-    grad_residual = dy_own.astype(F32) + grad_resid
-    grad_o = grad_residual.astype(BF)
+    if not fused:
+        grad_chosen = grad_gates * chosen
+        grad_logits = router_probs * (
+            grad_chosen - jnp.sum(router_probs * grad_chosen, axis=-1, keepdims=True)
+        )
+        grad_router = lax.dot_general(
+            normed.astype(F32), grad_logits, (((0,), (0,)), ((), ())), precision=HIGHEST
+        )
+        grad_normed = grad_normed + lax.dot_general(
+            grad_logits, router.astype(F32), (((1,), (1,)), ((), ())), precision=HIGHEST
+        )
+        grad_resid, gain_mlp_terms = rms_back(residual, scale_r, gain_mlp, grad_normed)
+        grad_residual = dy_own.astype(F32) + grad_resid
+        grad_o = grad_residual.astype(BF)
 
     grad_w_o, grad_w, grad_gains, grad_hidden, *extra = attend_backward(
         grad_o, q, k, v, mixed, qkv, stats, hidden, usable, w_o, w_qkv, gain_q, gain_k,
-        cos_wide, sin_wide, n_seq, n_bat, (weighted, w_down) if fused else None,
+        cos_wide, sin_wide, n_seq, n_bat,
+        (weighted, w_down, mine, grad_residual, gain_attn[None, :], small_grads) if fused else None,
     )
     grad_w_o = grad_w_o.reshape(n_bat, shard, dim)
     grad_w = grad_w.reshape(n_seq, n_bat, shard, 3 * wide)
-    grad_hidden = grad_hidden.astype(F32)
-    grad_x, gain_attn_terms = rms_back(x_own, rms_scale(x_own), gain_attn, grad_hidden)
-    grad_tokens = (grad_residual + grad_x).astype(BF)
-
-    zeros = jnp.zeros((dim,), F32)
-    small_grads = jnp.concatenate(
-        [
-            grad_router.T,
-            jnp.stack(
-                [
-                    jnp.sum(gain_attn_terms, axis=0),
-                    lax.dynamic_update_slice_in_dim(zeros, grad_gains[0], seq * wide, 0),
-                    lax.dynamic_update_slice_in_dim(zeros, grad_gains[1], seq * wide, 0),
-                    jnp.sum(gain_mlp_terms, axis=0),
-                ]
-            ),
-        ],
-        axis=0,
-    )
-    small_grads = jnp.transpose(small_grads.reshape(-1, n_seq, n_bat, shard), (1, 2, 0, 3))
-    small_grads = jax.vmap(jax.vmap(pack))(small_grads)
+    if not fused:
+        grad_hidden = grad_hidden.astype(F32)
+        grad_x, gain_attn_terms = rms_back(x_own, rms_scale(x_own), gain_attn, grad_hidden)
+        grad_tokens = (grad_residual + grad_x).astype(BF)
+
+        zeros = jnp.zeros((dim,), F32)
+        small_grads = jnp.concatenate(
+            [
+                grad_router.T,
+                jnp.stack(
+                    [
+                        jnp.sum(gain_attn_terms, axis=0),
+                        lax.dynamic_update_slice_in_dim(zeros, grad_gains[0], seq * wide, 0),
+                        lax.dynamic_update_slice_in_dim(zeros, grad_gains[1], seq * wide, 0),
+                        jnp.sum(gain_mlp_terms, axis=0),
+                    ]
+                ),
+            ],
+            axis=0,
+        )
+        small_grads = jnp.transpose(small_grads.reshape(-1, n_seq, n_bat, shard), (1, 2, 0, 3))
+        small_grads = jax.vmap(jax.vmap(pack))(small_grads)
+
     if fused:
         *grad_w, grad_w_o, small_grads, mixture = store_last(
-            grad_w, grad_w_o, small_grads, extra[0], n_seq, n_bat
+            grad_w, grad_w_o, extra[1], extra[0], n_seq, n_bat
         )
-        output = (residual + mixture).astype(BF)
+        output, grad_tokens, *grad_w, grad_w_o, grad_gate, grad_up, grad_down = finish(
+            residual, mixture, [grad_hidden, *grad_w, grad_w_o, grad_gate, grad_up, grad_down]
+        )
+        small_grads = lax.dynamic_slice_in_dim(small_grads, lax.rem(bat, 2) * shard, shard, 1)
     else:
         grad_gu = grad_gu.reshape(n_seq, depth, -1)
         grad_w, grad_w_o, grad_gu, small_grads = store_grads(
@@ -2008,7 +2172,7 @@
         grad_gu = jnp.transpose(grad_gu, (2, 3, 1, 0, 4)).reshape(2, local_experts, depth, hidden_units)
         grad_gu = grad_gu.astype(F32)
         grad_gate, grad_up = grad_gu[0], grad_gu[1]
-    small_grads = unpack(small_grads, (), (experts + 4, shard))
+        small_grads = unpack(small_grads, (), (experts + 4, shard))
 
     return (
         output.reshape(rows, span, dim),

time: 679 us -> 620 us (0.913)
  Pallas kernels: 617 us -> 595 us
  local copies, waits for them, and re-layouts: 27.5 us -> 10 us
  other arithmetic: 19 us -> 4.57 us
    pallas_call x1, Pallas kernels: 93 us -> 64.1 us  [load_first(): comm_call(kernel, [shape_of(lead, block) for lead, block in zip(leads, bl...]
    pallas_call x1, Pallas kernels: 90.6 us -> 119 us  [experts_forward(): comm_call(kernel, [shape_of((n_seq, n_bat), normed), jax.ShapeDtypeStruct...]
    pallas_call x1, Pallas kernels: 111 us -> 93.9 us  [attend_forward(): comm_call(kernel, outs + side_out, [pltpu.VMEM(stats.shape, F32), pltpu.V...]
    unnamed x66 -> x7, local copies, waits for them, and re-layouts: 11.3 us -> 0.04 us
    pallas_call x1 -> x2, Pallas kernels: 130 us -> 128 us  [the longest x1 119 us: experts_backward(): comm_call(kernel, [jax.ShapeDtypeStruct((own, dim), F32), jax.ShapeDtypeS...]
where the time goes in v6:
time: 620 us; the launch traced here: 611 us
  Pallas kernels  595 us (96%)
  local copies, waits for them, and re-layouts  10 us (2%)
    pallas_call x1, Pallas kernels, experts_forward(): comm_call(kernel, [shape_of((n_seq, n_bat), normed), jax.ShapeDtypeStruct...  119 us
    pallas_call x1, Pallas kernels, experts_backward(): comm_call(kernel, [jax.ShapeDtypeStruct((own, dim), F32), jax.ShapeDtypeS...  119 us
    pallas_call x1, Pallas kernels, attend_backward(): comm_call(kernel, [jax.ShapeDtypeStruct((wide, dim), BF), jax.ShapeDtypeS...  115 us
    pallas_call x1, Pallas kernels, attend_forward(): comm_call(kernel, outs + side_out, [pltpu.VMEM(stats.shape, F32), pltpu.V...  93.9 us
    pallas_call x1, Pallas kernels, store_last(): comm_call(kernel, [matrix] * 4 + [small_one, jax.ShapeDtypeStruct(mixture...  75.5 us
    pallas_call x1, Pallas kernels, load_first(): comm_call(kernel, [shape_of(lead, block) for lead, block in zip(leads, bl...  64.1 us

profile of v6, /device:TPU:9, one launch (start us, length us, event | category | flops | bytes accessed | tf_op | source)
XLA Modules:
  0.0 610.5 jit_solution(13189092015467260182)
XLA Ops:
  0.7 0.8 compare_and_fusion
  1.4 0.1 reshape.130
  1.5 0.6 convert_bitcast_fusion.refs_5_
  2.1 1.4 concatenate.9
  3.5 0.1 convert_element_type.26
  3.6 0.6 bitcast_convert_fusion.refs_6_
  4.2 64.1 %load_first.1 = (bf16[8,4,64,768]{3,2,1,0:T(8,128)(2,1)}, bf16[4,64,2048]{2,1,0:T(8,128)(2,1)}, bf16[2,8,64,2048]{3,2,1,0:T(8,128)(2,1)}, f32[8,8,128]{2,1,0:T(8,128)}, f32[8,4,8,128]{3,2,1,0:T(8,128)}) custom-call(bf16[64,2048]{1,0:T(8,128)(2,1)} %refs_0_.1, bf16[64,2048]{1,0:T(8,128)(2,1)} %refs_1_.1, bf16[64,2048]{1,0:T(8,128)(2,1)} %refs_2_.1, ...), custom_call_target="tpu_custom_call" | custom-call | tf_op jit(solution)/shard_map/load_first/pallas_call | solution.py:1184
  68.3 0.0 copy-start
  68.3 1.0 reshape.137
  69.3 0.0 copy-start.1
  69.3 0.1 reshape.138
  69.5 0.1 squeeze.18
  69.6 0.6 dynamic_slice.9
  70.2 0.1 squeeze.19
  70.3 0.6 dynamic_slice.10
  70.9 0.7 slice.50.refs_2_.refs_19_
  71.6 0.7 slice.55.refs_11_.refs_8_
  72.3 0.1 copy.52
  72.4 0.8 slice.57.refs_12_.refs_9_
  73.2 0.0 copy-done
  73.2 0.1 reshape.140
  73.3 0.7 reshape.141.refs_3_.refs_8_
  74.0 1.0 fusion
  75.0 1.0 pad_maximum_fusion
  76.0 0.0 copy-done.1
  76.0 0.1 reshape.144
  76.1 0.6 convert_element_type.28.refs_13_.refs_11_
  76.7 93.9 %attend_forward.1 = (bf16[1024,2048]{1,0:T(8,128)(2,1)}, f32[1024,768]{1,0:T(8,128)}, bf16[2,2,512,128]{3,2,1,0:T(8,128)(2,1)}, bf16[2,2,512,128]{3,2,1,0:T(8,12...) custom-call(bf16[1024,2048]{1,0:T(8,128)(2,1)} %bitcast.56, ...), custom_call_target="tpu_custom_call" | custom-call | tf_op jit(solution)/shard_map/attend_forward/pallas_call | solution.py:734
  170.6 118.7 %experts_forward.1 = (bf16[8,4,128,2048]{3,2,1,0:T(8,128)(2,1)}, bf16[4096,256]{1,0:T(8,128)(2,1)}, bf16[4096,512]{1,0:T(8,128)(2,1)}, f32[8,4,8,128]{3,2,1,0:T(8,128)}, bf16[8,256,512]{2,1,0:T(8,128)(2,1)}) custom-call(bf16[128,2048]{1,0:T(8,128)(2,1)} %get-tuple-element.68.refs_0_, f32[8,128]{1,0:T(8,128)} %get-tuple-element.69.refs_1_, ...), custom_call_target="tpu_custom_call" | custom-call | tf_op jit(solution)/shard_map/experts_forward/pallas_call | solution.py:1377
  289.3 118.5 %experts_backward.1 = (f32[128,2048]{1,0:T(8,128)}, bf16[128,2048]{1,0:T(8,128)(2,1)}, f32[16,2048]{1,0:T(8,128)}, f32[2,256,1024]{2,1,0:T(8,128)}, f32[2,256,1024]{2,1,0:T(8,128)}, /*index=5*/f32[256,2048]{1,0:T(8,128)}) custom-call(bf16[4096,512]{1,0:T(8,128)(2,1)} %get-tuple-element.71.refs_0_, bf16[4096,256]{1,0:T(8,128)(2,1)} %get-tuple-element.72.refs_1_.refs_15_, ...), custom_call_target="tpu_custom_call" | custom-call | tf_op jit(solution)/shard_map/experts_backward/pallas_call | solution.py:1581
  407.8 115.0 %attend_backward.1 = (bf16[256,2048]{1,0:T(8,128)(2,1)}, bf16[2048,768]{1,0:T(8,128)(2,1)}, f32[2,256]{1,0:T(2,128)}, bf16[128,2048]{1,0:T(8,128)(2,1)}, bf16[4,...) custom-call(bf16[128,2048]{1,0:T(8,128)(2,1)} %get-tuple-element.77.refs_0_, ...), custom_call_target="tpu_custom_call" | custom-call | tf_op jit(solution)/shard_map/attend_backward/pallas_call | solution.py:982
  522.9 75.5 %store_last.1 = (f32[64,2048]{1,0:T(8,128)}, f32[64,2048]{1,0:T(8,128)}, f32[64,2048]{1,0:T(8,128)}, f32[64,2048]{1,0:T(8,128)}, f32[16,128]{1,0:T(8,128)}, /*index=5*/f32[128,2048]{1,0:T(8,128)}) custom-call(bf16[8,4,64,768]{3,2,1,0:T(8,128)(2,1)} %bitcast.61, bf16[4,64,2048]{2,1,0:T(8,128)(2,1)} %bitcast.66, f32[16,2048]{1,0:T(8,128)} %get-tuple-element.89.refs_2_, ...), custom_call_target="tpu_custom_call" | custom-call | tf_op jit(solution)/shard_map/store_last/pallas_call | solution.py:1700
  598.3 9.0 %finish.1 = (bf16[128,2048]{1,0:T(8,128)(2,1)}, bf16[128,2048]{1,0:T(8,128)(2,1)}, f32[64,2048]{1,0:T(8,128)}, f32[64,2048]{1,0:T(8,128)}, f32[64,2048]{1,0:T(8,...) custom-call(f32[128,2048]{1,0:T(8,128)} %get-tuple-element.67.refs_6_.re, ...), custom_call_target="tpu_custom_call" | custom-call | tf_op jit(solution)/shard_map/finish/pallas_call | solution.py:1746
  607.3 1.4 dynamic-slice_bitcast_fusion.1
  608.8 1.3 dynamic-slice_bitcast_fusion
  (16 shorter events, 0.2 us)
Async XLA Ops:
  68.3 4.9 copy-start
  69.3 6.7 %copy-start.1 = (s32[2,64,4]{1,2,0:T(4,128)S(1)}, s32[2,64,4]{1,2,0:T(4,128)}, u32[]{:S(2)}) copy-start(s32[2,64,4]{1,2,0:T(4,128)} %param.20) | copy-start | bytes 6148

commit v7 on v6

--- a/solution.py
+++ b/solution.py
@@ -71,8 +71,9 @@
         return {"seq": self.chip(lax.rem(i + self.half, self.half)), "batch": self.b}
 
     def origin(self, m):
-        if m == 0:
-            return self.z
+        return self.z if m == 0 else self.origin_of(m)
+
+    def origin_of(self, m):
         last = self.half - 1
         upper = lax.div(2 * self.z, self.half)
         mirrored = self.z + upper * (last - 2 * self.z)
@@ -497,15 +498,15 @@
 
     def start(self):
         place = self.place
+        self.from_seq = {}
         self.from_twin = {
             j: self.wire.push(self.full.at[place.twin_at(2 * j)], self.twin.at[j], place.twin())
             for j in self.order
         }
 
-    def pass_on(self):
+    def pass_on(self, first=0, last=None):
         place = self.place
-        self.from_seq = {}
-        for j in self.order:
+        for j in self.order[first:last]:
             self.from_twin[j].wait_recv()
             block = self.full.at[place.seq_at(2 * j)]
             add_into(block, self.twin.at[j])
@@ -548,12 +549,15 @@
         return total
 
 
+def in_two(v):
+    high = v.astype(BF)
+    return high, (v - high.astype(F32)).astype(BF)
+
+
 def lane_sums(v):
-    ones = jnp.ones((8, v.shape[1]), F32)
-    sums = lax.dot_general(
-        ones, v, (((1,), (1,)), ((), ())), precision=HIGHEST, preferred_element_type=F32
-    )
-    return sums[0:1]
+    ones = jnp.ones((8, v.shape[1]), BF)
+    high, low = in_two(v)
+    return (dot_t(ones, high) + dot_t(ones, low))[0:1]
 
 
 def allowed_block(use, first, count, keys):
@@ -565,9 +569,13 @@
 STEP = 128
 
 
+def head_gain(place, gains_ref, which, wide, h):
+    first = pl.multiple_of(place.s * wide + h * HEAD, HEAD)
+    return gains_ref[1 + which : 2 + which, pl.ds(first, HEAD)]
+
+
 def attend_forward(
-    x_col, w_qkv, gain_attn, usable, w_o, gain_q, gain_k, cos_wide, sin_wide, n_seq, n_bat, rows,
-    side=None,
+    x_col, w_qkv, usable, w_o, gains, cos_wide, sin_wide, n_seq, n_bat, rows, side=None
 ):
     col, dim = x_col.shape
     three = w_qkv.shape[1]
@@ -582,11 +590,11 @@
     block = jax.ShapeDtypeStruct((span, dim), BF)
 
     def kernel(*refs):
-        (x_ref, w_ref, ga_ref, use_ref, wo_ref, gq_ref, gk_ref, cos_ref, sin_ref) = refs[:9]
-        refs = refs[9:]
+        (x_ref, w_ref, use_ref, wo_ref, gains_ref, cos_ref, sin_ref) = refs[:7]
+        refs = refs[7:]
         if side is not None:
-            dy_ref, own_ref, gm_ref, router_ref, chosen_ref = refs[:5]
-            refs = refs[5:]
+            dy_ref, own_ref, router_ref, chosen_ref = refs[:4]
+            refs = refs[4:]
         hid_ref, qkv_ref, q_ref, k_ref, v_ref, mix_ref, stat_ref, out_ref = refs[:8]
         refs = refs[8:]
         if side is not None:
@@ -614,12 +622,15 @@
             dy_line.start()
             dy_spread(0)
             dy_own = keep_own(dy_ref, dy_all.at[place.s, place.b], dy_keep, dy_sem)
-        for first in range(0, col, chunk):
-            at = slice(first, first + chunk)
+        def project(n, carry):
+            at = pl.ds(pl.multiple_of(n * chunk, chunk), chunk)
             x = x_ref[at, :].astype(F32)
-            hidden = (x * rms_scale(x) * ga_ref[...]).astype(BF)
+            hidden = (x * rms_scale(x) * gains_ref[0:1, :]).astype(BF)
             hid_ref[at, :] = hidden
             qkv_ref[at, :] = dot(hidden, w_ref[...])
+            return carry
+
+        lax.fori_loop(0, col // chunk, project, 0)
         for r in range(rows):
             for c in range(steps):
                 at = slice(r * length + c * STEP, r * length + (c + 1) * STEP)
@@ -643,12 +654,12 @@
             for c in range(steps):
                 inside = slice(c * STEP, (c + 1) * STEP)
                 at = slice(r * length + c * STEP, r * length + (c + 1) * STEP)
-                for which, gain_ref, target in ((0, gq_ref, q_ref), (1, gk_ref, k_ref)):
+                for which, target in ((0, q_ref), (1, k_ref)):
                     row = (r * 2 + which) * steps + c
                     factor = columns[:, row : row + 1]
                     for h in range(heads):
                         lanes = slice(which * wide + h * HEAD, which * wide + (h + 1) * HEAD)
-                        gain = gain_ref[0:1, h * HEAD : (h + 1) * HEAD]
+                        gain = head_gain(place, gains_ref, which, wide, h)
                         v = qkv_ref[at, lanes] * factor * gain
                         target[r, h, inside, :] = turn(
                             v, cos_ref[inside, :], sin_ref[inside, :]
@@ -692,7 +703,7 @@
                 continue
             residual = own_ref[at, :].astype(F32) + scatters[r].total()
             res_ref[at, :] = residual
-            normed_ref[at, :] = (residual * rms_scale(residual) * gm_ref[...]).astype(BF)
+            normed_ref[at, :] = (residual * rms_scale(residual) * gains_ref[3:4, :]).astype(BF)
         if side is not None:
             out_ref[...] = jnp.zeros_like(out_ref)
             logits = dot_t(router_ref[...].astype(BF), normed_ref[...])
@@ -708,7 +719,7 @@
     side_in, side_out, side_scratch = [], [], []
     slots = (1 + rows) * n_seq
     if side is not None:
-        dy, _, _, router, _ = side
+        dy, _, router, _ = side
         side_in = list(side)
         side_out = [
             shape_of((n_seq, n_bat), dy),
@@ -740,14 +751,14 @@
         slots,
         2,
         "attend_forward",
-        [vmem] * 9 + ([ANY] + [vmem] * 4 if side_in else []),
+        [vmem] * 7 + ([ANY] + [vmem] * 3 if side_in else []),
         [vmem] * 8 + ([ANY] + [vmem] * 4 if side_in else []),
-    )(x_col, w_qkv, gain_attn, usable, w_o, gain_q, gain_k, cos_wide, sin_wide, *side_in)
+    )(x_col, w_qkv, usable, w_o, gains, cos_wide, sin_wide, *side_in)
 
 
 def attend_backward(
-    grad_o, q, k, v, mixed, qkv, stats, hidden, usable, w_o, w_qkv, gain_q, gain_k,
-    cos_wide, sin_wide, n_seq, n_bat, side=None,
+    grad_o, q, k, v, mixed, qkv, stats, hidden, usable, w_o, w_qkv, gains, cos_wide, sin_wide,
+    n_seq, n_bat, side=None,
 ):
     rows, heads, length, _ = q.shape
     own, dim = grad_o.shape
@@ -761,11 +772,11 @@
 
     def kernel(*refs):
         (go_ref, q_ref, k_ref, v_ref, mix_ref, qkv_ref, stat_ref, hid_ref, use_ref, wo_ref,
-         w_ref, gq_ref, gk_ref, cos_ref, sin_ref) = refs[:15]
-        refs = refs[15:]
+         w_ref, gains_ref, cos_ref, sin_ref) = refs[:14]
+        refs = refs[14:]
         if side:
-            weighted_ref, down_ref, own_ref, res_ref, ga_ref, small_in = refs[:6]
-            refs = refs[6:]
+            weighted_ref, down_ref, own_ref, res_ref, small_in = refs[:5]
+            refs = refs[5:]
         gwo_ref, gw_ref, gain_ref, out_ref = refs[:4]
         refs = refs[4:]
         if side:
@@ -870,7 +881,7 @@
         take(0)
         for r in range(rows):
             if r:
-                scatters[r - 1].pass_on()
+                scatters[r - 1].pass_on(0, 1)
             dk[...] = jnp.zeros_like(dk)
             dv[...] = jnp.zeros_like(dv)
             for h in range(heads):
@@ -883,7 +894,7 @@
                 forward(len(todo))
                 while middles:
                     middles.pop(0).middle()
-            for which, g_ref, grads in ((0, gq_ref, dq), (1, gk_ref, dk)):
+            for which, grads in ((0, dq), (1, dk)):
                 for c in range(steps):
                     inside = slice(c * STEP, (c + 1) * STEP)
                     at = slice(r * length + c * STEP, r * length + (c + 1) * STEP)
@@ -898,13 +909,15 @@
                         gain_sums[which][h] = gain_sums[which][h] + jnp.sum(
                             back * flat, axis=0, keepdims=True
                         )
-                        weighted = back * g_ref[0:1, lanes]
+                        weighted = back * head_gain(place, gains_ref, which, wide, h)
                         grads[inside, lanes] = weighted
                         product = weighted * flat
                         products = product if products is None else products + product
                     row = which * steps + c
                     local[r, row : row + 1, :] = lane_sums(products)
             exchange = Exchange(place, wire, local.at[r], got.at[r])
+            if r:
+                scatters[r - 1].pass_on(1)
             dqkv[r, :, 2 * wide :] = dv[...].astype(BF)
             if r + 1 < rows:
                 take(r + 1)
@@ -926,22 +939,32 @@
                 gain_ref[which : which + 1, h * HEAD : (h + 1) * HEAD] = gain_sums[which][h]
 
         def hidden_load(part):
+            slot = lax.rem(part, 2)
+            at = pl.ds(pl.multiple_of(part * 256, 256), 256)
             return pltpu.make_async_copy(
-                hid_ref.at[:, pl.ds(part * 256, 256)], hid_buf.at[part % 2], hid_sems.at[part % 2]
+                hid_ref.at[:, at], hid_buf.at[slot], hid_sems.at[slot]
             )
 
         hidden_load(0).start()
         scatters[-1].pass_on()
-        for part in range(dim // 256):
-            at = slice(part * 256, (part + 1) * 256)
-            if part + 1 < dim // 256:
+
+        def weight_part(part, carry):
+            at = pl.ds(pl.multiple_of(part * 256, 256), 256)
+
+            @pl.when(part + 1 < dim // 256)
+            def _():
                 hidden_load(part + 1).start()
+
             hidden_load(part).wait()
-            gw_ref[at, :] = t_dot(hid_buf[part % 2], dqkv[...].reshape(col, three)).astype(BF)
+            held = hid_buf[lax.rem(part, 2)]
+            gw_ref[at, :] = t_dot(held, dqkv[...].reshape(col, three)).astype(BF)
             total = t_dot(mix_ref[0], go_all[0, :, :, at].reshape(length, 256))
             for r in range(1, rows):
                 total = total + t_dot(mix_ref[r], go_all[r, :, :, at].reshape(length, 256))
             gwo_ref[:, at] = total.astype(BF)
+            return carry
+
+        lax.fori_loop(0, dim // 256, weight_part, 0)
         for j in works:
             works[j].finish()
             mixture_ref[j] = mix_twin[j, place.b]
@@ -952,7 +975,7 @@
                 scatters[r].finish(out_ref, at)
                 continue
             x = own_ref[at, :].astype(F32)
-            grad, terms = rms_back(x, rms_scale(x), ga_ref[...], scatters[r].total())
+            grad, terms = rms_back(x, rms_scale(x), gains_ref[0:1, :], scatters[r].total())
             sums = sums + jnp.sum(terms, axis=0, keepdims=True)
             out_ref[at, :] = (res_ref[at, :] + grad).astype(BF)
         if side:
@@ -1005,10 +1028,10 @@
         5 * rows * n_seq + (3 * n_seq if side else 0),
         6,
         "attend_backward",
-        [vmem] * 7 + [ANY] + [vmem] * (7 + len(side or ())),
+        [vmem] * 7 + [ANY] + [vmem] * (6 + len(side or ())),
         [vmem] * (4 + len(side_out)),
-    )(grad_o, q, k, v, mixed, qkv, stats, hidden, usable, w_o, w_qkv, gain_q, gain_k,
-      cos_wide, sin_wide, *(side or ()))
+    )(grad_o, q, k, v, mixed, qkv, stats, hidden, usable, w_o, w_qkv, gains, cos_wide, sin_wide,
+      *(side or ()))
 
 
 class Across:
@@ -1072,9 +1095,9 @@
     def kernel(*refs):
         parts = refs[:3]
         wo_ref, x_ref, flag_ref, small_ref = refs[3:7]
-        w_ref, wo_all, x_col, flag_col, small_all = refs[7:12]
-        buffers = refs[12:17]
-        own_sems, cut_sems, x_sems, send_sems, recv_sems = refs[17:]
+        w_ref, wo_all, x_col, router_ref, gains_ref, use_ref = refs[7:13]
+        buffers = refs[13:16]
+        own_sems, cut_sems, x_sems, small_all, flag_col, send_sems, recv_sems = refs[16:]
         place = Place(n_seq, n_bat)
         place.greet(all_seq=True)
         wire = Wire(send_sems, recv_sems)
@@ -1125,25 +1148,18 @@
         own_w = pltpu.make_async_copy(buffers[0], w_ref.at[place.s, place.b], own_sems.at[0])
         own_w.start()
         copies = [own_w]
-        fetched = pltpu.make_async_copy(x_ref, buffers[4], own_sems.at[4])
+        fetched = pltpu.make_async_copy(x_ref, buffers[2], own_sems.at[2])
         fetched.start()
         fetched.wait()
         for r in range(rows):
             copy = pltpu.make_async_copy(
-                buffers[4].at[pl.ds(r * span, span)], x_col.at[r, place.s], x_sems.at[r]
+                buffers[2].at[pl.ds(r * span, span)], x_col.at[r, place.s], x_sems.at[r]
             )
             copy.start()
             copies.append(copy)
-        copies += [
-            keep_own(src, dst, buffers[i + 1], own_sems.at[i + 1])
-            for i, (src, dst) in enumerate(
-                (
-                    (wo_ref, wo_all.at[place.b]),
-                    (flag_ref, flag_col.at[place.s]),
-                    (small_ref, small_all.at[place.s, place.b]),
-                )
-            )
-        ]
+        copies.append(keep_own(wo_ref, wo_all.at[place.b], buffers[1], own_sems.at[1]))
+        flag_col[place.s] = flag_ref[...]
+        small_all[place.s, place.b] = small_ref[...]
         for j in range(1, place.half):
             small_work.step(j)
             flag_work.step(j)
@@ -1171,25 +1187,42 @@
             work.finish()
         for work in [small_work, flag_work] + x_works:
             work.finish()
+        left = lax.broadcasted_iota(jnp.int32, (8, 128), 1) < 64
+        for i in range(n_seq):
+            for k in range(0, n_bat, 2):
+                one, two = small_all[i, k], small_all[i, k + 1]
+                at = slice((i * n_bat + k) * 64, (i * n_bat + k + 2) * 64)
+                router_ref[:, at] = jnp.where(left, one, pltpu.roll(two, 64, axis=1))
+                gains_ref[:, at] = jnp.where(left, pltpu.roll(one, 64, axis=1), two)
+        for i in range(0, n_seq, 2):
+            one, two = flag_col[i], flag_col[i + 1]
+            use_ref[:, i * 64 : (i + 2) * 64] = jnp.where(left, one, pltpu.roll(two, 64, axis=1))
         for copy in copies:
             copy.wait()
         wire.drain()
 
-    every = (n_seq, n_bat)
     one = jax.ShapeDtypeStruct((shard, 3 * wide), BF)
     x_one = jax.ShapeDtypeStruct((span, dim), BF)
-    blocks = (one, w_out, x_one, flags, small)
-    leads = (every, (n_bat,), (rows, n_seq), (n_seq,), every)
-    held = (one, w_out, flags, small, mine)
+    held = (one, w_out, mine)
+    vmem = pl.BlockSpec(memory_space=pltpu.VMEM)
     return comm_call(
         kernel,
-        [shape_of(lead, block) for lead, block in zip(leads, blocks)],
+        [
+            shape_of((n_seq, n_bat), one),
+            shape_of((n_bat,), w_out),
+            shape_of((rows, n_seq), x_one),
+            jax.ShapeDtypeStruct((8, dim), F32),
+            jax.ShapeDtypeStruct((8, dim), F32),
+            jax.ShapeDtypeStruct((8, n_seq * span), F32),
+        ],
         [pltpu.VMEM(block.shape, block.dtype) for block in held]
-        + [pltpu.SemaphoreType.DMA((n,)) for n in (5, 3, rows)],
+        + [pltpu.SemaphoreType.DMA((n,)) for n in (3, 3, rows)]
+        + [pltpu.VMEM((n_seq, n_bat, 8, 128), F32), pltpu.VMEM((n_seq, 8, 128), F32)],
         slots,
         1,
         "load_first",
-        [ANY] * 7,
+        [ANY] * 5 + [vmem] * 2,
+        [ANY] * 3 + [vmem] * 3,
     )(*weights, w_out, mine, flags, small)
 
 
@@ -1197,7 +1230,7 @@
     at_expert = lax.broadcasted_iota(jnp.int32, (experts, units), 0)
     at_unit = lax.broadcasted_iota(jnp.int32, (experts, units), 1)
     low = (at_expert - first) * part
-    return jnp.where((at_unit >= low) & (at_unit < low + part), 1.0, 0.0).astype(F32)
+    return jnp.where((at_unit >= low) & (at_unit < low + part), 1.0, 0.0).astype(BF)
 
 
 def experts_forward(normed, gates, dy_all, gate, up, w_down, n_seq, n_bat):
@@ -1235,6 +1268,7 @@
         works[0].start()
         own = keep_own(x_ref, x_all.at[place.s, place.b], keep, own_sems.at[0])
         selected = pick_units(place.b * local_experts, experts, units, part)
+        selected_twice = jnp.concatenate([selected, selected], axis=0)
 
         def dy_load(g, slot):
             return pltpu.make_async_copy(dy_ref.at[g], dy_buf.at[slot], dy_sems.at[slot])
@@ -1303,22 +1337,10 @@
             wide_gates = []
             for i in range(n_bat):
                 inside = slice(i * x_ref.shape[0], (i + 1) * x_ref.shape[0])
-                wide_gates.append(
-                    lax.dot_general(
-                        gates_all[g, i],
-                        selected,
-                        (((0,), (0,)), ((), ())),
-                        precision=HIGHEST,
-                        preferred_element_type=F32,
-                    )
-                )
-                term_ref[g, i] = lax.dot_general(
-                    selected,
-                    product[inside, :],
-                    (((1,), (1,)), ((), ())),
-                    precision=HIGHEST,
-                    preferred_element_type=F32,
-                )
+                gates_two = jnp.concatenate(in_two(gates_all[g, i]), axis=0)
+                wide_gates.append(t_dot(gates_two, selected_twice))
+                high, low = in_two(product[inside, :])
+                term_ref[g, i] = dot_t(selected, high) + dot_t(selected, low)
             wide_gate = jnp.concatenate(wide_gates, axis=0)
             weighted_ref[at, :] = (active * wide_gate).astype(BF)
             grad_active = grad_back * wide_gate
@@ -1404,7 +1426,7 @@
 
 
 def experts_backward(
-    grad_pre, weighted, w_gu, terms, x_all, dy_all, residual, dy_own, gain_mlp, router, probs, chosen,
+    grad_pre, weighted, w_gu, terms, x_all, dy_all, residual, dy_own, gains, router, probs, chosen,
     local_experts, n_seq, n_bat,
 ):
     own = residual.shape[0]
@@ -1421,7 +1443,7 @@
 
     def kernel(*refs):
         grad_ref, weighted_ref, gu_ref, term_in, x_ref, dy_ref = refs[:6]
-        res_ref, own_dy_ref, gm_ref, router_ref, probs_ref, chosen_ref = refs[6:12]
+        res_ref, own_dy_ref, gains_ref, router_ref, probs_ref, chosen_ref = refs[6:12]
         out_ref, low_ref, small_ref, gate_out, up_out, down_out = refs[12:18]
         refs = refs[18:]
         away, twin, halves, full, line = refs[:5]
@@ -1444,17 +1466,31 @@
         def send(j):
             from_twin[j] = wire.push(away.at[j], twin.at[j], place.twin())
 
-        chunks = [("x", k) for k in list(range(1, n_seq)) + [0]] + [
-            ("y", k) for k in range(dim // 256)
-        ]
+        chunks = list(range(1, n_seq)) + [0]
 
         def chunk_load(n):
-            kind, k = chunks[n]
-            if kind == "x":
-                src = x_ref.at[:, pl.ds(pl.multiple_of(place.seq_at(k) * depth, depth), depth)]
-            else:
-                src = dy_ref.at[:, pl.ds(k * 256, 256)]
-            return pltpu.make_async_copy(src, columns.at[n % 2], column_sems.at[n % 2])
+            at = pl.ds(pl.multiple_of(place.seq_at(chunks[n]) * depth, depth), depth)
+            return pltpu.make_async_copy(x_ref.at[:, at], columns.at[n % 2], column_sems.at[n % 2])
+
+        def down_load(k):
+            slot = lax.rem(k, 2)
+            at = pl.ds(pl.multiple_of(k * 256, 256), 256)
+            return pltpu.make_async_copy(dy_ref.at[:, at], columns.at[slot], column_sems.at[slot])
+
+        def down_part(first, last):
+            down_load(first).start()
+
+            def one(k, carry):
+                @pl.when(k + 1 < last)
+                def _():
+                    down_load(k + 1).start()
+
+                down_load(k).wait()
+                at = pl.ds(pl.multiple_of(k * 256, 256), 256)
+                down_out[:, at] = t_dot(weighted_ref[...], columns[lax.rem(k, 2)])
+                return carry
+
+            lax.fori_loop(first, last, one, 0)
 
         chunk_load(0).start()
 
@@ -1474,22 +1510,17 @@
         def work_chunks(count):
             for n in range(done[0], min(done[0] + count, len(chunks))):
                 done[0] = n + 1
+                k = chunks[n]
                 if n + 1 < len(chunks):
                     chunk_load(n + 1).start()
                 chunk_load(n).wait()
-                kind, k = chunks[n]
-                if kind == "y":
-                    down_out[:, k * 256 : (k + 1) * 256] = t_dot(
-                        weighted_ref[...], columns[n % 2]
-                    )
+                value = t_dot(columns[n % 2], grad_ref[...]).astype(BF)
+                if k == 0:
+                    got[place.s] = value
                 else:
-                    value = t_dot(columns[n % 2], grad_ref[...]).astype(BF)
-                    if k == 0:
-                        got[place.s] = value
-                    else:
-                        sent[k] = value
-                if n and chunks[n - 1][0] == "x" and chunks[n - 1][1]:
-                    k = chunks[n - 1][1]
+                    sent[k] = value
+                if n:
+                    k = chunks[n - 1]
                     arrivals.append(wire.push(sent.at[k], got.at[place.s], place.seq_peer(k)))
 
         def pass_on(j):
@@ -1523,18 +1554,20 @@
             works[j].middle()
         for j in rest:
             works[j].start()
-        for j in term_order:
-            term_work.merge(j)
         for j in first:
             work_chunks(3)
             pass_on(j)
+        work_chunks(len(chunks))
+        for j in term_order:
+            term_work.merge(j)
         for j in rest:
-            work_chunks(1)
             works[j].middle()
-        for j in rest:
-            work_chunks(4)
+        cut = dim // 512
+        down_part(0, cut)
+        pass_on(rest[0])
+        down_part(cut, 2 * cut)
+        for j in rest[1:]:
             pass_on(j)
-        work_chunks(len(chunks))
         for copy in arrivals:
             copy.wait_recv()
         for i in range(n_seq):
@@ -1559,17 +1592,14 @@
         residual = res_ref[...]
         scale = rms_scale(residual)
         normal = residual * scale
-        normed = (normal * gm_ref[...]).astype(BF).astype(F32)
+        normed = (normal * gains_ref[3:4, :]).astype(BF)
         experts = probs.shape[0]
-        small_ref[0:experts, :] = lax.dot_general(
-            grad_logits, normed, (((1,), (0,)), ((), ())), precision=HIGHEST,
-            preferred_element_type=F32,
-        )
-        total = total + lax.dot_general(
-            grad_logits, router_ref[...], (((0,), (0,)), ((), ())), precision=HIGHEST,
-            preferred_element_type=F32,
-        )
-        grad, terms_of = rms_back(residual, scale, gm_ref[...], total)
+        logits_two = jnp.concatenate(in_two(grad_logits), axis=0)
+        products = dot(logits_two, normed)
+        small_ref[0:experts, :] = products[:experts] + products[experts:]
+        router = router_ref[...].astype(BF)
+        total = total + t_dot(logits_two, jnp.concatenate([router, router], axis=0))
+        grad, terms_of = rms_back(residual, scale, gains_ref[3:4, :], total)
         small_ref[experts + 3 : experts + 4, :] = jnp.sum(terms_of, axis=0, keepdims=True)
         grad = own_dy_ref[...].astype(F32) + grad
         out_ref[...] = grad
@@ -1606,7 +1636,7 @@
         "experts_backward",
         [vmem] * 3 + [ANY] * 3 + [vmem] * 6,
         [vmem] * 6,
-    )(grad_pre, weighted, w_gu, terms, x_all, dy_all, residual, dy_own, gain_mlp, router, probs, chosen)
+    )(grad_pre, weighted, w_gu, terms, x_all, dy_all, residual, dy_own, gains, router, probs, chosen)
 
 
 def store_last(grad_w, grad_wo, small, mixture, n_seq, n_bat):
@@ -1992,11 +2022,17 @@
         and n_seq == 8
         and shard == 64
         and experts == 8
+        and span == 64
+        and rows <= 8
         and n_seq * n_bat * own * dim <= 8 * 1024 * 1024
     )
     if fused:
-        w_qkv, w_o, x_col, flag_col, small_all = load_first(
-            (w_query, w_key, w_value), w_out, mine, flags, pack(small), rows, n_seq, n_bat
+        gains = jnp.stack([attn_gain, query_gain, key_gain, mlp_gain])
+        small = jnp.concatenate([w_router.T, jnp.pad(gains, ((0, 4), (0, 0)))], axis=1).astype(F32)
+        flags = (positions_own[None, :] < lengths[:, None]) & (key_mask == 1)
+        flags = jnp.pad(flags.astype(F32), ((0, 8 - rows), (0, 128 - span)))
+        w_qkv, w_o, x_col, router_t, gains, usable = load_first(
+            (w_query, w_key, w_value), w_out, mine, flags, small, rows, n_seq, n_bat
         )
     else:
         qkv_cut = jnp.stack([w_query, w_key, w_value]).reshape(3, shard, n_seq, wide)
@@ -2012,14 +2048,15 @@
     w_qkv = w_qkv.reshape(dim, 3 * wide)
     w_o = w_o.reshape(wide, dim)
     w_down = expert_down.reshape(local_experts * part, dim)
-    small_all = unpack(small_all, (n_seq, n_bat), small.shape)
-    small_all = jnp.transpose(small_all, (2, 0, 1, 3)).reshape(-1, dim)
-    router = small_all[:experts].T.astype(BF)
-    gain_attn, gain_mlp = small_all[experts], small_all[experts + 3]
-    gain_q = lax.dynamic_slice_in_dim(small_all[experts + 1], seq * wide, wide)
-    gain_k = lax.dynamic_slice_in_dim(small_all[experts + 2], seq * wide, wide)
-    usable = unpack(flag_col, (n_seq,), key_mask.shape)
-    usable = jnp.transpose(usable, (1, 0, 2)).reshape(rows, length)
+    if not fused:
+        small_all = unpack(small_all, (n_seq, n_bat), small.shape)
+        small_all = jnp.transpose(small_all, (2, 0, 1, 3)).reshape(-1, dim)
+        router = small_all[:experts].T.astype(BF)
+        gains = small_all[experts:]
+        gain_attn, gain_mlp = gains[0], gains[3]
+        usable = unpack(flag_col, (n_seq,), key_mask.shape)
+        usable = jnp.transpose(usable, (1, 0, 2)).reshape(rows, length)
+        router_t = small_all[:experts]
 
     expert_ids = jnp.arange(experts, dtype=jnp.int32)
     chosen_t = jnp.any(top_experts.reshape(own, -1).T[None] == expert_ids[:, None, None], axis=1)
@@ -2027,11 +2064,9 @@
     cos_part, sin_part = rotary_tables(jnp.arange(length, dtype=jnp.int32))
     cos_wide = jnp.concatenate([cos_part, cos_part], axis=1)
     sin_wide = jnp.concatenate([-sin_part, sin_part], axis=1)
-    gain_q, gain_k = gain_q[None, :], gain_k[None, :]
     hidden, qkv, q, k, v, mixed, stats, mixed_out, *extra = attend_forward(
-        x_col.reshape(col, dim), w_qkv, gain_attn[None, :], usable, w_o, gain_q, gain_k,
-        cos_wide, sin_wide, n_seq, n_bat, rows,
-        (dy_own, mine, gain_mlp[None, :], small_all[:experts], chosen_t) if fused else None,
+        x_col.reshape(col, dim), w_qkv, usable, w_o, gains, cos_wide, sin_wide, n_seq, n_bat, rows,
+        (dy_own, mine, router_t, chosen_t) if fused else None,
     )
     if not fused:
         x_own = mine.astype(F32)
@@ -2057,8 +2092,8 @@
             dy_all.reshape(-1, dim),
             residual,
             dy_own,
-            gain_mlp[None, :],
-            small_all[:experts],
+            gains,
+            router_t,
             probs_t,
             chosen_t,
             local_experts,
@@ -2124,9 +2159,9 @@
         grad_o = grad_residual.astype(BF)
 
     grad_w_o, grad_w, grad_gains, grad_hidden, *extra = attend_backward(
-        grad_o, q, k, v, mixed, qkv, stats, hidden, usable, w_o, w_qkv, gain_q, gain_k,
-        cos_wide, sin_wide, n_seq, n_bat,
-        (weighted, w_down, mine, grad_residual, gain_attn[None, :], small_grads) if fused else None,
+        grad_o, q, k, v, mixed, qkv, stats, hidden, usable, w_o, w_qkv, gains, cos_wide, sin_wide,
+        n_seq, n_bat,
+        (weighted, w_down, mine, grad_residual, small_grads) if fused else None,
     )
     grad_w_o = grad_w_o.reshape(n_bat, shard, dim)
     grad_w = grad_w.reshape(n_seq, n_bat, shard, 3 * wide)

time: 620 us -> 603 us (0.973)
  Pallas kernels: 595 us -> 585 us
  local copies, waits for them, and re-layouts: 10 us -> 2.87 us
where the time goes in v7:
time: 603 us; the launch traced here: 595 us
  Pallas kernels  585 us (97%)
  other arithmetic  6.04 us (1%)
    pallas_call x1, Pallas kernels, experts_backward(): comm_call(kernel, [jax.ShapeDtypeStruct((own, dim), F32), jax.ShapeDtypeS...  118 us
    pallas_call x1, Pallas kernels, experts_forward(): comm_call(kernel, [shape_of((n_seq, n_bat), normed), jax.ShapeDtypeStruct...  114 us
    pallas_call x1, Pallas kernels, attend_backward(): comm_call(kernel, [jax.ShapeDtypeStruct((wide, dim), BF), jax.ShapeDtypeS...  111 us
    pallas_call x1, Pallas kernels, attend_forward(): comm_call(kernel, outs + side_out, [pltpu.VMEM(stats.shape, F32), pltpu.V...  93.7 us
    pallas_call x1, Pallas kernels, store_last(): comm_call(kernel, [matrix] * 4 + [small_one, jax.ShapeDtypeStruct(mixture...  74.2 us
    pallas_call x1, Pallas kernels, load_first(): comm_call(kernel, [shape_of((n_seq, n_bat), one), shape_of((n_bat,), w_ou...  65.4 us

profile of v7, /device:TPU:9, one launch (start us, length us, event | category | flops | bytes accessed | tf_op | source)
XLA Modules:
  0.0 594.8 jit_solution(12635273206470612925)
XLA Ops:
  0.7 0.8 compare_and_fusion
  1.4 0.6 pad_convert_fusion.refs_5_
  2.0 0.7 fusion.8
  2.7 1.3 maximum_convert_fusion.refs_6_
  4.1 65.4 %load_first.1 = (bf16[8,4,64,768]{3,2,1,0:T(8,128)(2,1)}, bf16[4,64,2048]{2,1,0:T(8,128)(2,1)}, bf16[2,8,64,2048]{3,2,1,0:T(8,128)(2,1)}, f32[8,2048]{1,0:T(8,12...) custom-call(bf16[64,2048]{1,0:T(8,128)(2,1)} %refs_0_.1, bf16[64,2048]{1,0:T(8,128)(2,1)} %refs_1_.1, bf16[64,2048]{1,0:T(8,128)(2,1)} %refs_2_.1, ...), custom_call_target="tpu_custom_call" | custom-call | tf_op jit(solution)/shard_map/load_first/pallas_call | solution.py:1208
  69.5 0.0 copy-start
  69.5 1.0 fusion
  70.5 1.0 pad_maximum_fusion
  71.5 0.0 copy-done
  71.5 0.1 reshape.93
  71.6 0.6 convert_element_type.26.refs_10_.refs_11_
  72.2 93.7 %attend_forward.1 = (bf16[1024,2048]{1,0:T(8,128)(2,1)}, f32[1024,768]{1,0:T(8,128)}, bf16[2,2,512,128]{3,2,1,0:T(8,128)(2,1)}, bf16[2,2,512,128]{3,2,1,0:T(8,12...) custom-call(bf16[1024,2048]{1,0:T(8,128)(2,1)} %bitcast.43, ...), custom_call_target="tpu_custom_call" | custom-call | tf_op jit(solution)/shard_map/attend_forward/pallas_call | solution.py:745
  165.9 114.4 %experts_forward.1 = (bf16[8,4,128,2048]{3,2,1,0:T(8,128)(2,1)}, bf16[4096,256]{1,0:T(8,128)(2,1)}, bf16[4096,512]{1,0:T(8,128)(2,1)}, f32[8,4,8,128]{3,2,1,0:T(8,128)}, bf16[8,256,512]{2,1,0:T(8,128)(2,1)}) custom-call(bf16[128,2048]{1,0:T(8,128)(2,1)} %get-tuple-element.70.refs_0_, f32[8,128]{1,0:T(8,128)} %get-tuple-element.71.refs_1_, ...), custom_call_target="tpu_custom_call" | custom-call | tf_op jit(solution)/shard_map/experts_forward/pallas_call | solution.py:1399
  280.3 117.5 %experts_backward.1 = (f32[128,2048]{1,0:T(8,128)}, bf16[128,2048]{1,0:T(8,128)(2,1)}, f32[16,2048]{1,0:T(8,128)}, f32[2,256,1024]{2,1,0:T(8,128)}, f32[2,256,1024]{2,1,0:T(8,128)}, /*index=5*/f32[256,2048]{1,0:T(8,128)}) custom-call(bf16[4096,512]{1,0:T(8,128)(2,1)} %get-tuple-element.73.refs_0_, bf16[4096,256]{1,0:T(8,128)(2,1)} %get-tuple-element.74.refs_1_.refs_14_, ...), custom_call_target="tpu_custom_call" | custom-call | tf_op jit(solution)/shard_map/experts_backward/pallas_call | solution.py:1611
  397.8 110.6 %attend_backward.1 = (bf16[256,2048]{1,0:T(8,128)(2,1)}, bf16[2048,768]{1,0:T(8,128)(2,1)}, f32[2,256]{1,0:T(2,128)}, bf16[128,2048]{1,0:T(8,128)(2,1)}, bf16[4,...) custom-call(bf16[128,2048]{1,0:T(8,128)(2,1)} %get-tuple-element.79.refs_0_, ...), custom_call_target="tpu_custom_call" | custom-call | tf_op jit(solution)/shard_map/attend_backward/pallas_call | solution.py:1005
  508.4 74.2 %store_last.1 = (f32[64,2048]{1,0:T(8,128)}, f32[64,2048]{1,0:T(8,128)}, f32[64,2048]{1,0:T(8,128)}, f32[64,2048]{1,0:T(8,128)}, f32[16,128]{1,0:T(8,128)}, /*index=5*/f32[128,2048]{1,0:T(8,128)}) custom-call(bf16[8,4,64,768]{3,2,1,0:T(8,128)(2,1)} %bitcast.44, bf16[4,64,2048]{2,1,0:T(8,128)(2,1)} %bitcast.49, f32[16,2048]{1,0:T(8,128)} %get-tuple-element.91.refs_2_, ...), custom_call_target="tpu_custom_call" | custom-call | tf_op jit(solution)/shard_map/store_last/pallas_call | solution.py:1730
  582.6 9.0 %finish.1 = (bf16[128,2048]{1,0:T(8,128)(2,1)}, bf16[128,2048]{1,0:T(8,128)(2,1)}, f32[64,2048]{1,0:T(8,128)}, f32[64,2048]{1,0:T(8,128)}, f32[64,2048]{1,0:T(8,...) custom-call(f32[128,2048]{1,0:T(8,128)} %get-tuple-element.69.refs_6_.re, ...), custom_call_target="tpu_custom_call" | custom-call | tf_op jit(solution)/shard_map/finish/pallas_call | solution.py:1776
  591.6 1.4 dynamic-slice_bitcast_fusion.1
  593.0 1.3 dynamic-slice_bitcast_fusion
  (5 shorter events, 0.0 us)
Async XLA Ops:
  69.5 2.0 copy-start

commit v8 on v7

--- a/solution.py
+++ b/solution.py
@@ -2,6 +2,7 @@
 
 import jax
 import jax.numpy as jnp
+import numpy as np
 from jax import lax
 from jax.experimental import pallas as pl
 from jax.experimental.pallas import tpu as pltpu
@@ -38,11 +39,12 @@
     return scale * (weighted - normal * mean), grad * normal
 
 
-def rotary_tables(positions):
+def rotary_tables(length):
     half_head = HEAD // 2
-    frequency = 10000.0 ** (-2.0 * jnp.arange(half_head, dtype=F32) / HEAD)
-    angles = positions.astype(F32)[:, None] * frequency[None, :]
-    return jnp.cos(angles), jnp.sin(angles)
+    frequency = 10000.0 ** (-2.0 * np.arange(half_head, dtype=np.float32) / HEAD)
+    angles = np.arange(length, dtype=np.float32)[:, None] * frequency.astype(np.float32)[None, :]
+    cosines, sines = np.cos(angles), np.sin(angles)
+    return np.concatenate([cosines, cosines], axis=1), np.concatenate([-sines, sines], axis=1)
 
 
 ANY = pl.BlockSpec(memory_space=pl.ANY)
@@ -1514,14 +1516,16 @@
                 if n + 1 < len(chunks):
                     chunk_load(n + 1).start()
                 chunk_load(n).wait()
+                if n:
+                    last = chunks[n - 1]
+                    arrivals.append(
+                        wire.push(sent.at[last], got.at[place.s], place.seq_peer(last))
+                    )
                 value = t_dot(columns[n % 2], grad_ref[...]).astype(BF)
                 if k == 0:
                     got[place.s] = value
                 else:
                     sent[k] = value
-                if n:
-                    k = chunks[n - 1]
-                    arrivals.append(wire.push(sent.at[k], got.at[place.s], place.seq_peer(k)))
 
         def pass_on(j):
             works[j].finish()
@@ -1752,35 +1756,62 @@
 
 def finish(residual, mixture, grads):
     count = len(grads)
+    pieces = []
+    for i in sorted(range(count), key=lambda i: -grads[i].size):
+        large = grads[i].size >= 1 << 18 and grads[i].ndim == 3
+        pieces += [(i, k) for k in range(grads[i].shape[0])] if large else [(i, None)]
 
     def kernel(*refs):
         res_ref, mix_ref = refs[:2]
         ins, out_ref, outs = refs[2 : 2 + count], refs[2 + count], refs[3 + count : 3 + 2 * count]
-        buffers, sems = refs[3 + 2 * count : 3 + 3 * count], refs[-1]
+        refs = refs[3 + 2 * count :]
+        buffers, res_buf, mix_buf, out_buf, sems, own_sems = refs[:count], *refs[count:]
+
+        def piece(group, n):
+            i, k = pieces[n]
+            return group[i] if k is None else group[i].at[k]
+
         loads = []
-        for i in range(count):
-            copy = pltpu.make_async_copy(ins[i], buffers[i], sems.at[0, i])
+        for n in range(len(pieces)):
+            copy = pltpu.make_async_copy(piece(ins, n), piece(buffers, n), sems.at[0, n])
             copy.start()
             loads.append(copy)
-        out_ref[...] = (res_ref[...] + mix_ref[...]).astype(BF)
+            if n == 0:
+                first = pltpu.make_async_copy(res_ref, res_buf, own_sems.at[0])
+                second = pltpu.make_async_copy(mix_ref, mix_buf, own_sems.at[1])
+                first.start()
+                second.start()
         stores = []
-        for i in range(count):
-            loads[i].wait()
-            copy = pltpu.make_async_copy(buffers[i], outs[i], sems.at[1, i])
+        for n, load in enumerate(loads):
+            load.wait()
+            copy = pltpu.make_async_copy(piece(buffers, n), piece(outs, n), sems.at[1, n])
             copy.start()
             stores.append(copy)
+            if n == 0:
+                first.wait()
+                second.wait()
+                out_buf[...] = (res_buf[...] + mix_buf[...]).astype(BF)
+            if n == 1:
+                copy = pltpu.make_async_copy(out_buf, out_ref, own_sems.at[2])
+                copy.start()
+                stores.append(copy)
         for copy in stores:
             copy.wait()
 
-    vmem = pl.BlockSpec(memory_space=pltpu.VMEM)
     return pl.pallas_call(
         kernel,
         out_shape=[jax.ShapeDtypeStruct(residual.shape, BF)]
         + [jax.ShapeDtypeStruct(grad.shape, grad.dtype) for grad in grads],
-        in_specs=[vmem] * 2 + [ANY] * count,
-        out_specs=[vmem] + [ANY] * count,
+        in_specs=[ANY] * (2 + count),
+        out_specs=[ANY] * (1 + count),
         scratch_shapes=[pltpu.VMEM(grad.shape, grad.dtype) for grad in grads]
-        + [pltpu.SemaphoreType.DMA((2, count))],
+        + [
+            pltpu.VMEM(residual.shape, F32),
+            pltpu.VMEM(residual.shape, F32),
+            pltpu.VMEM(residual.shape, BF),
+            pltpu.SemaphoreType.DMA((2, len(pieces))),
+            pltpu.SemaphoreType.DMA((3,)),
+        ],
         compiler_params=pltpu.CompilerParams(vmem_limit_bytes=VMEM_LIMIT),
         name="finish",
     )(residual, mixture, *grads)
@@ -2061,9 +2092,7 @@
     expert_ids = jnp.arange(experts, dtype=jnp.int32)
     chosen_t = jnp.any(top_experts.reshape(own, -1).T[None] == expert_ids[:, None, None], axis=1)
     chosen_t = chosen_t.astype(F32)
-    cos_part, sin_part = rotary_tables(jnp.arange(length, dtype=jnp.int32))
-    cos_wide = jnp.concatenate([cos_part, cos_part], axis=1)
-    sin_wide = jnp.concatenate([-sin_part, sin_part], axis=1)
+    cos_wide, sin_wide = rotary_tables(length)
     hidden, qkv, q, k, v, mixed, stats, mixed_out, *extra = attend_forward(
         x_col.reshape(col, dim), w_qkv, usable, w_o, gains, cos_wide, sin_wide, n_seq, n_bat, rows,
         (dy_own, mine, router_t, chosen_t) if fused else None,

time: 603 us -> 598 us (level)
  no operation moved by 1% of the time
where the time goes in v8:
time: 598 us; the launch traced here: 591 us
  Pallas kernels  582 us (97%)
    pallas_call x1, Pallas kernels, experts_backward(): comm_call(kernel, [jax.ShapeDtypeStruct((own, dim), F32), jax.ShapeDtypeS...  116 us
    pallas_call x1, Pallas kernels, experts_forward(): comm_call(kernel, [shape_of((n_seq, n_bat), normed), jax.ShapeDtypeStruct...  114 us
    pallas_call x1, Pallas kernels, attend_backward(): comm_call(kernel, [jax.ShapeDtypeStruct((wide, dim), BF), jax.ShapeDtypeS...  111 us
    pallas_call x1, Pallas kernels, attend_forward(): comm_call(kernel, outs + side_out, [pltpu.VMEM(stats.shape, F32), pltpu.V...  93.7 us
    pallas_call x1, Pallas kernels, store_last(): comm_call(kernel, [matrix] * 4 + [small_one, jax.ShapeDtypeStruct(mixture...  74.2 us
    pallas_call x1, Pallas kernels, load_first(): comm_call(kernel, [shape_of((n_seq, n_bat), one), shape_of((n_bat,), w_ou...  65.4 us

profile of v8, /device:TPU:9, one launch (start us, length us, event | category | flops | bytes accessed | tf_op | source)
XLA Modules:
  0.0 591.1 jit_solution(15442688755708674466)
XLA Ops:
  0.7 0.8 compare_and_fusion
  1.4 0.6 pad_convert_fusion.refs_5_
  2.0 0.7 fusion.7
  2.7 1.3 maximum_convert_fusion.refs_6_
  4.1 65.4 %load_first.1 = (bf16[8,4,64,768]{3,2,1,0:T(8,128)(2,1)}, bf16[4,64,2048]{2,1,0:T(8,128)(2,1)}, bf16[2,8,64,2048]{3,2,1,0:T(8,128)(2,1)}, f32[8,2048]{1,0:T(8,12...) custom-call(bf16[64,2048]{1,0:T(8,128)(2,1)} %refs_0_.1, bf16[64,2048]{1,0:T(8,128)(2,1)} %refs_1_.1, bf16[64,2048]{1,0:T(8,128)(2,1)} %refs_2_.1, ...), custom_call_target="tpu_custom_call" | custom-call | tf_op jit(solution)/shard_map/load_first/pallas_call | solution.py:1210
  69.5 0.7 copy.35
  70.2 0.1 reshape.84
  70.3 0.6 convert_element_type.12.refs_10_.refs_11_
  70.9 93.7 %attend_forward.1 = (bf16[1024,2048]{1,0:T(8,128)(2,1)}, f32[1024,768]{1,0:T(8,128)}, bf16[2,2,512,128]{3,2,1,0:T(8,128)(2,1)}, bf16[2,2,512,128]{3,2,1,0:T(8,12...) custom-call(bf16[1024,2048]{1,0:T(8,128)(2,1)} %bitcast.43, ...), custom_call_target="tpu_custom_call" | custom-call | tf_op jit(solution)/shard_map/attend_forward/pallas_call | solution.py:747
  164.6 114.3 %experts_forward.1 = (bf16[8,4,128,2048]{3,2,1,0:T(8,128)(2,1)}, bf16[4096,256]{1,0:T(8,128)(2,1)}, bf16[4096,512]{1,0:T(8,128)(2,1)}, f32[8,4,8,128]{3,2,1,0:T(8,128)}, bf16[8,256,512]{2,1,0:T(8,128)(2,1)}) custom-call(bf16[128,2048]{1,0:T(8,128)(2,1)} %get-tuple-element.70.refs_0_, f32[8,128]{1,0:T(8,128)} %get-tuple-element.71.refs_1_, ...), custom_call_target="tpu_custom_call" | custom-call | tf_op jit(solution)/shard_map/experts_forward/pallas_call | solution.py:1401
  278.9 116.2 %experts_backward.1 = (f32[128,2048]{1,0:T(8,128)}, bf16[128,2048]{1,0:T(8,128)(2,1)}, f32[16,2048]{1,0:T(8,128)}, f32[2,256,1024]{2,1,0:T(8,128)}, f32[2,256,1024]{2,1,0:T(8,128)}, /*index=5*/f32[256,2048]{1,0:T(8,128)}) custom-call(bf16[4096,512]{1,0:T(8,128)(2,1)} %get-tuple-element.73.refs_0_, bf16[4096,256]{1,0:T(8,128)(2,1)} %get-tuple-element.74.refs_1_.refs_14_, ...), custom_call_target="tpu_custom_call" | custom-call | tf_op jit(solution)/shard_map/experts_backward/pallas_call | solution.py:1615
  395.1 110.6 %attend_backward.1 = (bf16[256,2048]{1,0:T(8,128)(2,1)}, bf16[2048,768]{1,0:T(8,128)(2,1)}, f32[2,256]{1,0:T(2,128)}, bf16[128,2048]{1,0:T(8,128)(2,1)}, bf16[4,...) custom-call(bf16[128,2048]{1,0:T(8,128)(2,1)} %get-tuple-element.79.refs_0_, ...), custom_call_target="tpu_custom_call" | custom-call | tf_op jit(solution)/shard_map/attend_backward/pallas_call | solution.py:1007
  505.7 74.2 %store_last.1 = (f32[64,2048]{1,0:T(8,128)}, f32[64,2048]{1,0:T(8,128)}, f32[64,2048]{1,0:T(8,128)}, f32[64,2048]{1,0:T(8,128)}, f32[16,128]{1,0:T(8,128)}, /*index=5*/f32[128,2048]{1,0:T(8,128)}) custom-call(bf16[8,4,64,768]{3,2,1,0:T(8,128)(2,1)} %bitcast.44, bf16[4,64,2048]{2,1,0:T(8,128)(2,1)} %bitcast.49, f32[16,2048]{1,0:T(8,128)} %get-tuple-element.91.refs_2_, ...), custom_call_target="tpu_custom_call" | custom-call | tf_op jit(solution)/shard_map/store_last/pallas_call | solution.py:1734
  579.9 8.0 %finish.1 = (bf16[128,2048]{1,0:T(8,128)(2,1)}, bf16[128,2048]{1,0:T(8,128)(2,1)}, f32[64,2048]{1,0:T(8,128)}, f32[64,2048]{1,0:T(8,128)}, f32[64,2048]{1,0:T(8,...) custom-call(f32[128,2048]{1,0:T(8,128)} %get-tuple-element.69.refs_6_.re, ...), custom_call_target="tpu_custom_call" | custom-call | tf_op jit(solution)/shard_map/finish/pallas_call | solution.py:1801
  587.9 1.4 dynamic-slice_bitcast_fusion.1
  589.3 1.3 dynamic-slice_bitcast_fusion
  (2 shorter events, 0.0 us)

commit v9 on v8

--- a/solution.py
+++ b/solution.py
@@ -2090,8 +2090,8 @@
         router_t = small_all[:experts]
 
     expert_ids = jnp.arange(experts, dtype=jnp.int32)
-    chosen_t = jnp.any(top_experts.reshape(own, -1).T[None] == expert_ids[:, None, None], axis=1)
-    chosen_t = chosen_t.astype(F32)
+    named = top_experts.reshape(own, -1).T[None] == expert_ids[:, None, None]
+    chosen_t = jnp.sum(named.astype(F32), axis=1)
     cos_wide, sin_wide = rotary_tables(length)
     hidden, qkv, q, k, v, mixed, stats, mixed_out, *extra = attend_forward(
         x_col.reshape(col, dim), w_qkv, usable, w_o, gains, cos_wide, sin_wide, n_seq, n_bat, rows,

time: 598 us -> 598 us (level)
  no operation moved by 1% of the time
where the time goes in v9:
time: 598 us; the launch traced here: 591 us
  Pallas kernels  582 us (97%)
    pallas_call x1, Pallas kernels, experts_backward(): comm_call(kernel, [jax.ShapeDtypeStruct((own, dim), F32), jax.ShapeDtypeS...  116 us
    pallas_call x1, Pallas kernels, experts_forward(): comm_call(kernel, [shape_of((n_seq, n_bat), normed), jax.ShapeDtypeStruct...  114 us
    pallas_call x1, Pallas kernels, attend_backward(): comm_call(kernel, [jax.ShapeDtypeStruct((wide, dim), BF), jax.ShapeDtypeS...  111 us
    pallas_call x1, Pallas kernels, attend_forward(): comm_call(kernel, outs + side_out, [pltpu.VMEM(stats.shape, F32), pltpu.V...  93.7 us
    pallas_call x1, Pallas kernels, store_last(): comm_call(kernel, [matrix] * 4 + [small_one, jax.ShapeDtypeStruct(mixture...  74.2 us
    pallas_call x1, Pallas kernels, load_first(): comm_call(kernel, [shape_of((n_seq, n_bat), one), shape_of((n_bat,), w_ou...  65.4 us

profile of v9, /device:TPU:9, one launch (start us, length us, event | category | flops | bytes accessed | tf_op | source)
XLA Modules:
  0.0 591.1 jit_solution(17574236163218209085)
XLA Ops:
  0.7 0.8 compare_and_fusion
  1.4 0.6 pad_convert_fusion.refs_5_
  2.0 0.7 fusion.6
  2.7 1.3 maximum_convert_fusion.refs_6_
  4.1 65.4 %load_first.1 = (bf16[8,4,64,768]{3,2,1,0:T(8,128)(2,1)}, bf16[4,64,2048]{2,1,0:T(8,128)(2,1)}, bf16[2,8,64,2048]{3,2,1,0:T(8,128)(2,1)}, f32[8,2048]{1,0:T(8,12...) custom-call(bf16[64,2048]{1,0:T(8,128)(2,1)} %refs_0_.1, bf16[64,2048]{1,0:T(8,128)(2,1)} %refs_1_.1, bf16[64,2048]{1,0:T(8,128)(2,1)} %refs_2_.1, ...), custom_call_target="tpu_custom_call" | custom-call | tf_op jit(solution)/shard_map/load_first/pallas_call | solution.py:1210
  69.5 0.7 copy.35
  70.2 0.1 reshape.84
  70.2 0.6 convert_reduce_fusion.refs_10_.refs_11_
  70.8 93.7 %attend_forward.1 = (bf16[1024,2048]{1,0:T(8,128)(2,1)}, f32[1024,768]{1,0:T(8,128)}, bf16[2,2,512,128]{3,2,1,0:T(8,128)(2,1)}, bf16[2,2,512,128]{3,2,1,0:T(8,12...) custom-call(bf16[1024,2048]{1,0:T(8,128)(2,1)} %bitcast.43, ...), custom_call_target="tpu_custom_call" | custom-call | tf_op jit(solution)/shard_map/attend_forward/pallas_call | solution.py:747
  164.6 114.3 %experts_forward.1 = (bf16[8,4,128,2048]{3,2,1,0:T(8,128)(2,1)}, bf16[4096,256]{1,0:T(8,128)(2,1)}, bf16[4096,512]{1,0:T(8,128)(2,1)}, f32[8,4,8,128]{3,2,1,0:T(8,128)}, bf16[8,256,512]{2,1,0:T(8,128)(2,1)}) custom-call(bf16[128,2048]{1,0:T(8,128)(2,1)} %get-tuple-element.70.refs_0_, f32[8,128]{1,0:T(8,128)} %get-tuple-element.71.refs_1_, ...), custom_call_target="tpu_custom_call" | custom-call | tf_op jit(solution)/shard_map/experts_forward/pallas_call | solution.py:1401
  278.9 116.2 %experts_backward.1 = (f32[128,2048]{1,0:T(8,128)}, bf16[128,2048]{1,0:T(8,128)(2,1)}, f32[16,2048]{1,0:T(8,128)}, f32[2,256,1024]{2,1,0:T(8,128)}, f32[2,256,1024]{2,1,0:T(8,128)}, /*index=5*/f32[256,2048]{1,0:T(8,128)}) custom-call(bf16[4096,512]{1,0:T(8,128)(2,1)} %get-tuple-element.73.refs_0_, bf16[4096,256]{1,0:T(8,128)(2,1)} %get-tuple-element.74.refs_1_.refs_14_, ...), custom_call_target="tpu_custom_call" | custom-call | tf_op jit(solution)/shard_map/experts_backward/pallas_call | solution.py:1615
  395.1 110.6 %attend_backward.1 = (bf16[256,2048]{1,0:T(8,128)(2,1)}, bf16[2048,768]{1,0:T(8,128)(2,1)}, f32[2,256]{1,0:T(2,128)}, bf16[128,2048]{1,0:T(8,128)(2,1)}, bf16[4,...) custom-call(bf16[128,2048]{1,0:T(8,128)(2,1)} %get-tuple-element.79.refs_0_, ...), custom_call_target="tpu_custom_call" | custom-call | tf_op jit(solution)/shard_map/attend_backward/pallas_call | solution.py:1007
  505.7 74.2 %store_last.1 = (f32[64,2048]{1,0:T(8,128)}, f32[64,2048]{1,0:T(8,128)}, f32[64,2048]{1,0:T(8,128)}, f32[64,2048]{1,0:T(8,128)}, f32[16,128]{1,0:T(8,128)}, /*index=5*/f32[128,2048]{1,0:T(8,128)}) custom-call(bf16[8,4,64,768]{3,2,1,0:T(8,128)(2,1)} %bitcast.44, bf16[4,64,2048]{2,1,0:T(8,128)(2,1)} %bitcast.49, f32[16,2048]{1,0:T(8,128)} %get-tuple-element.91.refs_2_, ...), custom_call_target="tpu_custom_call" | custom-call | tf_op jit(solution)/shard_map/store_last/pallas_call | solution.py:1734
  579.9 8.0 %finish.1 = (bf16[128,2048]{1,0:T(8,128)(2,1)}, bf16[128,2048]{1,0:T(8,128)(2,1)}, f32[64,2048]{1,0:T(8,128)}, f32[64,2048]{1,0:T(8,128)}, f32[64,2048]{1,0:T(8,...) custom-call(f32[128,2048]{1,0:T(8,128)} %get-tuple-element.69.refs_6_.re, ...), custom_call_target="tpu_custom_call" | custom-call | tf_op jit(solution)/shard_map/finish/pallas_call | solution.py:1801
  587.9 1.4 dynamic-slice_bitcast_fusion.1
  589.3 1.3 dynamic-slice_bitcast_fusion
  (1 shorter events, 0.0 us)
